TPU v7x, 256 devices: a whole 4x4x8 slice. The times are simulated.
256 devices in a mesh: dp: 4 (over y), expert: 64 (over x, z, core).
Axes of the slice: x: 4, y: 4, z: 8, core: 2. Of those that a mesh axis runs over, the one named last changes fastest.
Arguments:
- unit_codes: bfloat16 [128, 256, 1536], P('expert', 'dp'), may hold values from -4 to 4
- block_scales: float32 [128, 12, 256], P('expert', None, 'dp'), may hold values from 0.05 to 2
- pair_list: int32 [2048, 2], replicated, may hold values from 0 to 127, as said below
Outputs:
- left_best: float32 [64, 32, 1536], P('expert', None, 'dp')
- right_best: float32 [64, 32, 1536], P('expert', None, 'dp')
Inputs may be any that keep to these rules, and one draw needn't show every extreme that they name: `pair_list`: row 32 * e + s names as its first expert one of 2 * e to 2 * e + 1, and as its second one of the 2 experts starting at 2 * ((e + o_s) mod n), with n = 64; the offsets o_s are nonzero, distinct over s, include 1, n / 2 and n - 1, and are the same for every e.
All inputs are finite; a program needn't handle non-finite values.
Results may differ from a plain program's by a relative error of at most 0.0017.
Values may be sent and summed in bfloat16 or wider, within the bound.
No kernel may reach another device: no remote copies, remote signals or barrier semaphores. Data moves between devices by JAX's collectives and lax.ppermute only.
A program may use at most 128 MiB of HBM per device.

v0:
```python
import math

import jax
import jax.numpy as jnp
from jax import lax
from jax.sharding import PartitionSpec as P

EPSILON = 1e-06


def body(unit_codes, block_scales, pair_list):
    num_devices = lax.axis_size("expert")
    groups = lax.axis_size("dp")
    my_index = lax.axis_index("expert")
    dp_index = lax.axis_index("dp")
    per_device, row_count, unit_count = unit_codes.shape
    num_blocks = block_scales.shape[1]
    block_len = unit_count // num_blocks
    slice_width = unit_count // groups
    factor = jnp.transpose(block_scales, (0, 2, 1))[:, :, :, None]
    acts = (
        unit_codes.astype(jnp.float32).reshape(per_device, row_count, num_blocks, block_len)
        * factor
    )
    acts = acts.reshape(per_device, row_count, unit_count).astype(jnp.bfloat16)
    slot_count = pair_list.shape[0] // num_devices
    pair_table = pair_list.reshape(num_devices, slot_count, 2)
    my_pairs = lax.dynamic_index_in_dim(pair_table, my_index, 0, keepdims=False)
    left_local = my_pairs[:, 0] % per_device
    right_dev = my_pairs[:, 1] // per_device
    is_asked = pair_table[:, :, 1] // per_device == my_index
    chosen = jnp.sum(jnp.where(is_asked, pair_table[:, :, 1] % per_device, 0), axis=1)
    in_use = jnp.any(is_asked, axis=1)
    chooser = ((chosen[:, None] == jnp.arange(per_device)[None, :]) & in_use[:, None]).astype(
        jnp.bfloat16
    )
    own_full = lax.all_gather(acts, "dp", axis=1, tiled=True)
    flattened = acts.reshape(per_device, -1)
    outbound = jnp.dot(chooser, flattened, preferred_element_type=jnp.float32).astype(jnp.bfloat16)
    received = lax.all_to_all(
        outbound.reshape((num_devices,) + acts.shape[1:]),
        "expert",
        split_axis=0,
        concat_axis=0,
        tiled=True,
    )
    wanted = jnp.take(received, right_dev, axis=0)
    partner = lax.all_to_all(wanted, "dp", split_axis=2, concat_axis=1, tiled=True)
    all_rows = partner.shape[1]
    own_square = (
        jnp.einsum("era,era->ea", own_full, own_full, preferred_element_type=jnp.float32) / all_rows
    )
    inv_own = 1.0 / jnp.sqrt(own_square + EPSILON)
    part_square = (
        jnp.einsum("srb,srb->sb", partner, partner, preferred_element_type=jnp.float32) / all_rows
    )
    inv_part = 1.0 / jnp.sqrt(part_square + EPSILON)

    def single(member):
        expert_pick, partner_block, inv_unit = member
        left_rows = jnp.take(own_full, expert_pick, axis=0)
        gram_block = jnp.einsum(
            "ra,rb->ab", left_rows, partner_block, preferred_element_type=jnp.float32
        )
        correlation = (
            gram_block
            / all_rows
            * jnp.take(inv_own, expert_pick, axis=0)[:, None]
            * inv_unit[None, :]
        )
        return (jnp.max(correlation, axis=1), jnp.max(correlation, axis=0))

    def several(member):
        return jax.vmap(single)(member)

    bundle = math.gcd(slot_count, 4)
    stacked = (
        left_local.reshape(-1, bundle),
        partner.reshape(-1, bundle, all_rows, slice_width),
        inv_part.reshape(-1, bundle, slice_width),
    )
    left_part, right_part = lax.map(several, stacked)
    left_part = left_part.reshape(slot_count, unit_count)
    right_part = right_part.reshape(slot_count, slice_width)
    left_all = lax.pmax(left_part, "dp")
    left_out = lax.dynamic_slice_in_dim(left_all, dp_index * slice_width, slice_width, 1)
    target = (right_dev[:, None] == jnp.arange(num_devices)[None, :]).astype(jnp.float32)
    outgoing = jnp.dot(
        target.T, right_part, precision=lax.Precision.HIGHEST, preferred_element_type=jnp.float32
    )
    returned = lax.all_to_all(outgoing, "expert", split_axis=0, concat_axis=0, tiled=True)
    offsets = pair_table[0, :, 1] // per_device
    source_dev = (my_index - offsets) % num_devices
    right_out = jnp.take(returned, source_dev, axis=0)
    return (left_out[None], right_out[None])


def solution(mesh):
    in_specs = (P("expert", "dp", None), P("expert", None, "dp"), P())
    out_specs = (P("expert", None, "dp"), P("expert", None, "dp"))
    return jax.shard_map(body, mesh=mesh, in_specs=in_specs, out_specs=out_specs, check_vma=False)
```

profile of v0, /device:TPU:32, one launch (start us, length us, event | category | flops | bytes accessed | tf_op | source)
XLA Modules:
  0.0 609.3 jit_solution(17279301070880780680)
XLA Ops:
  7.2 0.8 reshape.236
  8.0 0.8 copy.28
  8.8 0.3 mul.36
  9.1 0.1 mul.37
  9.2 1.1 multiply_convert_fusion
  10.3 0.4 copy.52
  10.7 0.1 fusion.29
  10.9 0.1 fusion.15
  11.0 3.7 convolution_convert_fusion
  14.7 7.1 %copy.53 = bf16[8,8,64,1536]{3,2,1,0:T(8,128)(2,1)} copy(bf16[8,8,64,1536]{3,1,2,0:T(8,128)(2,1)S(1)} %bitcast.117) | data formatting | bytes 25165824
  21.8 11.8 %all-to-all-start = ((bf16[64,64,1536]{2,1,0:T(8,128)(2,1)}), bf16[64,64,1536]{2,1,0:T(8,128)(2,1)}, u32[]{:S(2)}, u32[]{:S(2)}) async-start(bf16[64,64,1536]{2,1,0:T(8,128)(2,1)} %bitcast.116), calls=%async_computation | async-start | bytes 25165824 | tf_op jit(solution)/shard_map/all_to_all | solution.py:40
  33.6 273.5 %all-to-all-done = bf16[64,64,1536]{2,1,0:T(8,128)(2,1)} async-done(((bf16[64,64,1536]{2,1,0:T(8,128)(2,1)}), bf16[64,64,1536]{2,1,0:T(8,128)(2,1)}, u32[]{:S(2)}, u32[]{:S(2)}) %all-to-all-start) | async-done | bytes 12582944 | tf_op jit(solution)/shard_map/all_to_all | solution.py:40
  307.2 8.1 %gather_fusion.2 = bf16[32,64,1536]{2,1,0:T(8,128)(2,1)} fusion(bf16[64,64,1536]{2,1,0:T(8,128)(2,1)} %all-to-all-done, s32[1024]{0:T(1024)S(1)} %pad_clamp_fusion.2), kind=kCustom, calls=%fused_computation.2 | custom fusion | bytes 12583040 | tf_op jit(solution)/shard_map/jit(_take)/gather | solution.py:47
  315.3 6.1 broadcast_select_fusion
  321.4 18.4 %copy.29 = bf16[32,64,1536]{1,0,2:T(8,128)(2,1)} copy(bf16[32,64,1536]{2,1,0:T(8,128)(2,1)} %broadcast_select_fusion) | data formatting | bytes 12582912 | tf_op jit(solution)/shard_map/jit(_take)/select_n | solution.py:47
  339.8 12.8 %reshape.286 = bf16[4,2,393216]{2,1,0:T(2,128)(2,1)} reshape(bf16[1536,32,64]{2,1,0:T(8,128)(2,1)} %bitcast.118) | data formatting | bytes 12582912
  352.6 5.3 all-to-all-start.1
  357.9 0.2 all-gather.2.cloned.1.call-start
  358.1 0.5 all-gather.2.cloned.1.call-update
  358.7 0.1 squeeze.30
  358.8 43.0 %all-gather.2.cloned.1.call-done = bf16[2,256,1536]{2,1,0:T(8,128)(2,1)} async-done(((bf16[2,64,1536]{2,1,0:T(8,128)(2,1)}), bf16[2,256,1536]{2,1,0:T(8,128)(2,1)}) %all-gather.2.cloned.1.call-update) | async-done | bytes 1572880 | tf_op jit(solution)/shard_map/all_gather | solution.py:37
  401.8 1.7 fusion.12
  403.5 39.6 %all-to-all-done.1 = bf16[4,2,393216]{2,1,0:T(2,128)(2,1)} async-done(((bf16[4,2,393216]{2,1,0:T(2,128)(2,1)}), bf16[4,2,393216]{2,1,0:T(2,128)(2,1)}, u32[]{:S(2)}, u32[]{:S(2)}) %all-to-all-start.1) | async-done | bytes 6291488 | tf_op jit(solution)/shard_map/all_to_all | solution.py:48
  443.1 12.6 %reshape.287 = bf16[1536,32,64]{2,1,0:T(8,128)(2,1)} reshape(bf16[4,2,393216]{2,1,0:T(2,128)(2,1)} %all-to-all-done.1) | data formatting | bytes 12582912
  455.7 15.1 %copy.45 = bf16[32,64,4,384]{3,2,1,0:T(4,128)(2,1)} copy(bf16[32,64,4,384]{1,0,3,2:T(8,128)(2,1)} %bitcast.119) | data formatting | bytes 12582912 | tf_op jit(solution)/shard_map/all_to_all | solution.py:48
  470.8 4.3 copy.31
  475.2 2.7 copy-done.1
  477.8 1.9 fusion.11
  479.8 64.2 %while.12 = (s32[]{:T(128)}, f32[8,4,1536]{2,1,0:T(4,128)S(1)}, f32[8,4,384]{2,1,0:T(4,128)S(1)}, s32[8,4]{1,0:T(8,128)S(1)}, bf16[2,256,1536]{2,1,0:T(8,128)(2,...) while((s32[]{:T(128)}, f32[8,4,1536]{2,1,0:T(4,128)S(1)}, ...), condition=%wide.region_5.6_spmd, body=%wide.region_2.5_spmd.sunk | while | flops 1218975232 | bytes 10461917 | solution.py:82
  479.8 0.6 gather_fusion
  480.5 2.4 gather_fusion.1
  483.0 4.8 fusion.37
  487.9 0.6 gather_fusion
  488.5 2.4 gather_fusion.1
  491.0 4.8 fusion.37
  495.9 0.6 gather_fusion
  496.5 0.1 select_multiply_fusion.2
  496.6 2.4 gather_fusion.1
  499.0 4.8 fusion.37
  503.9 0.6 gather_fusion
  504.5 0.1 select_multiply_fusion.2
  504.6 2.4 gather_fusion.1
  507.0 4.8 fusion.37
  512.0 0.6 gather_fusion
  512.6 2.4 gather_fusion.1
  515.1 4.8 fusion.37
  520.0 0.6 gather_fusion
  520.6 2.4 gather_fusion.1
  523.1 4.8 fusion.37
  528.0 0.6 gather_fusion
  528.7 2.4 gather_fusion.1
  531.1 4.8 fusion.37
  536.0 0.6 gather_fusion
  536.7 2.4 gather_fusion.1
  539.1 4.8 fusion.37
  544.0 0.3 convolution_bitcast_fusion
  544.4 0.7 copy.33
  545.1 6.8 %all-to-all-start.2 = ((f32[64,1,384]{2,1,0:T(1,128)}), f32[64,1,384]{2,1,0:T(1,128)S(1)}, u32[]{:S(2)}, u32[]{:S(2)}) async-start(f32[64,1,384]{2,1,0:T(1,128)} %copy.33), calls=%async_computation.2 | async-start | bytes 196608 | tf_op jit(solution)/shard_map/all_to_all | solution.py:91
  551.9 0.7 reshape.241
  552.7 8.7 %all-to-all-done.2 = f32[64,1,384]{2,1,0:T(1,128)S(1)} async-done(((f32[64,1,384]{2,1,0:T(1,128)}), f32[64,1,384]{2,1,0:T(1,128)S(1)}, u32[]{:S(2)}, u32[]{:S(2)}) %all-to-all-start.2) | async-done | bytes 98336 | tf_op jit(solution)/shard_map/all_to_all | solution.py:91
  561.4 0.6 gather_fusion.3
  562.0 0.7 bitcast_select_fusion
  562.7 38.4 %all-reduce.2.cloned.1.call-done = f32[32,1536]{1,0:T(8,128)} async-done(((f32[32,1536]{1,0:T(8,128)}), f32[32,1536]{1,0:T(8,128)}) %all-reduce.2.cloned.1.call-update) | async-done | bytes 196624 | tf_op jit(solution)/shard_map/pmax | solution.py:85
  601.1 1.4 dynamic-slice_bitcast_fusion.1
  (77 shorter events, 1.2 us)
Async XLA Ops:
  10.3 4.4 copy-start.2
  21.8 285.4 %all-to-all-start = ((bf16[64,64,1536]{2,1,0:T(8,128)(2,1)}), bf16[64,64,1536]{2,1,0:T(8,128)(2,1)}, u32[]{:S(2)}, u32[]{:S(2)}) async-start(bf16[64,64,1536]{2,1,0:T(8,128)(2,1)} %bitcast.116), calls=%async_computation | async-start | bytes 25165824 | tf_op jit(solution)/shard_map/all_to_all | solution.py:40
  352.6 90.5 %all-to-all-start.1 = ((bf16[4,2,393216]{2,1,0:T(2,128)(2,1)}), bf16[4,2,393216]{2,1,0:T(2,128)(2,1)}, u32[]{:S(2)}, u32[]{:S(2)}) async-start(bf16[4,2,393216]{2,1,0:T(2,128)(2,1)} %reshape.286), calls=%async_computation.1 | async-start | bytes 12582912 | tf_op jit(solution)/shard_map/all_to_all | solution.py:48
  357.9 43.9 %all-gather.2.cloned.1.call-start = ((), (), s32[]{:S(2)}) async-start(), calls=%async_computation.3 | async-start | bytes 1966080 | tf_op jit(solution)/shard_map/all_gather | solution.py:37
  475.1 2.7 copy-start.1
  477.8 2.0 copy-start
  545.1 16.3 %all-to-all-start.2 = ((f32[64,1,384]{2,1,0:T(1,128)}), f32[64,1,384]{2,1,0:T(1,128)S(1)}, u32[]{:S(2)}, u32[]{:S(2)}) async-start(f32[64,1,384]{2,1,0:T(1,128)} %copy.33), calls=%async_computation.2 | async-start | bytes 196608 | tf_op jit(solution)/shard_map/all_to_all | solution.py:91
  551.9 49.2 %all-reduce.2.cloned.1.call-start = ((), (), s32[]{:S(2)}) async-start(), calls=%async_computation.4 | async-start | bytes 393216 | tf_op jit(solution)/shard_map/pmax | solution.py:85
Sparse Core Ops, SparseCore 0:
  360.5 41.1 all-gather.1
  555.0 45.9 all-reduce.1
where the time goes:
time: 611 us; the launch traced here: 609 us
  waiting for transfers between devices  404 us (66%)
  local copies, waits for them, and re-layouts  112 us (18%)
  matrix products  42.6 us (7%)
  starting transfers between devices  24.1 us (4%)
  between operations  14.3 us (2%)
  other arithmetic  12.7 us (2%)
    all_to_all x1, waiting for transfers between devices, body(): lax.all_to_all(outbound.reshape((num_devices,) + acts.shape[1:]), 'expert...  274 us
    all_gather x1, waiting for transfers between devices, body(): own_full = lax.all_gather(acts, 'dp', axis=1, tiled=True)  43 us
    all_to_all x1, waiting for transfers between devices, body(): lax.all_to_all(wanted, 'dp', split_axis=2, concat_axis=1, tiled=True)  39.6 us
    dot_general x8, matrix products, single(): jnp.einsum('ra,rb->ab', left_rows, partner_block, preferred_element_type=...  38.6 us
    pmax x1, waiting for transfers between devices, body(): left_all = lax.pmax(left_part, 'dp')  38.4 us
    unnamed x11, local copies, waits for them, and re-layouts  35.6 us
    gather x8, local copies, waits for them, and re-layouts, single(): left_rows = jnp.take(own_full, expert_pick, axis=0)  19.6 us
    all_to_all x2, local copies, waits for them, and re-layouts, body(): lax.all_to_all(wanted, 'dp', split_axis=2, concat_axis=1, tiled=True)  19.4 us
  transfers between devices with their start and end apart: 5, of which 5 were waited for; matrix products, arithmetic and copies ran while one was open for 1% of the time, Pallas kernels for 0%

commit v1 on v0

v1 whole, which is shorter than its diff:
```python
import math

import jax
import jax.numpy as jnp
import numpy as np
from jax import lax
from jax.experimental import pallas as pl
from jax.experimental.pallas import tpu as pltpu
from jax.sharding import Mesh
from jax.sharding import PartitionSpec as P

EPSILON = 1e-06

NX, NZ, NC, NY = 4, 8, 2, 4
NDEV = NX * NZ * NC
PER = 2
ROWS = 256
RB = ROWS // NY
UNITS = 1536
SLICES = NX * NY
WIDTH = UNITS // SLICES
QUARTER = UNITS // NY
SLOTS = 32
PAIRS = NX * SLOTS
LEFTS = NX * PER
BLOCK = 128
GROUP = 8
TILE = 256

VMEM = pl.BlockSpec(memory_space=pltpu.VMEM)
ANY = pl.BlockSpec(memory_space=pl.ANY)


def prepare(codes, scales):
    def kernel(codes_ref, scales_ref, acts_ref, slices_ref):
        column = [jnp.transpose(scales_ref[h]) for h in range(PER)]
        for k in range(UNITS // BLOCK):
            lanes = slice(k * BLOCK, (k + 1) * BLOCK)
            both = []
            for h in range(PER):
                value = codes_ref[h, :, lanes].astype(jnp.float32) * column[h][:, k : k + 1]
                rounded = value.astype(jnp.bfloat16)
                acts_ref[h, :, lanes] = rounded
                both.append(rounded.astype(jnp.float32))
            turned = jnp.transpose(jnp.concatenate(both, axis=0)).astype(jnp.bfloat16)
            done = 0
            while done < BLOCK:
                unit = k * BLOCK + done
                take = min(BLOCK - done, WIDTH - unit % WIDTH)
                slices_ref[unit // WIDTH, unit % WIDTH : unit % WIDTH + take, :] = turned[
                    done : done + take
                ]
                done += take

    return pl.pallas_call(
        kernel,
        in_specs=[VMEM, VMEM],
        out_specs=[VMEM, VMEM],
        out_shape=[
            jax.ShapeDtypeStruct((PER, RB, UNITS), jnp.bfloat16),
            jax.ShapeDtypeStruct((SLICES, WIDTH, PER * RB), jnp.bfloat16),
        ],
        name="prepare",
    )(codes, scales)


def normalise(pieces):
    def kernel(in_ref, out_ref):
        for x in range(NX):
            part = [in_ref[y * NX + x].astype(jnp.float32) for y in range(NY)]
            for h in range(PER):
                lanes = slice(h * RB, (h + 1) * RB)
                full = jnp.concatenate([p[:, lanes] for p in part], axis=1)
                square = jnp.sum(full * full, axis=1, keepdims=True) / ROWS
                inverse = 1.0 / jnp.sqrt(square + EPSILON)
                out_ref[x * PER + h] = (full * (inverse * (1.0 / ROWS))).astype(jnp.bfloat16)

    return pl.pallas_call(
        kernel,
        in_specs=[VMEM],
        out_specs=VMEM,
        out_shape=jax.ShapeDtypeStruct((LEFTS, WIDTH, ROWS), jnp.bfloat16),
        name="normalise",
    )(pieces)


def correlate(start, order, jidx, lpos, rpos, gathered, chunks, places):
    count = len(chunks)

    def kernel(start_ref, order_ref, jidx_ref, lpos_ref, rpos_ref, *refs):
        gathered_ref = refs[0]
        chunk_refs = refs[1 : 1 + count]
        left_ref, right_ref, acts, others, inv, sem = refs[1 + count :]
        copies = []
        for x in range(NX):
            for y in range(NY):
                copies.append(
                    pltpu.make_async_copy(
                        gathered_ref.at[x * NY + y],
                        acts.at[pl.ds(x * PER, PER), pl.ds(y * RB, RB), :],
                        sem.at[len(copies)],
                    )
                )
        for ref, (at, size) in zip(chunk_refs, places):
            copies.append(
                pltpu.make_async_copy(ref, others.at[pl.ds(at, size)], sem.at[len(copies)])
            )
        for copy in copies:
            copy.start()
        right_ref[...] = jnp.zeros_like(right_ref)
        for copy in copies[: NX * NY]:
            copy.wait()

        def norm(i, carry):
            for n in range(UNITS // TILE):
                lanes = slice(n * TILE, (n + 1) * TILE)
                value = acts[i, :, lanes].astype(jnp.float32)
                square = jnp.sum(value * value, axis=0, keepdims=True) / ROWS
                inv[pl.ds(i, 1), lanes] = 1.0 / jnp.sqrt(square + EPSILON)
            return carry

        lax.fori_loop(0, LEFTS, norm, 0)
        for copy in copies[NX * NY :]:
            copy.wait()

        def expert(i, carry):
            low = start_ref[i]
            high = start_ref[i + 1]
            scales = inv[pl.ds(i, 1), :]

            def block(b, carry):
                pairs = [
                    order_ref[jnp.minimum(low + b * GROUP + g, high - 1)] for g in range(GROUP)
                ]
                lhs = jnp.concatenate([others[jidx_ref[p]] for p in pairs], axis=0)
                best = [None] * GROUP
                tops = [[] for _ in range(GROUP)]
                for n in range(UNITS // TILE):
                    out = jnp.dot(
                        lhs,
                        acts[i, :, n * TILE : (n + 1) * TILE],
                        preferred_element_type=jnp.float32,
                    )
                    for g in range(GROUP):
                        one = out[g * WIDTH : (g + 1) * WIDTH]
                        for m in range(TILE // 128):
                            unit = n * TILE + m * 128
                            scale = scales[:, unit : unit + 128]
                            part = one[:, m * 128 : (m + 1) * 128]
                            tops[g].append(jnp.max(part, axis=0, keepdims=True) * scale)
                            if (unit + 128) % QUARTER == 0:
                                row = lpos_ref[pairs[g]] + (unit // QUARTER) * SLOTS
                                left_ref[pl.ds(row, 1), :] = jnp.concatenate(tops[g], axis=1)
                                tops[g] = []
                            scaled = part * scale
                            best[g] = scaled if best[g] is None else jnp.maximum(best[g], scaled)
                for g in range(GROUP):
                    top = jnp.max(jnp.transpose(best[g]), axis=0, keepdims=True)
                    right_ref[pl.ds(rpos_ref[pairs[g]], 1), :] = top
                return carry

            lax.fori_loop(0, (high - low + GROUP - 1) // GROUP, block, 0)
            return carry

        lax.fori_loop(0, LEFTS, expert, 0)

    return pl.pallas_call(
        kernel,
        grid_spec=pltpu.PrefetchScalarGridSpec(
            num_scalar_prefetch=5,
            grid=(1,),
            in_specs=[ANY] * (1 + count),
            out_specs=[VMEM, VMEM],
            scratch_shapes=[
                pltpu.VMEM((LEFTS, ROWS, UNITS), jnp.bfloat16),
                pltpu.VMEM((NZ * NC * LEFTS, WIDTH, ROWS), jnp.bfloat16),
                pltpu.VMEM((LEFTS, UNITS), jnp.float32),
                pltpu.SemaphoreType.DMA((NX * NY + count,)),
            ],
        ),
        out_shape=[
            jax.ShapeDtypeStruct((NX * NY * SLOTS, QUARTER), jnp.float32),
            jax.ShapeDtypeStruct((NDEV * NX, WIDTH), jnp.float32),
        ],
        compiler_params=pltpu.CompilerParams(vmem_limit_bytes=48 << 20),
        name="correlate",
    )(start, order, jidx, lpos, rpos, gathered, *chunks)


def finish_right(rows, returned):
    def kernel(rows_ref, in_ref, out_ref):
        for s in range(SLOTS):
            for x in range(NX):
                out_ref[s : s + 1, x * WIDTH : (x + 1) * WIDTH] = in_ref[x, pl.ds(rows_ref[s], 1), :]

    return pl.pallas_call(
        kernel,
        grid_spec=pltpu.PrefetchScalarGridSpec(
            num_scalar_prefetch=1, grid=(1,), in_specs=[VMEM], out_specs=VMEM
        ),
        out_shape=jax.ShapeDtypeStruct((SLOTS, QUARTER), jnp.float32),
        name="finish_right",
    )(rows, returned)


def shift(value, axis, by, size):
    return lax.ppermute(value, axis, [(i, (i + by) % size) for i in range(size)])


def swap(value):
    return lax.ppermute(value, "core", [(0, 1), (1, 0)])


def body(unit_codes, block_scales, pair_list):
    x = lax.axis_index("x")
    z = lax.axis_index("z")
    c = lax.axis_index("core")
    me = (x * NZ + z) * NC + c

    table = pair_list.reshape(NX, NZ * NC, SLOTS, 2)
    mine = lax.dynamic_index_in_dim(table, z * NC + c, 1, keepdims=False).reshape(PAIRS, 2)
    pair = jnp.arange(PAIRS, dtype=jnp.int32)
    left_index = (pair // SLOTS) * PER + mine[:, 0] % PER
    right_dev = mine[:, 1] // PER
    right_x = right_dev // (NZ * NC)
    right_z = (right_dev // NC) % NZ
    right_c = right_dev % NC
    jidx = (((right_c != c) * NZ + (right_z - z) % NZ) * NX + right_x) * PER + mine[:, 1] % PER
    before = (left_index[None, :] < left_index[:, None]) | (
        (left_index[None, :] == left_index[:, None]) & (pair[None, :] < pair[:, None])
    )
    rank = jnp.sum(before, axis=1, dtype=jnp.int32)
    order = jnp.sum(jnp.where(rank[None, :] == pair[:, None], pair[None, :], 0), axis=1)
    start = jnp.sum(
        left_index[None, :] < jnp.arange(LEFTS + 1, dtype=jnp.int32)[:, None],
        axis=1,
        dtype=jnp.int32,
    )
    lpos = (pair // SLOTS) * (NY * SLOTS) + pair % SLOTS
    rpos = right_dev * NX + pair // SLOTS
    offsets = pair_list[:SLOTS, 1] // PER
    source = (me - offsets) % NDEV
    rows = (source % (NZ * NC)) * NX + source // (NZ * NC)

    acts, slices = prepare(unit_codes, block_scales)
    gathered = lax.all_gather(acts, ("x", "dp"), axis=0, tiled=False)
    pieces = lax.all_to_all(slices, ("dp", "x"), split_axis=0, concat_axis=0, tiled=True)
    own = normalise(pieces)

    half = LEFTS // 2
    chunks, places = [], []

    def keep(value, rel, first=0):
        for other, part in enumerate((value, swap(value))):
            chunks.append(part)
            places.append(((other * NZ + rel) * LEFTS + first, value.shape[0]))

    keep(own, 0)
    up = down = own
    for k in range(1, NZ // 2):
        up = shift(up, "z", 1, NZ)
        down = shift(down, "z", -1, NZ)
        keep(up, NZ - k)
        keep(down, k)
    keep(shift(up[:half], "z", 1, NZ), NZ // 2, 0)
    keep(shift(down[half:], "z", -1, NZ), NZ // 2, half)

    left, right = correlate(start, order, jidx, lpos, rpos, gathered, chunks, places)
    returned = lax.all_to_all(
        right.reshape(NDEV, NX, WIDTH), ("x", "z", "core"), split_axis=0, concat_axis=0, tiled=True
    )
    right_out = finish_right(rows, returned.reshape(NX, NZ * NC * NX, WIDTH))
    spread = lax.all_to_all(
        left.reshape(NX * NY, SLOTS, QUARTER), ("x", "dp"), split_axis=0, concat_axis=0, tiled=True
    )
    left_out = jnp.max(spread, axis=0)
    return (left_out[None], right_out[None])


def solution(mesh):
    fine = Mesh(np.asarray(mesh.devices).reshape(NY, NX, NZ, NC), ("dp", "x", "z", "core"))
    expert = ("x", "z", "core")
    in_specs = (P(expert, "dp", None), P(expert, None, "dp"), P())
    out_specs = (P(expert, None, "dp"), P(expert, None, "dp"))
    return jax.shard_map(body, mesh=fine, in_specs=in_specs, out_specs=out_specs, check_vma=False)
```

time: 611 us -> 162 us (0.27)
  waiting for transfers between devices: 404 us -> 41 us
  local copies, waits for them, and re-layouts: 112 us -> 15.7 us
  matrix products: 42.6 us -> 0 us
  blocking collectives: 0 us -> 34.5 us
  Pallas kernels: 0 us -> 31.6 us
  other arithmetic: 12.7 us -> 2.85 us
    all_to_all x3 -> x1, waiting for transfers between devices: 322 us -> 11.2 us  [body(): lax.all_to_all(left.reshape(NX * NY, SLOTS, QUARTER), ('x', 'dp'), split_...]
    all_gather x1, waiting for transfers between devices: 43 us -> 0.01 us  [body(): gathered = lax.all_gather(acts, ('x', 'dp'), axis=0, tiled=False)]
    dot_general x10 -> x0, matrix products: 42.6 us -> none  [the longest x8 38.6 us: single(): jnp.einsum('ra,rb->ab', left_rows, partner_block, preferred_element_type=...]
    pmax x1 -> x0, waiting for transfers between devices: 38.4 us -> none  [body(): left_all = lax.pmax(left_part, 'dp')]
    all_to_all x0 -> x2, blocking collectives: none -> 34.5 us  [the longest x1 17.2 us: body(): lax.all_to_all(right.reshape(NDEV, NX, WIDTH), ('x', 'z', 'core'), split_...]
    gather x18 -> x0, local copies, waits for them, and re-layouts: 32.9 us -> none  [the longest x8 19.6 us: single(): left_rows = jnp.take(own_full, expert_pick, axis=0)]
    pallas_call x0 -> x4, Pallas kernels: none -> 31.6 us  [the longest x1 24.3 us: correlate(): pl.pallas_call(kernel, grid_spec=pltpu.PrefetchScalarGridSpec(num_scalar_...]
    ppermute x0 -> x17, waiting for transfers between devices: none -> 29.8 us  [the longest x8 29.7 us: shift(): lax.ppermute(value, axis, [(i, (i + by) % size) for i in range(size)])]
  transfers between devices with their start and end apart: 5 -> 19, of which waited for: 5 -> 8; matrix products, arithmetic and copies ran while one was open for 1% -> 2% of each run, Pallas kernels for 0% -> 3%
where the time goes in v1:
time: 162 us; the launch traced here: 161 us
  waiting for transfers between devices  41 us (25%)
  blocking collectives  34.5 us (21%)
  Pallas kernels  31.6 us (20%)
  starting transfers between devices  21.3 us (13%)
  local copies, waits for them, and re-layouts  15.7 us (10%)
  between operations  14.2 us (9%)
  other arithmetic  2.85 us (2%)
    ppermute x8, waiting for transfers between devices, shift(): lax.ppermute(value, axis, [(i, (i + by) % size) for i in range(size)])  29.7 us
    pallas_call x1, Pallas kernels, correlate(): pl.pallas_call(kernel, grid_spec=pltpu.PrefetchScalarGridSpec(num_scalar_...  24.3 us
    all_to_all x1, blocking collectives, body(): lax.all_to_all(right.reshape(NDEV, NX, WIDTH), ('x', 'z', 'core'), split_...  17.2 us
    all_to_all x1, blocking collectives, body(): lax.all_to_all(slices, ('dp', 'x'), split_axis=0, concat_axis=0, tiled=True)  17.2 us
    ppermute x8, starting transfers between devices, shift(): lax.ppermute(value, axis, [(i, (i + by) % size) for i in range(size)])  15.2 us
    unnamed x35, local copies, waits for them, and re-layouts  14.8 us
    all_to_all x1, waiting for transfers between devices, body(): lax.all_to_all(left.reshape(NX * NY, SLOTS, QUARTER), ('x', 'dp'), split_...  11.2 us
    all_to_all x1, starting transfers between devices, body(): lax.all_to_all(left.reshape(NX * NY, SLOTS, QUARTER), ('x', 'dp'), split_...  4.49 us
  transfers between devices with their start and end apart: 19, of which 8 were waited for; matrix products, arithmetic and copies ran while one was open for 2% of the time, Pallas kernels for 3%

profile of v1, /device:TPU:32, one launch (start us, length us, event | category | flops | bytes accessed | tf_op | source)
XLA Modules:
  0.0 161.2 jit_solution(11397215057016796910)
XLA Ops:
  7.2 0.0 all-gather.3.cloned.1.call-start
  7.2 1.3 copy.7.scales_ref
  8.5 2.5 %prepare.1 = (bf16[2,64,1536]{2,1,0:T(8,128)(2,1)}, bf16[16,96,128]{2,1,0:T(8,128)(2,1)}) custom-call(bf16[2,64,1536]{2,1,0:T(8,128)(2,1)} %codes_ref.1, f32[2,12,64]{2,1,0:T(8,128)} %copy.7.scales_ref), custom_call_target="tpu_custom_call" | custom-call | tf_op jit(solution)/shard_map/prepare/pallas_call | solution.py:55
  11.0 0.0 all-gather.3.cloned.1.call-update
  11.0 17.2 %all_to_all.15.in_ref = bf16[16,96,128]{2,1,0:T(8,128)(2,1)} all-to-all(bf16[16,96,128]{2,1,0:T(8,128)(2,1)} %get-tuple-element.7), channel_id=1, replica_groups=mesh['dp'=4,'x'=4,'z'=8,'core'=2] {'dp','x'}, dimensions={0} | all-to-all | bytes 786432 | tf_op jit(solution)/shard_map/all_to_all | solution.py:247
  28.2 2.5 %normalise.1.refs_1_ = bf16[8,96,256]{2,1,0:T(8,128)(2,1)} custom-call(bf16[16,96,128]{2,1,0:T(8,128)(2,1)} %all_to_all.15.in_ref), custom_call_target="tpu_custom_call" | custom-call | tf_op jit(solution)/shard_map/normalise/pallas_call | solution.py:78
  30.7 0.1 collective-permute-start.3
  30.9 1.9 %collective-permute-start.1 = (bf16[8,96,256]{2,1,0:T(8,128)(2,1)}, bf16[8,96,256]{2,1,0:T(8,128)(2,1)S(1)}, u32[]{:S(2)}, u32[]{:S(2)}) collective-permute-start(bf16[8,96,256]{2,1,0:T(8,128)(2,1)} %normalise.1.refs_1_), channel_id=1, source_target_pairs={{0,2},{2,4},{4,6},{6,8},{8,10},{10,12},{12,14},{14,0},{1,3},{3,5},... | collective-permute-start | bytes 1179656 | tf_op jit(solution)/shard_map/ppermute | solution.py:207
  32.8 8.1 %collective-permute-done.3.refs_5_ = bf16[8,96,256]{2,1,0:T(8,128)(2,1)S(1)} collective-permute-done((bf16[8,96,256]{2,1,0:T(8,128)(2,1)}, bf16[8,96,256]{2,1,0:T(8,128)(2,1)S(1)}, u32[]{:S(2)}, u32[]{:S(2)}) %collective-permute-start.3) | collective-permute-done | bytes 393248 | tf_op jit(solution)/shard_map/ppermute | solution.py:207
  40.8 3.4 %collective-permute-start.7 = (bf16[8,96,256]{2,1,0:T(8,128)(2,1)S(1)}, bf16[8,96,256]{2,1,0:T(8,128)(2,1)S(1)}, u32[]{:S(2)}, u32[]{:S(2)}) collective-permute-start(bf16[8,96,256]{2,1,0:T(8,128)(2,1)S(1)} %collective-permute-done.3.refs_5_), channel_id=1, source_target_pairs={{0,14},{2,0},{4,2},{6,4},{8,6},{10,8},{12,10},{14,12},{1,15},{3,1}... | collective-permute-start | bytes 1179656 | tf_op jit(solution)/shard_map/ppermute | solution.py:207
  44.2 0.4 collective-permute-done.1.refs_3_
  44.6 0.0 collective-permute-start.5
  44.6 5.9 %collective-permute-done.7.refs_9_ = bf16[8,96,256]{2,1,0:T(8,128)(2,1)S(1)} collective-permute-done((bf16[8,96,256]{2,1,0:T(8,128)(2,1)S(1)}, bf16[8,96,256]{2,1,0:T(8,128)(2,1)S(1)}, u32[]{:S(2)}, u32[]{:S(2)}) %collective-permute-start.7) | collective-permute-done | bytes 393248 | tf_op jit(solution)/shard_map/ppermute | solution.py:207
  50.5 3.6 %collective-permute-start.11 = (bf16[8,96,256]{2,1,0:T(8,128)(2,1)S(1)}, bf16[8,96,256]{2,1,0:T(8,128)(2,1)S(1)}, u32[]{:S(2)}, u32[]{:S(2)}) collective-permute-start(bf16[8,96,256]{2,1,0:T(8,128)(2,1)S(1)} %collective-permute-done.7.refs_9_), channel_id=1, source_target_pairs={{0,14},{2,0},{4,2},{6,4},{8,6},{10,8},{12,10},{14,12},{1,15},{3,1}... | collective-permute-start | bytes 1179656 | tf_op jit(solution)/shard_map/ppermute | solution.py:207
  54.1 0.8 reshape.94
  54.9 0.1 reshape.95
  55.0 0.0 collective-permute-start
  55.0 0.5 collective-permute-start.4
  55.5 0.1 collective-permute-start.2
  55.6 0.0 collective-permute-done.5.refs_7_
  55.6 0.4 collective-permute-start.8
  56.0 3.5 %collective-permute-done.11.refs_13_ = bf16[8,96,256]{2,1,0:T(8,128)(2,1)S(1)} collective-permute-done((bf16[8,96,256]{2,1,0:T(8,128)(2,1)S(1)}, bf16[8,96,256]{2,1,0:T(8,128)(2,1)S(1)}, u32[]{:S(2)}, u32[]{:S(2)}) %collective-permute-start.11) | collective-permute-done | bytes 393248 | tf_op jit(solution)/shard_map/ppermute | solution.py:207
  59.5 2.7 %collective-permute-start.9 = (bf16[8,96,256]{2,1,0:T(8,128)(2,1)S(1)}, bf16[8,96,256]{2,1,0:T(8,128)(2,1)S(1)}, u32[]{:S(2)}, u32[]{:S(2)}) collective-permute-start(bf16[8,96,256]{2,1,0:T(8,128)(2,1)S(1)} %collective-permute-done.5.refs_7_), channel_id=1, source_target_pairs={{0,2},{2,4},{4,6},{6,8},{8,10},{10,12},{12,14},{14,0},{1,3},{3,5},... | collective-permute-start | bytes 1179656 | tf_op jit(solution)/shard_map/ppermute | solution.py:207
  62.3 6.8 %collective-permute-done.9.refs_11_ = bf16[8,96,256]{2,1,0:T(8,128)(2,1)S(1)} collective-permute-done((bf16[8,96,256]{2,1,0:T(8,128)(2,1)S(1)}, bf16[8,96,256]{2,1,0:T(8,128)(2,1)S(1)}, u32[]{:S(2)}, u32[]{:S(2)}) %collective-permute-start.9) | collective-permute-done | bytes 393248 | tf_op jit(solution)/shard_map/ppermute | solution.py:207
  69.1 0.0 collective-permute-start.6
  69.1 0.0 collective-permute-done.refs_2_
  69.1 3.5 %collective-permute-start.15 = (bf16[4,96,256]{2,1,0:T(8,128)(2,1)S(1)}, bf16[4,96,256]{2,1,0:T(8,128)(2,1)S(1)}, u32[]{:S(2)}, u32[]{:S(2)}) collective-permute-start(bf16[4,96,256]{2,1,0:T(8,128)(2,1)S(1)} %slice.22), channel_id=1, source_target_pairs={{0,14},{2,0},{4,2},{6,4},{8,6},{10,8},{12,10},{14,12},{1,15},{3,1}... | collective-permute-start | bytes 589832 | tf_op jit(solution)/shard_map/ppermute | solution.py:207
  72.6 0.0 collective-permute-done.4.refs_6_
  72.7 0.0 collective-permute-done.2.refs_4_
  72.7 0.3 collective-permute-start.12
  73.0 0.0 collective-permute-done.8.refs_10_
  73.0 0.8 copy-done.1
  73.7 0.3 collective-permute-start.10
  74.0 0.2 convert_reduce_fusion
  74.2 3.3 %collective-permute-done.15.refs_17_ = bf16[4,96,256]{2,1,0:T(8,128)(2,1)S(1)} collective-permute-done((bf16[4,96,256]{2,1,0:T(8,128)(2,1)S(1)}, bf16[4,96,256]{2,1,0:T(8,128)(2,1)S(1)}, u32[]{:S(2)}, u32[]{:S(2)}) %collective-permute-start.15) | collective-permute-done | bytes 196640 | tf_op jit(solution)/shard_map/ppermute | solution.py:207
  77.5 0.7 copy-done.7
  78.2 1.8 %collective-permute-done.13.refs_15_ = bf16[4,96,256]{2,1,0:T(8,128)(2,1)S(1)} collective-permute-done((bf16[4,96,256]{2,1,0:T(8,128)(2,1)S(1)}, bf16[4,96,256]{2,1,0:T(8,128)(2,1)S(1)}, u32[]{:S(2)}, u32[]{:S(2)}) %collective-permute-start.13) | collective-permute-done | bytes 196640 | tf_op jit(solution)/shard_map/ppermute | solution.py:207
  80.0 0.0 collective-permute-start.14
  80.0 0.7 copy-done.9
  80.7 0.1 convert_reduce_fusion.1.start_ref
  80.8 0.6 select_reduce_fusion.order_ref
  81.4 0.8 copy-done.3
  82.2 0.8 copy-done.5
  83.0 0.0 collective-permute-done.16.refs_18_
  83.0 0.1 copy-done.16
  83.1 0.7 copy-done.11
  83.8 0.0 collective-permute-done.14.refs_16_
  83.8 0.7 copy-done.13
  84.4 1.0 copy-done
  85.4 1.0 copy-done.2
  86.4 1.0 copy-done.4
  87.4 1.0 copy-done.6
  88.4 0.9 copy-done.8
  89.4 0.9 copy-done.10
  90.3 0.9 copy-done.12
  91.2 0.9 copy-done.14
  92.1 0.7 copy-done.15
  92.8 24.3 %correlate.1 = (f32[512,384]{1,0:T(8,128)}, f32[256,96]{1,0:T(8,128)S(1)}) custom-call(s32[9]{0:T(128)S(1)} %convert_reduce_fusion.1.start_ref, s32[128]{0:T(128)S(1)} %copy-done.15, s32[128]{0:T(128)S(1)} %get-tuple-element.12.jidx_ref, s32[128]{0:T(128)S(1)} %get-tuple-element.14.lpos_ref, s32[128]{0:T(128)S(1)} %get-tuple-element.10.rpos_ref, ...), custom_call_target="tpu_custom_call" | custom-call | tf_op jit(solution)/shard_map/correlate/pallas_call | solution.py:167
  117.1 17.2 %all_to_all.16 = f32[64,4,96]{2,1,0:T(4,128)} all-to-all(f32[64,4,96]{2,1,0:T(4,128)S(1)} %bitcast.40), channel_id=1, replica_groups=mesh['dp'=4,'x'=4,'z'=8,'core'=2] {'x','z','core'}, dimensions={0} | all-to-all | bytes 196608 | tf_op jit(solution)/shard_map/all_to_all | solution.py:269
  134.4 4.5 %all-to-all-start.1 = ((f32[16,32,384]{2,1,0:T(8,128)}), f32[16,32,384]{2,1,0:T(8,128)S(1)}, u32[]{:S(2)}, u32[]{:S(2)}) async-start(f32[16,32,384]{2,1,0:T(8,128)} %bitcast.42), calls=%async_computation.1 | async-start | bytes 1572864 | tf_op jit(solution)/shard_map/all_to_all | solution.py:273
  138.9 1.2 fusion.11.rows_ref
  140.1 2.4 %finish_right.1 = f32[32,384]{1,0:T(8,128)} custom-call(s32[32]{0:T(128)} %fusion.11.rows_ref, f32[4,64,96]{2,1,0:T(8,128)} %bitcast.43), custom_call_target="tpu_custom_call" | custom-call | tf_op jit(solution)/shard_map/finish_right/pallas_call | solution.py:196
  142.5 11.2 %all-to-all-done.1 = f32[16,32,384]{2,1,0:T(8,128)S(1)} async-done(((f32[16,32,384]{2,1,0:T(8,128)}), f32[16,32,384]{2,1,0:T(8,128)S(1)}, u32[]{:S(2)}, u32[]{:S(2)}) %all-to-all-start.1) | async-done | bytes 786464 | tf_op jit(solution)/shard_map/all_to_all | solution.py:273
  153.7 0.7 reduce_max.9
  (29 shorter events, 0.2 us)
Async XLA Ops:
  7.2 77.3 %all-gather.3.cloned.1.call-start = ((), (), s32[]{:S(2)}) async-start(), calls=%async_computation.3 | async-start | bytes 6684672 | tf_op jit(solution)/shard_map/all_gather | solution.py:246
  30.7 10.1 %collective-permute-start.3 = (bf16[8,96,256]{2,1,0:T(8,128)(2,1)}, bf16[8,96,256]{2,1,0:T(8,128)(2,1)S(1)}, u32[]{:S(2)}, u32[]{:S(2)}) collective-permute-start(bf16[8,96,256]{2,1,0:T(8,128)(2,1)} %normalise.1.refs_1_), channel_id=1, source_target_pairs={{0,14},{2,0},{4,2},{6,4},{8,6},{10,8},{12,10},{14,12},{1,15},{3,1}... | collective-permute-start | bytes 1179656 | tf_op jit(solution)/shard_map/ppermute | solution.py:207
  30.9 13.7 %collective-permute-start.1 = (bf16[8,96,256]{2,1,0:T(8,128)(2,1)}, bf16[8,96,256]{2,1,0:T(8,128)(2,1)S(1)}, u32[]{:S(2)}, u32[]{:S(2)}) collective-permute-start(bf16[8,96,256]{2,1,0:T(8,128)(2,1)} %normalise.1.refs_1_), channel_id=1, source_target_pairs={{0,2},{2,4},{4,6},{6,8},{8,10},{10,12},{12,14},{14,0},{1,3},{3,5},... | collective-permute-start | bytes 1179656 | tf_op jit(solution)/shard_map/ppermute | solution.py:207
  40.8 9.6 %collective-permute-start.7 = (bf16[8,96,256]{2,1,0:T(8,128)(2,1)S(1)}, bf16[8,96,256]{2,1,0:T(8,128)(2,1)S(1)}, u32[]{:S(2)}, u32[]{:S(2)}) collective-permute-start(bf16[8,96,256]{2,1,0:T(8,128)(2,1)S(1)} %collective-permute-done.3.refs_5_), channel_id=1, source_target_pairs={{0,14},{2,0},{4,2},{6,4},{8,6},{10,8},{12,10},{14,12},{1,15},{3,1}... | collective-permute-start | bytes 1179656 | tf_op jit(solution)/shard_map/ppermute | solution.py:207
  44.6 11.0 %collective-permute-start.5 = (bf16[8,96,256]{2,1,0:T(8,128)(2,1)S(1)}, bf16[8,96,256]{2,1,0:T(8,128)(2,1)S(1)}, u32[]{:S(2)}, u32[]{:S(2)}) collective-permute-start(bf16[8,96,256]{2,1,0:T(8,128)(2,1)S(1)} %collective-permute-done.1.refs_3_), channel_id=1, source_target_pairs={{0,2},{2,4},{4,6},{6,8},{8,10},{10,12},{12,14},{14,0},{1,3},{3,5},... | collective-permute-start | bytes 1179656 | tf_op jit(solution)/shard_map/ppermute | solution.py:207
  50.5 9.1 %collective-permute-start.11 = (bf16[8,96,256]{2,1,0:T(8,128)(2,1)S(1)}, bf16[8,96,256]{2,1,0:T(8,128)(2,1)S(1)}, u32[]{:S(2)}, u32[]{:S(2)}) collective-permute-start(bf16[8,96,256]{2,1,0:T(8,128)(2,1)S(1)} %collective-permute-done.7.refs_9_), channel_id=1, source_target_pairs={{0,14},{2,0},{4,2},{6,4},{8,6},{10,8},{12,10},{14,12},{1,15},{3,1}... | collective-permute-start | bytes 1179656 | tf_op jit(solution)/shard_map/ppermute | solution.py:207
  55.0 14.1 %collective-permute-start = (bf16[8,96,256]{2,1,0:T(8,128)(2,1)}, bf16[8,96,256]{2,1,0:T(8,128)(2,1)S(1)}, u32[]{:S(2)}, u32[]{:S(2)}) collective-permute-start(bf16[8,96,256]{2,1,0:T(8,128)(2,1)} %normalise.1.refs_1_), channel_id=1, source_target_pairs={{0,1},{1,0},{2,3},{3,2},{4,5},{5,4},{6,7},{7,6},{8,9},{9,8},{10,11... | collective-permute-start | bytes 1179656 | tf_op jit(solution)/shard_map/ppermute | solution.py:211
  55.0 17.6 %collective-permute-start.4 = (bf16[8,96,256]{2,1,0:T(8,128)(2,1)S(1)}, bf16[8,96,256]{2,1,0:T(8,128)(2,1)S(1)}, u32[]{:S(2)}, u32[]{:S(2)}) collective-permute-start(bf16[8,96,256]{2,1,0:T(8,128)(2,1)S(1)} %collective-permute-done.3.refs_5_), channel_id=1, source_target_pairs={{0,1},{1,0},{2,3},{3,2},{4,5},{5,4},{6,7},{7,6},{8,9},{9,8},{10,11... | collective-permute-start | bytes 1179656 | tf_op jit(solution)/shard_map/ppermute | solution.py:211
  55.5 17.1 %collective-permute-start.2 = (bf16[8,96,256]{2,1,0:T(8,128)(2,1)S(1)}, bf16[8,96,256]{2,1,0:T(8,128)(2,1)S(1)}, u32[]{:S(2)}, u32[]{:S(2)}) collective-permute-start(bf16[8,96,256]{2,1,0:T(8,128)(2,1)S(1)} %collective-permute-done.1.refs_3_), channel_id=1, source_target_pairs={{0,1},{1,0},{2,3},{3,2},{4,5},{5,4},{6,7},{7,6},{8,9},{9,8},{10,11... | collective-permute-start | bytes 1179656 | tf_op jit(solution)/shard_map/ppermute | solution.py:211
  55.6 17.3 %collective-permute-start.8 = (bf16[8,96,256]{2,1,0:T(8,128)(2,1)S(1)}, bf16[8,96,256]{2,1,0:T(8,128)(2,1)S(1)}, u32[]{:S(2)}, u32[]{:S(2)}) collective-permute-start(bf16[8,96,256]{2,1,0:T(8,128)(2,1)S(1)} %collective-permute-done.7.refs_9_), channel_id=1, source_target_pairs={{0,1},{1,0},{2,3},{3,2},{4,5},{5,4},{6,7},{7,6},{8,9},{9,8},{10,11... | collective-permute-start | bytes 1179656 | tf_op jit(solution)/shard_map/ppermute | solution.py:211
  59.5 9.6 %collective-permute-start.9 = (bf16[8,96,256]{2,1,0:T(8,128)(2,1)S(1)}, bf16[8,96,256]{2,1,0:T(8,128)(2,1)S(1)}, u32[]{:S(2)}, u32[]{:S(2)}) collective-permute-start(bf16[8,96,256]{2,1,0:T(8,128)(2,1)S(1)} %collective-permute-done.5.refs_7_), channel_id=1, source_target_pairs={{0,2},{2,4},{4,6},{6,8},{8,10},{10,12},{12,14},{14,0},{1,3},{3,5},... | collective-permute-start | bytes 1179656 | tf_op jit(solution)/shard_map/ppermute | solution.py:207
  69.1 12.3 %collective-permute-start.6 = (bf16[8,96,256]{2,1,0:T(8,128)(2,1)S(1)}, bf16[8,96,256]{2,1,0:T(8,128)(2,1)S(1)}, u32[]{:S(2)}, u32[]{:S(2)}) collective-permute-start(bf16[8,96,256]{2,1,0:T(8,128)(2,1)S(1)} %collective-permute-done.5.refs_7_), channel_id=1, source_target_pairs={{0,1},{1,0},{2,3},{3,2},{4,5},{5,4},{6,7},{7,6},{8,9},{9,8},{10,11... | collective-permute-start | bytes 1179656 | tf_op jit(solution)/shard_map/ppermute | solution.py:211
  69.1 8.3 %collective-permute-start.15 = (bf16[4,96,256]{2,1,0:T(8,128)(2,1)S(1)}, bf16[4,96,256]{2,1,0:T(8,128)(2,1)S(1)}, u32[]{:S(2)}, u32[]{:S(2)}) collective-permute-start(bf16[4,96,256]{2,1,0:T(8,128)(2,1)S(1)} %slice.22), channel_id=1, source_target_pairs={{0,14},{2,0},{4,2},{6,4},{8,6},{10,8},{12,10},{14,12},{1,15},{3,1}... | collective-permute-start | bytes 589832 | tf_op jit(solution)/shard_map/ppermute | solution.py:207
  72.7 7.3 %collective-permute-start.13 = (bf16[4,96,256]{2,1,0:T(8,128)(2,1)S(1)}, bf16[4,96,256]{2,1,0:T(8,128)(2,1)S(1)}, u32[]{:S(2)}, u32[]{:S(2)}) collective-permute-start(bf16[4,96,256]{2,1,0:T(8,128)(2,1)S(1)} %slice.21), channel_id=1, source_target_pairs={{0,2},{2,4},{4,6},{6,8},{8,10},{10,12},{12,14},{14,0},{1,3},{3,5},... | collective-permute-start | bytes 589832 | tf_op jit(solution)/shard_map/ppermute | solution.py:207
  72.7 9.5 %collective-permute-start.12 = (bf16[8,96,256]{2,1,0:T(8,128)(2,1)S(1)}, bf16[8,96,256]{2,1,0:T(8,128)(2,1)S(1)}, u32[]{:S(2)}, u32[]{:S(2)}) collective-permute-start(bf16[8,96,256]{2,1,0:T(8,128)(2,1)S(1)} %collective-permute-done.11.refs_13_), channel_id=1, source_target_pairs={{0,1},{1,0},{2,3},{3,2},{4,5},{5,4},{6,7},{7,6},{8,9},{9,8},{10,11... | collective-permute-start | bytes 1179656 | tf_op jit(solution)/shard_map/ppermute | solution.py:211
  73.0 0.8 copy-start.1
  73.7 8.4 %collective-permute-start.10 = (bf16[8,96,256]{2,1,0:T(8,128)(2,1)S(1)}, bf16[8,96,256]{2,1,0:T(8,128)(2,1)S(1)}, u32[]{:S(2)}, u32[]{:S(2)}) collective-permute-start(bf16[8,96,256]{2,1,0:T(8,128)(2,1)S(1)} %collective-permute-done.9.refs_11_), channel_id=1, source_target_pairs={{0,1},{1,0},{2,3},{3,2},{4,5},{5,4},{6,7},{7,6},{8,9},{9,8},{10,11... | collective-permute-start | bytes 1179656 | tf_op jit(solution)/shard_map/ppermute | solution.py:211
  77.5 5.5 %collective-permute-start.16 = (bf16[4,96,256]{2,1,0:T(8,128)(2,1)S(1)}, bf16[4,96,256]{2,1,0:T(8,128)(2,1)S(1)}, u32[]{:S(2)}, u32[]{:S(2)}) collective-permute-start(bf16[4,96,256]{2,1,0:T(8,128)(2,1)S(1)} %collective-permute-done.15.refs_17_), channel_id=1, source_target_pairs={{0,1},{1,0},{2,3},{3,2},{4,5},{5,4},{6,7},{7,6},{8,9},{9,8},{10,11... | collective-permute-start | bytes 589832 | tf_op jit(solution)/shard_map/ppermute | solution.py:211
  77.5 0.7 copy-start.7
  80.0 3.8 %collective-permute-start.14 = (bf16[4,96,256]{2,1,0:T(8,128)(2,1)S(1)}, bf16[4,96,256]{2,1,0:T(8,128)(2,1)S(1)}, u32[]{:S(2)}, u32[]{:S(2)}) collective-permute-start(bf16[4,96,256]{2,1,0:T(8,128)(2,1)S(1)} %collective-permute-done.13.refs_15_), channel_id=1, source_target_pairs={{0,1},{1,0},{2,3},{3,2},{4,5},{5,4},{6,7},{7,6},{8,9},{9,8},{10,11... | collective-permute-start | bytes 589832 | tf_op jit(solution)/shard_map/ppermute | solution.py:211
  80.0 0.7 copy-start.9
  81.4 0.8 copy-start.3
  82.2 0.9 copy-start.16
  82.2 0.8 copy-start.5
  83.1 0.7 copy-start.11
  83.8 0.7 copy-start.13
  84.4 1.0 copy-start
  85.4 1.0 copy-start.2
  86.4 1.0 copy-start.4
  87.4 1.0 copy-start.6
  88.4 0.9 copy-start.8
  89.4 0.9 copy-start.10
  90.3 0.9 copy-start.12
  91.2 0.9 copy-start.14
  92.1 0.7 copy-start.15
  134.4 19.3 %all-to-all-start.1 = ((f32[16,32,384]{2,1,0:T(8,128)}), f32[16,32,384]{2,1,0:T(8,128)S(1)}, u32[]{:S(2)}, u32[]{:S(2)}) async-start(f32[16,32,384]{2,1,0:T(8,128)} %bitcast.42), calls=%async_computation.1 | async-start | bytes 1572864 | tf_op jit(solution)/shard_map/all_to_all | solution.py:273
Sparse Core Ops, SparseCore 0:
  11.1 68.9 all-gather.2

commit v2 on v1

--- a/solution.py
+++ b/solution.py
@@ -28,7 +28,7 @@
 TILE = 256
 
 VMEM = pl.BlockSpec(memory_space=pltpu.VMEM)
-ANY = pl.BlockSpec(memory_space=pl.ANY)
+HBM = pl.BlockSpec(memory_space=pltpu.HBM)
 
 
 def prepare(codes, scales):
@@ -90,7 +90,8 @@
     def kernel(start_ref, order_ref, jidx_ref, lpos_ref, rpos_ref, *refs):
         gathered_ref = refs[0]
         chunk_refs = refs[1 : 1 + count]
-        left_ref, right_ref, acts, others, inv, sem = refs[1 + count :]
+        left_refs = refs[1 + count : 1 + count + NX * NY]
+        right_ref, left, acts, others, inv, sem = refs[1 + count + NX * NY :]
         copies = []
         for x in range(NX):
             for y in range(NY):
@@ -149,8 +150,8 @@
                             part = one[:, m * 128 : (m + 1) * 128]
                             tops[g].append(jnp.max(part, axis=0, keepdims=True) * scale)
                             if (unit + 128) % QUARTER == 0:
-                                row = lpos_ref[pairs[g]] + (unit // QUARTER) * SLOTS
-                                left_ref[pl.ds(row, 1), :] = jnp.concatenate(tops[g], axis=1)
+                                row = lpos_ref[unit // QUARTER, pairs[g]]
+                                left[pl.ds(row, 1), :] = jnp.concatenate(tops[g], axis=1)
                                 tops[g] = []
                             scaled = part * scale
                             best[g] = scaled if best[g] is None else jnp.maximum(best[g], scaled)
@@ -163,25 +164,26 @@
             return carry
 
         lax.fori_loop(0, LEFTS, expert, 0)
+        for k in range(NX * NY):
+            left_refs[k][...] = left[k * SLOTS : (k + 1) * SLOTS, :]
 
     return pl.pallas_call(
         kernel,
         grid_spec=pltpu.PrefetchScalarGridSpec(
             num_scalar_prefetch=5,
             grid=(1,),
-            in_specs=[ANY] * (1 + count),
-            out_specs=[VMEM, VMEM],
+            in_specs=[HBM] * (1 + count),
+            out_specs=[VMEM] * (NX * NY + 1),
             scratch_shapes=[
+                pltpu.VMEM((NX * NY * SLOTS, QUARTER), jnp.float32),
                 pltpu.VMEM((LEFTS, ROWS, UNITS), jnp.bfloat16),
                 pltpu.VMEM((NZ * NC * LEFTS, WIDTH, ROWS), jnp.bfloat16),
                 pltpu.VMEM((LEFTS, UNITS), jnp.float32),
                 pltpu.SemaphoreType.DMA((NX * NY + count,)),
             ],
         ),
-        out_shape=[
-            jax.ShapeDtypeStruct((NX * NY * SLOTS, QUARTER), jnp.float32),
-            jax.ShapeDtypeStruct((NDEV * NX, WIDTH), jnp.float32),
-        ],
+        out_shape=[jax.ShapeDtypeStruct((SLOTS, QUARTER), jnp.float32)] * (NX * NY)
+        + [jax.ShapeDtypeStruct((NDEV * NX, WIDTH), jnp.float32)],
         compiler_params=pltpu.CompilerParams(vmem_limit_bytes=48 << 20),
         name="correlate",
     )(start, order, jidx, lpos, rpos, gathered, *chunks)
@@ -212,6 +214,7 @@
 
 
 def body(unit_codes, block_scales, pair_list):
+    y = lax.axis_index("dp")
     x = lax.axis_index("x")
     z = lax.axis_index("z")
     c = lax.axis_index("core")
@@ -236,7 +239,9 @@
         axis=1,
         dtype=jnp.int32,
     )
-    lpos = (pair // SLOTS) * (NY * SLOTS) + pair % SLOTS
+    quarter = jnp.arange(NY, dtype=jnp.int32)[:, None]
+    away = ((pair // SLOTS - x) % NX)[None, :] * NY + (quarter - y) % NY
+    lpos = away * SLOTS + (pair % SLOTS)[None, :]
     rpos = right_dev * NX + pair // SLOTS
     offsets = pair_list[:SLOTS, 1] // PER
     source = (me - offsets) % NDEV
@@ -265,15 +270,19 @@
     keep(shift(up[:half], "z", 1, NZ), NZ // 2, 0)
     keep(shift(down[half:], "z", -1, NZ), NZ // 2, half)
 
-    left, right = correlate(start, order, jidx, lpos, rpos, gathered, chunks, places)
+    chunks = [pltpu.with_memory_space_constraint(v, pltpu.HBM) for v in chunks]
+    *lefts, right = correlate(start, order, jidx, lpos, rpos, gathered, chunks, places)
     returned = lax.all_to_all(
         right.reshape(NDEV, NX, WIDTH), ("x", "z", "core"), split_axis=0, concat_axis=0, tiled=True
     )
+    left_out = lefts[0]
+    for k in range(1, NX * NY):
+        dx, dy = divmod(k, NY)
+        moves = [
+            (j * NX + i, (j + dy) % NY * NX + (i + dx) % NX) for j in range(NY) for i in range(NX)
+        ]
+        left_out = jnp.maximum(left_out, lax.ppermute(lefts[k], ("dp", "x"), moves))
     right_out = finish_right(rows, returned.reshape(NX, NZ * NC * NX, WIDTH))
-    spread = lax.all_to_all(
-        left.reshape(NX * NY, SLOTS, QUARTER), ("x", "dp"), split_axis=0, concat_axis=0, tiled=True
-    )
-    left_out = jnp.max(spread, axis=0)
     return (left_out[None], right_out[None])
 
 

time: 162 us -> 166 us (1.025)
  starting transfers between devices: 21.3 us -> 54.2 us
  blocking collectives: 34.5 us -> 17.2 us
  local copies, waits for them, and re-layouts: 15.7 us -> 5.08 us
    ppermute x0 -> x15, starting transfers between devices: none -> 28.1 us  [body(): left_out = jnp.maximum(left_out, lax.ppermute(lefts[k], ('dp', 'x'), moves))]
    all_to_all x1 -> x0, blocking collectives: 17.2 us -> none  [body(): lax.all_to_all(right.reshape(NDEV, NX, WIDTH), ('x', 'z', 'core'), split_...]
    unnamed x35 -> x29, local copies, waits for them, and re-layouts: 14.8 us -> 4.13 us
    all_to_all x1, starting transfers between devices: 4.49 us -> 9.28 us  [body(): lax.all_to_all(right.reshape(NDEV, NX, WIDTH), ('x', 'z', 'core'), split_...]
    all_to_all x1, waiting for transfers between devices: 11.2 us -> 9.31 us  [body(): lax.all_to_all(right.reshape(NDEV, NX, WIDTH), ('x', 'z', 'core'), split_...]
  transfers between devices with their start and end apart: 19 -> 34, of which waited for: 8 -> 9; matrix products, arithmetic and copies ran while one was open for 2% -> 2% of each run, Pallas kernels for 3% -> 2%
where the time goes in v2:
time: 166 us; the launch traced here: 165 us
  starting transfers between devices  54.2 us (33%)
  waiting for transfers between devices  41.2 us (25%)
  Pallas kernels  30.7 us (18%)
  blocking collectives  17.2 us (10%)
  between operations  14.3 us (9%)
  local copies, waits for them, and re-layouts  5.08 us (3%)
  other arithmetic  2.48 us (1%)
    ppermute x8, waiting for transfers between devices, shift(): lax.ppermute(value, axis, [(i, (i + by) % size) for i in range(size)])  30.9 us
    ppermute x15, starting transfers between devices, body(): left_out = jnp.maximum(left_out, lax.ppermute(lefts[k], ('dp', 'x'), moves))  28.1 us
    pallas_call x1, Pallas kernels, correlate(): pl.pallas_call(kernel, grid_spec=pltpu.PrefetchScalarGridSpec(num_scalar_...  23.4 us
    all_to_all x1, blocking collectives, body(): lax.all_to_all(slices, ('dp', 'x'), split_axis=0, concat_axis=0, tiled=True)  17.2 us
    ppermute x8, starting transfers between devices, shift(): lax.ppermute(value, axis, [(i, (i + by) % size) for i in range(size)])  15.5 us
    all_to_all x1, waiting for transfers between devices, body(): lax.all_to_all(right.reshape(NDEV, NX, WIDTH), ('x', 'z', 'core'), split_...  9.31 us
    all_to_all x1, starting transfers between devices, body(): lax.all_to_all(right.reshape(NDEV, NX, WIDTH), ('x', 'z', 'core'), split_...  9.28 us
    unnamed x29, local copies, waits for them, and re-layouts  4.13 us
  transfers between devices with their start and end apart: 34, of which 9 were waited for; matrix products, arithmetic and copies ran while one was open for 2% of the time, Pallas kernels for 2%

profile of v2, /device:TPU:32, one launch (start us, length us, event | category | flops | bytes accessed | tf_op | source)
XLA Modules:
  0.0 165.1 jit_solution(9945890067311671497)
XLA Ops:
  7.2 0.0 all-gather.3.cloned.1.call-start
  7.2 1.3 copy.7.scales_ref
  8.5 2.4 %prepare.1 = (bf16[2,64,1536]{2,1,0:T(8,128)(2,1)}, bf16[16,96,128]{2,1,0:T(8,128)(2,1)}) custom-call(bf16[2,64,1536]{2,1,0:T(8,128)(2,1)} %codes_ref.1, f32[2,12,64]{2,1,0:T(8,128)} %copy.7.scales_ref), custom_call_target="tpu_custom_call" | custom-call | tf_op jit(solution)/shard_map/prepare/pallas_call | solution.py:55
  11.0 0.0 all-gather.3.cloned.1.call-update
  11.0 17.2 %all_to_all.10.in_ref = bf16[16,96,128]{2,1,0:T(8,128)(2,1)} all-to-all(bf16[16,96,128]{2,1,0:T(8,128)(2,1)} %get-tuple-element.22), channel_id=1, replica_groups=mesh['dp'=4,'x'=4,'z'=8,'core'=2] {'dp','x'}, dimensions={0} | all-to-all | bytes 786432 | tf_op jit(solution)/shard_map/all_to_all | solution.py:252
  28.2 2.5 %normalise.1.refs_1_ = bf16[8,96,256]{2,1,0:T(8,128)(2,1)} custom-call(bf16[16,96,128]{2,1,0:T(8,128)(2,1)} %all_to_all.10.in_ref), custom_call_target="tpu_custom_call" | custom-call | tf_op jit(solution)/shard_map/normalise/pallas_call | solution.py:78
  30.7 0.1 collective-permute-start.3
  30.8 1.9 %collective-permute-start.1 = (bf16[8,96,256]{2,1,0:T(8,128)(2,1)}, bf16[8,96,256]{2,1,0:T(8,128)(2,1)S(1)}, u32[]{:S(2)}, u32[]{:S(2)}) collective-permute-start(bf16[8,96,256]{2,1,0:T(8,128)(2,1)} %normalise.1.refs_1_), channel_id=1, source_target_pairs={{0,2},{2,4},{4,6},{6,8},{8,10},{10,12},{12,14},{14,0},{1,3},{3,5},... | collective-permute-start | bytes 1179656 | tf_op jit(solution)/shard_map/ppermute | solution.py:209
  32.8 8.1 %collective-permute-done.3.refs_5_ = bf16[8,96,256]{2,1,0:T(8,128)(2,1)S(1)} collective-permute-done((bf16[8,96,256]{2,1,0:T(8,128)(2,1)}, bf16[8,96,256]{2,1,0:T(8,128)(2,1)S(1)}, u32[]{:S(2)}, u32[]{:S(2)}) %collective-permute-start.3) | collective-permute-done | bytes 393248 | tf_op jit(solution)/shard_map/ppermute | solution.py:209
  40.8 3.4 %collective-permute-start.7 = (bf16[8,96,256]{2,1,0:T(8,128)(2,1)S(1)}, bf16[8,96,256]{2,1,0:T(8,128)(2,1)S(1)}, u32[]{:S(2)}, u32[]{:S(2)}) collective-permute-start(bf16[8,96,256]{2,1,0:T(8,128)(2,1)S(1)} %collective-permute-done.3.refs_5_), channel_id=1, source_target_pairs={{0,14},{2,0},{4,2},{6,4},{8,6},{10,8},{12,10},{14,12},{1,15},{3,1}... | collective-permute-start | bytes 1179656 | tf_op jit(solution)/shard_map/ppermute | solution.py:209
  44.2 0.8 reshape.138
  45.0 0.1 reshape.139
  45.1 0.0 collective-permute-done.1.refs_3_
  45.1 0.1 collective-permute-start.5
  45.2 5.3 %collective-permute-done.7.refs_9_ = bf16[8,96,256]{2,1,0:T(8,128)(2,1)S(1)} collective-permute-done((bf16[8,96,256]{2,1,0:T(8,128)(2,1)S(1)}, bf16[8,96,256]{2,1,0:T(8,128)(2,1)S(1)}, u32[]{:S(2)}, u32[]{:S(2)}) %collective-permute-start.7) | collective-permute-done | bytes 393248 | tf_op jit(solution)/shard_map/ppermute | solution.py:209
  50.5 3.6 %collective-permute-start.11 = (bf16[8,96,256]{2,1,0:T(8,128)(2,1)S(1)}, bf16[8,96,256]{2,1,0:T(8,128)(2,1)S(1)}, u32[]{:S(2)}, u32[]{:S(2)}) collective-permute-start(bf16[8,96,256]{2,1,0:T(8,128)(2,1)S(1)} %collective-permute-done.7.refs_9_), channel_id=1, source_target_pairs={{0,14},{2,0},{4,2},{6,4},{8,6},{10,8},{12,10},{14,12},{1,15},{3,1}... | collective-permute-start | bytes 1179656 | tf_op jit(solution)/shard_map/ppermute | solution.py:209
  54.1 0.1 convert_reduce_fusion.1.start_ref
  54.2 0.1 collective-permute-start
  54.3 0.5 collective-permute-start.4
  54.8 0.1 collective-permute-start.2
  54.9 0.6 collective-permute-done.5.refs_7_
  55.5 4.0 %collective-permute-done.11.refs_13_ = bf16[8,96,256]{2,1,0:T(8,128)(2,1)S(1)} collective-permute-done((bf16[8,96,256]{2,1,0:T(8,128)(2,1)S(1)}, bf16[8,96,256]{2,1,0:T(8,128)(2,1)S(1)}, u32[]{:S(2)}, u32[]{:S(2)}) %collective-permute-start.11) | collective-permute-done | bytes 393248 | tf_op jit(solution)/shard_map/ppermute | solution.py:209
  59.5 2.7 %collective-permute-start.9 = (bf16[8,96,256]{2,1,0:T(8,128)(2,1)S(1)}, bf16[8,96,256]{2,1,0:T(8,128)(2,1)S(1)}, u32[]{:S(2)}, u32[]{:S(2)}) collective-permute-start(bf16[8,96,256]{2,1,0:T(8,128)(2,1)S(1)} %collective-permute-done.5.refs_7_), channel_id=1, source_target_pairs={{0,2},{2,4},{4,6},{6,8},{8,10},{10,12},{12,14},{14,0},{1,3},{3,5},... | collective-permute-start | bytes 1179656 | tf_op jit(solution)/shard_map/ppermute | solution.py:209
  62.2 0.2 convert_reduce_fusion
  62.4 6.4 %collective-permute-done.9.refs_11_ = bf16[8,96,256]{2,1,0:T(8,128)(2,1)S(1)} collective-permute-done((bf16[8,96,256]{2,1,0:T(8,128)(2,1)S(1)}, bf16[8,96,256]{2,1,0:T(8,128)(2,1)S(1)}, u32[]{:S(2)}, u32[]{:S(2)}) %collective-permute-start.9) | collective-permute-done | bytes 393248 | tf_op jit(solution)/shard_map/ppermute | solution.py:209
  68.8 0.0 collective-permute-start.6
  68.9 3.8 %collective-permute-start.15 = (bf16[4,96,256]{2,1,0:T(8,128)(2,1)S(1)}, bf16[4,96,256]{2,1,0:T(8,128)(2,1)S(1)}, u32[]{:S(2)}, u32[]{:S(2)}) collective-permute-start(bf16[4,96,256]{2,1,0:T(8,128)(2,1)S(1)} %slice.22), channel_id=1, source_target_pairs={{0,14},{2,0},{4,2},{6,4},{8,6},{10,8},{12,10},{14,12},{1,15},{3,1}... | collective-permute-start | bytes 589832 | tf_op jit(solution)/shard_map/ppermute | solution.py:209
  72.6 0.0 collective-permute-done.4.refs_6_
  72.6 0.0 collective-permute-start.13
  72.7 0.3 collective-permute-start.12
  73.0 0.3 collective-permute-start.10
  73.3 0.1 select_reduce_fusion.order_ref
  73.4 4.1 %collective-permute-done.15.refs_17_ = bf16[4,96,256]{2,1,0:T(8,128)(2,1)S(1)} collective-permute-done((bf16[4,96,256]{2,1,0:T(8,128)(2,1)S(1)}, bf16[4,96,256]{2,1,0:T(8,128)(2,1)S(1)}, u32[]{:S(2)}, u32[]{:S(2)}) %collective-permute-start.15) | collective-permute-done | bytes 196640 | tf_op jit(solution)/shard_map/ppermute | solution.py:209
  77.5 0.0 collective-permute-start.16
  77.5 2.5 %collective-permute-done.13.refs_15_ = bf16[4,96,256]{2,1,0:T(8,128)(2,1)S(1)} collective-permute-done((bf16[4,96,256]{2,1,0:T(8,128)(2,1)S(1)}, bf16[4,96,256]{2,1,0:T(8,128)(2,1)S(1)}, u32[]{:S(2)}, u32[]{:S(2)}) %collective-permute-start.13) | collective-permute-done | bytes 196640 | tf_op jit(solution)/shard_map/ppermute | solution.py:209
  80.0 0.0 collective-permute-start.14
  80.0 0.1 multiply_add_fusion.lpos_ref
  80.1 0.7 copy-done.8
  80.8 0.2 copy-done.9
  81.0 0.6 copy-done.10
  81.5 0.0 collective-permute-done.14.refs_16_
  81.5 0.7 copy-done.13
  82.3 23.4 %correlate.1 = (f32[32,384]{1,0:T(8,128)S(1)}, f32[32,384]{1,0:T(8,128)S(1)}, f32[32,384]{1,0:T(8,128)S(1)}, f32[32,384]{1,0:T(8,128)S(1)}, f32[32,384]{1,0:T(8,...) custom-call(s32[9]{0:T(128)S(1)} %convert_reduce_fusion.1.start_ref,, ...), custom_call_target="tpu_custom_call" | custom-call | tf_op jit(solution)/shard_map/correlate/pallas_call | solution.py:170
  105.7 0.1 collective-permute-start.17
  105.8 2.7 %collective-permute-start.18 = (f32[32,384]{1,0:T(8,128)S(1)}, f32[32,384]{1,0:T(8,128)S(1)}, u32[]{:S(2)}, u32[]{:S(2)}) collective-permute-start(f32[32,384]{1,0:T(8,128)S(1)} %get-tuple-element.25), channel_id=1, source_target_pairs={{0,128},{16,144},{32,160},{48,176},{64,192},{80,208},{96,224},{112... | collective-permute-start | bytes 147464 | tf_op jit(solution)/shard_map/ppermute | solution.py:284
  108.4 1.7 %collective-permute-start.19 = (f32[32,384]{1,0:T(8,128)S(1)}, f32[32,384]{1,0:T(8,128)S(1)}, u32[]{:S(2)}, u32[]{:S(2)}) collective-permute-start(f32[32,384]{1,0:T(8,128)S(1)} %get-tuple-element.26), channel_id=1, source_target_pairs={{0,192},{16,208},{32,224},{48,240},{64,0},{80,16},{96,32},{112,48}... | collective-permute-start | bytes 147464 | tf_op jit(solution)/shard_map/ppermute | solution.py:284
  110.1 0.6 collective-permute-start.21
  110.7 0.9 collective-permute-done.17
  111.6 0.9 collective-permute-start.22
  112.4 5.1 %collective-permute-start.23 = (f32[32,384]{1,0:T(8,128)S(1)}, f32[32,384]{1,0:T(8,128)S(1)}, u32[]{:S(2)}, u32[]{:S(2)}) collective-permute-start(f32[32,384]{1,0:T(8,128)S(1)} %get-tuple-element.30), channel_id=1, source_target_pairs={{0,208},{16,224},{32,240},{48,192},{64,16},{80,32},{96,48},{112,0}... | collective-permute-start | bytes 147464 | tf_op jit(solution)/shard_map/ppermute | solution.py:284
  117.5 0.9 collective-permute-start.24
  118.4 1.1 collective-permute-start.25
  119.6 3.6 %collective-permute-start.26 = (f32[32,384]{1,0:T(8,128)S(1)}, f32[32,384]{1,0:T(8,128)S(1)}, u32[]{:S(2)}, u32[]{:S(2)}) collective-permute-start(f32[32,384]{1,0:T(8,128)S(1)} %get-tuple-element.33), channel_id=1, source_target_pairs={{0,160},{16,176},{32,128},{48,144},{64,224},{80,240},{96,192},{112... | collective-permute-start | bytes 147464 | tf_op jit(solution)/shard_map/ppermute | solution.py:284
  123.1 4.1 %collective-permute-start.27 = (f32[32,384]{1,0:T(8,128)S(1)}, f32[32,384]{1,0:T(8,128)S(1)}, u32[]{:S(2)}, u32[]{:S(2)}) collective-permute-start(f32[32,384]{1,0:T(8,128)S(1)} %get-tuple-element.34), channel_id=1, source_target_pairs={{0,224},{16,240},{32,192},{48,208},{64,32},{80,48},{96,0},{112,16}... | collective-permute-start | bytes 147464 | tf_op jit(solution)/shard_map/ppermute | solution.py:284
  127.3 0.5 collective-permute-start.28
  127.8 0.3 collective-permute-start.29
  128.1 2.2 %collective-permute-start.30 = (f32[32,384]{1,0:T(8,128)S(1)}, f32[32,384]{1,0:T(8,128)S(1)}, u32[]{:S(2)}, u32[]{:S(2)}) collective-permute-start(f32[32,384]{1,0:T(8,128)S(1)} %get-tuple-element.37), channel_id=1, source_target_pairs={{0,176},{16,128},{32,144},{48,160},{64,240},{80,192},{96,208},{112... | collective-permute-start | bytes 147464 | tf_op jit(solution)/shard_map/ppermute | solution.py:284
  130.3 4.4 %collective-permute-start.31 = (f32[32,384]{1,0:T(8,128)S(1)}, f32[32,384]{1,0:T(8,128)S(1)}, u32[]{:S(2)}, u32[]{:S(2)}) collective-permute-start(f32[32,384]{1,0:T(8,128)S(1)} %get-tuple-element.38), channel_id=1, source_target_pairs={{0,240},{16,192},{32,208},{48,224},{64,48},{80,0},{96,16},{112,32}... | collective-permute-start | bytes 147464 | tf_op jit(solution)/shard_map/ppermute | solution.py:284
  134.7 1.3 fusion.11.rows_ref
  135.9 9.3 %all-to-all-start.1 = ((f32[64,4,96]{2,1,0:T(4,128)}), f32[64,4,96]{2,1,0:T(4,128)S(1)}, u32[]{:S(2)}, u32[]{:S(2)}) async-start(f32[64,4,96]{2,1,0:T(4,128)} %bitcast.6), calls=%async_computation.1 | async-start | bytes 262144 | tf_op jit(solution)/shard_map/all_to_all | solution.py:275
  145.3 0.7 maximum_bitcast_fusion
  145.9 9.3 %all-to-all-done.1 = f32[64,4,96]{2,1,0:T(4,128)S(1)} async-done(((f32[64,4,96]{2,1,0:T(4,128)}), f32[64,4,96]{2,1,0:T(4,128)S(1)}, u32[]{:S(2)}, u32[]{:S(2)}) %all-to-all-start.1) | async-done | bytes 98336 | tf_op jit(solution)/shard_map/all_to_all | solution.py:275
  155.3 0.7 copy-done.2
  155.9 2.4 %finish_right.1 = f32[32,384]{1,0:T(8,128)} custom-call(s32[32]{0:T(128)} %fusion.11.rows_ref, f32[4,64,96]{2,1,0:T(8,128)} %bitcast.41), custom_call_target="tpu_custom_call" | custom-call | tf_op jit(solution)/shard_map/finish_right/pallas_call | solution.py:198
  (55 shorter events, 0.2 us)
Async XLA Ops:
  7.2 74.4 %all-gather.3.cloned.1.call-start = ((), (), s32[]{:S(2)}) async-start(), calls=%async_computation.2 | async-start | bytes 6684672 | tf_op jit(solution)/shard_map/all_gather | solution.py:251
  30.7 10.1 %collective-permute-start.3 = (bf16[8,96,256]{2,1,0:T(8,128)(2,1)}, bf16[8,96,256]{2,1,0:T(8,128)(2,1)S(1)}, u32[]{:S(2)}, u32[]{:S(2)}) collective-permute-start(bf16[8,96,256]{2,1,0:T(8,128)(2,1)} %normalise.1.refs_1_), channel_id=1, source_target_pairs={{0,14},{2,0},{4,2},{6,4},{8,6},{10,8},{12,10},{14,12},{1,15},{3,1}... | collective-permute-start | bytes 1179656 | tf_op jit(solution)/shard_map/ppermute | solution.py:209
  30.8 14.3 %collective-permute-start.1 = (bf16[8,96,256]{2,1,0:T(8,128)(2,1)}, bf16[8,96,256]{2,1,0:T(8,128)(2,1)S(1)}, u32[]{:S(2)}, u32[]{:S(2)}) collective-permute-start(bf16[8,96,256]{2,1,0:T(8,128)(2,1)} %normalise.1.refs_1_), channel_id=1, source_target_pairs={{0,2},{2,4},{4,6},{6,8},{8,10},{10,12},{12,14},{14,0},{1,3},{3,5},... | collective-permute-start | bytes 1179656 | tf_op jit(solution)/shard_map/ppermute | solution.py:209
  40.8 41.4 %copy-start.3 = (bf16[8,96,256]{2,1,0:T(8,128)(2,1)}, bf16[8,96,256]{2,1,0:T(8,128)(2,1)S(1)}, u32[]{:S(2)}) copy-start(bf16[8,96,256]{2,1,0:T(8,128)(2,1)S(1)} %collective-permute-done.3.refs_5_) | copy-start | bytes 1179652
  40.8 9.6 %collective-permute-start.7 = (bf16[8,96,256]{2,1,0:T(8,128)(2,1)S(1)}, bf16[8,96,256]{2,1,0:T(8,128)(2,1)S(1)}, u32[]{:S(2)}, u32[]{:S(2)}) collective-permute-start(bf16[8,96,256]{2,1,0:T(8,128)(2,1)S(1)} %collective-permute-done.3.refs_5_), channel_id=1, source_target_pairs={{0,14},{2,0},{4,2},{6,4},{8,6},{10,8},{12,10},{14,12},{1,15},{3,1}... | collective-permute-start | bytes 1179656 | tf_op jit(solution)/shard_map/ppermute | solution.py:209
  45.1 37.1 %copy-start.4 = (bf16[8,96,256]{2,1,0:T(8,128)(2,1)}, bf16[8,96,256]{2,1,0:T(8,128)(2,1)S(1)}, u32[]{:S(2)}) copy-start(bf16[8,96,256]{2,1,0:T(8,128)(2,1)S(1)} %collective-permute-done.1.refs_3_) | copy-start | bytes 1179652
  45.1 10.4 %collective-permute-start.5 = (bf16[8,96,256]{2,1,0:T(8,128)(2,1)S(1)}, bf16[8,96,256]{2,1,0:T(8,128)(2,1)S(1)}, u32[]{:S(2)}, u32[]{:S(2)}) collective-permute-start(bf16[8,96,256]{2,1,0:T(8,128)(2,1)S(1)} %collective-permute-done.1.refs_3_), channel_id=1, source_target_pairs={{0,2},{2,4},{4,6},{6,8},{8,10},{10,12},{12,14},{14,0},{1,3},{3,5},... | collective-permute-start | bytes 1179656 | tf_op jit(solution)/shard_map/ppermute | solution.py:209
  50.5 31.8 %copy-start.5 = (bf16[8,96,256]{2,1,0:T(8,128)(2,1)}, bf16[8,96,256]{2,1,0:T(8,128)(2,1)S(1)}, u32[]{:S(2)}) copy-start(bf16[8,96,256]{2,1,0:T(8,128)(2,1)S(1)} %collective-permute-done.7.refs_9_) | copy-start | bytes 1179652
  50.5 9.1 %collective-permute-start.11 = (bf16[8,96,256]{2,1,0:T(8,128)(2,1)S(1)}, bf16[8,96,256]{2,1,0:T(8,128)(2,1)S(1)}, u32[]{:S(2)}, u32[]{:S(2)}) collective-permute-start(bf16[8,96,256]{2,1,0:T(8,128)(2,1)S(1)} %collective-permute-done.7.refs_9_), channel_id=1, source_target_pairs={{0,14},{2,0},{4,2},{6,4},{8,6},{10,8},{12,10},{14,12},{1,15},{3,1}... | collective-permute-start | bytes 1179656 | tf_op jit(solution)/shard_map/ppermute | solution.py:209
  54.2 14.6 %collective-permute-start = (bf16[8,96,256]{2,1,0:T(8,128)(2,1)}, bf16[8,96,256]{2,1,0:T(8,128)(2,1)S(1)}, u32[]{:S(2)}, u32[]{:S(2)}) collective-permute-start(bf16[8,96,256]{2,1,0:T(8,128)(2,1)} %normalise.1.refs_1_), channel_id=1, source_target_pairs={{0,1},{1,0},{2,3},{3,2},{4,5},{5,4},{6,7},{7,6},{8,9},{9,8},{10,11... | collective-permute-start | bytes 1179656 | tf_op jit(solution)/shard_map/ppermute | solution.py:213
  54.3 18.3 %collective-permute-start.4 = (bf16[8,96,256]{2,1,0:T(8,128)(2,1)S(1)}, bf16[8,96,256]{2,1,0:T(8,128)(2,1)}, u32[]{:S(2)}, u32[]{:S(2)}) collective-permute-start(bf16[8,96,256]{2,1,0:T(8,128)(2,1)S(1)} %collective-permute-done.3.refs_5_), channel_id=1, source_target_pairs={{0,1},{1,0},{2,3},{3,2},{4,5},{5,4},{6,7},{7,6},{8,9},{9,8},{10,11... | collective-permute-start | bytes 1179656 | tf_op jit(solution)/shard_map/ppermute | solution.py:213
  54.8 17.9 %collective-permute-start.2 = (bf16[8,96,256]{2,1,0:T(8,128)(2,1)S(1)}, bf16[8,96,256]{2,1,0:T(8,128)(2,1)}, u32[]{:S(2)}, u32[]{:S(2)}) collective-permute-start(bf16[8,96,256]{2,1,0:T(8,128)(2,1)S(1)} %collective-permute-done.1.refs_3_), channel_id=1, source_target_pairs={{0,1},{1,0},{2,3},{3,2},{4,5},{5,4},{6,7},{7,6},{8,9},{9,8},{10,11... | collective-permute-start | bytes 1179656 | tf_op jit(solution)/shard_map/ppermute | solution.py:213
  55.5 26.7 %copy-start.6 = (bf16[8,96,256]{2,1,0:T(8,128)(2,1)}, bf16[8,96,256]{2,1,0:T(8,128)(2,1)S(1)}, u32[]{:S(2)}) copy-start(bf16[8,96,256]{2,1,0:T(8,128)(2,1)S(1)} %collective-permute-done.5.refs_7_) | copy-start | bytes 1179652
  55.5 17.5 %collective-permute-start.8 = (bf16[8,96,256]{2,1,0:T(8,128)(2,1)S(1)}, bf16[8,96,256]{2,1,0:T(8,128)(2,1)}, u32[]{:S(2)}, u32[]{:S(2)}) collective-permute-start(bf16[8,96,256]{2,1,0:T(8,128)(2,1)S(1)} %collective-permute-done.7.refs_9_), channel_id=1, source_target_pairs={{0,1},{1,0},{2,3},{3,2},{4,5},{5,4},{6,7},{7,6},{8,9},{9,8},{10,11... | collective-permute-start | bytes 1179656 | tf_op jit(solution)/shard_map/ppermute | solution.py:213
  59.5 22.7 %copy-start = (bf16[8,96,256]{2,1,0:T(8,128)(2,1)}, bf16[8,96,256]{2,1,0:T(8,128)(2,1)S(1)}, u32[]{:S(2)}) copy-start(bf16[8,96,256]{2,1,0:T(8,128)(2,1)S(1)} %collective-permute-done.11.refs_13_) | copy-start | bytes 1179652
  59.5 9.3 %collective-permute-start.9 = (bf16[8,96,256]{2,1,0:T(8,128)(2,1)S(1)}, bf16[8,96,256]{2,1,0:T(8,128)(2,1)S(1)}, u32[]{:S(2)}, u32[]{:S(2)}) collective-permute-start(bf16[8,96,256]{2,1,0:T(8,128)(2,1)S(1)} %collective-permute-done.5.refs_7_), channel_id=1, source_target_pairs={{0,2},{2,4},{4,6},{6,8},{8,10},{10,12},{12,14},{14,0},{1,3},{3,5},... | collective-permute-start | bytes 1179656 | tf_op jit(solution)/shard_map/ppermute | solution.py:209
  68.8 13.4 %copy-start.1 = (bf16[8,96,256]{2,1,0:T(8,128)(2,1)}, bf16[8,96,256]{2,1,0:T(8,128)(2,1)S(1)}, u32[]{:S(2)}) copy-start(bf16[8,96,256]{2,1,0:T(8,128)(2,1)S(1)} %collective-permute-done.9.refs_11_) | copy-start | bytes 1179652
  68.8 11.2 %collective-permute-start.6 = (bf16[8,96,256]{2,1,0:T(8,128)(2,1)S(1)}, bf16[8,96,256]{2,1,0:T(8,128)(2,1)S(1)}, u32[]{:S(2)}, u32[]{:S(2)}) collective-permute-start(bf16[8,96,256]{2,1,0:T(8,128)(2,1)S(1)} %collective-permute-done.5.refs_7_), channel_id=1, source_target_pairs={{0,1},{1,0},{2,3},{3,2},{4,5},{5,4},{6,7},{7,6},{8,9},{9,8},{10,11... | collective-permute-start | bytes 1179656 | tf_op jit(solution)/shard_map/ppermute | solution.py:213
  68.9 13.4 %copy-start.7 = (bf16[8,96,256]{2,1,0:T(8,128)(2,1)}, bf16[8,96,256]{2,1,0:T(8,128)(2,1)S(1)}, u32[]{:S(2)}) copy-start(bf16[8,96,256]{2,1,0:T(8,128)(2,1)S(1)} %collective-permute-done.refs_2_) | copy-start | bytes 1179652
  68.9 8.6 %collective-permute-start.15 = (bf16[4,96,256]{2,1,0:T(8,128)(2,1)S(1)}, bf16[4,96,256]{2,1,0:T(8,128)(2,1)S(1)}, u32[]{:S(2)}, u32[]{:S(2)}) collective-permute-start(bf16[4,96,256]{2,1,0:T(8,128)(2,1)S(1)} %slice.22), channel_id=1, source_target_pairs={{0,14},{2,0},{4,2},{6,4},{8,6},{10,8},{12,10},{14,12},{1,15},{3,1}... | collective-permute-start | bytes 589832 | tf_op jit(solution)/shard_map/ppermute | solution.py:209
  72.6 7.3 %collective-permute-start.13 = (bf16[4,96,256]{2,1,0:T(8,128)(2,1)S(1)}, bf16[4,96,256]{2,1,0:T(8,128)(2,1)S(1)}, u32[]{:S(2)}, u32[]{:S(2)}) collective-permute-start(bf16[4,96,256]{2,1,0:T(8,128)(2,1)S(1)} %slice.21), channel_id=1, source_target_pairs={{0,2},{2,4},{4,6},{6,8},{8,10},{10,12},{12,14},{14,0},{1,3},{3,5},... | collective-permute-start | bytes 589832 | tf_op jit(solution)/shard_map/ppermute | solution.py:209
  72.7 7.4 %collective-permute-start.12 = (bf16[8,96,256]{2,1,0:T(8,128)(2,1)S(1)}, bf16[8,96,256]{2,1,0:T(8,128)(2,1)S(1)}, u32[]{:S(2)}, u32[]{:S(2)}) collective-permute-start(bf16[8,96,256]{2,1,0:T(8,128)(2,1)S(1)} %collective-permute-done.11.refs_13_), channel_id=1, source_target_pairs={{0,1},{1,0},{2,3},{3,2},{4,5},{5,4},{6,7},{7,6},{8,9},{9,8},{10,11... | collective-permute-start | bytes 1179656 | tf_op jit(solution)/shard_map/ppermute | solution.py:213
  73.0 7.1 %collective-permute-start.10 = (bf16[8,96,256]{2,1,0:T(8,128)(2,1)S(1)}, bf16[8,96,256]{2,1,0:T(8,128)(2,1)S(1)}, u32[]{:S(2)}, u32[]{:S(2)}) collective-permute-start(bf16[8,96,256]{2,1,0:T(8,128)(2,1)S(1)} %collective-permute-done.9.refs_11_), channel_id=1, source_target_pairs={{0,1},{1,0},{2,3},{3,2},{4,5},{5,4},{6,7},{7,6},{8,9},{9,8},{10,11... | collective-permute-start | bytes 1179656 | tf_op jit(solution)/shard_map/ppermute | solution.py:213
  77.5 4.8 %copy-start.11 = (bf16[4,96,256]{2,1,0:T(8,128)(2,1)}, bf16[4,96,256]{2,1,0:T(8,128)(2,1)S(1)}, u32[]{:S(2)}) copy-start(bf16[4,96,256]{2,1,0:T(8,128)(2,1)S(1)} %collective-permute-done.15.refs_17_) | copy-start | bytes 589828
  77.5 3.3 %collective-permute-start.16 = (bf16[4,96,256]{2,1,0:T(8,128)(2,1)S(1)}, bf16[4,96,256]{2,1,0:T(8,128)(2,1)S(1)}, u32[]{:S(2)}, u32[]{:S(2)}) collective-permute-start(bf16[4,96,256]{2,1,0:T(8,128)(2,1)S(1)} %collective-permute-done.15.refs_17_), channel_id=1, source_target_pairs={{0,1},{1,0},{2,3},{3,2},{4,5},{5,4},{6,7},{7,6},{8,9},{9,8},{10,11... | collective-permute-start | bytes 589832 | tf_op jit(solution)/shard_map/ppermute | solution.py:213
  80.0 0.8 copy-start.12
  80.0 1.6 collective-permute-start.14
  80.0 0.7 copy-start.8
  80.0 0.9 copy-start.9
  80.8 0.7 copy-start.10
  81.5 0.7 copy-start.13
  105.7 5.9 %collective-permute-start.17 = (f32[32,384]{1,0:T(8,128)S(1)}, f32[32,384]{1,0:T(8,128)S(1)}, u32[]{:S(2)}, u32[]{:S(2)}) collective-permute-start(f32[32,384]{1,0:T(8,128)S(1)} %get-tuple-element.24), channel_id=1, source_target_pairs={{0,64},{16,80},{32,96},{48,112},{64,128},{80,144},{96,160},{112,17... | collective-permute-start | bytes 147464 | tf_op jit(solution)/shard_map/ppermute | solution.py:284
  105.8 6.7 %collective-permute-start.18 = (f32[32,384]{1,0:T(8,128)S(1)}, f32[32,384]{1,0:T(8,128)S(1)}, u32[]{:S(2)}, u32[]{:S(2)}) collective-permute-start(f32[32,384]{1,0:T(8,128)S(1)} %get-tuple-element.25), channel_id=1, source_target_pairs={{0,128},{16,144},{32,160},{48,176},{64,192},{80,208},{96,224},{112... | collective-permute-start | bytes 147464 | tf_op jit(solution)/shard_map/ppermute | solution.py:284
  108.4 9.1 %collective-permute-start.19 = (f32[32,384]{1,0:T(8,128)S(1)}, f32[32,384]{1,0:T(8,128)S(1)}, u32[]{:S(2)}, u32[]{:S(2)}) collective-permute-start(f32[32,384]{1,0:T(8,128)S(1)} %get-tuple-element.26), channel_id=1, source_target_pairs={{0,192},{16,208},{32,224},{48,240},{64,0},{80,16},{96,32},{112,48}... | collective-permute-start | bytes 147464 | tf_op jit(solution)/shard_map/ppermute | solution.py:284
  110.1 8.3 %collective-permute-start.20 = (f32[32,384]{1,0:T(8,128)S(1)}, f32[32,384]{1,0:T(8,128)S(1)}, u32[]{:S(2)}, u32[]{:S(2)}) collective-permute-start(f32[32,384]{1,0:T(8,128)S(1)} %get-tuple-element.27), channel_id=1, source_target_pairs={{0,16},{16,32},{32,48},{48,0},{64,80},{80,96},{96,112},{112,64},{1... | collective-permute-start | bytes 147464 | tf_op jit(solution)/shard_map/ppermute | solution.py:284
  110.1 9.4 %collective-permute-start.21 = (f32[32,384]{1,0:T(8,128)S(1)}, f32[32,384]{1,0:T(8,128)S(1)}, u32[]{:S(2)}, u32[]{:S(2)}) collective-permute-start(f32[32,384]{1,0:T(8,128)S(1)} %get-tuple-element.28), channel_id=1, source_target_pairs={{0,80},{16,96},{32,112},{48,64},{64,144},{80,160},{96,176},{112,12... | collective-permute-start | bytes 147464 | tf_op jit(solution)/shard_map/ppermute | solution.py:284
  111.6 11.6 %collective-permute-start.22 = (f32[32,384]{1,0:T(8,128)S(1)}, f32[32,384]{1,0:T(8,128)S(1)}, u32[]{:S(2)}, u32[]{:S(2)}) collective-permute-start(f32[32,384]{1,0:T(8,128)S(1)} %get-tuple-element.29), channel_id=1, source_target_pairs={{0,144},{16,160},{32,176},{48,128},{64,208},{80,224},{96,240},{112... | collective-permute-start | bytes 147464 | tf_op jit(solution)/shard_map/ppermute | solution.py:284
  112.4 14.8 %collective-permute-start.23 = (f32[32,384]{1,0:T(8,128)S(1)}, f32[32,384]{1,0:T(8,128)S(1)}, u32[]{:S(2)}, u32[]{:S(2)}) collective-permute-start(f32[32,384]{1,0:T(8,128)S(1)} %get-tuple-element.30), channel_id=1, source_target_pairs={{0,208},{16,224},{32,240},{48,192},{64,16},{80,32},{96,48},{112,0}... | collective-permute-start | bytes 147464 | tf_op jit(solution)/shard_map/ppermute | solution.py:284
  117.5 10.3 %collective-permute-start.24 = (f32[32,384]{1,0:T(8,128)S(1)}, f32[32,384]{1,0:T(8,128)S(1)}, u32[]{:S(2)}, u32[]{:S(2)}) collective-permute-start(f32[32,384]{1,0:T(8,128)S(1)} %get-tuple-element.31), channel_id=1, source_target_pairs={{0,32},{16,48},{32,0},{48,16},{64,96},{80,112},{96,64},{112,80},{1... | collective-permute-start | bytes 147464 | tf_op jit(solution)/shard_map/ppermute | solution.py:284
  118.4 9.7 %collective-permute-start.25 = (f32[32,384]{1,0:T(8,128)S(1)}, f32[32,384]{1,0:T(8,128)S(1)}, u32[]{:S(2)}, u32[]{:S(2)}) collective-permute-start(f32[32,384]{1,0:T(8,128)S(1)} %get-tuple-element.32), channel_id=1, source_target_pairs={{0,96},{16,112},{32,64},{48,80},{64,160},{80,176},{96,128},{112,14... | collective-permute-start | bytes 147464 | tf_op jit(solution)/shard_map/ppermute | solution.py:284
  119.6 10.7 %collective-permute-start.26 = (f32[32,384]{1,0:T(8,128)S(1)}, f32[32,384]{1,0:T(8,128)S(1)}, u32[]{:S(2)}, u32[]{:S(2)}) collective-permute-start(f32[32,384]{1,0:T(8,128)S(1)} %get-tuple-element.33), channel_id=1, source_target_pairs={{0,160},{16,176},{32,128},{48,144},{64,224},{80,240},{96,192},{112... | collective-permute-start | bytes 147464 | tf_op jit(solution)/shard_map/ppermute | solution.py:284
  123.1 22.1 %collective-permute-start.27 = (f32[32,384]{1,0:T(8,128)S(1)}, f32[32,384]{1,0:T(8,128)S(1)}, u32[]{:S(2)}, u32[]{:S(2)}) collective-permute-start(f32[32,384]{1,0:T(8,128)S(1)} %get-tuple-element.34), channel_id=1, source_target_pairs={{0,224},{16,240},{32,192},{48,208},{64,32},{80,48},{96,0},{112,16}... | collective-permute-start | bytes 147464 | tf_op jit(solution)/shard_map/ppermute | solution.py:284
  127.3 18.0 %collective-permute-start.28 = (f32[32,384]{1,0:T(8,128)S(1)}, f32[32,384]{1,0:T(8,128)S(1)}, u32[]{:S(2)}, u32[]{:S(2)}) collective-permute-start(f32[32,384]{1,0:T(8,128)S(1)} %get-tuple-element.35), channel_id=1, source_target_pairs={{0,48},{16,0},{32,16},{48,32},{64,112},{80,64},{96,80},{112,96},{1... | collective-permute-start | bytes 147464 | tf_op jit(solution)/shard_map/ppermute | solution.py:284
  127.8 17.5 %collective-permute-start.29 = (f32[32,384]{1,0:T(8,128)S(1)}, f32[32,384]{1,0:T(8,128)S(1)}, u32[]{:S(2)}, u32[]{:S(2)}) collective-permute-start(f32[32,384]{1,0:T(8,128)S(1)} %get-tuple-element.36), channel_id=1, source_target_pairs={{0,112},{16,64},{32,80},{48,96},{64,176},{80,128},{96,144},{112,16... | collective-permute-start | bytes 147464 | tf_op jit(solution)/shard_map/ppermute | solution.py:284
  128.1 17.1 %collective-permute-start.30 = (f32[32,384]{1,0:T(8,128)S(1)}, f32[32,384]{1,0:T(8,128)S(1)}, u32[]{:S(2)}, u32[]{:S(2)}) collective-permute-start(f32[32,384]{1,0:T(8,128)S(1)} %get-tuple-element.37), channel_id=1, source_target_pairs={{0,176},{16,128},{32,144},{48,160},{64,240},{80,192},{96,208},{112... | collective-permute-start | bytes 147464 | tf_op jit(solution)/shard_map/ppermute | solution.py:284
  130.3 15.0 %collective-permute-start.31 = (f32[32,384]{1,0:T(8,128)S(1)}, f32[32,384]{1,0:T(8,128)S(1)}, u32[]{:S(2)}, u32[]{:S(2)}) collective-permute-start(f32[32,384]{1,0:T(8,128)S(1)} %get-tuple-element.38), channel_id=1, source_target_pairs={{0,240},{16,192},{32,208},{48,224},{64,48},{80,0},{96,16},{112,32}... | collective-permute-start | bytes 147464 | tf_op jit(solution)/shard_map/ppermute | solution.py:284
  135.9 19.3 %all-to-all-start.1 = ((f32[64,4,96]{2,1,0:T(4,128)}), f32[64,4,96]{2,1,0:T(4,128)S(1)}, u32[]{:S(2)}, u32[]{:S(2)}) async-start(f32[64,4,96]{2,1,0:T(4,128)} %bitcast.6), calls=%async_computation.1 | async-start | bytes 262144 | tf_op jit(solution)/shard_map/all_to_all | solution.py:275
  155.3 0.7 copy-start.2
Sparse Core Ops, SparseCore 0:
  11.1 68.9 all-gather.2

commit v3 on v2

v3 whole, which is shorter than its diff:
```python
import jax
import jax.numpy as jnp
import numpy as np
from jax import lax
from jax.experimental import pallas as pl
from jax.experimental.pallas import tpu as pltpu
from jax.sharding import Mesh
from jax.sharding import PartitionSpec as P

EPSILON = 1e-06

NX, NZ, NC, NY = 4, 8, 2, 4
NDEV = NX * NZ * NC
PER = 2
ROWS = 256
RB = ROWS // NY
UNITS = 1536
SLICES = NX * NY
WIDTH = UNITS // SLICES
QUARTER = UNITS // NY
SLOTS = 32
QROWS = QUARTER // 128 * SLOTS
LROWS = NY * QROWS
PAIRS = NX * SLOTS
LEFTS = NX * PER
BLOCK = 128
HALF = LEFTS // 2
GROUP = 8
TILE = 256

VMEM = pl.BlockSpec(memory_space=pltpu.VMEM)
HBM = pl.BlockSpec(memory_space=pltpu.HBM)


def prepare(codes, scales):
    def kernel(codes_ref, scales_ref, acts_ref, slices_ref):
        column = [jnp.transpose(scales_ref[:, h, :]) for h in range(PER)]
        for k in range(UNITS // BLOCK):
            low = k * BLOCK
            both = []
            for h in range(PER):
                value = codes_ref[h, :, low : low + BLOCK].astype(jnp.float32)
                rounded = (value * column[h][:, k : k + 1]).astype(jnp.bfloat16)
                acts_ref[h, :, low : low + BLOCK] = rounded
                both.append(rounded.astype(jnp.float32))
            turned = jnp.transpose(jnp.concatenate(both, axis=0)).astype(jnp.bfloat16)
            done = 0
            while done < BLOCK:
                unit = low + done
                take = min(BLOCK - done, WIDTH - unit % WIDTH)
                slices_ref[unit // WIDTH, unit % WIDTH : unit % WIDTH + take, :] = turned[
                    done : done + take
                ]
                done += take

    return pl.pallas_call(
        kernel,
        in_specs=[VMEM, VMEM],
        out_specs=[VMEM] * 2,
        out_shape=[
            jax.ShapeDtypeStruct((PER, RB, UNITS), jnp.bfloat16),
            jax.ShapeDtypeStruct((SLICES, WIDTH, PER * RB), jnp.bfloat16),
        ],
        name="prepare",
    )(codes, scales)


def normalise(pieces):
    def kernel(in_ref, *out_refs):
        for x in range(NX):
            part = [in_ref[y * NX + x].astype(jnp.float32) for y in range(NY)]
            for h in range(PER):
                lanes = slice(h * RB, (h + 1) * RB)
                full = jnp.concatenate([p[:, lanes] for p in part], axis=1)
                square = jnp.sum(full * full, axis=1, keepdims=True) / ROWS
                inverse = 1.0 / jnp.sqrt(square + EPSILON)
                at = x * PER + h
                out_refs[at // HALF][at % HALF] = (full * (inverse * (1.0 / ROWS))).astype(jnp.bfloat16)

    return pl.pallas_call(
        kernel,
        in_specs=[VMEM],
        out_specs=[VMEM] * 2,
        out_shape=[jax.ShapeDtypeStruct((HALF, WIDTH, ROWS), jnp.bfloat16)] * 2,
        name="normalise",
    )(pieces)


def correlate(start, order, jidx, lpos, rpos, gathered, chunks, places):
    count = len(chunks)

    def kernel(start_ref, order_ref, jidx_ref, lpos_ref, rpos_ref, gathered_ref, *refs):
        chunk_refs = refs[:count]
        left_refs = refs[count : count + NX]
        right_ref, left, acts, others, norms, sem = refs[count + NX :]
        loads = [
            pltpu.make_async_copy(ref, others.at[pl.ds(at, size)], sem.at[n])
            for n, (ref, (at, size)) in enumerate(zip(chunk_refs, places))
        ]

        def rows_of(x, y):
            return pltpu.make_async_copy(
                gathered_ref.at[x * NY + y],
                acts.at[pl.ds(x * PER, PER), pl.ds(y * RB, RB), :],
                sem.at[count + x * NY + y],
            )

        for load in loads:
            load.start()
        for x in range(NX):
            for y in range(NY):
                rows_of(x, y).start()
        right_ref[...] = jnp.zeros_like(right_ref)
        for load in loads:
            load.wait()

        def expert(i, carry):
            @pl.when(i % PER == 0)
            def _():
                for y in range(NY):
                    rows_of(i // PER, y).wait()

            for n in range(UNITS // TILE):
                lanes = slice(n * TILE, (n + 1) * TILE)
                value = acts[i, :, lanes].astype(jnp.float32)
                square = jnp.sum(value * value, axis=0, keepdims=True) / ROWS
                norms[:, lanes] = 1.0 / jnp.sqrt(square + EPSILON)
            low = start_ref[i]
            high = start_ref[i + 1]
            scales = norms[...]

            def block(first, size):
                pairs = [order_ref[jnp.minimum(first + g, high - 1)] for g in range(size)]
                lhs = jnp.concatenate([others[jidx_ref[p]] for p in pairs], axis=0)
                best = [None] * size
                for n in range(UNITS // TILE):
                    out = jnp.dot(
                        lhs,
                        acts[i, :, n * TILE : (n + 1) * TILE],
                        preferred_element_type=jnp.float32,
                    )
                    for g in range(size):
                        one = out[g * WIDTH : (g + 1) * WIDTH]
                        for m in range(TILE // 128):
                            unit = n * TILE + m * 128
                            scale = scales[:, unit : unit + 128]
                            part = one[:, m * 128 : (m + 1) * 128]
                            top = jnp.max(part, axis=0, keepdims=True) * scale
                            row = lpos_ref[unit // QUARTER, pairs[g]] + unit % QUARTER // 128 * SLOTS
                            left[pl.ds(row, 1), :] = top
                            scaled = part * scale
                            best[g] = scaled if best[g] is None else jnp.maximum(best[g], scaled)
                for g in range(size):
                    top = jnp.max(jnp.transpose(best[g]), axis=0, keepdims=True)
                    right_ref[pl.ds(rpos_ref[pairs[g]], 1), :] = top

            rest = (high - low) % GROUP
            full = (high - low) // GROUP + (rest > GROUP // 2).astype(jnp.int32)

            def step(b, carry):
                block(low + b * GROUP, GROUP)
                return carry

            lax.fori_loop(0, full, step, 0)

            @pl.when((rest > 0) & (rest <= GROUP // 2))
            def _():
                block(low + full * GROUP, GROUP // 2)

            return carry

        lax.fori_loop(0, LEFTS, expert, 0)
        for k, ref in enumerate(left_refs):
            ref[...] = left[k * LROWS : (k + 1) * LROWS, :]

    return pl.pallas_call(
        kernel,
        grid_spec=pltpu.PrefetchScalarGridSpec(
            num_scalar_prefetch=5,
            grid=(1,),
            in_specs=[HBM] * (1 + count),
            out_specs=[VMEM] * (NX + 1),
            scratch_shapes=[
                pltpu.VMEM((NX * LROWS, 128), jnp.float32),
                pltpu.VMEM((LEFTS, ROWS, UNITS), jnp.bfloat16),
                pltpu.VMEM((NZ * NC * LEFTS, WIDTH, ROWS), jnp.bfloat16),
                pltpu.VMEM((1, UNITS), jnp.float32),
                pltpu.SemaphoreType.DMA((count + NX * NY,)),
            ],
        ),
        out_shape=[jax.ShapeDtypeStruct((LROWS, 128), jnp.float32)] * NX
        + [jax.ShapeDtypeStruct((NDEV * NX, WIDTH), jnp.float32)],
        compiler_params=pltpu.CompilerParams(vmem_limit_bytes=24 << 20),
        name="correlate",
    )(start, order, jidx, lpos, rpos, gathered, *chunks)


def finish_right(rows, returned):
    def kernel(rows_ref, in_ref, out_ref):
        for s in range(SLOTS):
            for x in range(NX):
                out_ref[s : s + 1, x * WIDTH : (x + 1) * WIDTH] = in_ref[x, pl.ds(rows_ref[s], 1), :]

    return pl.pallas_call(
        kernel,
        grid_spec=pltpu.PrefetchScalarGridSpec(
            num_scalar_prefetch=1, grid=(1,), in_specs=[VMEM], out_specs=VMEM
        ),
        out_shape=jax.ShapeDtypeStruct((SLOTS, QUARTER), jnp.float32),
        name="finish_right",
    )(rows, returned)


def meet(parts):
    def kernel(*refs):
        for k in range(NY):
            rows = slice(k * QROWS, (k + 1) * QROWS)
            best = refs[0][rows, :]
            for ref in refs[1:NX]:
                best = jnp.maximum(best, ref[rows, :])
            refs[NX + k][...] = best

    return pl.pallas_call(
        kernel,
        in_specs=[VMEM] * NX,
        out_specs=[VMEM] * NY,
        out_shape=[jax.ShapeDtypeStruct((QROWS, 128), jnp.float32)] * NY,
        name="meet",
    )(*parts)


def finish_left(parts):
    def kernel(*refs):
        for t in range(QUARTER // 128):
            rows = slice(t * SLOTS, (t + 1) * SLOTS)
            best = refs[0][rows, :]
            for ref in refs[1:NY]:
                best = jnp.maximum(best, ref[rows, :])
            refs[NY][:, t * 128 : (t + 1) * 128] = best

    return pl.pallas_call(
        kernel,
        in_specs=[VMEM] * NY,
        out_specs=VMEM,
        out_shape=jax.ShapeDtypeStruct((SLOTS, QUARTER), jnp.float32),
        name="finish_left",
    )(*parts)


def in_hbm(value):
    return pltpu.with_memory_space_constraint(value, pltpu.HBM)


def shift(value, axis, by, size):
    return lax.ppermute(value, axis, [(i, (i + by) % size) for i in range(size)])


def swap(value):
    return lax.ppermute(value, "core", [(0, 1), (1, 0)])


def body(unit_codes, block_scales, pair_list):
    y = lax.axis_index("dp")
    x = lax.axis_index("x")
    z = lax.axis_index("z")
    c = lax.axis_index("core")
    me = (x * NZ + z) * NC + c

    table = pair_list.reshape(NX, NZ * NC, SLOTS, 2)
    mine = lax.dynamic_index_in_dim(table, z * NC + c, 1, keepdims=False).reshape(PAIRS, 2)
    pair = jnp.arange(PAIRS, dtype=jnp.int32)
    right_dev = mine[:, 1] // PER
    right_x = right_dev // (NZ * NC)
    right_z = (right_dev // NC) % NZ
    right_c = right_dev % NC
    jidx = (((right_c != c) * NZ + (right_z - z) % NZ) * NX + right_x) * PER + mine[:, 1] % PER
    key = (pair // SLOTS) * PER + mine[:, 0] % PER
    before = (key[None, :] < key[:, None]) | (
        (key[None, :] == key[:, None]) & (pair[None, :] < pair[:, None])
    )
    rank = jnp.sum(before, axis=1, dtype=jnp.int32)
    order = jnp.sum(jnp.where(rank[None, :] == pair[:, None], pair[None, :], 0), axis=1)
    start = jnp.sum(
        key[None, :] < jnp.arange(LEFTS + 1, dtype=jnp.int32)[:, None], axis=1, dtype=jnp.int32
    )
    quarter = jnp.arange(NY, dtype=jnp.int32)[:, None]
    lpos = ((pair // SLOTS - x) % NX * LROWS + pair % SLOTS)[None, :] + (quarter - y) % NY * QROWS
    rpos = right_dev * NX + pair // SLOTS
    offsets = pair_list[:SLOTS, 1] // PER
    source = (me - offsets) % NDEV
    rows = (source % (NZ * NC)) * NX + source // (NZ * NC)

    acts, slices = prepare(unit_codes, jnp.transpose(block_scales, (1, 0, 2)))
    pieces = lax.all_to_all(slices, ("dp", "x"), split_axis=0, concat_axis=0, tiled=True)
    gathered = in_hbm(lax.all_gather(acts, ("x", "dp"), axis=0, tiled=False))
    own = normalise(pieces)

    chunks, places = [], []

    def keep(value, rel, chain):
        for other, part in enumerate((value, swap(value))):
            chunks.append(in_hbm(part))
            places.append(((other * NZ + rel) * LEFTS + chain * HALF, HALF))

    up, down = list(own), list(own)
    for chain in range(2):
        keep(own[chain], 0, chain)
    for k in range(1, NZ // 2):
        for chain in range(2):
            up[chain] = shift(up[chain], "z", 1, NZ)
            down[chain] = shift(down[chain], "z", -1, NZ)
        for chain in range(2):
            keep(up[chain], NZ - k, chain)
            keep(down[chain], k, chain)
    keep(shift(up[0], "z", 1, NZ), NZ // 2, 0)
    keep(shift(down[1], "z", -1, NZ), NZ // 2, 1)

    *left, right = correlate(start, order, jidx, lpos, rpos, gathered, chunks, places)
    returned = lax.all_to_all(
        right.reshape(NDEV, NX, WIDTH), ("x", "z", "core"), split_axis=0, concat_axis=0, tiled=True
    )
    right_out = finish_right(rows, returned.reshape(NX, NZ * NC * NX, WIDTH))
    parts = meet([left[0]] + [shift(left[k], "x", k, NX) for k in range(1, NX)])
    left_out = finish_left([parts[0]] + [shift(parts[k], "dp", k, NY) for k in range(1, NY)])
    return (left_out[None], right_out[None])


def solution(mesh):
    fine = Mesh(np.asarray(mesh.devices).reshape(NY, NX, NZ, NC), ("dp", "x", "z", "core"))
    expert = ("x", "z", "core")
    in_specs = (P(expert, "dp", None), P(expert, None, "dp"), P())
    out_specs = (P(expert, None, "dp"), P(expert, None, "dp"))
    return jax.shard_map(body, mesh=fine, in_specs=in_specs, out_specs=out_specs, check_vma=False)
```

time: 166 us -> 141 us (0.85)
  blocking collectives: 17.2 us -> 0 us
  waiting for transfers between devices: 41.2 us -> 34.8 us
  starting transfers between devices: 54.2 us -> 49.4 us
  Pallas kernels: 30.7 us -> 33.1 us
    ppermute x15 -> x0, starting transfers between devices: 28.1 us -> none  [body(): left_out = jnp.maximum(left_out, lax.ppermute(lefts[k], ('dp', 'x'), moves))]
    all_to_all x1 -> x0, blocking collectives: 17.2 us -> none  [body(): lax.all_to_all(slices, ('dp', 'x'), split_axis=0, concat_axis=0, tiled=True)]
    ppermute x8 -> x20, starting transfers between devices: 15.5 us -> 31.7 us  [shift(): lax.ppermute(value, axis, [(i, (i + by) % size) for i in range(size)])]
    ppermute x8 -> x20, waiting for transfers between devices: 30.9 us -> 17.2 us  [shift(): lax.ppermute(value, axis, [(i, (i + by) % size) for i in range(size)])]
    all_to_all x0 -> x1, waiting for transfers between devices: none -> 9.14 us  [body(): lax.all_to_all(slices, ('dp', 'x'), split_axis=0, concat_axis=0, tiled=True)]
    all_to_all x1, waiting for transfers between devices: 9.31 us -> 0.48 us  [body(): lax.all_to_all(right.reshape(NDEV, NX, WIDTH), ('x', 'z', 'core'), split_...]
    all_gather x1, waiting for transfers between devices: 0.01 us -> 7.12 us  [body(): gathered = in_hbm(lax.all_gather(acts, ('x', 'dp'), axis=0, tiled=False))]
    all_to_all x0 -> x1, starting transfers between devices: none -> 7.05 us  [body(): lax.all_to_all(slices, ('dp', 'x'), split_axis=0, concat_axis=0, tiled=True)]
  transfers between devices with their start and end apart: 34 -> 39, of which waited for: 9 -> 14; matrix products, arithmetic and copies ran while one was open for 2% -> 2% of each run, Pallas kernels for 2% -> 5%
where the time goes in v3:
time: 141 us; the launch traced here: 139 us
  starting transfers between devices  49.4 us (35%)
  waiting for transfers between devices  34.8 us (25%)
  Pallas kernels  33.1 us (23%)
  between operations  14.5 us (10%)
  local copies, waits for them, and re-layouts  5.16 us (4%)
  other arithmetic  1.77 us (1%)
    ppermute x20, starting transfers between devices, shift(): lax.ppermute(value, axis, [(i, (i + by) % size) for i in range(size)])  31.7 us
    pallas_call x1, Pallas kernels, correlate(): pl.pallas_call(kernel, grid_spec=pltpu.PrefetchScalarGridSpec(num_scalar_...  22.5 us
    ppermute x20, waiting for transfers between devices, shift(): lax.ppermute(value, axis, [(i, (i + by) % size) for i in range(size)])  17.2 us
    all_to_all x1, waiting for transfers between devices, body(): lax.all_to_all(slices, ('dp', 'x'), split_axis=0, concat_axis=0, tiled=True)  9.14 us
    all_to_all x1, starting transfers between devices, body(): lax.all_to_all(right.reshape(NDEV, NX, WIDTH), ('x', 'z', 'core'), split_...  8.4 us
    all_gather x1, waiting for transfers between devices, body(): gathered = in_hbm(lax.all_gather(acts, ('x', 'dp'), axis=0, tiled=False))  7.12 us
    all_to_all x1, starting transfers between devices, body(): lax.all_to_all(slices, ('dp', 'x'), split_axis=0, concat_axis=0, tiled=True)  7.05 us
    unnamed x76, local copies, waits for them, and re-layouts  4.24 us
  transfers between devices with their start and end apart: 39, of which 14 were waited for; matrix products, arithmetic and copies ran while one was open for 2% of the time, Pallas kernels for 5%

profile of v3, /device:TPU:32, one launch (start us, length us, event | category | flops | bytes accessed | tf_op | source)
XLA Modules:
  0.0 138.8 jit_solution(15231476191524871642)
XLA Ops:
  7.2 0.0 all-gather.3.cloned.1.call-start
  7.2 2.5 %prepare.1 = (bf16[2,64,1536]{2,1,0:T(8,128)(2,1)}, bf16[16,96,128]{2,1,0:T(8,128)(2,1)}) custom-call(bf16[2,64,1536]{2,1,0:T(8,128)(2,1)} %codes_ref.1, f32[12,2,64]{2,1,0:T(2,128)} %bitcast.44), custom_call_target="tpu_custom_call" | custom-call | tf_op jit(solution)/shard_map/prepare/pallas_call | solution.py:56
  9.7 7.0 %all-to-all-start = ((bf16[16,96,128]{2,1,0:T(8,128)(2,1)}), bf16[16,96,128]{2,1,0:T(8,128)(2,1)S(1)}, u32[]{:S(2)}, u32[]{:S(2)}) async-start(bf16[16,96,128]{2,1,0:T(8,128)(2,1)} %get-tuple-element.16), calls=%async_computation | async-start | bytes 786432 | tf_op jit(solution)/shard_map/all_to_all | solution.py:294
  16.7 0.8 reshape.139
  17.6 0.1 reshape.140
  17.7 9.1 %all-to-all-done.in_ref = bf16[16,96,128]{2,1,0:T(8,128)(2,1)S(1)} async-done(((bf16[16,96,128]{2,1,0:T(8,128)(2,1)}), bf16[16,96,128]{2,1,0:T(8,128)(2,1)S(1)}, u32[]{:S(2)}, u32[]{:S(2)}) %all-to-all-start) | async-done | bytes 393248 | tf_op jit(solution)/shard_map/all_to_all | solution.py:294
  26.8 0.8 copy-done.1
  27.6 2.5 %normalise.1 = (bf16[4,96,256]{2,1,0:T(8,128)(2,1)}, bf16[4,96,256]{2,1,0:T(8,128)(2,1)}) custom-call(bf16[16,96,128]{2,1,0:T(8,128)(2,1)} %copy-done.1), custom_call_target="tpu_custom_call" | custom-call | tf_op jit(solution)/shard_map/normalise/pallas_call | solution.py:80
  30.0 0.1 collective-permute-start.4
  30.1 1.9 %collective-permute-start.2 = (bf16[4,96,256]{2,1,0:T(8,128)(2,1)}, bf16[4,96,256]{2,1,0:T(8,128)(2,1)S(1)}, u32[]{:S(2)}, u32[]{:S(2)}) collective-permute-start(bf16[4,96,256]{2,1,0:T(8,128)(2,1)} %get-tuple-element.17.refs_0_), channel_id=1, source_target_pairs={{0,2},{2,4},{4,6},{6,8},{8,10},{10,12},{12,14},{14,0},{1,3},{3,5},... | collective-permute-start | bytes 589832 | tf_op jit(solution)/shard_map/ppermute | solution.py:255
  32.1 3.9 %collective-permute-start.8 = (bf16[4,96,256]{2,1,0:T(8,128)(2,1)}, bf16[4,96,256]{2,1,0:T(8,128)(2,1)S(1)}, u32[]{:S(2)}, u32[]{:S(2)}) collective-permute-start(bf16[4,96,256]{2,1,0:T(8,128)(2,1)} %get-tuple-element.18.refs_2_), channel_id=1, source_target_pairs={{0,14},{2,0},{4,2},{6,4},{8,6},{10,8},{12,10},{14,12},{1,15},{3,1}... | collective-permute-start | bytes 589832 | tf_op jit(solution)/shard_map/ppermute | solution.py:255
  36.0 0.2 collective-permute-done.4.refs_6_
  36.2 0.1 collective-permute-start.1
  36.4 3.5 %collective-permute-done.2.refs_4_ = bf16[4,96,256]{2,1,0:T(8,128)(2,1)S(1)} collective-permute-done((bf16[4,96,256]{2,1,0:T(8,128)(2,1)}, bf16[4,96,256]{2,1,0:T(8,128)(2,1)S(1)}, u32[]{:S(2)}, u32[]{:S(2)}) %collective-permute-start.2) | collective-permute-done | bytes 196640 | tf_op jit(solution)/shard_map/ppermute | solution.py:255
  39.9 3.2 %collective-permute-start.12 = (bf16[4,96,256]{2,1,0:T(8,128)(2,1)S(1)}, bf16[4,96,256]{2,1,0:T(8,128)(2,1)S(1)}, u32[]{:S(2)}, u32[]{:S(2)}) collective-permute-start(bf16[4,96,256]{2,1,0:T(8,128)(2,1)S(1)} %collective-permute-done.4.refs_6_), channel_id=1, source_target_pairs={{0,14},{2,0},{4,2},{6,4},{8,6},{10,8},{12,10},{14,12},{1,15},{3,1}... | collective-permute-start | bytes 589832 | tf_op jit(solution)/shard_map/ppermute | solution.py:255
  43.1 0.1 collective-permute-start.10
  43.2 1.6 %collective-permute-done.6.refs_8_ = bf16[4,96,256]{2,1,0:T(8,128)(2,1)S(1)} collective-permute-done((bf16[4,96,256]{2,1,0:T(8,128)(2,1)}, bf16[4,96,256]{2,1,0:T(8,128)(2,1)S(1)}, u32[]{:S(2)}, u32[]{:S(2)}) %collective-permute-start.6) | collective-permute-done | bytes 196640 | tf_op jit(solution)/shard_map/ppermute | solution.py:255
  44.8 0.1 convert_reduce_fusion.1.start_ref
  44.9 3.0 %collective-permute-start.16 = (bf16[4,96,256]{2,1,0:T(8,128)(2,1)S(1)}, bf16[4,96,256]{2,1,0:T(8,128)(2,1)S(1)}, u32[]{:S(2)}, u32[]{:S(2)}) collective-permute-start(bf16[4,96,256]{2,1,0:T(8,128)(2,1)S(1)} %collective-permute-done.8.refs_10_), channel_id=1, source_target_pairs={{0,14},{2,0},{4,2},{6,4},{8,6},{10,8},{12,10},{14,12},{1,15},{3,1}... | collective-permute-start | bytes 589832 | tf_op jit(solution)/shard_map/ppermute | solution.py:255
  47.9 0.2 collective-permute-start.9
  48.2 2.3 %collective-permute-done.10.refs_12_ = bf16[4,96,256]{2,1,0:T(8,128)(2,1)S(1)} collective-permute-done((bf16[4,96,256]{2,1,0:T(8,128)(2,1)S(1)}, bf16[4,96,256]{2,1,0:T(8,128)(2,1)S(1)}, u32[]{:S(2)}, u32[]{:S(2)}) %collective-permute-start.10) | collective-permute-done | bytes 196640 | tf_op jit(solution)/shard_map/ppermute | solution.py:255
  50.5 2.4 %collective-permute-start.20 = (bf16[4,96,256]{2,1,0:T(8,128)(2,1)S(1)}, bf16[4,96,256]{2,1,0:T(8,128)(2,1)S(1)}, u32[]{:S(2)}, u32[]{:S(2)}) collective-permute-start(bf16[4,96,256]{2,1,0:T(8,128)(2,1)S(1)} %collective-permute-done.12.refs_14_), channel_id=1, source_target_pairs={{0,14},{2,0},{4,2},{6,4},{8,6},{10,8},{12,10},{14,12},{1,15},{3,1}... | collective-permute-start | bytes 589832 | tf_op jit(solution)/shard_map/ppermute | solution.py:255
  52.9 0.4 collective-permute-start.13
  53.3 0.6 collective-permute-start.18
  53.9 1.4 collective-permute-done.14.refs_16_
  55.3 2.6 %collective-permute-start.24 = (bf16[4,96,256]{2,1,0:T(8,128)(2,1)S(1)}, bf16[4,96,256]{2,1,0:T(8,128)(2,1)S(1)}, u32[]{:S(2)}, u32[]{:S(2)}) collective-permute-start(bf16[4,96,256]{2,1,0:T(8,128)(2,1)S(1)} %collective-permute-done.16.refs_18_), channel_id=1, source_target_pairs={{0,14},{2,0},{4,2},{6,4},{8,6},{10,8},{12,10},{14,12},{1,15},{3,1}... | collective-permute-start | bytes 589832 | tf_op jit(solution)/shard_map/ppermute | solution.py:255
  57.9 0.2 collective-permute-start.17
  58.0 0.2 convert_reduce_fusion
  58.2 0.1 collective-permute-start.22
  58.3 2.5 %collective-permute-done.18.refs_20_ = bf16[4,96,256]{2,1,0:T(8,128)(2,1)S(1)} collective-permute-done((bf16[4,96,256]{2,1,0:T(8,128)(2,1)S(1)}, bf16[4,96,256]{2,1,0:T(8,128)(2,1)S(1)}, u32[]{:S(2)}, u32[]{:S(2)}) %collective-permute-start.18) | collective-permute-done | bytes 196640 | tf_op jit(solution)/shard_map/ppermute | solution.py:255
  60.9 0.5 collective-permute-start.21
  61.4 1.3 collective-permute-done.24.refs_26_
  62.6 1.1 collective-permute-start.26
  63.8 1.4 %collective-permute-start.28 = (bf16[4,96,256]{2,1,0:T(8,128)(2,1)S(1)}, bf16[4,96,256]{2,1,0:T(8,128)(2,1)S(1)}, u32[]{:S(2)}, u32[]{:S(2)}) collective-permute-start(bf16[4,96,256]{2,1,0:T(8,128)(2,1)S(1)} %collective-permute-done.24.refs_26_), channel_id=1, source_target_pairs={{0,14},{2,0},{4,2},{6,4},{8,6},{10,8},{12,10},{14,12},{1,15},{3,1}... | collective-permute-start | bytes 589832 | tf_op jit(solution)/shard_map/ppermute | solution.py:255
  65.2 0.1 select_reduce_fusion.order_ref
  65.3 0.8 collective-permute-done.22.refs_24_
  66.2 0.5 collective-permute-start.25
  66.7 0.1 collective-permute-start.23
  66.8 3.4 %collective-permute-done.26.refs_28_ = bf16[4,96,256]{2,1,0:T(8,128)(2,1)S(1)} collective-permute-done((bf16[4,96,256]{2,1,0:T(8,128)(2,1)S(1)}, bf16[4,96,256]{2,1,0:T(8,128)(2,1)S(1)}, u32[]{:S(2)}, u32[]{:S(2)}) %collective-permute-start.26) | collective-permute-done | bytes 196640 | tf_op jit(solution)/shard_map/ppermute | solution.py:255
  70.2 0.3 collective-permute-done.28.refs_30_
  70.5 0.2 collective-permute-start.29
  70.7 0.1 broadcast_add_fusion.lpos_ref
  70.8 0.8 collective-permute-done.27.refs_29_
  71.7 0.7 copy-done.34
  72.4 7.1 %all-gather.3.cloned.1.call-done = bf16[32,64,1536]{2,1,0:T(8,128)(2,1)} async-done(((bf16[2,64,1536]{2,1,0:T(8,128)(2,1)}), bf16[32,64,1536]{2,1,0:T(8,128)(2,1)}) %all-gather.3.cloned.1.call-update) | async-done | bytes 6291472 | tf_op jit(solution)/shard_map/all_gather | solution.py:295
  79.6 22.5 %correlate.1 = (f32[384,128]{1,0:T(8,128)S(1)}, f32[384,128]{1,0:T(8,128)S(1)}, f32[384,128]{1,0:T(8,128)S(1)}, f32[384,128]{1,0:T(8,128)S(1)}, f32[256,96]{1,0:T(8,128)}) custom-call(s32[9]{0:T(128)S(1)} %convert_reduce_fusion.1.start_ref, s32[128]{0:T(128)S(1)} %select_reduce_fusion.order_ref, s32[128]{0:T(128)S(1)} %get-tuple-element.30.jidx_ref, ...), custom_call_target="tpu_custom_call" | custom-call | tf_op jit(solution)/shard_map/correlate/pallas_call | solution.py:176
  102.1 0.7 copy-done
  102.8 1.5 %collective-permute-start.30 = (f32[384,128]{1,0:T(8,128)S(1)}, f32[384,128]{1,0:T(8,128)S(1)}, u32[]{:S(2)}, u32[]{:S(2)}) collective-permute-start(f32[384,128]{1,0:T(8,128)S(1)} %get-tuple-element.20), channel_id=1, source_target_pairs={{0,16},{16,32},{32,48},{48,0},{1,17},{17,33},{33,49},{49,1},{2,18}... | collective-permute-start | bytes 589832 | tf_op jit(solution)/shard_map/ppermute | solution.py:255
  104.2 2.7 %collective-permute-start.31 = (f32[384,128]{1,0:T(8,128)S(1)}, f32[384,128]{1,0:T(8,128)S(1)}, u32[]{:S(2)}, u32[]{:S(2)}) collective-permute-start(f32[384,128]{1,0:T(8,128)S(1)} %get-tuple-element.21), channel_id=1, source_target_pairs={{0,32},{16,48},{32,0},{48,16},{1,33},{17,49},{33,1},{49,17},{2,34}... | collective-permute-start | bytes 589832 | tf_op jit(solution)/shard_map/ppermute | solution.py:255
  106.9 1.5 %collective-permute-start.32 = (f32[384,128]{1,0:T(8,128)S(1)}, f32[384,128]{1,0:T(8,128)S(1)}, u32[]{:S(2)}, u32[]{:S(2)}) collective-permute-start(f32[384,128]{1,0:T(8,128)S(1)} %get-tuple-element.22), channel_id=1, source_target_pairs={{0,48},{16,0},{32,16},{48,32},{1,49},{17,1},{33,17},{49,33},{2,50}... | collective-permute-start | bytes 589832 | tf_op jit(solution)/shard_map/ppermute | solution.py:255
  108.4 8.4 %all-to-all-start.1 = ((f32[64,4,96]{2,1,0:T(4,128)}), f32[64,4,96]{2,1,0:T(4,128)S(1)}, u32[]{:S(2)}, u32[]{:S(2)}) async-start(f32[64,4,96]{2,1,0:T(4,128)} %bitcast.7), calls=%async_computation.1 | async-start | bytes 262144 | tf_op jit(solution)/shard_map/all_to_all | solution.py:319
  116.9 0.6 copy-done.3
  117.5 0.1 copy-done.4
  117.6 0.1 copy-done.5
  117.6 1.9 %meet.1 = (f32[96,128]{1,0:T(8,128)}, f32[96,128]{1,0:T(8,128)}, f32[96,128]{1,0:T(8,128)}, f32[96,128]{1,0:T(8,128)}) custom-call(f32[384,128]{1,0:T(8,128)} %copy-done, f32[384,128]{1,0:T(8,128)} %copy-done.3, f32[384,128]{1,0:T(8,128)} %copy-done.4, f32[384,128]{1,0:T(8,128)} %copy-done.5), custom_call_target="tpu_custom_call" | custom-call | tf_op jit(solution)/shard_map/meet/pallas_call | solution.py:223
  119.5 1.4 %collective-permute-start.33 = (f32[96,128]{1,0:T(8,128)}, f32[96,128]{1,0:T(8,128)S(1)}, u32[]{:S(2)}, u32[]{:S(2)}) collective-permute-start(f32[96,128]{1,0:T(8,128)} %get-tuple-element.24), channel_id=1, source_target_pairs={{0,64},{64,128},{128,192},{192,0},{1,65},{65,129},{129,193},{193,1... | collective-permute-start | bytes 147464 | tf_op jit(solution)/shard_map/ppermute | solution.py:255
  121.0 2.7 %collective-permute-start.34 = (f32[96,128]{1,0:T(8,128)}, f32[96,128]{1,0:T(8,128)S(1)}, u32[]{:S(2)}, u32[]{:S(2)}) collective-permute-start(f32[96,128]{1,0:T(8,128)} %get-tuple-element.25), channel_id=1, source_target_pairs={{0,128},{64,192},{128,0},{192,64},{1,129},{65,193},{129,1},{193,65... | collective-permute-start | bytes 147464 | tf_op jit(solution)/shard_map/ppermute | solution.py:255
  123.7 1.4 %collective-permute-start.35 = (f32[96,128]{1,0:T(8,128)}, f32[96,128]{1,0:T(8,128)S(1)}, u32[]{:S(2)}, u32[]{:S(2)}) collective-permute-start(f32[96,128]{1,0:T(8,128)} %get-tuple-element.26), channel_id=1, source_target_pairs={{0,192},{64,0},{128,64},{192,128},{1,193},{65,1},{129,65},{193,129... | collective-permute-start | bytes 147464 | tf_op jit(solution)/shard_map/ppermute | solution.py:255
  125.1 1.2 fusion.13.rows_ref
  126.4 0.5 all-to-all-done.1
  126.8 0.6 copy-done.2
  127.5 2.4 %finish_right.1 = f32[32,384]{1,0:T(8,128)} custom-call(s32[32]{0:T(128)} %fusion.13.rows_ref, f32[4,64,96]{2,1,0:T(8,128)} %bitcast.41), custom_call_target="tpu_custom_call" | custom-call | tf_op jit(solution)/shard_map/finish_right/pallas_call | solution.py:204
  129.9 0.6 copy-done.35
  130.5 1.5 %finish_left.1 = f32[32,384]{1,0:T(8,128)} custom-call(f32[96,128]{1,0:T(8,128)} %get-tuple-element.23.refs_0_, f32[96,128]{1,0:T(8,128)} %copy-done.35, f32[96,128]{1,0:T(8,128)} %copy-done.36, f32[96,128]{1,0:T(8,128)} %copy-done.37), custom_call_target="tpu_custom_call" | custom-call | tf_op jit(solution)/shard_map/finish_left/pallas_call | solution.py:241
  (110 shorter events, 0.4 us)
Async XLA Ops:
  7.2 72.3 %all-gather.3.cloned.1.call-start = ((), (), s32[]{:S(2)}) async-start(), calls=%async_computation.2 | async-start | bytes 6684672 | tf_op jit(solution)/shard_map/all_gather | solution.py:295
  9.7 17.1 %all-to-all-start = ((bf16[16,96,128]{2,1,0:T(8,128)(2,1)}), bf16[16,96,128]{2,1,0:T(8,128)(2,1)S(1)}, u32[]{:S(2)}, u32[]{:S(2)}) async-start(bf16[16,96,128]{2,1,0:T(8,128)(2,1)} %get-tuple-element.16), calls=%async_computation | async-start | bytes 786432 | tf_op jit(solution)/shard_map/all_to_all | solution.py:294
  30.0 6.2 %collective-permute-start.4 = (bf16[4,96,256]{2,1,0:T(8,128)(2,1)}, bf16[4,96,256]{2,1,0:T(8,128)(2,1)S(1)}, u32[]{:S(2)}, u32[]{:S(2)}) collective-permute-start(bf16[4,96,256]{2,1,0:T(8,128)(2,1)} %get-tuple-element.17.refs_0_), channel_id=1, source_target_pairs={{0,14},{2,0},{4,2},{6,4},{8,6},{10,8},{12,10},{14,12},{1,15},{3,1}... | collective-permute-start | bytes 589832 | tf_op jit(solution)/shard_map/ppermute | solution.py:255
  30.1 9.7 %collective-permute-start.2 = (bf16[4,96,256]{2,1,0:T(8,128)(2,1)}, bf16[4,96,256]{2,1,0:T(8,128)(2,1)S(1)}, u32[]{:S(2)}, u32[]{:S(2)}) collective-permute-start(bf16[4,96,256]{2,1,0:T(8,128)(2,1)} %get-tuple-element.17.refs_0_), channel_id=1, source_target_pairs={{0,2},{2,4},{4,6},{6,8},{8,10},{10,12},{12,14},{14,0},{1,3},{3,5},... | collective-permute-start | bytes 589832 | tf_op jit(solution)/shard_map/ppermute | solution.py:255
  32.1 11.0 %collective-permute-start = (bf16[4,96,256]{2,1,0:T(8,128)(2,1)}, bf16[4,96,256]{2,1,0:T(8,128)(2,1)S(1)}, u32[]{:S(2)}, u32[]{:S(2)}) collective-permute-start(bf16[4,96,256]{2,1,0:T(8,128)(2,1)} %get-tuple-element.17.refs_0_), channel_id=1, source_target_pairs={{0,1},{1,0},{2,3},{3,2},{4,5},{5,4},{6,7},{7,6},{8,9},{9,8},{10,11... | collective-permute-start | bytes 589832 | tf_op jit(solution)/shard_map/ppermute | solution.py:259
  32.1 11.0 %collective-permute-start.8 = (bf16[4,96,256]{2,1,0:T(8,128)(2,1)}, bf16[4,96,256]{2,1,0:T(8,128)(2,1)S(1)}, u32[]{:S(2)}, u32[]{:S(2)}) collective-permute-start(bf16[4,96,256]{2,1,0:T(8,128)(2,1)} %get-tuple-element.18.refs_2_), channel_id=1, source_target_pairs={{0,14},{2,0},{4,2},{6,4},{8,6},{10,8},{12,10},{14,12},{1,15},{3,1}... | collective-permute-start | bytes 589832 | tf_op jit(solution)/shard_map/ppermute | solution.py:255
  36.0 8.8 %collective-permute-start.6 = (bf16[4,96,256]{2,1,0:T(8,128)(2,1)}, bf16[4,96,256]{2,1,0:T(8,128)(2,1)S(1)}, u32[]{:S(2)}, u32[]{:S(2)}) collective-permute-start(bf16[4,96,256]{2,1,0:T(8,128)(2,1)} %get-tuple-element.18.refs_2_), channel_id=1, source_target_pairs={{0,2},{2,4},{4,6},{6,8},{8,10},{10,12},{12,14},{14,0},{1,3},{3,5},... | collective-permute-start | bytes 589832 | tf_op jit(solution)/shard_map/ppermute | solution.py:255
  36.2 43.3 %copy-start.6 = (bf16[4,96,256]{2,1,0:T(8,128)(2,1)}, bf16[4,96,256]{2,1,0:T(8,128)(2,1)S(1)}, u32[]{:S(2)}) copy-start(bf16[4,96,256]{2,1,0:T(8,128)(2,1)S(1)} %collective-permute-done.4.refs_6_) | copy-start | bytes 589828
  36.2 8.7 %collective-permute-start.1 = (bf16[4,96,256]{2,1,0:T(8,128)(2,1)}, bf16[4,96,256]{2,1,0:T(8,128)(2,1)S(1)}, u32[]{:S(2)}, u32[]{:S(2)}) collective-permute-start(bf16[4,96,256]{2,1,0:T(8,128)(2,1)} %get-tuple-element.18.refs_2_), channel_id=1, source_target_pairs={{0,1},{1,0},{2,3},{3,2},{4,5},{5,4},{6,7},{7,6},{8,9},{9,8},{10,11... | collective-permute-start | bytes 589832 | tf_op jit(solution)/shard_map/ppermute | solution.py:259
  39.9 39.6 %copy-start.7 = (bf16[4,96,256]{2,1,0:T(8,128)(2,1)}, bf16[4,96,256]{2,1,0:T(8,128)(2,1)S(1)}, u32[]{:S(2)}) copy-start(bf16[4,96,256]{2,1,0:T(8,128)(2,1)S(1)} %collective-permute-done.2.refs_4_) | copy-start | bytes 589828
  39.9 8.1 %collective-permute-start.12 = (bf16[4,96,256]{2,1,0:T(8,128)(2,1)S(1)}, bf16[4,96,256]{2,1,0:T(8,128)(2,1)S(1)}, u32[]{:S(2)}, u32[]{:S(2)}) collective-permute-start(bf16[4,96,256]{2,1,0:T(8,128)(2,1)S(1)} %collective-permute-done.4.refs_6_), channel_id=1, source_target_pairs={{0,14},{2,0},{4,2},{6,4},{8,6},{10,8},{12,10},{14,12},{1,15},{3,1}... | collective-permute-start | bytes 589832 | tf_op jit(solution)/shard_map/ppermute | solution.py:255
  43.1 36.4 %copy-start.8 = (bf16[4,96,256]{2,1,0:T(8,128)(2,1)}, bf16[4,96,256]{2,1,0:T(8,128)(2,1)S(1)}, u32[]{:S(2)}) copy-start(bf16[4,96,256]{2,1,0:T(8,128)(2,1)S(1)} %collective-permute-done.refs_1_) | copy-start | bytes 589828
  43.1 5.1 %collective-permute-start.5 = (bf16[4,96,256]{2,1,0:T(8,128)(2,1)S(1)}, bf16[4,96,256]{2,1,0:T(8,128)(2,1)S(1)}, u32[]{:S(2)}, u32[]{:S(2)}) collective-permute-start(bf16[4,96,256]{2,1,0:T(8,128)(2,1)S(1)} %collective-permute-done.4.refs_6_), channel_id=1, source_target_pairs={{0,1},{1,0},{2,3},{3,2},{4,5},{5,4},{6,7},{7,6},{8,9},{9,8},{10,11... | collective-permute-start | bytes 589832 | tf_op jit(solution)/shard_map/ppermute | solution.py:259
  43.1 36.4 %copy-start.9 = (bf16[4,96,256]{2,1,0:T(8,128)(2,1)}, bf16[4,96,256]{2,1,0:T(8,128)(2,1)S(1)}, u32[]{:S(2)}) copy-start(bf16[4,96,256]{2,1,0:T(8,128)(2,1)S(1)} %collective-permute-done.8.refs_10_) | copy-start | bytes 589828
  43.1 7.3 %collective-permute-start.10 = (bf16[4,96,256]{2,1,0:T(8,128)(2,1)S(1)}, bf16[4,96,256]{2,1,0:T(8,128)(2,1)S(1)}, u32[]{:S(2)}, u32[]{:S(2)}) collective-permute-start(bf16[4,96,256]{2,1,0:T(8,128)(2,1)S(1)} %collective-permute-done.2.refs_4_), channel_id=1, source_target_pairs={{0,2},{2,4},{4,6},{6,8},{8,10},{10,12},{12,14},{14,0},{1,3},{3,5},... | collective-permute-start | bytes 589832 | tf_op jit(solution)/shard_map/ppermute | solution.py:255
  44.8 34.8 %copy-start.10 = (bf16[4,96,256]{2,1,0:T(8,128)(2,1)}, bf16[4,96,256]{2,1,0:T(8,128)(2,1)S(1)}, u32[]{:S(2)}) copy-start(bf16[4,96,256]{2,1,0:T(8,128)(2,1)S(1)} %collective-permute-done.6.refs_8_) | copy-start | bytes 589828
  44.8 5.7 %collective-permute-start.3 = (bf16[4,96,256]{2,1,0:T(8,128)(2,1)S(1)}, bf16[4,96,256]{2,1,0:T(8,128)(2,1)S(1)}, u32[]{:S(2)}, u32[]{:S(2)}) collective-permute-start(bf16[4,96,256]{2,1,0:T(8,128)(2,1)S(1)} %collective-permute-done.2.refs_4_), channel_id=1, source_target_pairs={{0,1},{1,0},{2,3},{3,2},{4,5},{5,4},{6,7},{7,6},{8,9},{9,8},{10,11... | collective-permute-start | bytes 589832 | tf_op jit(solution)/shard_map/ppermute | solution.py:259
  44.9 34.6 %copy-start.11 = (bf16[4,96,256]{2,1,0:T(8,128)(2,1)}, bf16[4,96,256]{2,1,0:T(8,128)(2,1)S(1)}, u32[]{:S(2)}) copy-start(bf16[4,96,256]{2,1,0:T(8,128)(2,1)S(1)} %collective-permute-done.1.refs_3_) | copy-start | bytes 589828
  44.9 7.9 %collective-permute-start.16 = (bf16[4,96,256]{2,1,0:T(8,128)(2,1)S(1)}, bf16[4,96,256]{2,1,0:T(8,128)(2,1)S(1)}, u32[]{:S(2)}, u32[]{:S(2)}) collective-permute-start(bf16[4,96,256]{2,1,0:T(8,128)(2,1)S(1)} %collective-permute-done.8.refs_10_), channel_id=1, source_target_pairs={{0,14},{2,0},{4,2},{6,4},{8,6},{10,8},{12,10},{14,12},{1,15},{3,1}... | collective-permute-start | bytes 589832 | tf_op jit(solution)/shard_map/ppermute | solution.py:255
  47.9 31.6 %copy-start.12 = (bf16[4,96,256]{2,1,0:T(8,128)(2,1)}, bf16[4,96,256]{2,1,0:T(8,128)(2,1)S(1)}, u32[]{:S(2)}) copy-start(bf16[4,96,256]{2,1,0:T(8,128)(2,1)S(1)} %collective-permute-done.12.refs_14_) | copy-start | bytes 589828
  47.9 5.4 %collective-permute-start.9 = (bf16[4,96,256]{2,1,0:T(8,128)(2,1)S(1)}, bf16[4,96,256]{2,1,0:T(8,128)(2,1)S(1)}, u32[]{:S(2)}, u32[]{:S(2)}) collective-permute-start(bf16[4,96,256]{2,1,0:T(8,128)(2,1)S(1)} %collective-permute-done.8.refs_10_), channel_id=1, source_target_pairs={{0,1},{1,0},{2,3},{3,2},{4,5},{5,4},{6,7},{7,6},{8,9},{9,8},{10,11... | collective-permute-start | bytes 589832 | tf_op jit(solution)/shard_map/ppermute | solution.py:259
  48.2 31.4 %copy-start.13 = (bf16[4,96,256]{2,1,0:T(8,128)(2,1)}, bf16[4,96,256]{2,1,0:T(8,128)(2,1)S(1)}, u32[]{:S(2)}) copy-start(bf16[4,96,256]{2,1,0:T(8,128)(2,1)S(1)} %collective-permute-done.5.refs_7_) | copy-start | bytes 589828
  48.2 7.1 %collective-permute-start.14 = (bf16[4,96,256]{2,1,0:T(8,128)(2,1)S(1)}, bf16[4,96,256]{2,1,0:T(8,128)(2,1)S(1)}, u32[]{:S(2)}, u32[]{:S(2)}) collective-permute-start(bf16[4,96,256]{2,1,0:T(8,128)(2,1)S(1)} %collective-permute-done.6.refs_8_), channel_id=1, source_target_pairs={{0,2},{2,4},{4,6},{6,8},{8,10},{10,12},{12,14},{14,0},{1,3},{3,5},... | collective-permute-start | bytes 589832 | tf_op jit(solution)/shard_map/ppermute | solution.py:255
  50.4 29.1 %copy-start.14 = (bf16[4,96,256]{2,1,0:T(8,128)(2,1)}, bf16[4,96,256]{2,1,0:T(8,128)(2,1)S(1)}, u32[]{:S(2)}) copy-start(bf16[4,96,256]{2,1,0:T(8,128)(2,1)S(1)} %collective-permute-done.10.refs_12_) | copy-start | bytes 589828
  50.4 4.8 %collective-permute-start.7 = (bf16[4,96,256]{2,1,0:T(8,128)(2,1)S(1)}, bf16[4,96,256]{2,1,0:T(8,128)(2,1)S(1)}, u32[]{:S(2)}, u32[]{:S(2)}) collective-permute-start(bf16[4,96,256]{2,1,0:T(8,128)(2,1)S(1)} %collective-permute-done.6.refs_8_), channel_id=1, source_target_pairs={{0,1},{1,0},{2,3},{3,2},{4,5},{5,4},{6,7},{7,6},{8,9},{9,8},{10,11... | collective-permute-start | bytes 589832 | tf_op jit(solution)/shard_map/ppermute | solution.py:259
  50.4 29.1 %copy-start.15 = (bf16[4,96,256]{2,1,0:T(8,128)(2,1)}, bf16[4,96,256]{2,1,0:T(8,128)(2,1)S(1)}, u32[]{:S(2)}) copy-start(bf16[4,96,256]{2,1,0:T(8,128)(2,1)S(1)} %collective-permute-done.3.refs_5_) | copy-start | bytes 589828
  50.5 7.4 %collective-permute-start.20 = (bf16[4,96,256]{2,1,0:T(8,128)(2,1)S(1)}, bf16[4,96,256]{2,1,0:T(8,128)(2,1)S(1)}, u32[]{:S(2)}, u32[]{:S(2)}) collective-permute-start(bf16[4,96,256]{2,1,0:T(8,128)(2,1)S(1)} %collective-permute-done.12.refs_14_), channel_id=1, source_target_pairs={{0,14},{2,0},{4,2},{6,4},{8,6},{10,8},{12,10},{14,12},{1,15},{3,1}... | collective-permute-start | bytes 589832 | tf_op jit(solution)/shard_map/ppermute | solution.py:255
  52.9 26.7 %copy-start.16 = (bf16[4,96,256]{2,1,0:T(8,128)(2,1)}, bf16[4,96,256]{2,1,0:T(8,128)(2,1)S(1)}, u32[]{:S(2)}) copy-start(bf16[4,96,256]{2,1,0:T(8,128)(2,1)S(1)} %collective-permute-done.16.refs_18_) | copy-start | bytes 589828
  52.9 5.3 %collective-permute-start.13 = (bf16[4,96,256]{2,1,0:T(8,128)(2,1)S(1)}, bf16[4,96,256]{2,1,0:T(8,128)(2,1)S(1)}, u32[]{:S(2)}, u32[]{:S(2)}) collective-permute-start(bf16[4,96,256]{2,1,0:T(8,128)(2,1)S(1)} %collective-permute-done.12.refs_14_), channel_id=1, source_target_pairs={{0,1},{1,0},{2,3},{3,2},{4,5},{5,4},{6,7},{7,6},{8,9},{9,8},{10,11... | collective-permute-start | bytes 589832 | tf_op jit(solution)/shard_map/ppermute | solution.py:259
  53.3 26.3 %copy-start.17 = (bf16[4,96,256]{2,1,0:T(8,128)(2,1)}, bf16[4,96,256]{2,1,0:T(8,128)(2,1)S(1)}, u32[]{:S(2)}) copy-start(bf16[4,96,256]{2,1,0:T(8,128)(2,1)S(1)} %collective-permute-done.9.refs_11_) | copy-start | bytes 589828
  53.3 7.5 %collective-permute-start.18 = (bf16[4,96,256]{2,1,0:T(8,128)(2,1)S(1)}, bf16[4,96,256]{2,1,0:T(8,128)(2,1)S(1)}, u32[]{:S(2)}, u32[]{:S(2)}) collective-permute-start(bf16[4,96,256]{2,1,0:T(8,128)(2,1)S(1)} %collective-permute-done.10.refs_12_), channel_id=1, source_target_pairs={{0,2},{2,4},{4,6},{6,8},{8,10},{10,12},{12,14},{14,0},{1,3},{3,5},... | collective-permute-start | bytes 589832 | tf_op jit(solution)/shard_map/ppermute | solution.py:255
  55.3 24.3 %copy-start.18 = (bf16[4,96,256]{2,1,0:T(8,128)(2,1)}, bf16[4,96,256]{2,1,0:T(8,128)(2,1)S(1)}, u32[]{:S(2)}) copy-start(bf16[4,96,256]{2,1,0:T(8,128)(2,1)S(1)} %collective-permute-done.14.refs_16_) | copy-start | bytes 589828
  55.3 5.6 %collective-permute-start.11 = (bf16[4,96,256]{2,1,0:T(8,128)(2,1)S(1)}, bf16[4,96,256]{2,1,0:T(8,128)(2,1)S(1)}, u32[]{:S(2)}, u32[]{:S(2)}) collective-permute-start(bf16[4,96,256]{2,1,0:T(8,128)(2,1)S(1)} %collective-permute-done.10.refs_12_), channel_id=1, source_target_pairs={{0,1},{1,0},{2,3},{3,2},{4,5},{5,4},{6,7},{7,6},{8,9},{9,8},{10,11... | collective-permute-start | bytes 589832 | tf_op jit(solution)/shard_map/ppermute | solution.py:259
  55.3 24.3 %copy-start.19 = (bf16[4,96,256]{2,1,0:T(8,128)(2,1)}, bf16[4,96,256]{2,1,0:T(8,128)(2,1)S(1)}, u32[]{:S(2)}) copy-start(bf16[4,96,256]{2,1,0:T(8,128)(2,1)S(1)} %collective-permute-done.7.refs_9_) | copy-start | bytes 589828
  55.3 7.3 %collective-permute-start.24 = (bf16[4,96,256]{2,1,0:T(8,128)(2,1)S(1)}, bf16[4,96,256]{2,1,0:T(8,128)(2,1)S(1)}, u32[]{:S(2)}, u32[]{:S(2)}) collective-permute-start(bf16[4,96,256]{2,1,0:T(8,128)(2,1)S(1)} %collective-permute-done.16.refs_18_), channel_id=1, source_target_pairs={{0,14},{2,0},{4,2},{6,4},{8,6},{10,8},{12,10},{14,12},{1,15},{3,1}... | collective-permute-start | bytes 589832 | tf_op jit(solution)/shard_map/ppermute | solution.py:255
  57.9 21.6 %copy-start.20 = (bf16[4,96,256]{2,1,0:T(8,128)(2,1)}, bf16[4,96,256]{2,1,0:T(8,128)(2,1)S(1)}, u32[]{:S(2)}) copy-start(bf16[4,96,256]{2,1,0:T(8,128)(2,1)S(1)} %collective-permute-done.20.refs_22_) | copy-start | bytes 589828
  57.9 5.9 %collective-permute-start.17 = (bf16[4,96,256]{2,1,0:T(8,128)(2,1)S(1)}, bf16[4,96,256]{2,1,0:T(8,128)(2,1)S(1)}, u32[]{:S(2)}, u32[]{:S(2)}) collective-permute-start(bf16[4,96,256]{2,1,0:T(8,128)(2,1)S(1)} %collective-permute-done.16.refs_18_), channel_id=1, source_target_pairs={{0,1},{1,0},{2,3},{3,2},{4,5},{5,4},{6,7},{7,6},{8,9},{9,8},{10,11... | collective-permute-start | bytes 589832 | tf_op jit(solution)/shard_map/ppermute | solution.py:259
  58.2 21.3 %copy-start.21 = (bf16[4,96,256]{2,1,0:T(8,128)(2,1)}, bf16[4,96,256]{2,1,0:T(8,128)(2,1)S(1)}, u32[]{:S(2)}) copy-start(bf16[4,96,256]{2,1,0:T(8,128)(2,1)S(1)} %collective-permute-done.13.refs_15_) | copy-start | bytes 589828
  58.2 7.9 %collective-permute-start.22 = (bf16[4,96,256]{2,1,0:T(8,128)(2,1)S(1)}, bf16[4,96,256]{2,1,0:T(8,128)(2,1)S(1)}, u32[]{:S(2)}, u32[]{:S(2)}) collective-permute-start(bf16[4,96,256]{2,1,0:T(8,128)(2,1)S(1)} %collective-permute-done.14.refs_16_), channel_id=1, source_target_pairs={{0,2},{2,4},{4,6},{6,8},{8,10},{10,12},{12,14},{14,0},{1,3},{3,5},... | collective-permute-start | bytes 589832 | tf_op jit(solution)/shard_map/ppermute | solution.py:255
  60.8 18.7 %copy-start.22 = (bf16[4,96,256]{2,1,0:T(8,128)(2,1)}, bf16[4,96,256]{2,1,0:T(8,128)(2,1)S(1)}, u32[]{:S(2)}) copy-start(bf16[4,96,256]{2,1,0:T(8,128)(2,1)S(1)} %collective-permute-done.18.refs_20_) | copy-start | bytes 589828
  60.8 5.3 %collective-permute-start.15 = (bf16[4,96,256]{2,1,0:T(8,128)(2,1)S(1)}, bf16[4,96,256]{2,1,0:T(8,128)(2,1)S(1)}, u32[]{:S(2)}, u32[]{:S(2)}) collective-permute-start(bf16[4,96,256]{2,1,0:T(8,128)(2,1)S(1)} %collective-permute-done.14.refs_16_), channel_id=1, source_target_pairs={{0,1},{1,0},{2,3},{3,2},{4,5},{5,4},{6,7},{7,6},{8,9},{9,8},{10,11... | collective-permute-start | bytes 589832 | tf_op jit(solution)/shard_map/ppermute | solution.py:259
  60.8 9.9 %copy-start.23 = (bf16[4,96,256]{2,1,0:T(8,128)(2,1)}, bf16[4,96,256]{2,1,0:T(8,128)(2,1)S(1)}, u32[]{:S(2)}) copy-start(bf16[4,96,256]{2,1,0:T(8,128)(2,1)S(1)} %collective-permute-done.11.refs_13_) | copy-start | bytes 589828
  60.9 5.8 %collective-permute-start.21 = (bf16[4,96,256]{2,1,0:T(8,128)(2,1)S(1)}, bf16[4,96,256]{2,1,0:T(8,128)(2,1)S(1)}, u32[]{:S(2)}, u32[]{:S(2)}) collective-permute-start(bf16[4,96,256]{2,1,0:T(8,128)(2,1)S(1)} %collective-permute-done.20.refs_22_), channel_id=1, source_target_pairs={{0,1},{1,0},{2,3},{3,2},{4,5},{5,4},{6,7},{7,6},{8,9},{9,8},{10,11... | collective-permute-start | bytes 589832 | tf_op jit(solution)/shard_map/ppermute | solution.py:259
  62.6 8.2 %copy-start.24 = (bf16[4,96,256]{2,1,0:T(8,128)(2,1)}, bf16[4,96,256]{2,1,0:T(8,128)(2,1)S(1)}, u32[]{:S(2)}) copy-start(bf16[4,96,256]{2,1,0:T(8,128)(2,1)S(1)} %collective-permute-done.24.refs_26_) | copy-start | bytes 589828
  62.6 7.6 %collective-permute-start.26 = (bf16[4,96,256]{2,1,0:T(8,128)(2,1)S(1)}, bf16[4,96,256]{2,1,0:T(8,128)(2,1)S(1)}, u32[]{:S(2)}, u32[]{:S(2)}) collective-permute-start(bf16[4,96,256]{2,1,0:T(8,128)(2,1)S(1)} %collective-permute-done.18.refs_20_), channel_id=1, source_target_pairs={{0,2},{2,4},{4,6},{6,8},{8,10},{10,12},{12,14},{14,0},{1,3},{3,5},... | collective-permute-start | bytes 589832 | tf_op jit(solution)/shard_map/ppermute | solution.py:255
  63.8 7.1 %copy-start.25 = (bf16[4,96,256]{2,1,0:T(8,128)(2,1)}, bf16[4,96,256]{2,1,0:T(8,128)(2,1)S(1)}, u32[]{:S(2)}) copy-start(bf16[4,96,256]{2,1,0:T(8,128)(2,1)S(1)} %collective-permute-done.17.refs_19_) | copy-start | bytes 589828
  63.8 6.7 %collective-permute-start.28 = (bf16[4,96,256]{2,1,0:T(8,128)(2,1)S(1)}, bf16[4,96,256]{2,1,0:T(8,128)(2,1)S(1)}, u32[]{:S(2)}, u32[]{:S(2)}) collective-permute-start(bf16[4,96,256]{2,1,0:T(8,128)(2,1)S(1)} %collective-permute-done.24.refs_26_), channel_id=1, source_target_pairs={{0,14},{2,0},{4,2},{6,4},{8,6},{10,8},{12,10},{14,12},{1,15},{3,1}... | collective-permute-start | bytes 589832 | tf_op jit(solution)/shard_map/ppermute | solution.py:255
  66.2 5.5 %copy-start.26 = (bf16[4,96,256]{2,1,0:T(8,128)(2,1)}, bf16[4,96,256]{2,1,0:T(8,128)(2,1)S(1)}, u32[]{:S(2)}) copy-start(bf16[4,96,256]{2,1,0:T(8,128)(2,1)S(1)} %collective-permute-done.22.refs_24_) | copy-start | bytes 589828
  66.2 4.6 %collective-permute-start.19 = (bf16[4,96,256]{2,1,0:T(8,128)(2,1)S(1)}, bf16[4,96,256]{2,1,0:T(8,128)(2,1)S(1)}, u32[]{:S(2)}, u32[]{:S(2)}) collective-permute-start(bf16[4,96,256]{2,1,0:T(8,128)(2,1)S(1)} %collective-permute-done.18.refs_20_), channel_id=1, source_target_pairs={{0,1},{1,0},{2,3},{3,2},{4,5},{5,4},{6,7},{7,6},{8,9},{9,8},{10,11... | collective-permute-start | bytes 589832 | tf_op jit(solution)/shard_map/ppermute | solution.py:259
  66.2 5.5 %copy-start.27 = (bf16[4,96,256]{2,1,0:T(8,128)(2,1)}, bf16[4,96,256]{2,1,0:T(8,128)(2,1)S(1)}, u32[]{:S(2)}) copy-start(bf16[4,96,256]{2,1,0:T(8,128)(2,1)S(1)} %collective-permute-done.15.refs_17_) | copy-start | bytes 589828
  66.2 4.6 %collective-permute-start.25 = (bf16[4,96,256]{2,1,0:T(8,128)(2,1)S(1)}, bf16[4,96,256]{2,1,0:T(8,128)(2,1)S(1)}, u32[]{:S(2)}, u32[]{:S(2)}) collective-permute-start(bf16[4,96,256]{2,1,0:T(8,128)(2,1)S(1)} %collective-permute-done.24.refs_26_), channel_id=1, source_target_pairs={{0,1},{1,0},{2,3},{3,2},{4,5},{5,4},{6,7},{7,6},{8,9},{9,8},{10,11... | collective-permute-start | bytes 589832 | tf_op jit(solution)/shard_map/ppermute | solution.py:259
  66.7 5.0 %copy-start.28 = (bf16[4,96,256]{2,1,0:T(8,128)(2,1)}, bf16[4,96,256]{2,1,0:T(8,128)(2,1)S(1)}, u32[]{:S(2)}) copy-start(bf16[4,96,256]{2,1,0:T(8,128)(2,1)S(1)} %collective-permute-done.21.refs_23_) | copy-start | bytes 589828
  66.7 4.1 %collective-permute-start.23 = (bf16[4,96,256]{2,1,0:T(8,128)(2,1)S(1)}, bf16[4,96,256]{2,1,0:T(8,128)(2,1)S(1)}, u32[]{:S(2)}, u32[]{:S(2)}) collective-permute-start(bf16[4,96,256]{2,1,0:T(8,128)(2,1)S(1)} %collective-permute-done.22.refs_24_), channel_id=1, source_target_pairs={{0,1},{1,0},{2,3},{3,2},{4,5},{5,4},{6,7},{7,6},{8,9},{9,8},{10,11... | collective-permute-start | bytes 589832 | tf_op jit(solution)/shard_map/ppermute | solution.py:259
  70.2 1.5 %copy-start.29 = (bf16[4,96,256]{2,1,0:T(8,128)(2,1)}, bf16[4,96,256]{2,1,0:T(8,128)(2,1)S(1)}, u32[]{:S(2)}) copy-start(bf16[4,96,256]{2,1,0:T(8,128)(2,1)S(1)} %collective-permute-done.26.refs_28_) | copy-start | bytes 589828
  70.2 1.4 %collective-permute-start.27 = (bf16[4,96,256]{2,1,0:T(8,128)(2,1)S(1)}, bf16[4,96,256]{2,1,0:T(8,128)(2,1)S(1)}, u32[]{:S(2)}, u32[]{:S(2)}) collective-permute-start(bf16[4,96,256]{2,1,0:T(8,128)(2,1)S(1)} %collective-permute-done.26.refs_28_), channel_id=1, source_target_pairs={{0,1},{1,0},{2,3},{3,2},{4,5},{5,4},{6,7},{7,6},{8,9},{9,8},{10,11... | collective-permute-start | bytes 589832 | tf_op jit(solution)/shard_map/ppermute | solution.py:259
  70.5 1.2 copy-start.30
  70.5 1.9 %collective-permute-start.29 = (bf16[4,96,256]{2,1,0:T(8,128)(2,1)S(1)}, bf16[4,96,256]{2,1,0:T(8,128)(2,1)}, u32[]{:S(2)}, u32[]{:S(2)}) collective-permute-start(bf16[4,96,256]{2,1,0:T(8,128)(2,1)S(1)} %collective-permute-done.28.refs_30_), channel_id=1, source_target_pairs={{0,1},{1,0},{2,3},{3,2},{4,5},{5,4},{6,7},{7,6},{8,9},{9,8},{10,11... | collective-permute-start | bytes 589832 | tf_op jit(solution)/shard_map/ppermute | solution.py:259
  102.8 14.0 %collective-permute-start.30 = (f32[384,128]{1,0:T(8,128)S(1)}, f32[384,128]{1,0:T(8,128)S(1)}, u32[]{:S(2)}, u32[]{:S(2)}) collective-permute-start(f32[384,128]{1,0:T(8,128)S(1)} %get-tuple-element.20), channel_id=1, source_target_pairs={{0,16},{16,32},{32,48},{48,0},{1,17},{17,33},{33,49},{49,1},{2,18}... | collective-permute-start | bytes 589832 | tf_op jit(solution)/shard_map/ppermute | solution.py:255
  104.2 12.6 %collective-permute-start.31 = (f32[384,128]{1,0:T(8,128)S(1)}, f32[384,128]{1,0:T(8,128)S(1)}, u32[]{:S(2)}, u32[]{:S(2)}) collective-permute-start(f32[384,128]{1,0:T(8,128)S(1)} %get-tuple-element.21), channel_id=1, source_target_pairs={{0,32},{16,48},{32,0},{48,16},{1,33},{17,49},{33,1},{49,17},{2,34}... | collective-permute-start | bytes 589832 | tf_op jit(solution)/shard_map/ppermute | solution.py:255
  106.9 9.9 %collective-permute-start.32 = (f32[384,128]{1,0:T(8,128)S(1)}, f32[384,128]{1,0:T(8,128)S(1)}, u32[]{:S(2)}, u32[]{:S(2)}) collective-permute-start(f32[384,128]{1,0:T(8,128)S(1)} %get-tuple-element.22), channel_id=1, source_target_pairs={{0,48},{16,0},{32,16},{48,32},{1,49},{17,1},{33,17},{49,33},{2,50}... | collective-permute-start | bytes 589832 | tf_op jit(solution)/shard_map/ppermute | solution.py:255
  108.4 18.4 %all-to-all-start.1 = ((f32[64,4,96]{2,1,0:T(4,128)}), f32[64,4,96]{2,1,0:T(4,128)S(1)}, u32[]{:S(2)}, u32[]{:S(2)}) async-start(f32[64,4,96]{2,1,0:T(4,128)} %bitcast.7), calls=%async_computation.1 | async-start | bytes 262144 | tf_op jit(solution)/shard_map/all_to_all | solution.py:319
  119.5 10.3 %collective-permute-start.33 = (f32[96,128]{1,0:T(8,128)}, f32[96,128]{1,0:T(8,128)S(1)}, u32[]{:S(2)}, u32[]{:S(2)}) collective-permute-start(f32[96,128]{1,0:T(8,128)} %get-tuple-element.24), channel_id=1, source_target_pairs={{0,64},{64,128},{128,192},{192,0},{1,65},{65,129},{129,193},{193,1... | collective-permute-start | bytes 147464 | tf_op jit(solution)/shard_map/ppermute | solution.py:255
  121.0 8.9 %collective-permute-start.34 = (f32[96,128]{1,0:T(8,128)}, f32[96,128]{1,0:T(8,128)S(1)}, u32[]{:S(2)}, u32[]{:S(2)}) collective-permute-start(f32[96,128]{1,0:T(8,128)} %get-tuple-element.25), channel_id=1, source_target_pairs={{0,128},{64,192},{128,0},{192,64},{1,129},{65,193},{129,1},{193,65... | collective-permute-start | bytes 147464 | tf_op jit(solution)/shard_map/ppermute | solution.py:255
  123.7 6.2 %collective-permute-start.35 = (f32[96,128]{1,0:T(8,128)}, f32[96,128]{1,0:T(8,128)S(1)}, u32[]{:S(2)}, u32[]{:S(2)}) collective-permute-start(f32[96,128]{1,0:T(8,128)} %get-tuple-element.26), channel_id=1, source_target_pairs={{0,192},{64,0},{128,64},{192,128},{1,193},{65,1},{129,65},{193,129... | collective-permute-start | bytes 147464 | tf_op jit(solution)/shard_map/ppermute | solution.py:255
  (13 other events, 9.4 us)
Sparse Core Ops, SparseCore 0:
  10.5 68.9 all-gather.2

commit v4 on v3

--- a/solution.py
+++ b/solution.py
@@ -25,7 +25,7 @@
 LEFTS = NX * PER
 BLOCK = 128
 HALF = LEFTS // 2
-GROUP = 8
+GROUP = 16
 TILE = 256
 
 VMEM = pl.BlockSpec(memory_space=pltpu.VMEM)
@@ -105,9 +105,11 @@
                 sem.at[count + x * NY + y],
             )
 
+        for y in range(NY):
+            rows_of(0, y).start()
         for load in loads:
             load.start()
-        for x in range(NX):
+        for x in range(1, NX):
             for y in range(NY):
                 rows_of(x, y).start()
         right_ref[...] = jnp.zeros_like(right_ref)
@@ -154,18 +156,25 @@
                     top = jnp.max(jnp.transpose(best[g]), axis=0, keepdims=True)
                     right_ref[pl.ds(rpos_ref[pairs[g]], 1), :] = top
 
-            rest = (high - low) % GROUP
-            full = (high - low) // GROUP + (rest > GROUP // 2).astype(jnp.int32)
+            total = high - low
+            rest = total % GROUP
+            most = total // GROUP + (rest > 12).astype(jnp.int32)
+            rest = jnp.where(rest > 12, 0, rest)
+            eight = (rest > 4).astype(jnp.int32)
 
             def step(b, carry):
                 block(low + b * GROUP, GROUP)
                 return carry
 
-            lax.fori_loop(0, full, step, 0)
-
-            @pl.when((rest > 0) & (rest <= GROUP // 2))
+            lax.fori_loop(0, most, step, 0)
+
+            @pl.when(eight > 0)
             def _():
-                block(low + full * GROUP, GROUP // 2)
+                block(low + most * GROUP, 8)
+
+            @pl.when(rest - 8 * eight > 0)
+            def _():
+                block(low + most * GROUP + 8 * eight, 4)
 
             return carry
 
@@ -195,20 +204,32 @@
     )(start, order, jidx, lpos, rpos, gathered, *chunks)
 
 
-def finish_right(rows, returned):
-    def kernel(rows_ref, in_ref, out_ref):
-        for s in range(SLOTS):
-            for x in range(NX):
-                out_ref[s : s + 1, x * WIDTH : (x + 1) * WIDTH] = in_ref[x, pl.ds(rows_ref[s], 1), :]
+def finish(rows, returned, parts):
+    def kernel(rows_ref, in_ref, *refs):
+        part_refs, (left_ref, right_ref, picked) = refs[:NY], refs[NY:]
+        for x in range(NX):
+            for s in range(SLOTS):
+                picked[x, s : s + 1, :] = in_ref[x, pl.ds(rows_ref[s], 1), :]
+            right_ref[:, x * WIDTH : (x + 1) * WIDTH] = picked[x]
+        for t in range(QUARTER // 128):
+            some = slice(t * SLOTS, (t + 1) * SLOTS)
+            best = part_refs[0][some, :]
+            for ref in part_refs[1:]:
+                best = jnp.maximum(best, ref[some, :])
+            left_ref[:, t * 128 : (t + 1) * 128] = best
 
     return pl.pallas_call(
         kernel,
         grid_spec=pltpu.PrefetchScalarGridSpec(
-            num_scalar_prefetch=1, grid=(1,), in_specs=[VMEM], out_specs=VMEM
+            num_scalar_prefetch=1,
+            grid=(1,),
+            in_specs=[VMEM] * (1 + NY),
+            out_specs=[VMEM] * 2,
+            scratch_shapes=[pltpu.VMEM((NX, SLOTS, WIDTH), jnp.float32)],
         ),
-        out_shape=jax.ShapeDtypeStruct((SLOTS, QUARTER), jnp.float32),
-        name="finish_right",
-    )(rows, returned)
+        out_shape=[jax.ShapeDtypeStruct((SLOTS, QUARTER), jnp.float32)] * 2,
+        name="finish",
+    )(rows, returned, *parts)
 
 
 def meet(parts):
@@ -229,26 +250,12 @@
     )(*parts)
 
 
-def finish_left(parts):
-    def kernel(*refs):
-        for t in range(QUARTER // 128):
-            rows = slice(t * SLOTS, (t + 1) * SLOTS)
-            best = refs[0][rows, :]
-            for ref in refs[1:NY]:
-                best = jnp.maximum(best, ref[rows, :])
-            refs[NY][:, t * 128 : (t + 1) * 128] = best
-
-    return pl.pallas_call(
-        kernel,
-        in_specs=[VMEM] * NY,
-        out_specs=VMEM,
-        out_shape=jax.ShapeDtypeStruct((SLOTS, QUARTER), jnp.float32),
-        name="finish_left",
-    )(*parts)
-
-
 def in_hbm(value):
     return pltpu.with_memory_space_constraint(value, pltpu.HBM)
+
+
+def in_vmem(value):
+    return pltpu.with_memory_space_constraint(value, pltpu.VMEM)
 
 
 def shift(value, axis, by, size):
@@ -315,13 +322,15 @@
     keep(shift(up[0], "z", 1, NZ), NZ // 2, 0)
     keep(shift(down[1], "z", -1, NZ), NZ // 2, 1)
 
+    order, rows = lax.optimization_barrier((order, rows))
     *left, right = correlate(start, order, jidx, lpos, rpos, gathered, chunks, places)
     returned = lax.all_to_all(
         right.reshape(NDEV, NX, WIDTH), ("x", "z", "core"), split_axis=0, concat_axis=0, tiled=True
     )
-    right_out = finish_right(rows, returned.reshape(NX, NZ * NC * NX, WIDTH))
-    parts = meet([left[0]] + [shift(left[k], "x", k, NX) for k in range(1, NX)])
-    left_out = finish_left([parts[0]] + [shift(parts[k], "dp", k, NY) for k in range(1, NY)])
+    parts = meet([left[0]] + [in_vmem(shift(left[k], "x", k, NX)) for k in range(1, NX)])
+    parts = [parts[0]] + [in_vmem(shift(parts[k], "dp", k, NY)) for k in range(1, NY)]
+    returned = in_vmem(returned.reshape(NX, NZ * NC * NX, WIDTH))
+    left_out, right_out = finish(rows, returned, parts)
     return (left_out[None], right_out[None])
 
 

time: 141 us -> 137 us (0.972)
  Pallas kernels: 33.1 us -> 30.1 us
  local copies, waits for them, and re-layouts: 5.16 us -> 3.36 us
  waiting for transfers between devices: 34.8 us -> 36.3 us
    all_to_all x1, waiting for transfers between devices: 0.48 us -> 2.78 us  [body(): lax.all_to_all(right.reshape(NDEV, NX, WIDTH), ('x', 'z', 'core'), split_...]
    unnamed x76 -> x62, local copies, waits for them, and re-layouts: 4.24 us -> 2.44 us
    pallas_call x2 -> x1, Pallas kernels: 3.85 us -> 2.23 us  [finish(): pl.pallas_call(kernel, grid_spec=pltpu.PrefetchScalarGridSpec(num_scalar_...]
  transfers between devices with their start and end apart: 39 -> 39, of which waited for: 14 -> 15; matrix products, arithmetic and copies ran while one was open for 2% -> 2% of each run, Pallas kernels for 5% -> 3%
where the time goes in v4:
time: 137 us; the launch traced here: 135 us
  starting transfers between devices  48.6 us (35%)
  waiting for transfers between devices  36.3 us (26%)
  Pallas kernels  30.1 us (22%)
  between operations  14.5 us (11%)
  local copies, waits for them, and re-layouts  3.36 us (2%)
  other arithmetic  1.82 us (1%)
    ppermute x20, starting transfers between devices, shift(): lax.ppermute(value, axis, [(i, (i + by) % size) for i in range(size)])  31 us
    pallas_call x1, Pallas kernels, correlate(): pl.pallas_call(kernel, grid_spec=pltpu.PrefetchScalarGridSpec(num_scalar_...  21.4 us
    ppermute x20, waiting for transfers between devices, shift(): lax.ppermute(value, axis, [(i, (i + by) % size) for i in range(size)])  16.9 us
    all_to_all x1, waiting for transfers between devices, body(): lax.all_to_all(slices, ('dp', 'x'), split_axis=0, concat_axis=0, tiled=True)  9.12 us
    all_to_all x1, starting transfers between devices, body(): lax.all_to_all(right.reshape(NDEV, NX, WIDTH), ('x', 'z', 'core'), split_...  8.25 us
    all_to_all x1, starting transfers between devices, body(): lax.all_to_all(slices, ('dp', 'x'), split_axis=0, concat_axis=0, tiled=True)  7.05 us
    all_gather x1, waiting for transfers between devices, body(): gathered = in_hbm(lax.all_gather(acts, ('x', 'dp'), axis=0, tiled=False))  6.99 us
    all_to_all x1, waiting for transfers between devices, body(): lax.all_to_all(right.reshape(NDEV, NX, WIDTH), ('x', 'z', 'core'), split_...  2.78 us
  transfers between devices with their start and end apart: 39, of which 15 were waited for; matrix products, arithmetic and copies ran while one was open for 2% of the time, Pallas kernels for 3%

profile of v4, /device:TPU:32, one launch (start us, length us, event | category | flops | bytes accessed | tf_op | source)
XLA Modules:
  0.0 134.7 jit_solution(10963339671541685867)
XLA Ops:
  7.2 0.0 all-gather.3.cloned.1.call-start
  7.2 2.5 %prepare.1 = (bf16[2,64,1536]{2,1,0:T(8,128)(2,1)}, bf16[16,96,128]{2,1,0:T(8,128)(2,1)}) custom-call(bf16[2,64,1536]{2,1,0:T(8,128)(2,1)} %codes_ref.1, f32[12,2,64]{2,1,0:T(2,128)} %bitcast.42), custom_call_target="tpu_custom_call" | custom-call | tf_op jit(solution)/shard_map/prepare/pallas_call | solution.py:56
  9.7 0.0 all-gather.3.cloned.1.call-update
  9.7 7.0 %all-to-all-start = ((bf16[16,96,128]{2,1,0:T(8,128)(2,1)}), bf16[16,96,128]{2,1,0:T(8,128)(2,1)S(1)}, u32[]{:S(2)}, u32[]{:S(2)}) async-start(bf16[16,96,128]{2,1,0:T(8,128)(2,1)} %get-tuple-element.22), calls=%async_computation | async-start | bytes 786432 | tf_op jit(solution)/shard_map/all_to_all | solution.py:301
  16.8 0.8 reshape.139
  17.6 0.1 reshape.140
  17.7 9.1 %all-to-all-done.in_ref = bf16[16,96,128]{2,1,0:T(8,128)(2,1)S(1)} async-done(((bf16[16,96,128]{2,1,0:T(8,128)(2,1)}), bf16[16,96,128]{2,1,0:T(8,128)(2,1)S(1)}, u32[]{:S(2)}, u32[]{:S(2)}) %all-to-all-start) | async-done | bytes 393248 | tf_op jit(solution)/shard_map/all_to_all | solution.py:301
  26.8 0.7 copy-done.1
  27.6 2.4 %normalise.1 = (bf16[4,96,256]{2,1,0:T(8,128)(2,1)}, bf16[4,96,256]{2,1,0:T(8,128)(2,1)}) custom-call(bf16[16,96,128]{2,1,0:T(8,128)(2,1)} %copy-done.1), custom_call_target="tpu_custom_call" | custom-call | tf_op jit(solution)/shard_map/normalise/pallas_call | solution.py:80
  30.0 0.1 collective-permute-start.4
  30.1 1.9 %collective-permute-start.2 = (bf16[4,96,256]{2,1,0:T(8,128)(2,1)}, bf16[4,96,256]{2,1,0:T(8,128)(2,1)S(1)}, u32[]{:S(2)}, u32[]{:S(2)}) collective-permute-start(bf16[4,96,256]{2,1,0:T(8,128)(2,1)} %get-tuple-element.23.refs_0_), channel_id=1, source_target_pairs={{0,2},{2,4},{4,6},{6,8},{8,10},{10,12},{12,14},{14,0},{1,3},{3,5},... | collective-permute-start | bytes 589832 | tf_op jit(solution)/shard_map/ppermute | solution.py:262
  32.0 0.0 collective-permute-start
  32.0 3.9 %collective-permute-start.8 = (bf16[4,96,256]{2,1,0:T(8,128)(2,1)}, bf16[4,96,256]{2,1,0:T(8,128)(2,1)S(1)}, u32[]{:S(2)}, u32[]{:S(2)}) collective-permute-start(bf16[4,96,256]{2,1,0:T(8,128)(2,1)} %get-tuple-element.24.refs_2_), channel_id=1, source_target_pairs={{0,14},{2,0},{4,2},{6,4},{8,6},{10,8},{12,10},{14,12},{1,15},{3,1}... | collective-permute-start | bytes 589832 | tf_op jit(solution)/shard_map/ppermute | solution.py:262
  36.0 0.2 collective-permute-done.4.refs_6_
  36.2 0.2 collective-permute-start.1
  36.4 3.5 %collective-permute-done.2.refs_4_ = bf16[4,96,256]{2,1,0:T(8,128)(2,1)S(1)} collective-permute-done((bf16[4,96,256]{2,1,0:T(8,128)(2,1)}, bf16[4,96,256]{2,1,0:T(8,128)(2,1)S(1)}, u32[]{:S(2)}, u32[]{:S(2)}) %collective-permute-start.2) | collective-permute-done | bytes 196640 | tf_op jit(solution)/shard_map/ppermute | solution.py:262
  39.9 3.2 %collective-permute-start.12 = (bf16[4,96,256]{2,1,0:T(8,128)(2,1)S(1)}, bf16[4,96,256]{2,1,0:T(8,128)(2,1)S(1)}, u32[]{:S(2)}, u32[]{:S(2)}) collective-permute-start(bf16[4,96,256]{2,1,0:T(8,128)(2,1)S(1)} %collective-permute-done.4.refs_6_), channel_id=1, source_target_pairs={{0,14},{2,0},{4,2},{6,4},{8,6},{10,8},{12,10},{14,12},{1,15},{3,1}... | collective-permute-start | bytes 589832 | tf_op jit(solution)/shard_map/ppermute | solution.py:262
  43.1 0.1 collective-permute-start.10
  43.2 1.6 %collective-permute-done.6.refs_8_ = bf16[4,96,256]{2,1,0:T(8,128)(2,1)S(1)} collective-permute-done((bf16[4,96,256]{2,1,0:T(8,128)(2,1)}, bf16[4,96,256]{2,1,0:T(8,128)(2,1)S(1)}, u32[]{:S(2)}, u32[]{:S(2)}) %collective-permute-start.6) | collective-permute-done | bytes 196640 | tf_op jit(solution)/shard_map/ppermute | solution.py:262
  44.8 0.2 convert_reduce_fusion
  45.0 3.0 %collective-permute-start.16 = (bf16[4,96,256]{2,1,0:T(8,128)(2,1)S(1)}, bf16[4,96,256]{2,1,0:T(8,128)(2,1)S(1)}, u32[]{:S(2)}, u32[]{:S(2)}) collective-permute-start(bf16[4,96,256]{2,1,0:T(8,128)(2,1)S(1)} %collective-permute-done.8.refs_10_), channel_id=1, source_target_pairs={{0,14},{2,0},{4,2},{6,4},{8,6},{10,8},{12,10},{14,12},{1,15},{3,1}... | collective-permute-start | bytes 589832 | tf_op jit(solution)/shard_map/ppermute | solution.py:262
  48.0 0.2 collective-permute-start.9
  48.2 2.2 %collective-permute-done.10.refs_12_ = bf16[4,96,256]{2,1,0:T(8,128)(2,1)S(1)} collective-permute-done((bf16[4,96,256]{2,1,0:T(8,128)(2,1)S(1)}, bf16[4,96,256]{2,1,0:T(8,128)(2,1)S(1)}, u32[]{:S(2)}, u32[]{:S(2)}) %collective-permute-start.10) | collective-permute-done | bytes 196640 | tf_op jit(solution)/shard_map/ppermute | solution.py:262
  50.4 2.4 %collective-permute-start.20 = (bf16[4,96,256]{2,1,0:T(8,128)(2,1)S(1)}, bf16[4,96,256]{2,1,0:T(8,128)(2,1)S(1)}, u32[]{:S(2)}, u32[]{:S(2)}) collective-permute-start(bf16[4,96,256]{2,1,0:T(8,128)(2,1)S(1)} %collective-permute-done.12.refs_14_), channel_id=1, source_target_pairs={{0,14},{2,0},{4,2},{6,4},{8,6},{10,8},{12,10},{14,12},{1,15},{3,1}... | collective-permute-start | bytes 589832 | tf_op jit(solution)/shard_map/ppermute | solution.py:262
  52.8 1.3 fusion.10.rows_ref
  54.1 0.2 collective-permute-start.13
  54.3 1.0 collective-permute-done.14.refs_16_
  55.3 2.5 %collective-permute-start.24 = (bf16[4,96,256]{2,1,0:T(8,128)(2,1)S(1)}, bf16[4,96,256]{2,1,0:T(8,128)(2,1)S(1)}, u32[]{:S(2)}, u32[]{:S(2)}) collective-permute-start(bf16[4,96,256]{2,1,0:T(8,128)(2,1)S(1)} %collective-permute-done.16.refs_18_), channel_id=1, source_target_pairs={{0,14},{2,0},{4,2},{6,4},{8,6},{10,8},{12,10},{14,12},{1,15},{3,1}... | collective-permute-start | bytes 589832 | tf_op jit(solution)/shard_map/ppermute | solution.py:262
  57.9 0.2 collective-permute-start.17
  58.0 0.1 select_reduce_fusion.order_ref
  58.2 0.1 collective-permute-start.22
  58.3 3.2 %collective-permute-done.18.refs_20_ = bf16[4,96,256]{2,1,0:T(8,128)(2,1)S(1)} collective-permute-done((bf16[4,96,256]{2,1,0:T(8,128)(2,1)S(1)}, bf16[4,96,256]{2,1,0:T(8,128)(2,1)S(1)}, u32[]{:S(2)}, u32[]{:S(2)}) %collective-permute-start.18) | collective-permute-done | bytes 196640 | tf_op jit(solution)/shard_map/ppermute | solution.py:262
  61.5 0.5 collective-permute-start.21
  62.0 0.7 collective-permute-done.24.refs_26_
  62.7 1.2 collective-permute-start.26
  63.8 1.4 %collective-permute-start.28 = (bf16[4,96,256]{2,1,0:T(8,128)(2,1)S(1)}, bf16[4,96,256]{2,1,0:T(8,128)(2,1)S(1)}, u32[]{:S(2)}, u32[]{:S(2)}) collective-permute-start(bf16[4,96,256]{2,1,0:T(8,128)(2,1)S(1)} %collective-permute-done.24.refs_26_), channel_id=1, source_target_pairs={{0,14},{2,0},{4,2},{6,4},{8,6},{10,8},{12,10},{14,12},{1,15},{3,1}... | collective-permute-start | bytes 589832 | tf_op jit(solution)/shard_map/ppermute | solution.py:262
  65.2 0.1 convert_reduce_fusion.1.start_ref
  65.3 0.6 collective-permute-done.22.refs_24_
  65.9 0.0 collective-permute-start.19
  65.9 0.5 collective-permute-start.25
  66.4 0.1 collective-permute-start.23
  66.5 3.6 %collective-permute-done.26.refs_28_ = bf16[4,96,256]{2,1,0:T(8,128)(2,1)S(1)} collective-permute-done((bf16[4,96,256]{2,1,0:T(8,128)(2,1)S(1)}, bf16[4,96,256]{2,1,0:T(8,128)(2,1)S(1)}, u32[]{:S(2)}, u32[]{:S(2)}) %collective-permute-start.26) | collective-permute-done | bytes 196640 | tf_op jit(solution)/shard_map/ppermute | solution.py:262
  70.1 0.4 collective-permute-done.28.refs_30_
  70.5 0.5 collective-permute-start.29
  70.9 0.1 broadcast_add_fusion.lpos_ref
  71.1 0.5 collective-permute-done.27.refs_29_
  71.6 0.1 copy-done.27
  71.7 0.1 copy-done.28
  71.8 0.1 copy-done.29
  71.8 0.7 copy-done.30
  72.5 7.0 %all-gather.3.cloned.1.call-done = bf16[32,64,1536]{2,1,0:T(8,128)(2,1)} async-done(((bf16[2,64,1536]{2,1,0:T(8,128)(2,1)}), bf16[32,64,1536]{2,1,0:T(8,128)(2,1)}) %all-gather.3.cloned.1.call-update) | async-done | bytes 6291472 | tf_op jit(solution)/shard_map/all_gather | solution.py:302
  79.6 21.4 %correlate.1 = (f32[384,128]{1,0:T(8,128)S(1)}, f32[384,128]{1,0:T(8,128)S(1)}, f32[384,128]{1,0:T(8,128)S(1)}, f32[384,128]{1,0:T(8,128)S(1)}, f32[256,96]{1,0:T(8,128)}) custom-call(s32[9]{0:T(128)S(1)} %convert_reduce_fusion.1.start_ref, s32[128]{0:T(128)S(1)} %select_reduce_fusion.order_ref, s32[128]{0:T(128)S(1)} %get-tuple-element.38.jidx_ref, ...), custom_call_target="tpu_custom_call" | custom-call | tf_op jit(solution)/shard_map/correlate/pallas_call | solution.py:185
  101.0 0.7 copy-done
  101.7 1.5 %collective-permute-start.30 = (f32[384,128]{1,0:T(8,128)S(1)}, f32[384,128]{1,0:T(8,128)S(1)}, u32[]{:S(2)}, u32[]{:S(2)}) collective-permute-start(f32[384,128]{1,0:T(8,128)S(1)} %get-tuple-element.27), channel_id=1, source_target_pairs={{0,16},{16,32},{32,48},{48,0},{1,17},{17,33},{33,49},{49,1},{2,18}... | collective-permute-start | bytes 589832 | tf_op jit(solution)/shard_map/ppermute | solution.py:262
  103.2 2.7 %collective-permute-start.31 = (f32[384,128]{1,0:T(8,128)S(1)}, f32[384,128]{1,0:T(8,128)S(1)}, u32[]{:S(2)}, u32[]{:S(2)}) collective-permute-start(f32[384,128]{1,0:T(8,128)S(1)} %get-tuple-element.28), channel_id=1, source_target_pairs={{0,32},{16,48},{32,0},{48,16},{1,33},{17,49},{33,1},{49,17},{2,34}... | collective-permute-start | bytes 589832 | tf_op jit(solution)/shard_map/ppermute | solution.py:262
  105.8 1.5 %collective-permute-start.32 = (f32[384,128]{1,0:T(8,128)S(1)}, f32[384,128]{1,0:T(8,128)S(1)}, u32[]{:S(2)}, u32[]{:S(2)}) collective-permute-start(f32[384,128]{1,0:T(8,128)S(1)} %get-tuple-element.29), channel_id=1, source_target_pairs={{0,48},{16,0},{32,16},{48,32},{1,49},{17,1},{33,17},{49,33},{2,50}... | collective-permute-start | bytes 589832 | tf_op jit(solution)/shard_map/ppermute | solution.py:262
  107.3 8.3 %all-to-all-start.1 = ((f32[64,4,96]{2,1,0:T(4,128)}), f32[64,4,96]{2,1,0:T(4,128)S(1)}, u32[]{:S(2)}, u32[]{:S(2)}) async-start(f32[64,4,96]{2,1,0:T(4,128)} %bitcast.6), calls=%async_computation.1 | async-start | bytes 262144 | tf_op jit(solution)/shard_map/all_to_all | solution.py:327
  115.6 1.7 %meet.1 = (f32[96,128]{1,0:T(8,128)}, f32[96,128]{1,0:T(8,128)}, f32[96,128]{1,0:T(8,128)}, f32[96,128]{1,0:T(8,128)}) custom-call(f32[384,128]{1,0:T(8,128)} %copy-done, f32[384,128]{1,0:T(8,128)S(1)} %collective-permute-done.30.refs_1_, f32[384,128]{1,0:T(8,128)S(1)} %collective-permute-done.31.refs_2_, f32[384,128]{1,0:T(8,128)S(1)} %collective-permute-done.32.refs_3_), custom_call_target="tpu_custom_call" | custom-call | tf_op jit(solution)/shard_map/meet/pallas_call | solution.py:244
  117.2 1.4 %collective-permute-start.33 = (f32[96,128]{1,0:T(8,128)}, f32[96,128]{1,0:T(8,128)S(1)}, u32[]{:S(2)}, u32[]{:S(2)}) collective-permute-start(f32[96,128]{1,0:T(8,128)} %get-tuple-element.31), channel_id=1, source_target_pairs={{0,64},{64,128},{128,192},{192,0},{1,65},{65,129},{129,193},{193,1... | collective-permute-start | bytes 147464 | tf_op jit(solution)/shard_map/ppermute | solution.py:262
  118.7 2.7 %collective-permute-start.34 = (f32[96,128]{1,0:T(8,128)}, f32[96,128]{1,0:T(8,128)S(1)}, u32[]{:S(2)}, u32[]{:S(2)}) collective-permute-start(f32[96,128]{1,0:T(8,128)} %get-tuple-element.32), channel_id=1, source_target_pairs={{0,128},{64,192},{128,0},{192,64},{1,129},{65,193},{129,1},{193,65... | collective-permute-start | bytes 147464 | tf_op jit(solution)/shard_map/ppermute | solution.py:262
  121.4 1.4 %collective-permute-start.35 = (f32[96,128]{1,0:T(8,128)}, f32[96,128]{1,0:T(8,128)S(1)}, u32[]{:S(2)}, u32[]{:S(2)}) collective-permute-start(f32[96,128]{1,0:T(8,128)} %get-tuple-element.33), channel_id=1, source_target_pairs={{0,192},{64,0},{128,64},{192,128},{1,193},{65,1},{129,65},{193,129... | collective-permute-start | bytes 147464 | tf_op jit(solution)/shard_map/ppermute | solution.py:262
  122.8 2.8 %all-to-all-done.1 = f32[64,4,96]{2,1,0:T(4,128)S(1)} async-done(((f32[64,4,96]{2,1,0:T(4,128)}), f32[64,4,96]{2,1,0:T(4,128)S(1)}, u32[]{:S(2)}, u32[]{:S(2)}) %all-to-all-start.1) | async-done | bytes 98336 | tf_op jit(solution)/shard_map/all_to_all | solution.py:327
  125.6 0.1 collective-permute-done.35.refs_3_
  125.7 2.2 %finish.1 = (f32[32,384]{1,0:T(8,128)}, f32[32,384]{1,0:T(8,128)}) custom-call(s32[32]{0:T(128)} %fusion.10.rows_ref, f32[4,64,96]{2,1,0:T(8,128)S(1)} %bitcast.40, f32[96,128]{1,0:T(8,128)} %get-tuple-element.30.refs_0_, f32[96,128]{1,0:T(8,128)S(1)} %collective-permute-done.33.refs_1_, f32[96,128]{1,0:T(8,128)S(1)} %collective-permute-done.34.refs_2_, ...), custom_call_target="tpu_custom_call" | custom-call | tf_op jit(solution)/shard_map/finish/pallas_call | solution.py:221
  (95 shorter events, 0.3 us)
Async XLA Ops:
  7.2 72.3 %all-gather.3.cloned.1.call-start = ((), (), s32[]{:S(2)}) async-start(), calls=%async_computation.2 | async-start | bytes 6684672 | tf_op jit(solution)/shard_map/all_gather | solution.py:302
  9.7 17.1 %all-to-all-start = ((bf16[16,96,128]{2,1,0:T(8,128)(2,1)}), bf16[16,96,128]{2,1,0:T(8,128)(2,1)S(1)}, u32[]{:S(2)}, u32[]{:S(2)}) async-start(bf16[16,96,128]{2,1,0:T(8,128)(2,1)} %get-tuple-element.22), calls=%async_computation | async-start | bytes 786432 | tf_op jit(solution)/shard_map/all_to_all | solution.py:301
  30.0 6.2 %collective-permute-start.4 = (bf16[4,96,256]{2,1,0:T(8,128)(2,1)}, bf16[4,96,256]{2,1,0:T(8,128)(2,1)S(1)}, u32[]{:S(2)}, u32[]{:S(2)}) collective-permute-start(bf16[4,96,256]{2,1,0:T(8,128)(2,1)} %get-tuple-element.23.refs_0_), channel_id=1, source_target_pairs={{0,14},{2,0},{4,2},{6,4},{8,6},{10,8},{12,10},{14,12},{1,15},{3,1}... | collective-permute-start | bytes 589832 | tf_op jit(solution)/shard_map/ppermute | solution.py:262
  30.1 9.7 %collective-permute-start.2 = (bf16[4,96,256]{2,1,0:T(8,128)(2,1)}, bf16[4,96,256]{2,1,0:T(8,128)(2,1)S(1)}, u32[]{:S(2)}, u32[]{:S(2)}) collective-permute-start(bf16[4,96,256]{2,1,0:T(8,128)(2,1)} %get-tuple-element.23.refs_0_), channel_id=1, source_target_pairs={{0,2},{2,4},{4,6},{6,8},{8,10},{10,12},{12,14},{14,0},{1,3},{3,5},... | collective-permute-start | bytes 589832 | tf_op jit(solution)/shard_map/ppermute | solution.py:262
  32.0 11.0 %collective-permute-start = (bf16[4,96,256]{2,1,0:T(8,128)(2,1)}, bf16[4,96,256]{2,1,0:T(8,128)(2,1)S(1)}, u32[]{:S(2)}, u32[]{:S(2)}) collective-permute-start(bf16[4,96,256]{2,1,0:T(8,128)(2,1)} %get-tuple-element.23.refs_0_), channel_id=1, source_target_pairs={{0,1},{1,0},{2,3},{3,2},{4,5},{5,4},{6,7},{7,6},{8,9},{9,8},{10,11... | collective-permute-start | bytes 589832 | tf_op jit(solution)/shard_map/ppermute | solution.py:266
  32.0 11.0 %collective-permute-start.8 = (bf16[4,96,256]{2,1,0:T(8,128)(2,1)}, bf16[4,96,256]{2,1,0:T(8,128)(2,1)S(1)}, u32[]{:S(2)}, u32[]{:S(2)}) collective-permute-start(bf16[4,96,256]{2,1,0:T(8,128)(2,1)} %get-tuple-element.24.refs_2_), channel_id=1, source_target_pairs={{0,14},{2,0},{4,2},{6,4},{8,6},{10,8},{12,10},{14,12},{1,15},{3,1}... | collective-permute-start | bytes 589832 | tf_op jit(solution)/shard_map/ppermute | solution.py:262
  36.0 8.8 %collective-permute-start.6 = (bf16[4,96,256]{2,1,0:T(8,128)(2,1)}, bf16[4,96,256]{2,1,0:T(8,128)(2,1)S(1)}, u32[]{:S(2)}, u32[]{:S(2)}) collective-permute-start(bf16[4,96,256]{2,1,0:T(8,128)(2,1)} %get-tuple-element.24.refs_2_), channel_id=1, source_target_pairs={{0,2},{2,4},{4,6},{6,8},{8,10},{10,12},{12,14},{14,0},{1,3},{3,5},... | collective-permute-start | bytes 589832 | tf_op jit(solution)/shard_map/ppermute | solution.py:262
  36.2 43.3 %copy-start.2 = (bf16[4,96,256]{2,1,0:T(8,128)(2,1)}, bf16[4,96,256]{2,1,0:T(8,128)(2,1)S(1)}, u32[]{:S(2)}) copy-start(bf16[4,96,256]{2,1,0:T(8,128)(2,1)S(1)} %collective-permute-done.4.refs_6_) | copy-start | bytes 589828
  36.2 8.8 %collective-permute-start.1 = (bf16[4,96,256]{2,1,0:T(8,128)(2,1)}, bf16[4,96,256]{2,1,0:T(8,128)(2,1)S(1)}, u32[]{:S(2)}, u32[]{:S(2)}) collective-permute-start(bf16[4,96,256]{2,1,0:T(8,128)(2,1)} %get-tuple-element.24.refs_2_), channel_id=1, source_target_pairs={{0,1},{1,0},{2,3},{3,2},{4,5},{5,4},{6,7},{7,6},{8,9},{9,8},{10,11... | collective-permute-start | bytes 589832 | tf_op jit(solution)/shard_map/ppermute | solution.py:266
  39.9 39.6 %copy-start.3 = (bf16[4,96,256]{2,1,0:T(8,128)(2,1)}, bf16[4,96,256]{2,1,0:T(8,128)(2,1)S(1)}, u32[]{:S(2)}) copy-start(bf16[4,96,256]{2,1,0:T(8,128)(2,1)S(1)} %collective-permute-done.2.refs_4_) | copy-start | bytes 589828
  39.9 8.1 %collective-permute-start.12 = (bf16[4,96,256]{2,1,0:T(8,128)(2,1)S(1)}, bf16[4,96,256]{2,1,0:T(8,128)(2,1)S(1)}, u32[]{:S(2)}, u32[]{:S(2)}) collective-permute-start(bf16[4,96,256]{2,1,0:T(8,128)(2,1)S(1)} %collective-permute-done.4.refs_6_), channel_id=1, source_target_pairs={{0,14},{2,0},{4,2},{6,4},{8,6},{10,8},{12,10},{14,12},{1,15},{3,1}... | collective-permute-start | bytes 589832 | tf_op jit(solution)/shard_map/ppermute | solution.py:262
  43.1 36.4 %copy-start.4 = (bf16[4,96,256]{2,1,0:T(8,128)(2,1)}, bf16[4,96,256]{2,1,0:T(8,128)(2,1)S(1)}, u32[]{:S(2)}) copy-start(bf16[4,96,256]{2,1,0:T(8,128)(2,1)S(1)} %collective-permute-done.refs_1_) | copy-start | bytes 589828
  43.1 5.1 %collective-permute-start.5 = (bf16[4,96,256]{2,1,0:T(8,128)(2,1)S(1)}, bf16[4,96,256]{2,1,0:T(8,128)(2,1)S(1)}, u32[]{:S(2)}, u32[]{:S(2)}) collective-permute-start(bf16[4,96,256]{2,1,0:T(8,128)(2,1)S(1)} %collective-permute-done.4.refs_6_), channel_id=1, source_target_pairs={{0,1},{1,0},{2,3},{3,2},{4,5},{5,4},{6,7},{7,6},{8,9},{9,8},{10,11... | collective-permute-start | bytes 589832 | tf_op jit(solution)/shard_map/ppermute | solution.py:266
  43.1 36.4 %copy-start.5 = (bf16[4,96,256]{2,1,0:T(8,128)(2,1)}, bf16[4,96,256]{2,1,0:T(8,128)(2,1)S(1)}, u32[]{:S(2)}) copy-start(bf16[4,96,256]{2,1,0:T(8,128)(2,1)S(1)} %collective-permute-done.8.refs_10_) | copy-start | bytes 589828
  43.1 7.3 %collective-permute-start.10 = (bf16[4,96,256]{2,1,0:T(8,128)(2,1)S(1)}, bf16[4,96,256]{2,1,0:T(8,128)(2,1)S(1)}, u32[]{:S(2)}, u32[]{:S(2)}) collective-permute-start(bf16[4,96,256]{2,1,0:T(8,128)(2,1)S(1)} %collective-permute-done.2.refs_4_), channel_id=1, source_target_pairs={{0,2},{2,4},{4,6},{6,8},{8,10},{10,12},{12,14},{14,0},{1,3},{3,5},... | collective-permute-start | bytes 589832 | tf_op jit(solution)/shard_map/ppermute | solution.py:262
  44.8 34.8 %copy-start.6 = (bf16[4,96,256]{2,1,0:T(8,128)(2,1)}, bf16[4,96,256]{2,1,0:T(8,128)(2,1)S(1)}, u32[]{:S(2)}) copy-start(bf16[4,96,256]{2,1,0:T(8,128)(2,1)S(1)} %collective-permute-done.6.refs_8_) | copy-start | bytes 589828
  44.8 5.7 %collective-permute-start.3 = (bf16[4,96,256]{2,1,0:T(8,128)(2,1)S(1)}, bf16[4,96,256]{2,1,0:T(8,128)(2,1)S(1)}, u32[]{:S(2)}, u32[]{:S(2)}) collective-permute-start(bf16[4,96,256]{2,1,0:T(8,128)(2,1)S(1)} %collective-permute-done.2.refs_4_), channel_id=1, source_target_pairs={{0,1},{1,0},{2,3},{3,2},{4,5},{5,4},{6,7},{7,6},{8,9},{9,8},{10,11... | collective-permute-start | bytes 589832 | tf_op jit(solution)/shard_map/ppermute | solution.py:266
  45.0 34.6 %copy-start.7 = (bf16[4,96,256]{2,1,0:T(8,128)(2,1)}, bf16[4,96,256]{2,1,0:T(8,128)(2,1)S(1)}, u32[]{:S(2)}) copy-start(bf16[4,96,256]{2,1,0:T(8,128)(2,1)S(1)} %collective-permute-done.1.refs_3_) | copy-start | bytes 589828
  45.0 9.1 %collective-permute-start.16 = (bf16[4,96,256]{2,1,0:T(8,128)(2,1)S(1)}, bf16[4,96,256]{2,1,0:T(8,128)(2,1)S(1)}, u32[]{:S(2)}, u32[]{:S(2)}) collective-permute-start(bf16[4,96,256]{2,1,0:T(8,128)(2,1)S(1)} %collective-permute-done.8.refs_10_), channel_id=1, source_target_pairs={{0,14},{2,0},{4,2},{6,4},{8,6},{10,8},{12,10},{14,12},{1,15},{3,1}... | collective-permute-start | bytes 589832 | tf_op jit(solution)/shard_map/ppermute | solution.py:262
  48.0 31.6 %copy-start.8 = (bf16[4,96,256]{2,1,0:T(8,128)(2,1)}, bf16[4,96,256]{2,1,0:T(8,128)(2,1)S(1)}, u32[]{:S(2)}) copy-start(bf16[4,96,256]{2,1,0:T(8,128)(2,1)S(1)} %collective-permute-done.12.refs_14_) | copy-start | bytes 589828
  48.0 6.3 %collective-permute-start.9 = (bf16[4,96,256]{2,1,0:T(8,128)(2,1)S(1)}, bf16[4,96,256]{2,1,0:T(8,128)(2,1)S(1)}, u32[]{:S(2)}, u32[]{:S(2)}) collective-permute-start(bf16[4,96,256]{2,1,0:T(8,128)(2,1)S(1)} %collective-permute-done.8.refs_10_), channel_id=1, source_target_pairs={{0,1},{1,0},{2,3},{3,2},{4,5},{5,4},{6,7},{7,6},{8,9},{9,8},{10,11... | collective-permute-start | bytes 589832 | tf_op jit(solution)/shard_map/ppermute | solution.py:266
  48.2 31.4 %copy-start.9 = (bf16[4,96,256]{2,1,0:T(8,128)(2,1)}, bf16[4,96,256]{2,1,0:T(8,128)(2,1)S(1)}, u32[]{:S(2)}) copy-start(bf16[4,96,256]{2,1,0:T(8,128)(2,1)S(1)} %collective-permute-done.5.refs_7_) | copy-start | bytes 589828
  48.2 7.1 %collective-permute-start.14 = (bf16[4,96,256]{2,1,0:T(8,128)(2,1)S(1)}, bf16[4,96,256]{2,1,0:T(8,128)(2,1)S(1)}, u32[]{:S(2)}, u32[]{:S(2)}) collective-permute-start(bf16[4,96,256]{2,1,0:T(8,128)(2,1)S(1)} %collective-permute-done.6.refs_8_), channel_id=1, source_target_pairs={{0,2},{2,4},{4,6},{6,8},{8,10},{10,12},{12,14},{14,0},{1,3},{3,5},... | collective-permute-start | bytes 589832 | tf_op jit(solution)/shard_map/ppermute | solution.py:262
  50.4 29.2 %copy-start.10 = (bf16[4,96,256]{2,1,0:T(8,128)(2,1)}, bf16[4,96,256]{2,1,0:T(8,128)(2,1)S(1)}, u32[]{:S(2)}) copy-start(bf16[4,96,256]{2,1,0:T(8,128)(2,1)S(1)} %collective-permute-done.10.refs_12_) | copy-start | bytes 589828
  50.4 4.9 %collective-permute-start.7 = (bf16[4,96,256]{2,1,0:T(8,128)(2,1)S(1)}, bf16[4,96,256]{2,1,0:T(8,128)(2,1)S(1)}, u32[]{:S(2)}, u32[]{:S(2)}) collective-permute-start(bf16[4,96,256]{2,1,0:T(8,128)(2,1)S(1)} %collective-permute-done.6.refs_8_), channel_id=1, source_target_pairs={{0,1},{1,0},{2,3},{3,2},{4,5},{5,4},{6,7},{7,6},{8,9},{9,8},{10,11... | collective-permute-start | bytes 589832 | tf_op jit(solution)/shard_map/ppermute | solution.py:266
  50.4 29.2 %copy-start.11 = (bf16[4,96,256]{2,1,0:T(8,128)(2,1)}, bf16[4,96,256]{2,1,0:T(8,128)(2,1)S(1)}, u32[]{:S(2)}) copy-start(bf16[4,96,256]{2,1,0:T(8,128)(2,1)S(1)} %collective-permute-done.3.refs_5_) | copy-start | bytes 589828
  50.4 7.4 %collective-permute-start.20 = (bf16[4,96,256]{2,1,0:T(8,128)(2,1)S(1)}, bf16[4,96,256]{2,1,0:T(8,128)(2,1)S(1)}, u32[]{:S(2)}, u32[]{:S(2)}) collective-permute-start(bf16[4,96,256]{2,1,0:T(8,128)(2,1)S(1)} %collective-permute-done.12.refs_14_), channel_id=1, source_target_pairs={{0,14},{2,0},{4,2},{6,4},{8,6},{10,8},{12,10},{14,12},{1,15},{3,1}... | collective-permute-start | bytes 589832 | tf_op jit(solution)/shard_map/ppermute | solution.py:262
  54.1 25.5 %copy-start.12 = (bf16[4,96,256]{2,1,0:T(8,128)(2,1)}, bf16[4,96,256]{2,1,0:T(8,128)(2,1)S(1)}, u32[]{:S(2)}) copy-start(bf16[4,96,256]{2,1,0:T(8,128)(2,1)S(1)} %collective-permute-done.16.refs_18_) | copy-start | bytes 589828
  54.1 4.0 %collective-permute-start.13 = (bf16[4,96,256]{2,1,0:T(8,128)(2,1)S(1)}, bf16[4,96,256]{2,1,0:T(8,128)(2,1)S(1)}, u32[]{:S(2)}, u32[]{:S(2)}) collective-permute-start(bf16[4,96,256]{2,1,0:T(8,128)(2,1)S(1)} %collective-permute-done.12.refs_14_), channel_id=1, source_target_pairs={{0,1},{1,0},{2,3},{3,2},{4,5},{5,4},{6,7},{7,6},{8,9},{9,8},{10,11... | collective-permute-start | bytes 589832 | tf_op jit(solution)/shard_map/ppermute | solution.py:266
  54.3 25.3 %copy-start.13 = (bf16[4,96,256]{2,1,0:T(8,128)(2,1)}, bf16[4,96,256]{2,1,0:T(8,128)(2,1)S(1)}, u32[]{:S(2)}) copy-start(bf16[4,96,256]{2,1,0:T(8,128)(2,1)S(1)} %collective-permute-done.9.refs_11_) | copy-start | bytes 589828
  54.3 7.2 %collective-permute-start.18 = (bf16[4,96,256]{2,1,0:T(8,128)(2,1)S(1)}, bf16[4,96,256]{2,1,0:T(8,128)(2,1)S(1)}, u32[]{:S(2)}, u32[]{:S(2)}) collective-permute-start(bf16[4,96,256]{2,1,0:T(8,128)(2,1)S(1)} %collective-permute-done.10.refs_12_), channel_id=1, source_target_pairs={{0,2},{2,4},{4,6},{6,8},{8,10},{10,12},{12,14},{14,0},{1,3},{3,5},... | collective-permute-start | bytes 589832 | tf_op jit(solution)/shard_map/ppermute | solution.py:262
  55.3 24.2 %copy-start.14 = (bf16[4,96,256]{2,1,0:T(8,128)(2,1)}, bf16[4,96,256]{2,1,0:T(8,128)(2,1)S(1)}, u32[]{:S(2)}) copy-start(bf16[4,96,256]{2,1,0:T(8,128)(2,1)S(1)} %collective-permute-done.14.refs_16_) | copy-start | bytes 589828
  55.3 6.2 %collective-permute-start.11 = (bf16[4,96,256]{2,1,0:T(8,128)(2,1)S(1)}, bf16[4,96,256]{2,1,0:T(8,128)(2,1)S(1)}, u32[]{:S(2)}, u32[]{:S(2)}) collective-permute-start(bf16[4,96,256]{2,1,0:T(8,128)(2,1)S(1)} %collective-permute-done.10.refs_12_), channel_id=1, source_target_pairs={{0,1},{1,0},{2,3},{3,2},{4,5},{5,4},{6,7},{7,6},{8,9},{9,8},{10,11... | collective-permute-start | bytes 589832 | tf_op jit(solution)/shard_map/ppermute | solution.py:266
  55.3 24.2 %copy-start.15 = (bf16[4,96,256]{2,1,0:T(8,128)(2,1)}, bf16[4,96,256]{2,1,0:T(8,128)(2,1)S(1)}, u32[]{:S(2)}) copy-start(bf16[4,96,256]{2,1,0:T(8,128)(2,1)S(1)} %collective-permute-done.7.refs_9_) | copy-start | bytes 589828
  55.3 7.3 %collective-permute-start.24 = (bf16[4,96,256]{2,1,0:T(8,128)(2,1)S(1)}, bf16[4,96,256]{2,1,0:T(8,128)(2,1)S(1)}, u32[]{:S(2)}, u32[]{:S(2)}) collective-permute-start(bf16[4,96,256]{2,1,0:T(8,128)(2,1)S(1)} %collective-permute-done.16.refs_18_), channel_id=1, source_target_pairs={{0,14},{2,0},{4,2},{6,4},{8,6},{10,8},{12,10},{14,12},{1,15},{3,1}... | collective-permute-start | bytes 589832 | tf_op jit(solution)/shard_map/ppermute | solution.py:262
  57.9 21.6 %copy-start.16 = (bf16[4,96,256]{2,1,0:T(8,128)(2,1)}, bf16[4,96,256]{2,1,0:T(8,128)(2,1)S(1)}, u32[]{:S(2)}) copy-start(bf16[4,96,256]{2,1,0:T(8,128)(2,1)S(1)} %collective-permute-done.20.refs_22_) | copy-start | bytes 589828
  57.9 6.0 %collective-permute-start.17 = (bf16[4,96,256]{2,1,0:T(8,128)(2,1)S(1)}, bf16[4,96,256]{2,1,0:T(8,128)(2,1)S(1)}, u32[]{:S(2)}, u32[]{:S(2)}) collective-permute-start(bf16[4,96,256]{2,1,0:T(8,128)(2,1)S(1)} %collective-permute-done.16.refs_18_), channel_id=1, source_target_pairs={{0,1},{1,0},{2,3},{3,2},{4,5},{5,4},{6,7},{7,6},{8,9},{9,8},{10,11... | collective-permute-start | bytes 589832 | tf_op jit(solution)/shard_map/ppermute | solution.py:266
  58.1 12.3 %copy-start.17 = (bf16[4,96,256]{2,1,0:T(8,128)(2,1)}, bf16[4,96,256]{2,1,0:T(8,128)(2,1)S(1)}, u32[]{:S(2)}) copy-start(bf16[4,96,256]{2,1,0:T(8,128)(2,1)S(1)} %collective-permute-done.13.refs_15_) | copy-start | bytes 589828
  58.2 7.7 %collective-permute-start.22 = (bf16[4,96,256]{2,1,0:T(8,128)(2,1)S(1)}, bf16[4,96,256]{2,1,0:T(8,128)(2,1)S(1)}, u32[]{:S(2)}, u32[]{:S(2)}) collective-permute-start(bf16[4,96,256]{2,1,0:T(8,128)(2,1)S(1)} %collective-permute-done.14.refs_16_), channel_id=1, source_target_pairs={{0,2},{2,4},{4,6},{6,8},{8,10},{10,12},{12,14},{14,0},{1,3},{3,5},... | collective-permute-start | bytes 589832 | tf_op jit(solution)/shard_map/ppermute | solution.py:262
  61.5 18.0 %copy-start.18 = (bf16[4,96,256]{2,1,0:T(8,128)(2,1)}, bf16[4,96,256]{2,1,0:T(8,128)(2,1)S(1)}, u32[]{:S(2)}) copy-start(bf16[4,96,256]{2,1,0:T(8,128)(2,1)S(1)} %collective-permute-done.18.refs_20_) | copy-start | bytes 589828
  61.5 4.5 %collective-permute-start.15 = (bf16[4,96,256]{2,1,0:T(8,128)(2,1)S(1)}, bf16[4,96,256]{2,1,0:T(8,128)(2,1)S(1)}, u32[]{:S(2)}, u32[]{:S(2)}) collective-permute-start(bf16[4,96,256]{2,1,0:T(8,128)(2,1)S(1)} %collective-permute-done.14.refs_16_), channel_id=1, source_target_pairs={{0,1},{1,0},{2,3},{3,2},{4,5},{5,4},{6,7},{7,6},{8,9},{9,8},{10,11... | collective-permute-start | bytes 589832 | tf_op jit(solution)/shard_map/ppermute | solution.py:266
  61.5 9.5 %copy-start.19 = (bf16[4,96,256]{2,1,0:T(8,128)(2,1)}, bf16[4,96,256]{2,1,0:T(8,128)(2,1)S(1)}, u32[]{:S(2)}) copy-start(bf16[4,96,256]{2,1,0:T(8,128)(2,1)S(1)} %collective-permute-done.11.refs_13_) | copy-start | bytes 589828
  61.5 4.9 %collective-permute-start.21 = (bf16[4,96,256]{2,1,0:T(8,128)(2,1)S(1)}, bf16[4,96,256]{2,1,0:T(8,128)(2,1)S(1)}, u32[]{:S(2)}, u32[]{:S(2)}) collective-permute-start(bf16[4,96,256]{2,1,0:T(8,128)(2,1)S(1)} %collective-permute-done.20.refs_22_), channel_id=1, source_target_pairs={{0,1},{1,0},{2,3},{3,2},{4,5},{5,4},{6,7},{7,6},{8,9},{9,8},{10,11... | collective-permute-start | bytes 589832 | tf_op jit(solution)/shard_map/ppermute | solution.py:266
  62.7 8.4 %copy-start.20 = (bf16[4,96,256]{2,1,0:T(8,128)(2,1)}, bf16[4,96,256]{2,1,0:T(8,128)(2,1)S(1)}, u32[]{:S(2)}) copy-start(bf16[4,96,256]{2,1,0:T(8,128)(2,1)S(1)} %collective-permute-done.24.refs_26_) | copy-start | bytes 589828
  62.7 7.5 %collective-permute-start.26 = (bf16[4,96,256]{2,1,0:T(8,128)(2,1)S(1)}, bf16[4,96,256]{2,1,0:T(8,128)(2,1)S(1)}, u32[]{:S(2)}, u32[]{:S(2)}) collective-permute-start(bf16[4,96,256]{2,1,0:T(8,128)(2,1)S(1)} %collective-permute-done.18.refs_20_), channel_id=1, source_target_pairs={{0,2},{2,4},{4,6},{6,8},{8,10},{10,12},{12,14},{14,0},{1,3},{3,5},... | collective-permute-start | bytes 589832 | tf_op jit(solution)/shard_map/ppermute | solution.py:262
  63.8 7.2 %copy-start.21 = (bf16[4,96,256]{2,1,0:T(8,128)(2,1)}, bf16[4,96,256]{2,1,0:T(8,128)(2,1)S(1)}, u32[]{:S(2)}) copy-start(bf16[4,96,256]{2,1,0:T(8,128)(2,1)S(1)} %collective-permute-done.17.refs_19_) | copy-start | bytes 589828
  63.8 6.7 %collective-permute-start.28 = (bf16[4,96,256]{2,1,0:T(8,128)(2,1)S(1)}, bf16[4,96,256]{2,1,0:T(8,128)(2,1)S(1)}, u32[]{:S(2)}, u32[]{:S(2)}) collective-permute-start(bf16[4,96,256]{2,1,0:T(8,128)(2,1)S(1)} %collective-permute-done.24.refs_26_), channel_id=1, source_target_pairs={{0,14},{2,0},{4,2},{6,4},{8,6},{10,8},{12,10},{14,12},{1,15},{3,1}... | collective-permute-start | bytes 589832 | tf_op jit(solution)/shard_map/ppermute | solution.py:262
  65.9 5.7 %copy-start.22 = (bf16[4,96,256]{2,1,0:T(8,128)(2,1)}, bf16[4,96,256]{2,1,0:T(8,128)(2,1)S(1)}, u32[]{:S(2)}) copy-start(bf16[4,96,256]{2,1,0:T(8,128)(2,1)S(1)} %collective-permute-done.22.refs_24_) | copy-start | bytes 589828
  65.9 5.1 %collective-permute-start.19 = (bf16[4,96,256]{2,1,0:T(8,128)(2,1)S(1)}, bf16[4,96,256]{2,1,0:T(8,128)(2,1)S(1)}, u32[]{:S(2)}, u32[]{:S(2)}) collective-permute-start(bf16[4,96,256]{2,1,0:T(8,128)(2,1)S(1)} %collective-permute-done.18.refs_20_), channel_id=1, source_target_pairs={{0,1},{1,0},{2,3},{3,2},{4,5},{5,4},{6,7},{7,6},{8,9},{9,8},{10,11... | collective-permute-start | bytes 589832 | tf_op jit(solution)/shard_map/ppermute | solution.py:266
  65.9 5.6 %copy-start.23 = (bf16[4,96,256]{2,1,0:T(8,128)(2,1)}, bf16[4,96,256]{2,1,0:T(8,128)(2,1)S(1)}, u32[]{:S(2)}) copy-start(bf16[4,96,256]{2,1,0:T(8,128)(2,1)S(1)} %collective-permute-done.15.refs_17_) | copy-start | bytes 589828
  65.9 5.1 %collective-permute-start.25 = (bf16[4,96,256]{2,1,0:T(8,128)(2,1)S(1)}, bf16[4,96,256]{2,1,0:T(8,128)(2,1)S(1)}, u32[]{:S(2)}, u32[]{:S(2)}) collective-permute-start(bf16[4,96,256]{2,1,0:T(8,128)(2,1)S(1)} %collective-permute-done.24.refs_26_), channel_id=1, source_target_pairs={{0,1},{1,0},{2,3},{3,2},{4,5},{5,4},{6,7},{7,6},{8,9},{9,8},{10,11... | collective-permute-start | bytes 589832 | tf_op jit(solution)/shard_map/ppermute | solution.py:266
  66.4 5.1 %copy-start.24 = (bf16[4,96,256]{2,1,0:T(8,128)(2,1)}, bf16[4,96,256]{2,1,0:T(8,128)(2,1)S(1)}, u32[]{:S(2)}) copy-start(bf16[4,96,256]{2,1,0:T(8,128)(2,1)S(1)} %collective-permute-done.21.refs_23_) | copy-start | bytes 589828
  66.4 4.6 %collective-permute-start.23 = (bf16[4,96,256]{2,1,0:T(8,128)(2,1)S(1)}, bf16[4,96,256]{2,1,0:T(8,128)(2,1)S(1)}, u32[]{:S(2)}, u32[]{:S(2)}) collective-permute-start(bf16[4,96,256]{2,1,0:T(8,128)(2,1)S(1)} %collective-permute-done.22.refs_24_), channel_id=1, source_target_pairs={{0,1},{1,0},{2,3},{3,2},{4,5},{5,4},{6,7},{7,6},{8,9},{9,8},{10,11... | collective-permute-start | bytes 589832 | tf_op jit(solution)/shard_map/ppermute | solution.py:266
  70.1 1.5 %copy-start.25 = (bf16[4,96,256]{2,1,0:T(8,128)(2,1)}, bf16[4,96,256]{2,1,0:T(8,128)(2,1)S(1)}, u32[]{:S(2)}) copy-start(bf16[4,96,256]{2,1,0:T(8,128)(2,1)S(1)} %collective-permute-done.26.refs_28_) | copy-start | bytes 589828
  70.1 1.4 %collective-permute-start.27 = (bf16[4,96,256]{2,1,0:T(8,128)(2,1)S(1)}, bf16[4,96,256]{2,1,0:T(8,128)(2,1)S(1)}, u32[]{:S(2)}, u32[]{:S(2)}) collective-permute-start(bf16[4,96,256]{2,1,0:T(8,128)(2,1)S(1)} %collective-permute-done.26.refs_28_), channel_id=1, source_target_pairs={{0,1},{1,0},{2,3},{3,2},{4,5},{5,4},{6,7},{7,6},{8,9},{9,8},{10,11... | collective-permute-start | bytes 589832 | tf_op jit(solution)/shard_map/ppermute | solution.py:266
  70.5 1.1 copy-start.26
  70.5 2.0 %collective-permute-start.29 = (bf16[4,96,256]{2,1,0:T(8,128)(2,1)S(1)}, bf16[4,96,256]{2,1,0:T(8,128)(2,1)}, u32[]{:S(2)}, u32[]{:S(2)}) collective-permute-start(bf16[4,96,256]{2,1,0:T(8,128)(2,1)S(1)} %collective-permute-done.28.refs_30_), channel_id=1, source_target_pairs={{0,1},{1,0},{2,3},{3,2},{4,5},{5,4},{6,7},{7,6},{8,9},{9,8},{10,11... | collective-permute-start | bytes 589832 | tf_op jit(solution)/shard_map/ppermute | solution.py:266
  101.7 13.9 %collective-permute-start.30 = (f32[384,128]{1,0:T(8,128)S(1)}, f32[384,128]{1,0:T(8,128)S(1)}, u32[]{:S(2)}, u32[]{:S(2)}) collective-permute-start(f32[384,128]{1,0:T(8,128)S(1)} %get-tuple-element.27), channel_id=1, source_target_pairs={{0,16},{16,32},{32,48},{48,0},{1,17},{17,33},{33,49},{49,1},{2,18}... | collective-permute-start | bytes 589832 | tf_op jit(solution)/shard_map/ppermute | solution.py:262
  103.2 12.4 %collective-permute-start.31 = (f32[384,128]{1,0:T(8,128)S(1)}, f32[384,128]{1,0:T(8,128)S(1)}, u32[]{:S(2)}, u32[]{:S(2)}) collective-permute-start(f32[384,128]{1,0:T(8,128)S(1)} %get-tuple-element.28), channel_id=1, source_target_pairs={{0,32},{16,48},{32,0},{48,16},{1,33},{17,49},{33,1},{49,17},{2,34}... | collective-permute-start | bytes 589832 | tf_op jit(solution)/shard_map/ppermute | solution.py:262
  105.8 9.7 %collective-permute-start.32 = (f32[384,128]{1,0:T(8,128)S(1)}, f32[384,128]{1,0:T(8,128)S(1)}, u32[]{:S(2)}, u32[]{:S(2)}) collective-permute-start(f32[384,128]{1,0:T(8,128)S(1)} %get-tuple-element.29), channel_id=1, source_target_pairs={{0,48},{16,0},{32,16},{48,32},{1,49},{17,1},{33,17},{49,33},{2,50}... | collective-permute-start | bytes 589832 | tf_op jit(solution)/shard_map/ppermute | solution.py:262
  107.3 18.3 %all-to-all-start.1 = ((f32[64,4,96]{2,1,0:T(4,128)}), f32[64,4,96]{2,1,0:T(4,128)S(1)}, u32[]{:S(2)}, u32[]{:S(2)}) async-start(f32[64,4,96]{2,1,0:T(4,128)} %bitcast.6), calls=%async_computation.1 | async-start | bytes 262144 | tf_op jit(solution)/shard_map/all_to_all | solution.py:327
  117.2 8.4 %collective-permute-start.33 = (f32[96,128]{1,0:T(8,128)}, f32[96,128]{1,0:T(8,128)S(1)}, u32[]{:S(2)}, u32[]{:S(2)}) collective-permute-start(f32[96,128]{1,0:T(8,128)} %get-tuple-element.31), channel_id=1, source_target_pairs={{0,64},{64,128},{128,192},{192,0},{1,65},{65,129},{129,193},{193,1... | collective-permute-start | bytes 147464 | tf_op jit(solution)/shard_map/ppermute | solution.py:262
  118.7 6.9 %collective-permute-start.34 = (f32[96,128]{1,0:T(8,128)}, f32[96,128]{1,0:T(8,128)S(1)}, u32[]{:S(2)}, u32[]{:S(2)}) collective-permute-start(f32[96,128]{1,0:T(8,128)} %get-tuple-element.32), channel_id=1, source_target_pairs={{0,128},{64,192},{128,0},{192,64},{1,129},{65,193},{129,1},{193,65... | collective-permute-start | bytes 147464 | tf_op jit(solution)/shard_map/ppermute | solution.py:262
  121.4 4.3 %collective-permute-start.35 = (f32[96,128]{1,0:T(8,128)}, f32[96,128]{1,0:T(8,128)S(1)}, u32[]{:S(2)}, u32[]{:S(2)}) collective-permute-start(f32[96,128]{1,0:T(8,128)} %get-tuple-element.33), channel_id=1, source_target_pairs={{0,192},{64,0},{128,64},{192,128},{1,193},{65,1},{129,65},{193,129... | collective-permute-start | bytes 147464 | tf_op jit(solution)/shard_map/ppermute | solution.py:262
  (6 other events, 4.3 us)
Sparse Core Ops, SparseCore 0:
  10.5 68.9 all-gather.2

commit v5 on v4

v5 whole, which is shorter than its diff:
```python
import jax
import jax.numpy as jnp
import numpy as np
from jax import lax
from jax.experimental import pallas as pl
from jax.experimental.pallas import tpu as pltpu
from jax.sharding import Mesh
from jax.sharding import PartitionSpec as P

EPSILON = 1e-06

NX, NZ, NC, NY = 4, 8, 2, 4
NDEV = NX * NZ * NC
PER = 2
ROWS = 256
RB = ROWS // NY
UNITS = 1536
QUARTER = UNITS // NY
SLOTS = 32
QROWS = QUARTER // 128 * SLOTS
LEFTS = NX * PER
BLOCK = 128
GROUP = 4
TILE = 256

VMEM = pl.BlockSpec(memory_space=pltpu.VMEM)
HBM = pl.BlockSpec(memory_space=pltpu.HBM)


def prepare(codes, scales):
    def kernel(codes_ref, scales_ref, acts_ref, slices_ref):
        column = [jnp.transpose(scales_ref[:, h, :]) for h in range(PER)]
        for k in range(UNITS // BLOCK):
            low = k * BLOCK
            both = []
            for h in range(PER):
                value = codes_ref[h, :, low : low + BLOCK].astype(jnp.float32)
                rounded = (value * column[h][:, k : k + 1]).astype(jnp.bfloat16)
                acts_ref[h, :, low : low + BLOCK] = rounded
                both.append(rounded.astype(jnp.float32))
            turned = jnp.transpose(jnp.concatenate(both, axis=0)).astype(jnp.bfloat16)
            first = low % QUARTER
            slices_ref[low // QUARTER, first : first + BLOCK, :] = turned

    return pl.pallas_call(
        kernel,
        in_specs=[VMEM, VMEM],
        out_specs=[VMEM] * 2,
        out_shape=[
            jax.ShapeDtypeStruct((PER, RB, UNITS), jnp.bfloat16),
            jax.ShapeDtypeStruct((NY, QUARTER, PER * RB), jnp.bfloat16),
        ],
        name="prepare",
    )(codes, scales)


def normalise(pieces):
    def kernel(in_ref, *out_refs):
        for k in range(QUARTER // 128):
            units = slice(k * 128, (k + 1) * 128)
            part = [in_ref[y, units, :].astype(jnp.float32) for y in range(NY)]
            for h in range(PER):
                lanes = slice(h * RB, (h + 1) * RB)
                full = jnp.concatenate([p[:, lanes] for p in part], axis=1)
                square = jnp.sum(full * full, axis=1, keepdims=True) / ROWS
                inverse = 1.0 / jnp.sqrt(square + EPSILON)
                out_refs[h][units, :] = (full * (inverse * (1.0 / ROWS))).astype(jnp.bfloat16)

    return pl.pallas_call(
        kernel,
        in_specs=[VMEM],
        out_specs=[VMEM] * PER,
        out_shape=[jax.ShapeDtypeStruct((QUARTER, ROWS), jnp.bfloat16)] * PER,
        name="normalise",
    )(pieces)


def correlate(start, order, jidx, lpos, rpos, gathered, chunks, places):
    count = len(chunks)

    def kernel(start_ref, order_ref, jidx_ref, lpos_ref, rpos_ref, gathered_ref, *refs):
        chunk_refs = refs[:count]
        left_refs = refs[count : count + NY]
        right_ref, left, acts, others, norms, sem = refs[count + NY :]
        loads = [
            pltpu.make_async_copy(ref, others.at[at], sem.at[n])
            for n, (ref, at) in enumerate(zip(chunk_refs, places))
        ]

        def rows_of(x, y):
            return pltpu.make_async_copy(
                gathered_ref.at[x * NY + y],
                acts.at[pl.ds(x * PER, PER), pl.ds(y * RB, RB), :],
                sem.at[count + x * NY + y],
            )

        for y in range(NY):
            rows_of(0, y).start()
        for load in loads:
            load.start()
        for x in range(1, NX):
            for y in range(NY):
                rows_of(x, y).start()
        right_ref[...] = jnp.zeros_like(right_ref)
        for load in loads:
            load.wait()

        def expert(i, carry):
            @pl.when(i % PER == 0)
            def _():
                for y in range(NY):
                    rows_of(i // PER, y).wait()

            for n in range(UNITS // TILE):
                lanes = slice(n * TILE, (n + 1) * TILE)
                value = acts[i, :, lanes].astype(jnp.float32)
                square = jnp.sum(value * value, axis=0, keepdims=True) / ROWS
                norms[:, lanes] = 1.0 / jnp.sqrt(square + EPSILON)
            low = start_ref[i]
            high = start_ref[i + 1]
            scales = norms[...]

            def block(first, size):
                pairs = [order_ref[first + g] for g in range(size)]
                lhs = jnp.concatenate([others[jidx_ref[p]] for p in pairs], axis=0)
                best = [None] * size
                for n in range(UNITS // TILE):
                    out = jnp.dot(
                        lhs,
                        acts[i, :, n * TILE : (n + 1) * TILE],
                        preferred_element_type=jnp.float32,
                    )
                    for g in range(size):
                        one = out[g * QUARTER : (g + 1) * QUARTER]
                        for m in range(TILE // 128):
                            unit = n * TILE + m * 128
                            scale = scales[:, unit : unit + 128]
                            part = one[:, m * 128 : (m + 1) * 128]
                            top = jnp.max(part, axis=0, keepdims=True) * scale
                            row = lpos_ref[unit // QUARTER, pairs[g]] + unit % QUARTER // 128 * SLOTS
                            left[pl.ds(row, 1), :] = top
                            scaled = part * scale
                            best[g] = scaled if best[g] is None else jnp.maximum(best[g], scaled)
                for g in range(size):
                    top = jnp.max(jnp.transpose(best[g]), axis=0, keepdims=True)
                    right_ref[pl.ds(rpos_ref[pairs[g]], 1), :] = top

            most = (high - low) // GROUP
            rest = (high - low) % GROUP
            two = rest // 2

            def step(b, carry):
                block(low + b * GROUP, GROUP)
                return carry

            lax.fori_loop(0, most, step, 0)

            @pl.when(two > 0)
            def _():
                block(low + most * GROUP, 2)

            @pl.when(rest % 2 > 0)
            def _():
                block(low + most * GROUP + 2 * two, 1)

            return carry

        lax.fori_loop(0, LEFTS, expert, 0)
        for k, ref in enumerate(left_refs):
            ref[...] = left[k * QROWS : (k + 1) * QROWS, :]

    return pl.pallas_call(
        kernel,
        grid_spec=pltpu.PrefetchScalarGridSpec(
            num_scalar_prefetch=5,
            grid=(1,),
            in_specs=[HBM] * (1 + count),
            out_specs=[VMEM] * (NY + 1),
            scratch_shapes=[
                pltpu.VMEM((NY * QROWS, 128), jnp.float32),
                pltpu.VMEM((LEFTS, ROWS, UNITS), jnp.bfloat16),
                pltpu.VMEM((NZ * NC * PER, QUARTER, ROWS), jnp.bfloat16),
                pltpu.VMEM((1, UNITS), jnp.float32),
                pltpu.SemaphoreType.DMA((count + NX * NY,)),
            ],
        ),
        out_shape=[jax.ShapeDtypeStruct((QROWS, 128), jnp.float32)] * NY
        + [jax.ShapeDtypeStruct((NZ * NC * NX, QUARTER), jnp.float32)],
        compiler_params=pltpu.CompilerParams(vmem_limit_bytes=24 << 20),
        name="correlate",
    )(start, order, jidx, lpos, rpos, gathered, *chunks)


def finish(rows, returned, choice, parts):
    def kernel(rows_ref, in_ref, choice_ref, *refs):
        part_refs, (left_ref, right_ref) = refs[:NX], refs[NX:]
        for s in range(SLOTS):
            right_ref[s : s + 1, :] = in_ref[pl.ds(rows_ref[s], 1), :]
        chosen = choice_ref[...]
        for t in range(QUARTER // 128):
            some = slice(t * SLOTS, (t + 1) * SLOTS)
            value = part_refs[0][some, :]
            for k in range(1, NX):
                value = jnp.where(chosen == k, part_refs[k][some, :], value)
            left_ref[:, t * 128 : (t + 1) * 128] = value

    return pl.pallas_call(
        kernel,
        grid_spec=pltpu.PrefetchScalarGridSpec(
            num_scalar_prefetch=1,
            grid=(1,),
            in_specs=[VMEM] * (2 + NX),
            out_specs=[VMEM] * 2,
        ),
        out_shape=[jax.ShapeDtypeStruct((SLOTS, QUARTER), jnp.float32)] * 2,
        name="finish",
    )(rows, returned, choice, *parts)


def meet(parts):
    def kernel(*refs):
        best = refs[0][...]
        for ref in refs[1:NY]:
            best = jnp.maximum(best, ref[...])
        refs[NY][...] = best

    return pl.pallas_call(
        kernel,
        in_specs=[VMEM] * NY,
        out_specs=VMEM,
        out_shape=jax.ShapeDtypeStruct((QROWS, 128), jnp.float32),
        name="meet",
    )(*parts)


def in_hbm(value):
    return pltpu.with_memory_space_constraint(value, pltpu.HBM)


def in_vmem(value):
    return pltpu.with_memory_space_constraint(value, pltpu.VMEM)


def shift(value, axis, by, size):
    return lax.ppermute(value, axis, [(i, (i + by) % size) for i in range(size)])


def swap(value):
    return lax.ppermute(value, "core", [(0, 1), (1, 0)])


def body(unit_codes, block_scales, pair_list):
    y = lax.axis_index("dp")
    x = lax.axis_index("x")
    z = lax.axis_index("z")
    c = lax.axis_index("core")
    me = (x * NZ + z) * NC + c

    table = pair_list.reshape(NX, NZ * NC, SLOTS, 2)
    group = lax.dynamic_index_in_dim(table, z * NC + c, 1, keepdims=False)
    group_x = group[:, :, 1] // (PER * NZ * NC)
    here = group_x == x
    mine = jnp.sum(jnp.where(here[:, :, None], group, 0), axis=0)
    pair = jnp.arange(SLOTS, dtype=jnp.int32)
    left_x = mine[:, 0] // (PER * NZ * NC)
    right_dev = mine[:, 1] // PER
    right_z = (right_dev // NC) % NZ
    right_c = right_dev % NC
    jidx = ((right_c != c) * NZ + (right_z - z) % NZ) * PER + mine[:, 1] % PER
    key = left_x * PER + mine[:, 0] % PER
    before = (key[None, :] < key[:, None]) | (
        (key[None, :] == key[:, None]) & (pair[None, :] < pair[:, None])
    )
    rank = jnp.sum(before, axis=1, dtype=jnp.int32)
    order = jnp.sum(jnp.where(rank[None, :] == pair[:, None], pair[None, :], 0), axis=1)
    start = jnp.sum(
        key[None, :] < jnp.arange(LEFTS + 1, dtype=jnp.int32)[:, None], axis=1, dtype=jnp.int32
    )
    quarter = jnp.arange(NY, dtype=jnp.int32)[:, None]
    lpos = pair[None, :] + (quarter - y) % NY * QROWS
    rpos = (right_z * NC + right_c) * NX + left_x
    own_x = lax.dynamic_index_in_dim(group_x, x, 0, keepdims=False)
    choice = jnp.broadcast_to(((x - own_x) % NX)[:, None], (SLOTS, 128))
    offsets = pair_list[:SLOTS, 1] // PER
    source = (me - offsets) % NDEV
    rows = (source % (NZ * NC)) * NX + source // (NZ * NC)

    acts, slices = prepare(unit_codes, jnp.transpose(block_scales, (1, 0, 2)))
    pieces = lax.all_to_all(slices, "dp", split_axis=0, concat_axis=0, tiled=True)
    gathered = in_hbm(lax.all_gather(acts, ("x", "dp"), axis=0, tiled=False))
    own = normalise(pieces)

    chunks, places = [], []

    def keep(value, rel, h):
        for other, part in enumerate((value, swap(value))):
            chunks.append(in_hbm(part))
            places.append((other * NZ + rel) * PER + h)

    up, down = list(own), list(own)
    for h in range(PER):
        keep(own[h], 0, h)
    for k in range(1, NZ // 2):
        for h in range(PER):
            up[h] = shift(up[h], "z", 1, NZ)
            down[h] = shift(down[h], "z", -1, NZ)
        for h in range(PER):
            keep(up[h], NZ - k, h)
            keep(down[h], k, h)
    keep(shift(up[0], "z", 1, NZ), NZ // 2, 0)
    keep(shift(down[1], "z", -1, NZ), NZ // 2, 1)

    order, rows, choice = lax.optimization_barrier((order, rows, choice))
    *left, right = correlate(start, order, jidx, lpos, rpos, gathered, chunks, places)
    returned = lax.all_to_all(
        right.reshape(NZ * NC, NX, QUARTER), ("z", "core"), split_axis=0, concat_axis=0, tiled=True
    )
    best = meet([left[0]] + [in_vmem(shift(left[k], "dp", k, NY)) for k in range(1, NY)])
    parts = [best] + [in_vmem(shift(best, "x", k, NX)) for k in range(1, NX)]
    returned = in_vmem(returned.reshape(NZ * NC * NX, QUARTER))
    left_out, right_out = finish(rows, returned, choice, parts)
    return (left_out[None], right_out[None])


def solution(mesh):
    fine = Mesh(np.asarray(mesh.devices).reshape(NY, NX, NZ, NC), ("dp", "x", "z", "core"))
    expert = ("x", "z", "core")
    in_specs = (P(expert, "dp", None), P(expert, None, "dp"), P())
    out_specs = (P(expert, None, "dp"), P(expert, None, "dp"))
    return jax.shard_map(body, mesh=fine, in_specs=in_specs, out_specs=out_specs, check_vma=False)
```

time: 137 us -> 134 us (0.978)
  waiting for transfers between devices: 36.3 us -> 41.8 us
  starting transfers between devices: 48.6 us -> 44.2 us
  Pallas kernels: 30.1 us -> 26.6 us
    ppermute x20, waiting for transfers between devices: 16.9 us -> 23.8 us  [shift(): lax.ppermute(value, axis, [(i, (i + by) % size) for i in range(size)])]
    all_to_all x2, waiting for transfers between devices: 11.9 us -> 7.13 us  [the longest x1 7.12 us: body(): lax.all_to_all(slices, 'dp', split_axis=0, concat_axis=0, tiled=True)]
    all_to_all x2, starting transfers between devices: 15.3 us -> 12 us  [the longest x1 7.57 us: body(): lax.all_to_all(right.reshape(NZ * NC, NX, QUARTER), ('z', 'core'), split_...]
    pallas_call x1, Pallas kernels: 21.4 us -> 18.1 us  [correlate(): pl.pallas_call(kernel, grid_spec=pltpu.PrefetchScalarGridSpec(num_scalar_...]
    all_gather x1, waiting for transfers between devices: 6.99 us -> 9.99 us  [body(): gathered = in_hbm(lax.all_gather(acts, ('x', 'dp'), axis=0, tiled=False))]
    ppermute x20, starting transfers between devices: 31 us -> 29.5 us  [shift(): lax.ppermute(value, axis, [(i, (i + by) % size) for i in range(size)])]
  transfers between devices with their start and end apart: 39 -> 39, of which waited for: 15 -> 17; matrix products, arithmetic and copies ran while one was open for 2% -> 2% of each run, Pallas kernels for 3% -> 3%
where the time goes in v5:
time: 134 us; the launch traced here: 133 us
  starting transfers between devices  44.2 us (33%)
  waiting for transfers between devices  41.8 us (31%)
  Pallas kernels  26.6 us (20%)
  between operations  14.4 us (11%)
  local copies, waits for them, and re-layouts  4.33 us (3%)
  other arithmetic  1.78 us (1%)
    ppermute x20, starting transfers between devices, shift(): lax.ppermute(value, axis, [(i, (i + by) % size) for i in range(size)])  29.5 us
    ppermute x20, waiting for transfers between devices, shift(): lax.ppermute(value, axis, [(i, (i + by) % size) for i in range(size)])  23.8 us
    pallas_call x1, Pallas kernels, correlate(): pl.pallas_call(kernel, grid_spec=pltpu.PrefetchScalarGridSpec(num_scalar_...  18.1 us
    all_gather x1, waiting for transfers between devices, body(): gathered = in_hbm(lax.all_gather(acts, ('x', 'dp'), axis=0, tiled=False))  9.99 us
    all_to_all x1, starting transfers between devices, body(): lax.all_to_all(right.reshape(NZ * NC, NX, QUARTER), ('z', 'core'), split_...  7.57 us
    all_to_all x1, waiting for transfers between devices, body(): lax.all_to_all(slices, 'dp', split_axis=0, concat_axis=0, tiled=True)  7.12 us
    all_to_all x1, starting transfers between devices, body(): lax.all_to_all(slices, 'dp', split_axis=0, concat_axis=0, tiled=True)  4.48 us
  transfers between devices with their start and end apart: 39, of which 17 were waited for; matrix products, arithmetic and copies ran while one was open for 2% of the time, Pallas kernels for 3%

profile of v5, /device:TPU:32, one launch (start us, length us, event | category | flops | bytes accessed | tf_op | source)
XLA Modules:
  0.0 133.1 jit_solution(3552021971343165562)
XLA Ops:
  7.2 0.0 all-gather.3.cloned.1.call-start
  7.2 2.5 %prepare.1 = (bf16[2,64,1536]{2,1,0:T(8,128)(2,1)}, bf16[4,384,128]{2,1,0:T(8,128)(2,1)}) custom-call(bf16[2,64,1536]{2,1,0:T(8,128)(2,1)} %codes_ref.1, f32[12,2,64]{2,1,0:T(2,128)} %bitcast.71), custom_call_target="tpu_custom_call" | custom-call | tf_op jit(solution)/shard_map/prepare/pallas_call | solution.py:45
  9.7 0.0 all-gather.3.cloned.1.call-update
  9.7 4.5 %all-to-all-start = ((bf16[4,384,128]{2,1,0:T(8,128)(2,1)}), bf16[4,384,128]{2,1,0:T(8,128)(2,1)S(1)}, u32[]{:S(2)}, u32[]{:S(2)}) async-start(bf16[4,384,128]{2,1,0:T(8,128)(2,1)} %get-tuple-element.19), calls=%async_computation | async-start | bytes 786432 | tf_op jit(solution)/shard_map/all_to_all | solution.py:289
  14.2 0.8 reshape.106
  15.1 7.1 %all-to-all-done.in_ref = bf16[4,384,128]{2,1,0:T(8,128)(2,1)S(1)} async-done(((bf16[4,384,128]{2,1,0:T(8,128)(2,1)}), bf16[4,384,128]{2,1,0:T(8,128)(2,1)S(1)}, u32[]{:S(2)}, u32[]{:S(2)}) %all-to-all-start) | async-done | bytes 393248 | tf_op jit(solution)/shard_map/all_to_all | solution.py:289
  22.2 0.7 copy-done.1
  23.0 2.4 %normalise.1 = (bf16[384,256]{1,0:T(8,128)(2,1)}, bf16[384,256]{1,0:T(8,128)(2,1)}) custom-call(bf16[4,384,128]{2,1,0:T(8,128)(2,1)} %copy-done.1), custom_call_target="tpu_custom_call" | custom-call | tf_op jit(solution)/shard_map/normalise/pallas_call | solution.py:69
  25.4 0.1 collective-permute-start.4
  25.5 1.9 %collective-permute-start.2 = (bf16[384,256]{1,0:T(8,128)(2,1)}, bf16[384,256]{1,0:T(8,128)(2,1)S(1)}, u32[]{:S(2)}, u32[]{:S(2)}) collective-permute-start(bf16[384,256]{1,0:T(8,128)(2,1)} %get-tuple-element.20.refs_0_), channel_id=1, source_target_pairs={{0,2},{2,4},{4,6},{6,8},{8,10},{10,12},{12,14},{14,0},{1,3},{3,5},... | collective-permute-start | bytes 589832 | tf_op jit(solution)/shard_map/ppermute | solution.py:245
  27.4 4.0 %collective-permute-start.8 = (bf16[384,256]{1,0:T(8,128)(2,1)}, bf16[384,256]{1,0:T(8,128)(2,1)S(1)}, u32[]{:S(2)}, u32[]{:S(2)}) collective-permute-start(bf16[384,256]{1,0:T(8,128)(2,1)} %get-tuple-element.21.refs_2_), channel_id=1, source_target_pairs={{0,14},{2,0},{4,2},{6,4},{8,6},{10,8},{12,10},{14,12},{1,15},{3,1}... | collective-permute-start | bytes 589832 | tf_op jit(solution)/shard_map/ppermute | solution.py:245
  31.4 0.2 collective-permute-done.4.refs_6_
  31.5 0.2 collective-permute-start.1
  31.7 3.5 %collective-permute-done.2.refs_4_ = bf16[384,256]{1,0:T(8,128)(2,1)S(1)} collective-permute-done((bf16[384,256]{1,0:T(8,128)(2,1)}, bf16[384,256]{1,0:T(8,128)(2,1)S(1)}, u32[]{:S(2)}, u32[]{:S(2)}) %collective-permute-start.2) | collective-permute-done | bytes 196640 | tf_op jit(solution)/shard_map/ppermute | solution.py:245
  35.2 3.2 %collective-permute-start.12 = (bf16[384,256]{1,0:T(8,128)(2,1)S(1)}, bf16[384,256]{1,0:T(8,128)(2,1)S(1)}, u32[]{:S(2)}, u32[]{:S(2)}) collective-permute-start(bf16[384,256]{1,0:T(8,128)(2,1)S(1)} %collective-permute-done.4.refs_6_), channel_id=1, source_target_pairs={{0,14},{2,0},{4,2},{6,4},{8,6},{10,8},{12,10},{14,12},{1,15},{3,1}... | collective-permute-start | bytes 589832 | tf_op jit(solution)/shard_map/ppermute | solution.py:245
  38.5 0.1 collective-permute-start.10
  38.6 1.6 %collective-permute-done.6.refs_8_ = bf16[384,256]{1,0:T(8,128)(2,1)S(1)} collective-permute-done((bf16[384,256]{1,0:T(8,128)(2,1)}, bf16[384,256]{1,0:T(8,128)(2,1)S(1)}, u32[]{:S(2)}, u32[]{:S(2)}) %collective-permute-start.6) | collective-permute-done | bytes 196640 | tf_op jit(solution)/shard_map/ppermute | solution.py:245
  40.1 0.2 convert_reduce_fusion
  40.3 0.1 select_reduce_fusion.order_ref
  40.4 3.0 %collective-permute-start.16 = (bf16[384,256]{1,0:T(8,128)(2,1)S(1)}, bf16[384,256]{1,0:T(8,128)(2,1)S(1)}, u32[]{:S(2)}, u32[]{:S(2)}) collective-permute-start(bf16[384,256]{1,0:T(8,128)(2,1)S(1)} %collective-permute-done.8.refs_10_), channel_id=1, source_target_pairs={{0,14},{2,0},{4,2},{6,4},{8,6},{10,8},{12,10},{14,12},{1,15},{3,1}... | collective-permute-start | bytes 589832 | tf_op jit(solution)/shard_map/ppermute | solution.py:245
  43.4 0.2 collective-permute-start.9
  43.7 2.1 %collective-permute-done.10.refs_12_ = bf16[384,256]{1,0:T(8,128)(2,1)S(1)} collective-permute-done((bf16[384,256]{1,0:T(8,128)(2,1)S(1)}, bf16[384,256]{1,0:T(8,128)(2,1)S(1)}, u32[]{:S(2)}, u32[]{:S(2)}) %collective-permute-start.10) | collective-permute-done | bytes 196640 | tf_op jit(solution)/shard_map/ppermute | solution.py:245
  45.8 2.5 %collective-permute-start.20 = (bf16[384,256]{1,0:T(8,128)(2,1)S(1)}, bf16[384,256]{1,0:T(8,128)(2,1)S(1)}, u32[]{:S(2)}, u32[]{:S(2)}) collective-permute-start(bf16[384,256]{1,0:T(8,128)(2,1)S(1)} %collective-permute-done.12.refs_14_), channel_id=1, source_target_pairs={{0,14},{2,0},{4,2},{6,4},{8,6},{10,8},{12,10},{14,12},{1,15},{3,1}... | collective-permute-start | bytes 589832 | tf_op jit(solution)/shard_map/ppermute | solution.py:245
  48.3 0.4 collective-permute-start.13
  48.8 0.6 collective-permute-start.18
  49.4 1.4 %collective-permute-done.14.refs_16_ = bf16[384,256]{1,0:T(8,128)(2,1)S(1)} collective-permute-done((bf16[384,256]{1,0:T(8,128)(2,1)S(1)}, bf16[384,256]{1,0:T(8,128)(2,1)S(1)}, u32[]{:S(2)}, u32[]{:S(2)}) %collective-permute-start.14) | collective-permute-done | bytes 196640 | tf_op jit(solution)/shard_map/ppermute | solution.py:245
  50.8 2.4 %collective-permute-start.24 = (bf16[384,256]{1,0:T(8,128)(2,1)S(1)}, bf16[384,256]{1,0:T(8,128)(2,1)S(1)}, u32[]{:S(2)}, u32[]{:S(2)}) collective-permute-start(bf16[384,256]{1,0:T(8,128)(2,1)S(1)} %collective-permute-done.16.refs_18_), channel_id=1, source_target_pairs={{0,14},{2,0},{4,2},{6,4},{8,6},{10,8},{12,10},{14,12},{1,15},{3,1}... | collective-permute-start | bytes 589832 | tf_op jit(solution)/shard_map/ppermute | solution.py:245
  53.2 0.2 collective-permute-start.17
  53.4 1.2 and_select_fusion.7
  54.6 0.7 broadcast_in_dim.34.choice_ref
  55.2 0.1 collective-permute-start.22
  55.4 1.0 collective-permute-done.18.refs_20_
  56.4 0.5 collective-permute-start.21
  56.9 1.3 collective-permute-done.24.refs_26_
  58.1 1.1 collective-permute-start.26
  59.3 1.3 collective-permute-start.28
  60.6 0.1 convert_reduce_fusion.1.start_ref
  60.7 2.5 %collective-permute-done.22.refs_24_ = bf16[384,256]{1,0:T(8,128)(2,1)S(1)} collective-permute-done((bf16[384,256]{1,0:T(8,128)(2,1)S(1)}, bf16[384,256]{1,0:T(8,128)(2,1)S(1)}, u32[]{:S(2)}, u32[]{:S(2)}) %collective-permute-start.22) | collective-permute-done | bytes 196640 | tf_op jit(solution)/shard_map/ppermute | solution.py:245
  63.2 0.5 collective-permute-start.25
  63.7 0.1 collective-permute-start.23
  63.8 3.4 %collective-permute-done.26.refs_28_ = bf16[384,256]{1,0:T(8,128)(2,1)S(1)} collective-permute-done((bf16[384,256]{1,0:T(8,128)(2,1)S(1)}, bf16[384,256]{1,0:T(8,128)(2,1)S(1)}, u32[]{:S(2)}, u32[]{:S(2)}) %collective-permute-start.26) | collective-permute-done | bytes 196640 | tf_op jit(solution)/shard_map/ppermute | solution.py:245
  67.2 0.0 collective-permute-start.27
  67.2 0.5 collective-permute-start.29
  67.7 0.1 iota_add_fusion.lpos_ref
  67.9 0.8 collective-permute-done.27.refs_29_
  68.7 0.7 copy-done.30
  69.4 10.0 %all-gather.3.cloned.1.call-done = bf16[32,64,1536]{2,1,0:T(8,128)(2,1)} async-done(((bf16[2,64,1536]{2,1,0:T(8,128)(2,1)}), bf16[32,64,1536]{2,1,0:T(8,128)(2,1)}) %all-gather.3.cloned.1.call-update) | async-done | bytes 6291472 | tf_op jit(solution)/shard_map/all_gather | solution.py:290
  79.5 18.1 %correlate.1 = (f32[96,128]{1,0:T(8,128)S(1)}, f32[96,128]{1,0:T(8,128)S(1)}, f32[96,128]{1,0:T(8,128)S(1)}, f32[96,128]{1,0:T(8,128)S(1)}, f32[64,384]{1,0:T(8,128)S(1)}) custom-call(s32[9]{0:T(128)S(1)} %convert_reduce_fusion.1.start_ref, s32[32]{0:T(128)S(1)} %select_reduce_fusion.order_ref, s32[32]{0:T(128)S(1)} %get-tuple-element.34.jidx_ref, ...), custom_call_target="tpu_custom_call" | custom-call | tf_op jit(solution)/shard_map/correlate/pallas_call | solution.py:172
  97.7 0.6 copy-done
  98.3 0.7 reshape.107
  99.0 7.6 %all-to-all-start.1 = ((f32[16,4,384]{2,1,0:T(4,128)}), f32[16,4,384]{2,1,0:T(4,128)S(1)}, u32[]{:S(2)}, u32[]{:S(2)}) async-start(f32[16,4,384]{2,1,0:T(4,128)} %reshape.107), calls=%async_computation.1 | async-start | bytes 196608 | tf_op jit(solution)/shard_map/all_to_all | solution.py:315
  106.5 1.4 %collective-permute-start.30 = (f32[96,128]{1,0:T(8,128)S(1)}, f32[96,128]{1,0:T(8,128)S(1)}, u32[]{:S(2)}, u32[]{:S(2)}) collective-permute-start(f32[96,128]{1,0:T(8,128)S(1)} %get-tuple-element.25), channel_id=1, source_target_pairs={{0,64},{64,128},{128,192},{192,0},{1,65},{65,129},{129,193},{193,1... | collective-permute-start | bytes 147464 | tf_op jit(solution)/shard_map/ppermute | solution.py:245
  108.0 2.7 %collective-permute-start.31 = (f32[96,128]{1,0:T(8,128)S(1)}, f32[96,128]{1,0:T(8,128)S(1)}, u32[]{:S(2)}, u32[]{:S(2)}) collective-permute-start(f32[96,128]{1,0:T(8,128)S(1)} %get-tuple-element.26), channel_id=1, source_target_pairs={{0,128},{64,192},{128,0},{192,64},{1,129},{65,193},{129,1},{193,65... | collective-permute-start | bytes 147464 | tf_op jit(solution)/shard_map/ppermute | solution.py:245
  110.7 1.4 %collective-permute-start.32 = (f32[96,128]{1,0:T(8,128)S(1)}, f32[96,128]{1,0:T(8,128)S(1)}, u32[]{:S(2)}, u32[]{:S(2)}) collective-permute-start(f32[96,128]{1,0:T(8,128)S(1)} %get-tuple-element.27), channel_id=1, source_target_pairs={{0,192},{64,0},{128,64},{192,128},{1,193},{65,1},{129,65},{193,129... | collective-permute-start | bytes 147464 | tf_op jit(solution)/shard_map/ppermute | solution.py:245
  112.2 1.4 %collective-permute-done.31.refs_2_ = f32[96,128]{1,0:T(8,128)S(1)} collective-permute-done((f32[96,128]{1,0:T(8,128)S(1)}, f32[96,128]{1,0:T(8,128)S(1)}, u32[]{:S(2)}, u32[]{:S(2)}) %collective-permute-start.31) | collective-permute-done | bytes 49184 | tf_op jit(solution)/shard_map/ppermute | solution.py:245
  113.6 1.2 collective-permute-done.32.refs_3_
  114.8 1.4 %meet.1.refs_0_ = f32[96,128]{1,0:T(8,128)} custom-call(f32[96,128]{1,0:T(8,128)} %copy-done, f32[96,128]{1,0:T(8,128)S(1)} %collective-permute-done.30.refs_1_, f32[96,128]{1,0:T(8,128)S(1)} %collective-permute-done.31.refs_2_, f32[96,128]{1,0:T(8,128)S(1)} %collective-permute-done.32.refs_3_), custom_call_target="tpu_custom_call" | custom-call | tf_op jit(solution)/shard_map/meet/pallas_call | solution.py:227
  116.2 1.5 %collective-permute-start.35 = (f32[96,128]{1,0:T(8,128)}, f32[96,128]{1,0:T(8,128)S(1)}, u32[]{:S(2)}, u32[]{:S(2)}) collective-permute-start(f32[96,128]{1,0:T(8,128)} %meet.1.refs_0_), channel_id=1, source_target_pairs={{0,48},{16,0},{32,16},{48,32},{1,49},{17,1},{33,17},{49,33},{2,50}... | collective-permute-start | bytes 147464 | tf_op jit(solution)/shard_map/ppermute | solution.py:245
  117.7 0.7 collective-permute-start.34
  118.4 1.3 collective-permute-start.33
  119.7 0.8 collective-permute-done.35.refs_3_
  120.5 3.0 %collective-permute-done.34.refs_2_ = f32[96,128]{1,0:T(8,128)S(1)} collective-permute-done((f32[96,128]{1,0:T(8,128)}, f32[96,128]{1,0:T(8,128)S(1)}, u32[]{:S(2)}, u32[]{:S(2)}) %collective-permute-start.34) | collective-permute-done | bytes 49184 | tf_op jit(solution)/shard_map/ppermute | solution.py:245
  123.5 0.5 collective-permute-done.33.refs_1_
  124.1 2.2 %finish.1 = (f32[32,384]{1,0:T(8,128)}, f32[32,384]{1,0:T(8,128)}) custom-call(s32[32]{0:T(128)} %get-tuple-element.16.rows_ref, f32[64,384]{1,0:T(8,128)S(1)} %reshape.108.in_ref, s32[32,128]{1,0:T(8,128)} %broadcast_in_dim.34.choice_ref, f32[96,128]{1,0:T(8,128)} %meet.1.refs_0_, f32[96,128]{1,0:T(8,128)S(1)} %collective-permute-done.33.refs_1_, ...), custom_call_target="tpu_custom_call" | custom-call | tf_op jit(solution)/shard_map/finish/pallas_call | solution.py:207
  (99 shorter events, 0.4 us)
Async XLA Ops:
  7.2 72.2 %all-gather.3.cloned.1.call-start = ((), (), s32[]{:S(2)}) async-start(), calls=%async_computation.2 | async-start | bytes 6684672 | tf_op jit(solution)/shard_map/all_gather | solution.py:290
  9.7 12.5 %all-to-all-start = ((bf16[4,384,128]{2,1,0:T(8,128)(2,1)}), bf16[4,384,128]{2,1,0:T(8,128)(2,1)S(1)}, u32[]{:S(2)}, u32[]{:S(2)}) async-start(bf16[4,384,128]{2,1,0:T(8,128)(2,1)} %get-tuple-element.19), calls=%async_computation | async-start | bytes 786432 | tf_op jit(solution)/shard_map/all_to_all | solution.py:289
  25.4 6.2 %collective-permute-start.4 = (bf16[384,256]{1,0:T(8,128)(2,1)}, bf16[384,256]{1,0:T(8,128)(2,1)S(1)}, u32[]{:S(2)}, u32[]{:S(2)}) collective-permute-start(bf16[384,256]{1,0:T(8,128)(2,1)} %get-tuple-element.20.refs_0_), channel_id=1, source_target_pairs={{0,14},{2,0},{4,2},{6,4},{8,6},{10,8},{12,10},{14,12},{1,15},{3,1}... | collective-permute-start | bytes 589832 | tf_op jit(solution)/shard_map/ppermute | solution.py:245
  25.5 9.8 %collective-permute-start.2 = (bf16[384,256]{1,0:T(8,128)(2,1)}, bf16[384,256]{1,0:T(8,128)(2,1)S(1)}, u32[]{:S(2)}, u32[]{:S(2)}) collective-permute-start(bf16[384,256]{1,0:T(8,128)(2,1)} %get-tuple-element.20.refs_0_), channel_id=1, source_target_pairs={{0,2},{2,4},{4,6},{6,8},{8,10},{10,12},{12,14},{14,0},{1,3},{3,5},... | collective-permute-start | bytes 589832 | tf_op jit(solution)/shard_map/ppermute | solution.py:245
  27.4 11.1 %collective-permute-start = (bf16[384,256]{1,0:T(8,128)(2,1)}, bf16[384,256]{1,0:T(8,128)(2,1)S(1)}, u32[]{:S(2)}, u32[]{:S(2)}) collective-permute-start(bf16[384,256]{1,0:T(8,128)(2,1)} %get-tuple-element.20.refs_0_), channel_id=1, source_target_pairs={{0,1},{1,0},{2,3},{3,2},{4,5},{5,4},{6,7},{7,6},{8,9},{9,8},{10,11... | collective-permute-start | bytes 589832 | tf_op jit(solution)/shard_map/ppermute | solution.py:249
  27.4 11.1 %collective-permute-start.8 = (bf16[384,256]{1,0:T(8,128)(2,1)}, bf16[384,256]{1,0:T(8,128)(2,1)S(1)}, u32[]{:S(2)}, u32[]{:S(2)}) collective-permute-start(bf16[384,256]{1,0:T(8,128)(2,1)} %get-tuple-element.21.refs_2_), channel_id=1, source_target_pairs={{0,14},{2,0},{4,2},{6,4},{8,6},{10,8},{12,10},{14,12},{1,15},{3,1}... | collective-permute-start | bytes 589832 | tf_op jit(solution)/shard_map/ppermute | solution.py:245
  31.3 8.8 %collective-permute-start.6 = (bf16[384,256]{1,0:T(8,128)(2,1)}, bf16[384,256]{1,0:T(8,128)(2,1)S(1)}, u32[]{:S(2)}, u32[]{:S(2)}) collective-permute-start(bf16[384,256]{1,0:T(8,128)(2,1)} %get-tuple-element.21.refs_2_), channel_id=1, source_target_pairs={{0,2},{2,4},{4,6},{6,8},{8,10},{10,12},{12,14},{14,0},{1,3},{3,5},... | collective-permute-start | bytes 589832 | tf_op jit(solution)/shard_map/ppermute | solution.py:245
  31.5 47.9 %copy-start.2 = (bf16[384,256]{1,0:T(8,128)(2,1)}, bf16[384,256]{1,0:T(8,128)(2,1)S(1)}, u32[]{:S(2)}) copy-start(bf16[384,256]{1,0:T(8,128)(2,1)S(1)} %collective-permute-done.4.refs_6_) | copy-start | bytes 589828
  31.5 8.9 %collective-permute-start.1 = (bf16[384,256]{1,0:T(8,128)(2,1)}, bf16[384,256]{1,0:T(8,128)(2,1)S(1)}, u32[]{:S(2)}, u32[]{:S(2)}) collective-permute-start(bf16[384,256]{1,0:T(8,128)(2,1)} %get-tuple-element.21.refs_2_), channel_id=1, source_target_pairs={{0,1},{1,0},{2,3},{3,2},{4,5},{5,4},{6,7},{7,6},{8,9},{9,8},{10,11... | collective-permute-start | bytes 589832 | tf_op jit(solution)/shard_map/ppermute | solution.py:249
  35.2 44.2 %copy-start.3 = (bf16[384,256]{1,0:T(8,128)(2,1)}, bf16[384,256]{1,0:T(8,128)(2,1)S(1)}, u32[]{:S(2)}) copy-start(bf16[384,256]{1,0:T(8,128)(2,1)S(1)} %collective-permute-done.2.refs_4_) | copy-start | bytes 589828
  35.2 8.2 %collective-permute-start.12 = (bf16[384,256]{1,0:T(8,128)(2,1)S(1)}, bf16[384,256]{1,0:T(8,128)(2,1)S(1)}, u32[]{:S(2)}, u32[]{:S(2)}) collective-permute-start(bf16[384,256]{1,0:T(8,128)(2,1)S(1)} %collective-permute-done.4.refs_6_), channel_id=1, source_target_pairs={{0,14},{2,0},{4,2},{6,4},{8,6},{10,8},{12,10},{14,12},{1,15},{3,1}... | collective-permute-start | bytes 589832 | tf_op jit(solution)/shard_map/ppermute | solution.py:245
  38.4 41.0 %copy-start.4 = (bf16[384,256]{1,0:T(8,128)(2,1)}, bf16[384,256]{1,0:T(8,128)(2,1)S(1)}, u32[]{:S(2)}) copy-start(bf16[384,256]{1,0:T(8,128)(2,1)S(1)} %collective-permute-done.refs_1_) | copy-start | bytes 589828
  38.4 5.2 %collective-permute-start.5 = (bf16[384,256]{1,0:T(8,128)(2,1)S(1)}, bf16[384,256]{1,0:T(8,128)(2,1)S(1)}, u32[]{:S(2)}, u32[]{:S(2)}) collective-permute-start(bf16[384,256]{1,0:T(8,128)(2,1)S(1)} %collective-permute-done.4.refs_6_), channel_id=1, source_target_pairs={{0,1},{1,0},{2,3},{3,2},{4,5},{5,4},{6,7},{7,6},{8,9},{9,8},{10,11... | collective-permute-start | bytes 589832 | tf_op jit(solution)/shard_map/ppermute | solution.py:249
  38.5 40.9 %copy-start.5 = (bf16[384,256]{1,0:T(8,128)(2,1)}, bf16[384,256]{1,0:T(8,128)(2,1)S(1)}, u32[]{:S(2)}) copy-start(bf16[384,256]{1,0:T(8,128)(2,1)S(1)} %collective-permute-done.8.refs_10_) | copy-start | bytes 589828
  38.5 7.3 %collective-permute-start.10 = (bf16[384,256]{1,0:T(8,128)(2,1)S(1)}, bf16[384,256]{1,0:T(8,128)(2,1)S(1)}, u32[]{:S(2)}, u32[]{:S(2)}) collective-permute-start(bf16[384,256]{1,0:T(8,128)(2,1)S(1)} %collective-permute-done.2.refs_4_), channel_id=1, source_target_pairs={{0,2},{2,4},{4,6},{6,8},{8,10},{10,12},{12,14},{14,0},{1,3},{3,5},... | collective-permute-start | bytes 589832 | tf_op jit(solution)/shard_map/ppermute | solution.py:245
  40.1 39.3 %copy-start.6 = (bf16[384,256]{1,0:T(8,128)(2,1)}, bf16[384,256]{1,0:T(8,128)(2,1)S(1)}, u32[]{:S(2)}) copy-start(bf16[384,256]{1,0:T(8,128)(2,1)S(1)} %collective-permute-done.6.refs_8_) | copy-start | bytes 589828
  40.1 5.7 %collective-permute-start.3 = (bf16[384,256]{1,0:T(8,128)(2,1)S(1)}, bf16[384,256]{1,0:T(8,128)(2,1)S(1)}, u32[]{:S(2)}, u32[]{:S(2)}) collective-permute-start(bf16[384,256]{1,0:T(8,128)(2,1)S(1)} %collective-permute-done.2.refs_4_), channel_id=1, source_target_pairs={{0,1},{1,0},{2,3},{3,2},{4,5},{5,4},{6,7},{7,6},{8,9},{9,8},{10,11... | collective-permute-start | bytes 589832 | tf_op jit(solution)/shard_map/ppermute | solution.py:249
  40.4 39.0 %copy-start.7 = (bf16[384,256]{1,0:T(8,128)(2,1)}, bf16[384,256]{1,0:T(8,128)(2,1)S(1)}, u32[]{:S(2)}) copy-start(bf16[384,256]{1,0:T(8,128)(2,1)S(1)} %collective-permute-done.1.refs_3_) | copy-start | bytes 589828
  40.4 7.9 %collective-permute-start.16 = (bf16[384,256]{1,0:T(8,128)(2,1)S(1)}, bf16[384,256]{1,0:T(8,128)(2,1)S(1)}, u32[]{:S(2)}, u32[]{:S(2)}) collective-permute-start(bf16[384,256]{1,0:T(8,128)(2,1)S(1)} %collective-permute-done.8.refs_10_), channel_id=1, source_target_pairs={{0,14},{2,0},{4,2},{6,4},{8,6},{10,8},{12,10},{14,12},{1,15},{3,1}... | collective-permute-start | bytes 589832 | tf_op jit(solution)/shard_map/ppermute | solution.py:245
  43.4 36.0 %copy-start.8 = (bf16[384,256]{1,0:T(8,128)(2,1)}, bf16[384,256]{1,0:T(8,128)(2,1)S(1)}, u32[]{:S(2)}) copy-start(bf16[384,256]{1,0:T(8,128)(2,1)S(1)} %collective-permute-done.12.refs_14_) | copy-start | bytes 589828
  43.4 5.3 %collective-permute-start.9 = (bf16[384,256]{1,0:T(8,128)(2,1)S(1)}, bf16[384,256]{1,0:T(8,128)(2,1)S(1)}, u32[]{:S(2)}, u32[]{:S(2)}) collective-permute-start(bf16[384,256]{1,0:T(8,128)(2,1)S(1)} %collective-permute-done.8.refs_10_), channel_id=1, source_target_pairs={{0,1},{1,0},{2,3},{3,2},{4,5},{5,4},{6,7},{7,6},{8,9},{9,8},{10,11... | collective-permute-start | bytes 589832 | tf_op jit(solution)/shard_map/ppermute | solution.py:249
  43.7 35.8 %copy-start.9 = (bf16[384,256]{1,0:T(8,128)(2,1)}, bf16[384,256]{1,0:T(8,128)(2,1)S(1)}, u32[]{:S(2)}) copy-start(bf16[384,256]{1,0:T(8,128)(2,1)S(1)} %collective-permute-done.5.refs_7_) | copy-start | bytes 589828
  43.7 7.1 %collective-permute-start.14 = (bf16[384,256]{1,0:T(8,128)(2,1)S(1)}, bf16[384,256]{1,0:T(8,128)(2,1)S(1)}, u32[]{:S(2)}, u32[]{:S(2)}) collective-permute-start(bf16[384,256]{1,0:T(8,128)(2,1)S(1)} %collective-permute-done.6.refs_8_), channel_id=1, source_target_pairs={{0,2},{2,4},{4,6},{6,8},{8,10},{10,12},{12,14},{14,0},{1,3},{3,5},... | collective-permute-start | bytes 589832 | tf_op jit(solution)/shard_map/ppermute | solution.py:245
  45.8 33.7 %copy-start.10 = (bf16[384,256]{1,0:T(8,128)(2,1)}, bf16[384,256]{1,0:T(8,128)(2,1)S(1)}, u32[]{:S(2)}) copy-start(bf16[384,256]{1,0:T(8,128)(2,1)S(1)} %collective-permute-done.10.refs_12_) | copy-start | bytes 589828
  45.8 5.0 %collective-permute-start.7 = (bf16[384,256]{1,0:T(8,128)(2,1)S(1)}, bf16[384,256]{1,0:T(8,128)(2,1)S(1)}, u32[]{:S(2)}, u32[]{:S(2)}) collective-permute-start(bf16[384,256]{1,0:T(8,128)(2,1)S(1)} %collective-permute-done.6.refs_8_), channel_id=1, source_target_pairs={{0,1},{1,0},{2,3},{3,2},{4,5},{5,4},{6,7},{7,6},{8,9},{9,8},{10,11... | collective-permute-start | bytes 589832 | tf_op jit(solution)/shard_map/ppermute | solution.py:249
  45.8 33.7 %copy-start.11 = (bf16[384,256]{1,0:T(8,128)(2,1)}, bf16[384,256]{1,0:T(8,128)(2,1)S(1)}, u32[]{:S(2)}) copy-start(bf16[384,256]{1,0:T(8,128)(2,1)S(1)} %collective-permute-done.3.refs_5_) | copy-start | bytes 589828
  45.8 7.4 %collective-permute-start.20 = (bf16[384,256]{1,0:T(8,128)(2,1)S(1)}, bf16[384,256]{1,0:T(8,128)(2,1)S(1)}, u32[]{:S(2)}, u32[]{:S(2)}) collective-permute-start(bf16[384,256]{1,0:T(8,128)(2,1)S(1)} %collective-permute-done.12.refs_14_), channel_id=1, source_target_pairs={{0,14},{2,0},{4,2},{6,4},{8,6},{10,8},{12,10},{14,12},{1,15},{3,1}... | collective-permute-start | bytes 589832 | tf_op jit(solution)/shard_map/ppermute | solution.py:245
  48.3 31.1 %copy-start.12 = (bf16[384,256]{1,0:T(8,128)(2,1)}, bf16[384,256]{1,0:T(8,128)(2,1)S(1)}, u32[]{:S(2)}) copy-start(bf16[384,256]{1,0:T(8,128)(2,1)S(1)} %collective-permute-done.16.refs_18_) | copy-start | bytes 589828
  48.3 6.9 %collective-permute-start.13 = (bf16[384,256]{1,0:T(8,128)(2,1)S(1)}, bf16[384,256]{1,0:T(8,128)(2,1)S(1)}, u32[]{:S(2)}, u32[]{:S(2)}) collective-permute-start(bf16[384,256]{1,0:T(8,128)(2,1)S(1)} %collective-permute-done.12.refs_14_), channel_id=1, source_target_pairs={{0,1},{1,0},{2,3},{3,2},{4,5},{5,4},{6,7},{7,6},{8,9},{9,8},{10,11... | collective-permute-start | bytes 589832 | tf_op jit(solution)/shard_map/ppermute | solution.py:249
  48.8 30.7 %copy-start.13 = (bf16[384,256]{1,0:T(8,128)(2,1)}, bf16[384,256]{1,0:T(8,128)(2,1)S(1)}, u32[]{:S(2)}) copy-start(bf16[384,256]{1,0:T(8,128)(2,1)S(1)} %collective-permute-done.9.refs_11_) | copy-start | bytes 589828
  48.8 7.6 %collective-permute-start.18 = (bf16[384,256]{1,0:T(8,128)(2,1)S(1)}, bf16[384,256]{1,0:T(8,128)(2,1)S(1)}, u32[]{:S(2)}, u32[]{:S(2)}) collective-permute-start(bf16[384,256]{1,0:T(8,128)(2,1)S(1)} %collective-permute-done.10.refs_12_), channel_id=1, source_target_pairs={{0,2},{2,4},{4,6},{6,8},{8,10},{10,12},{12,14},{14,0},{1,3},{3,5},... | collective-permute-start | bytes 589832 | tf_op jit(solution)/shard_map/ppermute | solution.py:245
  50.8 28.7 %copy-start.14 = (bf16[384,256]{1,0:T(8,128)(2,1)}, bf16[384,256]{1,0:T(8,128)(2,1)S(1)}, u32[]{:S(2)}) copy-start(bf16[384,256]{1,0:T(8,128)(2,1)S(1)} %collective-permute-done.14.refs_16_) | copy-start | bytes 589828
  50.8 5.6 %collective-permute-start.11 = (bf16[384,256]{1,0:T(8,128)(2,1)S(1)}, bf16[384,256]{1,0:T(8,128)(2,1)S(1)}, u32[]{:S(2)}, u32[]{:S(2)}) collective-permute-start(bf16[384,256]{1,0:T(8,128)(2,1)S(1)} %collective-permute-done.10.refs_12_), channel_id=1, source_target_pairs={{0,1},{1,0},{2,3},{3,2},{4,5},{5,4},{6,7},{7,6},{8,9},{9,8},{10,11... | collective-permute-start | bytes 589832 | tf_op jit(solution)/shard_map/ppermute | solution.py:249
  50.8 28.7 %copy-start.15 = (bf16[384,256]{1,0:T(8,128)(2,1)}, bf16[384,256]{1,0:T(8,128)(2,1)S(1)}, u32[]{:S(2)}) copy-start(bf16[384,256]{1,0:T(8,128)(2,1)S(1)} %collective-permute-done.7.refs_9_) | copy-start | bytes 589828
  50.8 7.3 %collective-permute-start.24 = (bf16[384,256]{1,0:T(8,128)(2,1)S(1)}, bf16[384,256]{1,0:T(8,128)(2,1)S(1)}, u32[]{:S(2)}, u32[]{:S(2)}) collective-permute-start(bf16[384,256]{1,0:T(8,128)(2,1)S(1)} %collective-permute-done.16.refs_18_), channel_id=1, source_target_pairs={{0,14},{2,0},{4,2},{6,4},{8,6},{10,8},{12,10},{14,12},{1,15},{3,1}... | collective-permute-start | bytes 589832 | tf_op jit(solution)/shard_map/ppermute | solution.py:245
  53.2 26.3 %copy-start.16 = (bf16[384,256]{1,0:T(8,128)(2,1)}, bf16[384,256]{1,0:T(8,128)(2,1)S(1)}, u32[]{:S(2)}) copy-start(bf16[384,256]{1,0:T(8,128)(2,1)S(1)} %collective-permute-done.20.refs_22_) | copy-start | bytes 589828
  53.2 6.0 %collective-permute-start.17 = (bf16[384,256]{1,0:T(8,128)(2,1)S(1)}, bf16[384,256]{1,0:T(8,128)(2,1)S(1)}, u32[]{:S(2)}, u32[]{:S(2)}) collective-permute-start(bf16[384,256]{1,0:T(8,128)(2,1)S(1)} %collective-permute-done.16.refs_18_), channel_id=1, source_target_pairs={{0,1},{1,0},{2,3},{3,2},{4,5},{5,4},{6,7},{7,6},{8,9},{9,8},{10,11... | collective-permute-start | bytes 589832 | tf_op jit(solution)/shard_map/ppermute | solution.py:249
  55.2 24.3 %copy-start.17 = (bf16[384,256]{1,0:T(8,128)(2,1)}, bf16[384,256]{1,0:T(8,128)(2,1)S(1)}, u32[]{:S(2)}) copy-start(bf16[384,256]{1,0:T(8,128)(2,1)S(1)} %collective-permute-done.13.refs_15_) | copy-start | bytes 589828
  55.2 8.0 %collective-permute-start.22 = (bf16[384,256]{1,0:T(8,128)(2,1)S(1)}, bf16[384,256]{1,0:T(8,128)(2,1)S(1)}, u32[]{:S(2)}, u32[]{:S(2)}) collective-permute-start(bf16[384,256]{1,0:T(8,128)(2,1)S(1)} %collective-permute-done.14.refs_16_), channel_id=1, source_target_pairs={{0,2},{2,4},{4,6},{6,8},{8,10},{10,12},{12,14},{14,0},{1,3},{3,5},... | collective-permute-start | bytes 589832 | tf_op jit(solution)/shard_map/ppermute | solution.py:245
  56.3 23.0 %copy-start.18 = (bf16[384,256]{1,0:T(8,128)(2,1)}, bf16[384,256]{1,0:T(8,128)(2,1)S(1)}, u32[]{:S(2)}) copy-start(bf16[384,256]{1,0:T(8,128)(2,1)S(1)} %collective-permute-done.18.refs_20_) | copy-start | bytes 589828
  56.3 6.9 %collective-permute-start.15 = (bf16[384,256]{1,0:T(8,128)(2,1)S(1)}, bf16[384,256]{1,0:T(8,128)(2,1)S(1)}, u32[]{:S(2)}, u32[]{:S(2)}) collective-permute-start(bf16[384,256]{1,0:T(8,128)(2,1)S(1)} %collective-permute-done.14.refs_16_), channel_id=1, source_target_pairs={{0,1},{1,0},{2,3},{3,2},{4,5},{5,4},{6,7},{7,6},{8,9},{9,8},{10,11... | collective-permute-start | bytes 589832 | tf_op jit(solution)/shard_map/ppermute | solution.py:249
  56.3 11.5 %copy-start.19 = (bf16[384,256]{1,0:T(8,128)(2,1)}, bf16[384,256]{1,0:T(8,128)(2,1)S(1)}, u32[]{:S(2)}) copy-start(bf16[384,256]{1,0:T(8,128)(2,1)S(1)} %collective-permute-done.11.refs_13_) | copy-start | bytes 589828
  56.4 7.4 %collective-permute-start.21 = (bf16[384,256]{1,0:T(8,128)(2,1)S(1)}, bf16[384,256]{1,0:T(8,128)(2,1)S(1)}, u32[]{:S(2)}, u32[]{:S(2)}) collective-permute-start(bf16[384,256]{1,0:T(8,128)(2,1)S(1)} %collective-permute-done.20.refs_22_), channel_id=1, source_target_pairs={{0,1},{1,0},{2,3},{3,2},{4,5},{5,4},{6,7},{7,6},{8,9},{9,8},{10,11... | collective-permute-start | bytes 589832 | tf_op jit(solution)/shard_map/ppermute | solution.py:249
  58.1 9.7 %copy-start.20 = (bf16[384,256]{1,0:T(8,128)(2,1)}, bf16[384,256]{1,0:T(8,128)(2,1)S(1)}, u32[]{:S(2)}) copy-start(bf16[384,256]{1,0:T(8,128)(2,1)S(1)} %collective-permute-done.24.refs_26_) | copy-start | bytes 589828
  58.1 9.1 %collective-permute-start.26 = (bf16[384,256]{1,0:T(8,128)(2,1)S(1)}, bf16[384,256]{1,0:T(8,128)(2,1)S(1)}, u32[]{:S(2)}, u32[]{:S(2)}) collective-permute-start(bf16[384,256]{1,0:T(8,128)(2,1)S(1)} %collective-permute-done.18.refs_20_), channel_id=1, source_target_pairs={{0,2},{2,4},{4,6},{6,8},{8,10},{10,12},{12,14},{14,0},{1,3},{3,5},... | collective-permute-start | bytes 589832 | tf_op jit(solution)/shard_map/ppermute | solution.py:245
  59.3 8.6 %copy-start.21 = (bf16[384,256]{1,0:T(8,128)(2,1)}, bf16[384,256]{1,0:T(8,128)(2,1)S(1)}, u32[]{:S(2)}) copy-start(bf16[384,256]{1,0:T(8,128)(2,1)S(1)} %collective-permute-done.17.refs_19_) | copy-start | bytes 589828
  59.3 8.0 %collective-permute-start.28 = (bf16[384,256]{1,0:T(8,128)(2,1)S(1)}, bf16[384,256]{1,0:T(8,128)(2,1)S(1)}, u32[]{:S(2)}, u32[]{:S(2)}) collective-permute-start(bf16[384,256]{1,0:T(8,128)(2,1)S(1)} %collective-permute-done.24.refs_26_), channel_id=1, source_target_pairs={{0,14},{2,0},{4,2},{6,4},{8,6},{10,8},{12,10},{14,12},{1,15},{3,1}... | collective-permute-start | bytes 589832 | tf_op jit(solution)/shard_map/ppermute | solution.py:245
  63.2 5.5 %copy-start.22 = (bf16[384,256]{1,0:T(8,128)(2,1)}, bf16[384,256]{1,0:T(8,128)(2,1)S(1)}, u32[]{:S(2)}) copy-start(bf16[384,256]{1,0:T(8,128)(2,1)S(1)} %collective-permute-done.22.refs_24_) | copy-start | bytes 589828
  63.2 4.6 %collective-permute-start.19 = (bf16[384,256]{1,0:T(8,128)(2,1)S(1)}, bf16[384,256]{1,0:T(8,128)(2,1)S(1)}, u32[]{:S(2)}, u32[]{:S(2)}) collective-permute-start(bf16[384,256]{1,0:T(8,128)(2,1)S(1)} %collective-permute-done.18.refs_20_), channel_id=1, source_target_pairs={{0,1},{1,0},{2,3},{3,2},{4,5},{5,4},{6,7},{7,6},{8,9},{9,8},{10,11... | collective-permute-start | bytes 589832 | tf_op jit(solution)/shard_map/ppermute | solution.py:249
  63.2 5.4 %copy-start.23 = (bf16[384,256]{1,0:T(8,128)(2,1)}, bf16[384,256]{1,0:T(8,128)(2,1)S(1)}, u32[]{:S(2)}) copy-start(bf16[384,256]{1,0:T(8,128)(2,1)S(1)} %collective-permute-done.15.refs_17_) | copy-start | bytes 589828
  63.2 4.6 %collective-permute-start.25 = (bf16[384,256]{1,0:T(8,128)(2,1)S(1)}, bf16[384,256]{1,0:T(8,128)(2,1)S(1)}, u32[]{:S(2)}, u32[]{:S(2)}) collective-permute-start(bf16[384,256]{1,0:T(8,128)(2,1)S(1)} %collective-permute-done.24.refs_26_), channel_id=1, source_target_pairs={{0,1},{1,0},{2,3},{3,2},{4,5},{5,4},{6,7},{7,6},{8,9},{9,8},{10,11... | collective-permute-start | bytes 589832 | tf_op jit(solution)/shard_map/ppermute | solution.py:249
  63.7 4.9 %copy-start.24 = (bf16[384,256]{1,0:T(8,128)(2,1)}, bf16[384,256]{1,0:T(8,128)(2,1)S(1)}, u32[]{:S(2)}) copy-start(bf16[384,256]{1,0:T(8,128)(2,1)S(1)} %collective-permute-done.21.refs_23_) | copy-start | bytes 589828
  63.7 4.1 %collective-permute-start.23 = (bf16[384,256]{1,0:T(8,128)(2,1)S(1)}, bf16[384,256]{1,0:T(8,128)(2,1)S(1)}, u32[]{:S(2)}, u32[]{:S(2)}) collective-permute-start(bf16[384,256]{1,0:T(8,128)(2,1)S(1)} %collective-permute-done.22.refs_24_), channel_id=1, source_target_pairs={{0,1},{1,0},{2,3},{3,2},{4,5},{5,4},{6,7},{7,6},{8,9},{9,8},{10,11... | collective-permute-start | bytes 589832 | tf_op jit(solution)/shard_map/ppermute | solution.py:249
  67.2 1.5 %copy-start.25 = (bf16[384,256]{1,0:T(8,128)(2,1)}, bf16[384,256]{1,0:T(8,128)(2,1)S(1)}, u32[]{:S(2)}) copy-start(bf16[384,256]{1,0:T(8,128)(2,1)S(1)} %collective-permute-done.26.refs_28_) | copy-start | bytes 589828
  67.2 1.4 %collective-permute-start.27 = (bf16[384,256]{1,0:T(8,128)(2,1)S(1)}, bf16[384,256]{1,0:T(8,128)(2,1)S(1)}, u32[]{:S(2)}, u32[]{:S(2)}) collective-permute-start(bf16[384,256]{1,0:T(8,128)(2,1)S(1)} %collective-permute-done.26.refs_28_), channel_id=1, source_target_pairs={{0,1},{1,0},{2,3},{3,2},{4,5},{5,4},{6,7},{7,6},{8,9},{9,8},{10,11... | collective-permute-start | bytes 589832 | tf_op jit(solution)/shard_map/ppermute | solution.py:249
  67.2 1.4 %copy-start.26 = (bf16[384,256]{1,0:T(8,128)(2,1)}, bf16[384,256]{1,0:T(8,128)(2,1)S(1)}, u32[]{:S(2)}) copy-start(bf16[384,256]{1,0:T(8,128)(2,1)S(1)} %collective-permute-done.28.refs_30_) | copy-start | bytes 589828
  67.2 2.2 %collective-permute-start.29 = (bf16[384,256]{1,0:T(8,128)(2,1)S(1)}, bf16[384,256]{1,0:T(8,128)(2,1)}, u32[]{:S(2)}, u32[]{:S(2)}) collective-permute-start(bf16[384,256]{1,0:T(8,128)(2,1)S(1)} %collective-permute-done.28.refs_30_), channel_id=1, source_target_pairs={{0,1},{1,0},{2,3},{3,2},{4,5},{5,4},{6,7},{7,6},{8,9},{9,8},{10,11... | collective-permute-start | bytes 589832 | tf_op jit(solution)/shard_map/ppermute | solution.py:249
  99.0 20.7 %all-to-all-start.1 = ((f32[16,4,384]{2,1,0:T(4,128)}), f32[16,4,384]{2,1,0:T(4,128)S(1)}, u32[]{:S(2)}, u32[]{:S(2)}) async-start(f32[16,4,384]{2,1,0:T(4,128)} %reshape.107), calls=%async_computation.1 | async-start | bytes 196608 | tf_op jit(solution)/shard_map/all_to_all | solution.py:315
  106.5 5.6 %collective-permute-start.30 = (f32[96,128]{1,0:T(8,128)S(1)}, f32[96,128]{1,0:T(8,128)S(1)}, u32[]{:S(2)}, u32[]{:S(2)}) collective-permute-start(f32[96,128]{1,0:T(8,128)S(1)} %get-tuple-element.25), channel_id=1, source_target_pairs={{0,64},{64,128},{128,192},{192,0},{1,65},{65,129},{129,193},{193,1... | collective-permute-start | bytes 147464 | tf_op jit(solution)/shard_map/ppermute | solution.py:245
  108.0 5.6 %collective-permute-start.31 = (f32[96,128]{1,0:T(8,128)S(1)}, f32[96,128]{1,0:T(8,128)S(1)}, u32[]{:S(2)}, u32[]{:S(2)}) collective-permute-start(f32[96,128]{1,0:T(8,128)S(1)} %get-tuple-element.26), channel_id=1, source_target_pairs={{0,128},{64,192},{128,0},{192,64},{1,129},{65,193},{129,1},{193,65... | collective-permute-start | bytes 147464 | tf_op jit(solution)/shard_map/ppermute | solution.py:245
  110.7 4.1 %collective-permute-start.32 = (f32[96,128]{1,0:T(8,128)S(1)}, f32[96,128]{1,0:T(8,128)S(1)}, u32[]{:S(2)}, u32[]{:S(2)}) collective-permute-start(f32[96,128]{1,0:T(8,128)S(1)} %get-tuple-element.27), channel_id=1, source_target_pairs={{0,192},{64,0},{128,64},{192,128},{1,193},{65,1},{129,65},{193,129... | collective-permute-start | bytes 147464 | tf_op jit(solution)/shard_map/ppermute | solution.py:245
  116.2 4.3 %collective-permute-start.35 = (f32[96,128]{1,0:T(8,128)}, f32[96,128]{1,0:T(8,128)S(1)}, u32[]{:S(2)}, u32[]{:S(2)}) collective-permute-start(f32[96,128]{1,0:T(8,128)} %meet.1.refs_0_), channel_id=1, source_target_pairs={{0,48},{16,0},{32,16},{48,32},{1,49},{17,1},{33,17},{49,33},{2,50}... | collective-permute-start | bytes 147464 | tf_op jit(solution)/shard_map/ppermute | solution.py:245
  117.7 5.8 %collective-permute-start.34 = (f32[96,128]{1,0:T(8,128)}, f32[96,128]{1,0:T(8,128)S(1)}, u32[]{:S(2)}, u32[]{:S(2)}) collective-permute-start(f32[96,128]{1,0:T(8,128)} %meet.1.refs_0_), channel_id=1, source_target_pairs={{0,32},{16,48},{32,0},{48,16},{1,33},{17,49},{33,1},{49,17},{2,34}... | collective-permute-start | bytes 147464 | tf_op jit(solution)/shard_map/ppermute | solution.py:245
  118.4 5.6 %collective-permute-start.33 = (f32[96,128]{1,0:T(8,128)}, f32[96,128]{1,0:T(8,128)S(1)}, u32[]{:S(2)}, u32[]{:S(2)}) collective-permute-start(f32[96,128]{1,0:T(8,128)} %meet.1.refs_0_), channel_id=1, source_target_pairs={{0,16},{16,32},{32,48},{48,0},{1,17},{17,33},{33,49},{49,1},{2,18}... | collective-permute-start | bytes 147464 | tf_op jit(solution)/shard_map/ppermute | solution.py:245
  (6 other events, 4.7 us)
Sparse Core Ops, SparseCore 0:
  10.5 68.8 all-gather.2

commit v6 on v5

--- a/solution.py
+++ b/solution.py
@@ -17,6 +17,7 @@
 UNITS = 1536
 QUARTER = UNITS // NY
 SLOTS = 32
+RSTEP = 8
 QROWS = QUARTER // 128 * SLOTS
 LEFTS = NX * PER
 BLOCK = 128
@@ -28,30 +29,41 @@
 
 
 def prepare(codes, scales):
-    def kernel(codes_ref, scales_ref, acts_ref, slices_ref):
-        column = [jnp.transpose(scales_ref[:, h, :]) for h in range(PER)]
+    def kernel(codes_ref, scales_ref, acts_ref):
+        first = pl.program_id(0) == 0
+        column = jnp.transpose(jnp.where(first, scales_ref[:, 0, :], scales_ref[:, 1, :]))
+        for k in range(UNITS // BLOCK):
+            lanes = slice(k * BLOCK, (k + 1) * BLOCK)
+            value = codes_ref[0, :, lanes].astype(jnp.float32) * column[:, k : k + 1]
+            acts_ref[0, :, lanes] = value.astype(jnp.bfloat16)
+
+    one = pl.BlockSpec((1, RB, UNITS), lambda h: (h, 0, 0))
+    return pl.pallas_call(
+        kernel,
+        grid=(PER,),
+        in_specs=[one, pl.BlockSpec((UNITS // BLOCK, PER, RB), lambda h: (0, 0, 0))],
+        out_specs=one,
+        out_shape=jax.ShapeDtypeStruct((PER, RB, UNITS), jnp.bfloat16),
+        name="prepare",
+    )(codes, scales)
+
+
+def turn(acts):
+    def kernel(acts_ref, slices_ref):
         for k in range(UNITS // BLOCK):
             low = k * BLOCK
-            both = []
-            for h in range(PER):
-                value = codes_ref[h, :, low : low + BLOCK].astype(jnp.float32)
-                rounded = (value * column[h][:, k : k + 1]).astype(jnp.bfloat16)
-                acts_ref[h, :, low : low + BLOCK] = rounded
-                both.append(rounded.astype(jnp.float32))
+            both = [acts_ref[h, :, low : low + BLOCK].astype(jnp.float32) for h in range(PER)]
             turned = jnp.transpose(jnp.concatenate(both, axis=0)).astype(jnp.bfloat16)
             first = low % QUARTER
             slices_ref[low // QUARTER, first : first + BLOCK, :] = turned
 
     return pl.pallas_call(
         kernel,
-        in_specs=[VMEM, VMEM],
-        out_specs=[VMEM] * 2,
-        out_shape=[
-            jax.ShapeDtypeStruct((PER, RB, UNITS), jnp.bfloat16),
-            jax.ShapeDtypeStruct((NY, QUARTER, PER * RB), jnp.bfloat16),
-        ],
-        name="prepare",
-    )(codes, scales)
+        in_specs=[VMEM],
+        out_specs=VMEM,
+        out_shape=jax.ShapeDtypeStruct((NY, QUARTER, PER * RB), jnp.bfloat16),
+        name="turn",
+    )(acts)
 
 
 def normalise(pieces):
@@ -81,7 +93,7 @@
     def kernel(start_ref, order_ref, jidx_ref, lpos_ref, rpos_ref, gathered_ref, *refs):
         chunk_refs = refs[:count]
         left_refs = refs[count : count + NY]
-        right_ref, left, acts, others, norms, sem = refs[count + NY :]
+        right_out, right_ref, left, acts, others, norms, sem, out_sem = refs[count + NY :]
         loads = [
             pltpu.make_async_copy(ref, others.at[at], sem.at[n])
             for n, (ref, at) in enumerate(zip(chunk_refs, places))
@@ -102,23 +114,29 @@
             for y in range(NY):
                 rows_of(x, y).start()
         right_ref[...] = jnp.zeros_like(right_ref)
+
+        def norm(x):
+            for y in range(NY):
+                rows_of(x, y).wait()
+            for i in range(PER):
+                for n in range(UNITS // TILE):
+                    lanes = slice(n * TILE, (n + 1) * TILE)
+                    value = acts[x * PER + i, :, lanes].astype(jnp.float32)
+                    square = jnp.sum(value * value, axis=0, keepdims=True) / ROWS
+                    norms[pl.ds(x * PER + i, 1), lanes] = 1.0 / jnp.sqrt(square + EPSILON)
+
+        norm(0)
         for load in loads:
             load.wait()
 
         def expert(i, carry):
-            @pl.when(i % PER == 0)
+            @pl.when((i % PER == 0) & (i > 0))
             def _():
-                for y in range(NY):
-                    rows_of(i // PER, y).wait()
-
-            for n in range(UNITS // TILE):
-                lanes = slice(n * TILE, (n + 1) * TILE)
-                value = acts[i, :, lanes].astype(jnp.float32)
-                square = jnp.sum(value * value, axis=0, keepdims=True) / ROWS
-                norms[:, lanes] = 1.0 / jnp.sqrt(square + EPSILON)
+                norm(i // PER)
+
             low = start_ref[i]
             high = start_ref[i + 1]
-            scales = norms[...]
+            scales = norms[pl.ds(i, 1), :]
 
             def block(first, size):
                 pairs = [order_ref[first + g] for g in range(size)]
@@ -166,8 +184,15 @@
             return carry
 
         lax.fori_loop(0, LEFTS, expert, 0)
-        for k, ref in enumerate(left_refs):
-            ref[...] = left[k * QROWS : (k + 1) * QROWS, :]
+        stores = [pltpu.make_async_copy(right_ref, right_out, out_sem.at[0])]
+        for k in range(1, NY):
+            some = left.at[pl.ds(k * QROWS, QROWS), :]
+            stores.append(pltpu.make_async_copy(some, left_refs[k], out_sem.at[k]))
+        for store in stores:
+            store.start()
+        left_refs[0][...] = left[:QROWS, :]
+        for store in stores:
+            store.wait()
 
     return pl.pallas_call(
         kernel,
@@ -175,17 +200,19 @@
             num_scalar_prefetch=5,
             grid=(1,),
             in_specs=[HBM] * (1 + count),
-            out_specs=[VMEM] * (NY + 1),
+            out_specs=[VMEM] + [HBM] * NY,
             scratch_shapes=[
+                pltpu.VMEM((NZ * NC * RSTEP, QUARTER), jnp.float32),
                 pltpu.VMEM((NY * QROWS, 128), jnp.float32),
                 pltpu.VMEM((LEFTS, ROWS, UNITS), jnp.bfloat16),
                 pltpu.VMEM((NZ * NC * PER, QUARTER, ROWS), jnp.bfloat16),
-                pltpu.VMEM((1, UNITS), jnp.float32),
+                pltpu.VMEM((LEFTS, UNITS), jnp.float32),
                 pltpu.SemaphoreType.DMA((count + NX * NY,)),
+                pltpu.SemaphoreType.DMA((NY,)),
             ],
         ),
         out_shape=[jax.ShapeDtypeStruct((QROWS, 128), jnp.float32)] * NY
-        + [jax.ShapeDtypeStruct((NZ * NC * NX, QUARTER), jnp.float32)],
+        + [jax.ShapeDtypeStruct((NZ * NC * RSTEP, QUARTER), jnp.float32)],
         compiler_params=pltpu.CompilerParams(vmem_limit_bytes=24 << 20),
         name="correlate",
     )(start, order, jidx, lpos, rpos, gathered, *chunks)
@@ -278,14 +305,15 @@
     )
     quarter = jnp.arange(NY, dtype=jnp.int32)[:, None]
     lpos = pair[None, :] + (quarter - y) % NY * QROWS
-    rpos = (right_z * NC + right_c) * NX + left_x
+    rpos = (right_z * NC + right_c) * RSTEP + left_x
     own_x = lax.dynamic_index_in_dim(group_x, x, 0, keepdims=False)
     choice = jnp.broadcast_to(((x - own_x) % NX)[:, None], (SLOTS, 128))
     offsets = pair_list[:SLOTS, 1] // PER
     source = (me - offsets) % NDEV
-    rows = (source % (NZ * NC)) * NX + source // (NZ * NC)
-
-    acts, slices = prepare(unit_codes, jnp.transpose(block_scales, (1, 0, 2)))
+    rows = (source % (NZ * NC)) * RSTEP + source // (NZ * NC)
+
+    acts = prepare(unit_codes, jnp.transpose(block_scales, (1, 0, 2)))
+    slices = turn(acts)
     pieces = lax.all_to_all(slices, "dp", split_axis=0, concat_axis=0, tiled=True)
     gathered = in_hbm(lax.all_gather(acts, ("x", "dp"), axis=0, tiled=False))
     own = normalise(pieces)
@@ -313,11 +341,11 @@
     order, rows, choice = lax.optimization_barrier((order, rows, choice))
     *left, right = correlate(start, order, jidx, lpos, rpos, gathered, chunks, places)
     returned = lax.all_to_all(
-        right.reshape(NZ * NC, NX, QUARTER), ("z", "core"), split_axis=0, concat_axis=0, tiled=True
+        right.reshape(NZ * NC, RSTEP, QUARTER), ("z", "core"), split_axis=0, concat_axis=0, tiled=True
     )
     best = meet([left[0]] + [in_vmem(shift(left[k], "dp", k, NY)) for k in range(1, NY)])
     parts = [best] + [in_vmem(shift(best, "x", k, NX)) for k in range(1, NX)]
-    returned = in_vmem(returned.reshape(NZ * NC * NX, QUARTER))
+    returned = in_vmem(returned.reshape(NZ * NC * RSTEP, QUARTER))
     left_out, right_out = finish(rows, returned, choice, parts)
     return (left_out[None], right_out[None])
 

time: 134 us -> 134 us (level)
  Pallas kernels: 26.6 us -> 29 us
    pallas_call x1 -> x2, Pallas kernels: 2.46 us -> 4.13 us  [the longest x1 2.21 us: prepare(): pl.pallas_call(kernel, grid=(PER,), in_specs=[one, pl.BlockSpec((UNITS //...]
    all_gather x1, waiting for transfers between devices: 9.99 us -> 8.4 us  [body(): gathered = in_hbm(lax.all_gather(acts, ('x', 'dp'), axis=0, tiled=False))]
  transfers between devices with their start and end apart: 39 -> 39, of which waited for: 17 -> 18; matrix products, arithmetic and copies ran while one was open for 2% -> 3% of each run, Pallas kernels for 3% -> 4%
where the time goes in v6:
time: 134 us; the launch traced here: 133 us
  starting transfers between devices  43.2 us (32%)
  waiting for transfers between devices  41 us (31%)
  Pallas kernels  29 us (22%)
  between operations  14.4 us (11%)
  local copies, waits for them, and re-layouts  3.65 us (3%)
  other arithmetic  1.87 us (1%)
    ppermute x20, starting transfers between devices, shift(): lax.ppermute(value, axis, [(i, (i + by) % size) for i in range(size)])  29.1 us
    ppermute x20, waiting for transfers between devices, shift(): lax.ppermute(value, axis, [(i, (i + by) % size) for i in range(size)])  24.6 us
    pallas_call x1, Pallas kernels, correlate(): pl.pallas_call(kernel, grid_spec=pltpu.PrefetchScalarGridSpec(num_scalar_...  18.9 us
    all_gather x1, waiting for transfers between devices, body(): gathered = in_hbm(lax.all_gather(acts, ('x', 'dp'), axis=0, tiled=False))  8.4 us
    all_to_all x1, starting transfers between devices, body(): lax.all_to_all(right.reshape(NZ * NC, RSTEP, QUARTER), ('z', 'core'), spl...  7.26 us
    all_to_all x1, waiting for transfers between devices, body(): lax.all_to_all(slices, 'dp', split_axis=0, concat_axis=0, tiled=True)  7.12 us
    all_to_all x1, starting transfers between devices, body(): lax.all_to_all(slices, 'dp', split_axis=0, concat_axis=0, tiled=True)  4.46 us
  transfers between devices with their start and end apart: 39, of which 18 were waited for; matrix products, arithmetic and copies ran while one was open for 3% of the time, Pallas kernels for 4%

profile of v6, /device:TPU:32, one launch (start us, length us, event | category | flops | bytes accessed | tf_op | source)
XLA Modules:
  0.0 133.1 jit_solution(10176962014757464637)
XLA Ops:
  7.2 0.0 all-gather.3.cloned.1.call-start
  7.2 2.2 %prepare.1.acts_ref = bf16[2,64,1536]{2,1,0:T(8,128)(2,1)} custom-call(bf16[2,64,1536]{2,1,0:T(8,128)(2,1)} %codes_ref.1, f32[12,2,64]{2,1,0:T(2,128)} %bitcast.74), custom_call_target="tpu_custom_call" | custom-call | tf_op jit(solution)/shard_map/prepare/pallas_call | solution.py:41
  9.4 0.0 all-gather.3.cloned.1.call-update
  9.4 1.9 %turn.1 = bf16[4,384,128]{2,1,0:T(8,128)(2,1)} custom-call(bf16[2,64,1536]{2,1,0:T(8,128)(2,1)} %prepare.1.acts_ref), custom_call_target="tpu_custom_call" | custom-call | tf_op jit(solution)/shard_map/turn/pallas_call | solution.py:60
  11.4 4.5 %all-to-all-start = ((bf16[4,384,128]{2,1,0:T(8,128)(2,1)}), bf16[4,384,128]{2,1,0:T(8,128)(2,1)S(1)}, u32[]{:S(2)}, u32[]{:S(2)}) async-start(bf16[4,384,128]{2,1,0:T(8,128)(2,1)} %turn.1), calls=%async_computation | async-start | bytes 786432 | tf_op jit(solution)/shard_map/all_to_all | solution.py:317
  15.8 0.8 reshape.106
  16.8 7.1 %all-to-all-done.in_ref = bf16[4,384,128]{2,1,0:T(8,128)(2,1)S(1)} async-done(((bf16[4,384,128]{2,1,0:T(8,128)(2,1)}), bf16[4,384,128]{2,1,0:T(8,128)(2,1)S(1)}, u32[]{:S(2)}, u32[]{:S(2)}) %all-to-all-start) | async-done | bytes 393248 | tf_op jit(solution)/shard_map/all_to_all | solution.py:317
  23.9 0.8 copy-done.1
  24.7 2.4 %normalise.1 = (bf16[384,256]{1,0:T(8,128)(2,1)}, bf16[384,256]{1,0:T(8,128)(2,1)}) custom-call(bf16[4,384,128]{2,1,0:T(8,128)(2,1)} %copy-done.1), custom_call_target="tpu_custom_call" | custom-call | tf_op jit(solution)/shard_map/normalise/pallas_call | solution.py:81
  27.0 0.1 collective-permute-start.4
  27.2 1.9 %collective-permute-start.2 = (bf16[384,256]{1,0:T(8,128)(2,1)}, bf16[384,256]{1,0:T(8,128)(2,1)S(1)}, u32[]{:S(2)}, u32[]{:S(2)}) collective-permute-start(bf16[384,256]{1,0:T(8,128)(2,1)} %get-tuple-element.16.refs_0_), channel_id=1, source_target_pairs={{0,2},{2,4},{4,6},{6,8},{8,10},{10,12},{12,14},{14,0},{1,3},{3,5},... | collective-permute-start | bytes 589832 | tf_op jit(solution)/shard_map/ppermute | solution.py:272
  29.1 3.9 %collective-permute-start.8 = (bf16[384,256]{1,0:T(8,128)(2,1)}, bf16[384,256]{1,0:T(8,128)(2,1)S(1)}, u32[]{:S(2)}, u32[]{:S(2)}) collective-permute-start(bf16[384,256]{1,0:T(8,128)(2,1)} %get-tuple-element.17.refs_2_), channel_id=1, source_target_pairs={{0,14},{2,0},{4,2},{6,4},{8,6},{10,8},{12,10},{14,12},{1,15},{3,1}... | collective-permute-start | bytes 589832 | tf_op jit(solution)/shard_map/ppermute | solution.py:272
  33.0 0.2 collective-permute-done.4.refs_6_
  33.2 0.1 collective-permute-start.1
  33.3 3.5 %collective-permute-done.2.refs_4_ = bf16[384,256]{1,0:T(8,128)(2,1)S(1)} collective-permute-done((bf16[384,256]{1,0:T(8,128)(2,1)}, bf16[384,256]{1,0:T(8,128)(2,1)S(1)}, u32[]{:S(2)}, u32[]{:S(2)}) %collective-permute-start.2) | collective-permute-done | bytes 196640 | tf_op jit(solution)/shard_map/ppermute | solution.py:272
  36.9 3.2 %collective-permute-start.12 = (bf16[384,256]{1,0:T(8,128)(2,1)S(1)}, bf16[384,256]{1,0:T(8,128)(2,1)S(1)}, u32[]{:S(2)}, u32[]{:S(2)}) collective-permute-start(bf16[384,256]{1,0:T(8,128)(2,1)S(1)} %collective-permute-done.4.refs_6_), channel_id=1, source_target_pairs={{0,14},{2,0},{4,2},{6,4},{8,6},{10,8},{12,10},{14,12},{1,15},{3,1}... | collective-permute-start | bytes 589832 | tf_op jit(solution)/shard_map/ppermute | solution.py:272
  40.1 0.1 collective-permute-start.10
  40.2 1.6 %collective-permute-done.6.refs_8_ = bf16[384,256]{1,0:T(8,128)(2,1)S(1)} collective-permute-done((bf16[384,256]{1,0:T(8,128)(2,1)}, bf16[384,256]{1,0:T(8,128)(2,1)S(1)}, u32[]{:S(2)}, u32[]{:S(2)}) %collective-permute-start.6) | collective-permute-done | bytes 196640 | tf_op jit(solution)/shard_map/ppermute | solution.py:272
  41.8 0.2 convert_reduce_fusion
  42.0 0.1 select_reduce_fusion.order_ref
  42.1 3.0 %collective-permute-start.16 = (bf16[384,256]{1,0:T(8,128)(2,1)S(1)}, bf16[384,256]{1,0:T(8,128)(2,1)S(1)}, u32[]{:S(2)}, u32[]{:S(2)}) collective-permute-start(bf16[384,256]{1,0:T(8,128)(2,1)S(1)} %collective-permute-done.8.refs_10_), channel_id=1, source_target_pairs={{0,14},{2,0},{4,2},{6,4},{8,6},{10,8},{12,10},{14,12},{1,15},{3,1}... | collective-permute-start | bytes 589832 | tf_op jit(solution)/shard_map/ppermute | solution.py:272
  45.1 0.2 collective-permute-start.9
  45.3 2.1 %collective-permute-done.10.refs_12_ = bf16[384,256]{1,0:T(8,128)(2,1)S(1)} collective-permute-done((bf16[384,256]{1,0:T(8,128)(2,1)S(1)}, bf16[384,256]{1,0:T(8,128)(2,1)S(1)}, u32[]{:S(2)}, u32[]{:S(2)}) %collective-permute-start.10) | collective-permute-done | bytes 196640 | tf_op jit(solution)/shard_map/ppermute | solution.py:272
  47.5 2.4 %collective-permute-start.20 = (bf16[384,256]{1,0:T(8,128)(2,1)S(1)}, bf16[384,256]{1,0:T(8,128)(2,1)S(1)}, u32[]{:S(2)}, u32[]{:S(2)}) collective-permute-start(bf16[384,256]{1,0:T(8,128)(2,1)S(1)} %collective-permute-done.12.refs_14_), channel_id=1, source_target_pairs={{0,14},{2,0},{4,2},{6,4},{8,6},{10,8},{12,10},{14,12},{1,15},{3,1}... | collective-permute-start | bytes 589832 | tf_op jit(solution)/shard_map/ppermute | solution.py:272
  49.9 0.1 collective-permute-done.16.refs_18_
  49.9 0.2 collective-permute-start.13
  50.1 1.1 collective-permute-start.18
  51.3 1.1 collective-permute-done.14.refs_16_
  52.4 2.4 %collective-permute-start.24 = (bf16[384,256]{1,0:T(8,128)(2,1)S(1)}, bf16[384,256]{1,0:T(8,128)(2,1)S(1)}, u32[]{:S(2)}, u32[]{:S(2)}) collective-permute-start(bf16[384,256]{1,0:T(8,128)(2,1)S(1)} %collective-permute-done.16.refs_18_), channel_id=1, source_target_pairs={{0,14},{2,0},{4,2},{6,4},{8,6},{10,8},{12,10},{14,12},{1,15},{3,1}... | collective-permute-start | bytes 589832 | tf_op jit(solution)/shard_map/ppermute | solution.py:272
  54.9 0.2 collective-permute-start.17
  55.0 1.3 and_select_fusion.7
  56.3 0.7 broadcast_in_dim.34.choice_ref
  57.0 0.2 collective-permute-start.22
  57.2 0.8 collective-permute-done.18.refs_20_
  58.0 0.5 collective-permute-start.21
  58.5 1.3 collective-permute-done.24.refs_26_
  59.8 1.4 %collective-permute-start.26 = (bf16[384,256]{1,0:T(8,128)(2,1)S(1)}, bf16[384,256]{1,0:T(8,128)(2,1)S(1)}, u32[]{:S(2)}, u32[]{:S(2)}) collective-permute-start(bf16[384,256]{1,0:T(8,128)(2,1)S(1)} %collective-permute-done.18.refs_20_), channel_id=1, source_target_pairs={{0,2},{2,4},{4,6},{6,8},{8,10},{10,12},{12,14},{14,0},{1,3},{3,5},... | collective-permute-start | bytes 589832 | tf_op jit(solution)/shard_map/ppermute | solution.py:272
  61.1 1.1 collective-permute-start.28
  62.2 0.1 convert_reduce_fusion.1.start_ref
  62.3 2.5 %collective-permute-done.22.refs_24_ = bf16[384,256]{1,0:T(8,128)(2,1)S(1)} collective-permute-done((bf16[384,256]{1,0:T(8,128)(2,1)S(1)}, bf16[384,256]{1,0:T(8,128)(2,1)S(1)}, u32[]{:S(2)}, u32[]{:S(2)}) %collective-permute-start.22) | collective-permute-done | bytes 196640 | tf_op jit(solution)/shard_map/ppermute | solution.py:272
  64.9 0.5 collective-permute-start.25
  65.4 0.1 collective-permute-start.23
  65.5 3.4 %collective-permute-done.26.refs_28_ = bf16[384,256]{1,0:T(8,128)(2,1)S(1)} collective-permute-done((bf16[384,256]{1,0:T(8,128)(2,1)S(1)}, bf16[384,256]{1,0:T(8,128)(2,1)S(1)}, u32[]{:S(2)}, u32[]{:S(2)}) %collective-permute-start.26) | collective-permute-done | bytes 196640 | tf_op jit(solution)/shard_map/ppermute | solution.py:272
  68.9 0.5 collective-permute-start.29
  69.4 0.1 iota_add_fusion.lpos_ref
  69.5 0.8 collective-permute-done.27.refs_29_
  70.4 0.7 copy-done.30
  71.0 8.4 %all-gather.3.cloned.1.call-done = bf16[32,64,1536]{2,1,0:T(8,128)(2,1)} async-done(((bf16[2,64,1536]{2,1,0:T(8,128)(2,1)}), bf16[32,64,1536]{2,1,0:T(8,128)(2,1)}) %all-gather.3.cloned.1.call-update) | async-done | bytes 6291472 | tf_op jit(solution)/shard_map/all_gather | solution.py:318
  79.6 18.9 %correlate.1 = (f32[96,128]{1,0:T(8,128)S(1)}, f32[96,128]{1,0:T(8,128)S(1)}, f32[96,128]{1,0:T(8,128)S(1)}, f32[96,128]{1,0:T(8,128)S(1)}, f32[128,384]{1,0:T(8,128)}) custom-call(s32[9]{0:T(128)S(1)} %convert_reduce_fusion.1.start_ref, s32[32]{0:T(128)S(1)} %select_reduce_fusion.order_ref, s32[32]{0:T(128)S(1)} %get-tuple-element.30.jidx_ref, ...), custom_call_target="tpu_custom_call" | custom-call | tf_op jit(solution)/shard_map/correlate/pallas_call | solution.py:197
  98.5 0.6 copy-done
  99.1 7.3 %all-to-all-start.1 = ((f32[16,8,384]{2,1,0:T(8,128)}), f32[16,8,384]{2,1,0:T(8,128)S(1)}, u32[]{:S(2)}, u32[]{:S(2)}) async-start(f32[16,8,384]{2,1,0:T(8,128)} %bitcast.10), calls=%async_computation.1 | async-start | bytes 393216 | tf_op jit(solution)/shard_map/all_to_all | solution.py:343
  106.4 1.4 %collective-permute-start.30 = (f32[96,128]{1,0:T(8,128)S(1)}, f32[96,128]{1,0:T(8,128)S(1)}, u32[]{:S(2)}, u32[]{:S(2)}) collective-permute-start(f32[96,128]{1,0:T(8,128)S(1)} %get-tuple-element.21), channel_id=1, source_target_pairs={{0,64},{64,128},{128,192},{192,0},{1,65},{65,129},{129,193},{193,1... | collective-permute-start | bytes 147464 | tf_op jit(solution)/shard_map/ppermute | solution.py:272
  107.8 2.7 %collective-permute-start.31 = (f32[96,128]{1,0:T(8,128)S(1)}, f32[96,128]{1,0:T(8,128)S(1)}, u32[]{:S(2)}, u32[]{:S(2)}) collective-permute-start(f32[96,128]{1,0:T(8,128)S(1)} %get-tuple-element.22), channel_id=1, source_target_pairs={{0,128},{64,192},{128,0},{192,64},{1,129},{65,193},{129,1},{193,65... | collective-permute-start | bytes 147464 | tf_op jit(solution)/shard_map/ppermute | solution.py:272
  110.5 1.4 %collective-permute-start.32 = (f32[96,128]{1,0:T(8,128)S(1)}, f32[96,128]{1,0:T(8,128)S(1)}, u32[]{:S(2)}, u32[]{:S(2)}) collective-permute-start(f32[96,128]{1,0:T(8,128)S(1)} %get-tuple-element.23), channel_id=1, source_target_pairs={{0,192},{64,0},{128,64},{192,128},{1,193},{65,1},{129,65},{193,129... | collective-permute-start | bytes 147464 | tf_op jit(solution)/shard_map/ppermute | solution.py:272
  112.0 1.4 %collective-permute-done.31.refs_2_ = f32[96,128]{1,0:T(8,128)S(1)} collective-permute-done((f32[96,128]{1,0:T(8,128)S(1)}, f32[96,128]{1,0:T(8,128)S(1)}, u32[]{:S(2)}, u32[]{:S(2)}) %collective-permute-start.31) | collective-permute-done | bytes 49184 | tf_op jit(solution)/shard_map/ppermute | solution.py:272
  113.4 1.2 collective-permute-done.32.refs_3_
  114.6 1.4 %meet.1.refs_0_ = f32[96,128]{1,0:T(8,128)} custom-call(f32[96,128]{1,0:T(8,128)} %copy-done, f32[96,128]{1,0:T(8,128)S(1)} %collective-permute-done.30.refs_1_, f32[96,128]{1,0:T(8,128)S(1)} %collective-permute-done.31.refs_2_, f32[96,128]{1,0:T(8,128)S(1)} %collective-permute-done.32.refs_3_), custom_call_target="tpu_custom_call" | custom-call | tf_op jit(solution)/shard_map/meet/pallas_call | solution.py:254
  116.0 0.9 collective-permute-start.35
  116.9 1.6 %collective-permute-start.34 = (f32[96,128]{1,0:T(8,128)}, f32[96,128]{1,0:T(8,128)S(1)}, u32[]{:S(2)}, u32[]{:S(2)}) collective-permute-start(f32[96,128]{1,0:T(8,128)} %meet.1.refs_0_), channel_id=1, source_target_pairs={{0,32},{16,48},{32,0},{48,16},{1,33},{17,49},{33,1},{49,17},{2,34}... | collective-permute-start | bytes 147464 | tf_op jit(solution)/shard_map/ppermute | solution.py:272
  118.6 0.1 collective-permute-start.33
  118.7 1.6 %collective-permute-done.35.refs_3_ = f32[96,128]{1,0:T(8,128)S(1)} collective-permute-done((f32[96,128]{1,0:T(8,128)}, f32[96,128]{1,0:T(8,128)S(1)}, u32[]{:S(2)}, u32[]{:S(2)}) %collective-permute-start.35) | collective-permute-done | bytes 49184 | tf_op jit(solution)/shard_map/ppermute | solution.py:272
  120.3 2.4 %collective-permute-done.34.refs_2_ = f32[96,128]{1,0:T(8,128)S(1)} collective-permute-done((f32[96,128]{1,0:T(8,128)}, f32[96,128]{1,0:T(8,128)S(1)}, u32[]{:S(2)}, u32[]{:S(2)}) %collective-permute-start.34) | collective-permute-done | bytes 49184 | tf_op jit(solution)/shard_map/ppermute | solution.py:272
  122.7 1.4 %collective-permute-done.33.refs_1_ = f32[96,128]{1,0:T(8,128)S(1)} collective-permute-done((f32[96,128]{1,0:T(8,128)}, f32[96,128]{1,0:T(8,128)S(1)}, u32[]{:S(2)}, u32[]{:S(2)}) %collective-permute-start.33) | collective-permute-done | bytes 49184 | tf_op jit(solution)/shard_map/ppermute | solution.py:272
  124.1 2.2 %finish.1 = (f32[32,384]{1,0:T(8,128)}, f32[32,384]{1,0:T(8,128)}) custom-call(s32[32]{0:T(128)} %get-tuple-element.14.rows_ref, f32[128,384]{1,0:T(8,128)S(1)} %bitcast.69, s32[32,128]{1,0:T(8,128)} %broadcast_in_dim.34.choice_ref, f32[96,128]{1,0:T(8,128)} %meet.1.refs_0_, f32[96,128]{1,0:T(8,128)S(1)} %collective-permute-done.33.refs_1_, ...), custom_call_target="tpu_custom_call" | custom-call | tf_op jit(solution)/shard_map/finish/pallas_call | solution.py:234
  (98 shorter events, 0.3 us)
Async XLA Ops:
  7.2 72.3 %all-gather.3.cloned.1.call-start = ((), (), s32[]{:S(2)}) async-start(), calls=%async_computation.2 | async-start | bytes 6684672 | tf_op jit(solution)/shard_map/all_gather | solution.py:318
  11.4 12.5 %all-to-all-start = ((bf16[4,384,128]{2,1,0:T(8,128)(2,1)}), bf16[4,384,128]{2,1,0:T(8,128)(2,1)S(1)}, u32[]{:S(2)}, u32[]{:S(2)}) async-start(bf16[4,384,128]{2,1,0:T(8,128)(2,1)} %turn.1), calls=%async_computation | async-start | bytes 786432 | tf_op jit(solution)/shard_map/all_to_all | solution.py:317
  27.0 6.2 %collective-permute-start.4 = (bf16[384,256]{1,0:T(8,128)(2,1)}, bf16[384,256]{1,0:T(8,128)(2,1)S(1)}, u32[]{:S(2)}, u32[]{:S(2)}) collective-permute-start(bf16[384,256]{1,0:T(8,128)(2,1)} %get-tuple-element.16.refs_0_), channel_id=1, source_target_pairs={{0,14},{2,0},{4,2},{6,4},{8,6},{10,8},{12,10},{14,12},{1,15},{3,1}... | collective-permute-start | bytes 589832 | tf_op jit(solution)/shard_map/ppermute | solution.py:272
  27.2 9.7 %collective-permute-start.2 = (bf16[384,256]{1,0:T(8,128)(2,1)}, bf16[384,256]{1,0:T(8,128)(2,1)S(1)}, u32[]{:S(2)}, u32[]{:S(2)}) collective-permute-start(bf16[384,256]{1,0:T(8,128)(2,1)} %get-tuple-element.16.refs_0_), channel_id=1, source_target_pairs={{0,2},{2,4},{4,6},{6,8},{8,10},{10,12},{12,14},{14,0},{1,3},{3,5},... | collective-permute-start | bytes 589832 | tf_op jit(solution)/shard_map/ppermute | solution.py:272
  29.1 11.0 %collective-permute-start = (bf16[384,256]{1,0:T(8,128)(2,1)}, bf16[384,256]{1,0:T(8,128)(2,1)S(1)}, u32[]{:S(2)}, u32[]{:S(2)}) collective-permute-start(bf16[384,256]{1,0:T(8,128)(2,1)} %get-tuple-element.16.refs_0_), channel_id=1, source_target_pairs={{0,1},{1,0},{2,3},{3,2},{4,5},{5,4},{6,7},{7,6},{8,9},{9,8},{10,11... | collective-permute-start | bytes 589832 | tf_op jit(solution)/shard_map/ppermute | solution.py:276
  29.1 11.0 %collective-permute-start.8 = (bf16[384,256]{1,0:T(8,128)(2,1)}, bf16[384,256]{1,0:T(8,128)(2,1)S(1)}, u32[]{:S(2)}, u32[]{:S(2)}) collective-permute-start(bf16[384,256]{1,0:T(8,128)(2,1)} %get-tuple-element.17.refs_2_), channel_id=1, source_target_pairs={{0,14},{2,0},{4,2},{6,4},{8,6},{10,8},{12,10},{14,12},{1,15},{3,1}... | collective-permute-start | bytes 589832 | tf_op jit(solution)/shard_map/ppermute | solution.py:272
  33.0 8.8 %collective-permute-start.6 = (bf16[384,256]{1,0:T(8,128)(2,1)}, bf16[384,256]{1,0:T(8,128)(2,1)S(1)}, u32[]{:S(2)}, u32[]{:S(2)}) collective-permute-start(bf16[384,256]{1,0:T(8,128)(2,1)} %get-tuple-element.17.refs_2_), channel_id=1, source_target_pairs={{0,2},{2,4},{4,6},{6,8},{8,10},{10,12},{12,14},{14,0},{1,3},{3,5},... | collective-permute-start | bytes 589832 | tf_op jit(solution)/shard_map/ppermute | solution.py:272
  33.2 46.2 %copy-start.2 = (bf16[384,256]{1,0:T(8,128)(2,1)}, bf16[384,256]{1,0:T(8,128)(2,1)S(1)}, u32[]{:S(2)}) copy-start(bf16[384,256]{1,0:T(8,128)(2,1)S(1)} %collective-permute-done.4.refs_6_) | copy-start | bytes 589828
  33.2 8.9 %collective-permute-start.1 = (bf16[384,256]{1,0:T(8,128)(2,1)}, bf16[384,256]{1,0:T(8,128)(2,1)S(1)}, u32[]{:S(2)}, u32[]{:S(2)}) collective-permute-start(bf16[384,256]{1,0:T(8,128)(2,1)} %get-tuple-element.17.refs_2_), channel_id=1, source_target_pairs={{0,1},{1,0},{2,3},{3,2},{4,5},{5,4},{6,7},{7,6},{8,9},{9,8},{10,11... | collective-permute-start | bytes 589832 | tf_op jit(solution)/shard_map/ppermute | solution.py:276
  36.9 42.6 %copy-start.3 = (bf16[384,256]{1,0:T(8,128)(2,1)}, bf16[384,256]{1,0:T(8,128)(2,1)S(1)}, u32[]{:S(2)}) copy-start(bf16[384,256]{1,0:T(8,128)(2,1)S(1)} %collective-permute-done.2.refs_4_) | copy-start | bytes 589828
  36.9 8.2 %collective-permute-start.12 = (bf16[384,256]{1,0:T(8,128)(2,1)S(1)}, bf16[384,256]{1,0:T(8,128)(2,1)S(1)}, u32[]{:S(2)}, u32[]{:S(2)}) collective-permute-start(bf16[384,256]{1,0:T(8,128)(2,1)S(1)} %collective-permute-done.4.refs_6_), channel_id=1, source_target_pairs={{0,14},{2,0},{4,2},{6,4},{8,6},{10,8},{12,10},{14,12},{1,15},{3,1}... | collective-permute-start | bytes 589832 | tf_op jit(solution)/shard_map/ppermute | solution.py:272
  40.1 39.4 %copy-start.4 = (bf16[384,256]{1,0:T(8,128)(2,1)}, bf16[384,256]{1,0:T(8,128)(2,1)S(1)}, u32[]{:S(2)}) copy-start(bf16[384,256]{1,0:T(8,128)(2,1)S(1)} %collective-permute-done.refs_1_) | copy-start | bytes 589828
  40.1 5.2 %collective-permute-start.5 = (bf16[384,256]{1,0:T(8,128)(2,1)S(1)}, bf16[384,256]{1,0:T(8,128)(2,1)S(1)}, u32[]{:S(2)}, u32[]{:S(2)}) collective-permute-start(bf16[384,256]{1,0:T(8,128)(2,1)S(1)} %collective-permute-done.4.refs_6_), channel_id=1, source_target_pairs={{0,1},{1,0},{2,3},{3,2},{4,5},{5,4},{6,7},{7,6},{8,9},{9,8},{10,11... | collective-permute-start | bytes 589832 | tf_op jit(solution)/shard_map/ppermute | solution.py:276
  40.1 39.4 %copy-start.5 = (bf16[384,256]{1,0:T(8,128)(2,1)}, bf16[384,256]{1,0:T(8,128)(2,1)S(1)}, u32[]{:S(2)}) copy-start(bf16[384,256]{1,0:T(8,128)(2,1)S(1)} %collective-permute-done.8.refs_10_) | copy-start | bytes 589828
  40.1 7.3 %collective-permute-start.10 = (bf16[384,256]{1,0:T(8,128)(2,1)S(1)}, bf16[384,256]{1,0:T(8,128)(2,1)S(1)}, u32[]{:S(2)}, u32[]{:S(2)}) collective-permute-start(bf16[384,256]{1,0:T(8,128)(2,1)S(1)} %collective-permute-done.2.refs_4_), channel_id=1, source_target_pairs={{0,2},{2,4},{4,6},{6,8},{8,10},{10,12},{12,14},{14,0},{1,3},{3,5},... | collective-permute-start | bytes 589832 | tf_op jit(solution)/shard_map/ppermute | solution.py:272
  41.8 37.7 %copy-start.6 = (bf16[384,256]{1,0:T(8,128)(2,1)}, bf16[384,256]{1,0:T(8,128)(2,1)S(1)}, u32[]{:S(2)}) copy-start(bf16[384,256]{1,0:T(8,128)(2,1)S(1)} %collective-permute-done.6.refs_8_) | copy-start | bytes 589828
  41.8 5.7 %collective-permute-start.3 = (bf16[384,256]{1,0:T(8,128)(2,1)S(1)}, bf16[384,256]{1,0:T(8,128)(2,1)S(1)}, u32[]{:S(2)}, u32[]{:S(2)}) collective-permute-start(bf16[384,256]{1,0:T(8,128)(2,1)S(1)} %collective-permute-done.2.refs_4_), channel_id=1, source_target_pairs={{0,1},{1,0},{2,3},{3,2},{4,5},{5,4},{6,7},{7,6},{8,9},{9,8},{10,11... | collective-permute-start | bytes 589832 | tf_op jit(solution)/shard_map/ppermute | solution.py:276
  42.1 37.4 %copy-start.7 = (bf16[384,256]{1,0:T(8,128)(2,1)}, bf16[384,256]{1,0:T(8,128)(2,1)S(1)}, u32[]{:S(2)}) copy-start(bf16[384,256]{1,0:T(8,128)(2,1)S(1)} %collective-permute-done.1.refs_3_) | copy-start | bytes 589828
  42.1 7.8 %collective-permute-start.16 = (bf16[384,256]{1,0:T(8,128)(2,1)S(1)}, bf16[384,256]{1,0:T(8,128)(2,1)S(1)}, u32[]{:S(2)}, u32[]{:S(2)}) collective-permute-start(bf16[384,256]{1,0:T(8,128)(2,1)S(1)} %collective-permute-done.8.refs_10_), channel_id=1, source_target_pairs={{0,14},{2,0},{4,2},{6,4},{8,6},{10,8},{12,10},{14,12},{1,15},{3,1}... | collective-permute-start | bytes 589832 | tf_op jit(solution)/shard_map/ppermute | solution.py:272
  45.1 34.4 %copy-start.8 = (bf16[384,256]{1,0:T(8,128)(2,1)}, bf16[384,256]{1,0:T(8,128)(2,1)S(1)}, u32[]{:S(2)}) copy-start(bf16[384,256]{1,0:T(8,128)(2,1)S(1)} %collective-permute-done.12.refs_14_) | copy-start | bytes 589828
  45.1 5.0 %collective-permute-start.9 = (bf16[384,256]{1,0:T(8,128)(2,1)S(1)}, bf16[384,256]{1,0:T(8,128)(2,1)S(1)}, u32[]{:S(2)}, u32[]{:S(2)}) collective-permute-start(bf16[384,256]{1,0:T(8,128)(2,1)S(1)} %collective-permute-done.8.refs_10_), channel_id=1, source_target_pairs={{0,1},{1,0},{2,3},{3,2},{4,5},{5,4},{6,7},{7,6},{8,9},{9,8},{10,11... | collective-permute-start | bytes 589832 | tf_op jit(solution)/shard_map/ppermute | solution.py:276
  45.3 34.2 %copy-start.9 = (bf16[384,256]{1,0:T(8,128)(2,1)}, bf16[384,256]{1,0:T(8,128)(2,1)S(1)}, u32[]{:S(2)}) copy-start(bf16[384,256]{1,0:T(8,128)(2,1)S(1)} %collective-permute-done.5.refs_7_) | copy-start | bytes 589828
  45.3 7.1 %collective-permute-start.14 = (bf16[384,256]{1,0:T(8,128)(2,1)S(1)}, bf16[384,256]{1,0:T(8,128)(2,1)S(1)}, u32[]{:S(2)}, u32[]{:S(2)}) collective-permute-start(bf16[384,256]{1,0:T(8,128)(2,1)S(1)} %collective-permute-done.6.refs_8_), channel_id=1, source_target_pairs={{0,2},{2,4},{4,6},{6,8},{8,10},{10,12},{12,14},{14,0},{1,3},{3,5},... | collective-permute-start | bytes 589832 | tf_op jit(solution)/shard_map/ppermute | solution.py:272
  47.4 32.1 %copy-start.10 = (bf16[384,256]{1,0:T(8,128)(2,1)}, bf16[384,256]{1,0:T(8,128)(2,1)S(1)}, u32[]{:S(2)}) copy-start(bf16[384,256]{1,0:T(8,128)(2,1)S(1)} %collective-permute-done.10.refs_12_) | copy-start | bytes 589828
  47.4 5.0 %collective-permute-start.7 = (bf16[384,256]{1,0:T(8,128)(2,1)S(1)}, bf16[384,256]{1,0:T(8,128)(2,1)S(1)}, u32[]{:S(2)}, u32[]{:S(2)}) collective-permute-start(bf16[384,256]{1,0:T(8,128)(2,1)S(1)} %collective-permute-done.6.refs_8_), channel_id=1, source_target_pairs={{0,1},{1,0},{2,3},{3,2},{4,5},{5,4},{6,7},{7,6},{8,9},{9,8},{10,11... | collective-permute-start | bytes 589832 | tf_op jit(solution)/shard_map/ppermute | solution.py:276
  47.4 32.1 %copy-start.11 = (bf16[384,256]{1,0:T(8,128)(2,1)}, bf16[384,256]{1,0:T(8,128)(2,1)S(1)}, u32[]{:S(2)}) copy-start(bf16[384,256]{1,0:T(8,128)(2,1)S(1)} %collective-permute-done.3.refs_5_) | copy-start | bytes 589828
  47.5 7.4 %collective-permute-start.20 = (bf16[384,256]{1,0:T(8,128)(2,1)S(1)}, bf16[384,256]{1,0:T(8,128)(2,1)S(1)}, u32[]{:S(2)}, u32[]{:S(2)}) collective-permute-start(bf16[384,256]{1,0:T(8,128)(2,1)S(1)} %collective-permute-done.12.refs_14_), channel_id=1, source_target_pairs={{0,14},{2,0},{4,2},{6,4},{8,6},{10,8},{12,10},{14,12},{1,15},{3,1}... | collective-permute-start | bytes 589832 | tf_op jit(solution)/shard_map/ppermute | solution.py:272
  49.9 29.6 %copy-start.12 = (bf16[384,256]{1,0:T(8,128)(2,1)}, bf16[384,256]{1,0:T(8,128)(2,1)S(1)}, u32[]{:S(2)}) copy-start(bf16[384,256]{1,0:T(8,128)(2,1)S(1)} %collective-permute-done.16.refs_18_) | copy-start | bytes 589828
  49.9 7.1 %collective-permute-start.13 = (bf16[384,256]{1,0:T(8,128)(2,1)S(1)}, bf16[384,256]{1,0:T(8,128)(2,1)S(1)}, u32[]{:S(2)}, u32[]{:S(2)}) collective-permute-start(bf16[384,256]{1,0:T(8,128)(2,1)S(1)} %collective-permute-done.12.refs_14_), channel_id=1, source_target_pairs={{0,1},{1,0},{2,3},{3,2},{4,5},{5,4},{6,7},{7,6},{8,9},{9,8},{10,11... | collective-permute-start | bytes 589832 | tf_op jit(solution)/shard_map/ppermute | solution.py:276
  50.1 29.4 %copy-start.13 = (bf16[384,256]{1,0:T(8,128)(2,1)}, bf16[384,256]{1,0:T(8,128)(2,1)S(1)}, u32[]{:S(2)}) copy-start(bf16[384,256]{1,0:T(8,128)(2,1)S(1)} %collective-permute-done.9.refs_11_) | copy-start | bytes 589828
  50.1 7.9 %collective-permute-start.18 = (bf16[384,256]{1,0:T(8,128)(2,1)S(1)}, bf16[384,256]{1,0:T(8,128)(2,1)S(1)}, u32[]{:S(2)}, u32[]{:S(2)}) collective-permute-start(bf16[384,256]{1,0:T(8,128)(2,1)S(1)} %collective-permute-done.10.refs_12_), channel_id=1, source_target_pairs={{0,2},{2,4},{4,6},{6,8},{8,10},{10,12},{12,14},{14,0},{1,3},{3,5},... | collective-permute-start | bytes 589832 | tf_op jit(solution)/shard_map/ppermute | solution.py:272
  52.4 27.1 %copy-start.14 = (bf16[384,256]{1,0:T(8,128)(2,1)}, bf16[384,256]{1,0:T(8,128)(2,1)S(1)}, u32[]{:S(2)}) copy-start(bf16[384,256]{1,0:T(8,128)(2,1)S(1)} %collective-permute-done.14.refs_16_) | copy-start | bytes 589828
  52.4 5.6 %collective-permute-start.11 = (bf16[384,256]{1,0:T(8,128)(2,1)S(1)}, bf16[384,256]{1,0:T(8,128)(2,1)S(1)}, u32[]{:S(2)}, u32[]{:S(2)}) collective-permute-start(bf16[384,256]{1,0:T(8,128)(2,1)S(1)} %collective-permute-done.10.refs_12_), channel_id=1, source_target_pairs={{0,1},{1,0},{2,3},{3,2},{4,5},{5,4},{6,7},{7,6},{8,9},{9,8},{10,11... | collective-permute-start | bytes 589832 | tf_op jit(solution)/shard_map/ppermute | solution.py:276
  52.4 27.1 %copy-start.15 = (bf16[384,256]{1,0:T(8,128)(2,1)}, bf16[384,256]{1,0:T(8,128)(2,1)S(1)}, u32[]{:S(2)}) copy-start(bf16[384,256]{1,0:T(8,128)(2,1)S(1)} %collective-permute-done.7.refs_9_) | copy-start | bytes 589828
  52.4 7.3 %collective-permute-start.24 = (bf16[384,256]{1,0:T(8,128)(2,1)S(1)}, bf16[384,256]{1,0:T(8,128)(2,1)S(1)}, u32[]{:S(2)}, u32[]{:S(2)}) collective-permute-start(bf16[384,256]{1,0:T(8,128)(2,1)S(1)} %collective-permute-done.16.refs_18_), channel_id=1, source_target_pairs={{0,14},{2,0},{4,2},{6,4},{8,6},{10,8},{12,10},{14,12},{1,15},{3,1}... | collective-permute-start | bytes 589832 | tf_op jit(solution)/shard_map/ppermute | solution.py:272
  54.9 24.7 %copy-start.16 = (bf16[384,256]{1,0:T(8,128)(2,1)}, bf16[384,256]{1,0:T(8,128)(2,1)S(1)}, u32[]{:S(2)}) copy-start(bf16[384,256]{1,0:T(8,128)(2,1)S(1)} %collective-permute-done.20.refs_22_) | copy-start | bytes 589828
  54.9 6.3 %collective-permute-start.17 = (bf16[384,256]{1,0:T(8,128)(2,1)S(1)}, bf16[384,256]{1,0:T(8,128)(2,1)S(1)}, u32[]{:S(2)}, u32[]{:S(2)}) collective-permute-start(bf16[384,256]{1,0:T(8,128)(2,1)S(1)} %collective-permute-done.16.refs_18_), channel_id=1, source_target_pairs={{0,1},{1,0},{2,3},{3,2},{4,5},{5,4},{6,7},{7,6},{8,9},{9,8},{10,11... | collective-permute-start | bytes 589832 | tf_op jit(solution)/shard_map/ppermute | solution.py:276
  57.0 22.6 %copy-start.17 = (bf16[384,256]{1,0:T(8,128)(2,1)}, bf16[384,256]{1,0:T(8,128)(2,1)S(1)}, u32[]{:S(2)}) copy-start(bf16[384,256]{1,0:T(8,128)(2,1)S(1)} %collective-permute-done.13.refs_15_) | copy-start | bytes 589828
  57.0 7.9 %collective-permute-start.22 = (bf16[384,256]{1,0:T(8,128)(2,1)S(1)}, bf16[384,256]{1,0:T(8,128)(2,1)S(1)}, u32[]{:S(2)}, u32[]{:S(2)}) collective-permute-start(bf16[384,256]{1,0:T(8,128)(2,1)S(1)} %collective-permute-done.14.refs_16_), channel_id=1, source_target_pairs={{0,2},{2,4},{4,6},{6,8},{8,10},{10,12},{12,14},{14,0},{1,3},{3,5},... | collective-permute-start | bytes 589832 | tf_op jit(solution)/shard_map/ppermute | solution.py:272
  58.0 21.5 %copy-start.18 = (bf16[384,256]{1,0:T(8,128)(2,1)}, bf16[384,256]{1,0:T(8,128)(2,1)S(1)}, u32[]{:S(2)}) copy-start(bf16[384,256]{1,0:T(8,128)(2,1)S(1)} %collective-permute-done.18.refs_20_) | copy-start | bytes 589828
  58.0 6.9 %collective-permute-start.15 = (bf16[384,256]{1,0:T(8,128)(2,1)S(1)}, bf16[384,256]{1,0:T(8,128)(2,1)S(1)}, u32[]{:S(2)}, u32[]{:S(2)}) collective-permute-start(bf16[384,256]{1,0:T(8,128)(2,1)S(1)} %collective-permute-done.14.refs_16_), channel_id=1, source_target_pairs={{0,1},{1,0},{2,3},{3,2},{4,5},{5,4},{6,7},{7,6},{8,9},{9,8},{10,11... | collective-permute-start | bytes 589832 | tf_op jit(solution)/shard_map/ppermute | solution.py:276
  58.0 11.4 %copy-start.19 = (bf16[384,256]{1,0:T(8,128)(2,1)}, bf16[384,256]{1,0:T(8,128)(2,1)S(1)}, u32[]{:S(2)}) copy-start(bf16[384,256]{1,0:T(8,128)(2,1)S(1)} %collective-permute-done.11.refs_13_) | copy-start | bytes 589828
  58.0 7.4 %collective-permute-start.21 = (bf16[384,256]{1,0:T(8,128)(2,1)S(1)}, bf16[384,256]{1,0:T(8,128)(2,1)S(1)}, u32[]{:S(2)}, u32[]{:S(2)}) collective-permute-start(bf16[384,256]{1,0:T(8,128)(2,1)S(1)} %collective-permute-done.20.refs_22_), channel_id=1, source_target_pairs={{0,1},{1,0},{2,3},{3,2},{4,5},{5,4},{6,7},{7,6},{8,9},{9,8},{10,11... | collective-permute-start | bytes 589832 | tf_op jit(solution)/shard_map/ppermute | solution.py:276
  59.8 9.7 %copy-start.20 = (bf16[384,256]{1,0:T(8,128)(2,1)}, bf16[384,256]{1,0:T(8,128)(2,1)S(1)}, u32[]{:S(2)}) copy-start(bf16[384,256]{1,0:T(8,128)(2,1)S(1)} %collective-permute-done.24.refs_26_) | copy-start | bytes 589828
  59.8 9.1 %collective-permute-start.26 = (bf16[384,256]{1,0:T(8,128)(2,1)S(1)}, bf16[384,256]{1,0:T(8,128)(2,1)S(1)}, u32[]{:S(2)}, u32[]{:S(2)}) collective-permute-start(bf16[384,256]{1,0:T(8,128)(2,1)S(1)} %collective-permute-done.18.refs_20_), channel_id=1, source_target_pairs={{0,2},{2,4},{4,6},{6,8},{8,10},{10,12},{12,14},{14,0},{1,3},{3,5},... | collective-permute-start | bytes 589832 | tf_op jit(solution)/shard_map/ppermute | solution.py:272
  61.1 8.4 %copy-start.21 = (bf16[384,256]{1,0:T(8,128)(2,1)}, bf16[384,256]{1,0:T(8,128)(2,1)S(1)}, u32[]{:S(2)}) copy-start(bf16[384,256]{1,0:T(8,128)(2,1)S(1)} %collective-permute-done.17.refs_19_) | copy-start | bytes 589828
  61.1 7.7 %collective-permute-start.28 = (bf16[384,256]{1,0:T(8,128)(2,1)S(1)}, bf16[384,256]{1,0:T(8,128)(2,1)S(1)}, u32[]{:S(2)}, u32[]{:S(2)}) collective-permute-start(bf16[384,256]{1,0:T(8,128)(2,1)S(1)} %collective-permute-done.24.refs_26_), channel_id=1, source_target_pairs={{0,14},{2,0},{4,2},{6,4},{8,6},{10,8},{12,10},{14,12},{1,15},{3,1}... | collective-permute-start | bytes 589832 | tf_op jit(solution)/shard_map/ppermute | solution.py:272
  64.8 5.5 %copy-start.22 = (bf16[384,256]{1,0:T(8,128)(2,1)}, bf16[384,256]{1,0:T(8,128)(2,1)S(1)}, u32[]{:S(2)}) copy-start(bf16[384,256]{1,0:T(8,128)(2,1)S(1)} %collective-permute-done.22.refs_24_) | copy-start | bytes 589828
  64.8 4.6 %collective-permute-start.19 = (bf16[384,256]{1,0:T(8,128)(2,1)S(1)}, bf16[384,256]{1,0:T(8,128)(2,1)S(1)}, u32[]{:S(2)}, u32[]{:S(2)}) collective-permute-start(bf16[384,256]{1,0:T(8,128)(2,1)S(1)} %collective-permute-done.18.refs_20_), channel_id=1, source_target_pairs={{0,1},{1,0},{2,3},{3,2},{4,5},{5,4},{6,7},{7,6},{8,9},{9,8},{10,11... | collective-permute-start | bytes 589832 | tf_op jit(solution)/shard_map/ppermute | solution.py:276
  64.9 5.4 %copy-start.23 = (bf16[384,256]{1,0:T(8,128)(2,1)}, bf16[384,256]{1,0:T(8,128)(2,1)S(1)}, u32[]{:S(2)}) copy-start(bf16[384,256]{1,0:T(8,128)(2,1)S(1)} %collective-permute-done.15.refs_17_) | copy-start | bytes 589828
  64.9 4.6 %collective-permute-start.25 = (bf16[384,256]{1,0:T(8,128)(2,1)S(1)}, bf16[384,256]{1,0:T(8,128)(2,1)S(1)}, u32[]{:S(2)}, u32[]{:S(2)}) collective-permute-start(bf16[384,256]{1,0:T(8,128)(2,1)S(1)} %collective-permute-done.24.refs_26_), channel_id=1, source_target_pairs={{0,1},{1,0},{2,3},{3,2},{4,5},{5,4},{6,7},{7,6},{8,9},{9,8},{10,11... | collective-permute-start | bytes 589832 | tf_op jit(solution)/shard_map/ppermute | solution.py:276
  65.4 4.9 %copy-start.24 = (bf16[384,256]{1,0:T(8,128)(2,1)}, bf16[384,256]{1,0:T(8,128)(2,1)S(1)}, u32[]{:S(2)}) copy-start(bf16[384,256]{1,0:T(8,128)(2,1)S(1)} %collective-permute-done.21.refs_23_) | copy-start | bytes 589828
  65.4 4.1 %collective-permute-start.23 = (bf16[384,256]{1,0:T(8,128)(2,1)S(1)}, bf16[384,256]{1,0:T(8,128)(2,1)S(1)}, u32[]{:S(2)}, u32[]{:S(2)}) collective-permute-start(bf16[384,256]{1,0:T(8,128)(2,1)S(1)} %collective-permute-done.22.refs_24_), channel_id=1, source_target_pairs={{0,1},{1,0},{2,3},{3,2},{4,5},{5,4},{6,7},{7,6},{8,9},{9,8},{10,11... | collective-permute-start | bytes 589832 | tf_op jit(solution)/shard_map/ppermute | solution.py:276
  68.8 1.5 %copy-start.25 = (bf16[384,256]{1,0:T(8,128)(2,1)}, bf16[384,256]{1,0:T(8,128)(2,1)S(1)}, u32[]{:S(2)}) copy-start(bf16[384,256]{1,0:T(8,128)(2,1)S(1)} %collective-permute-done.26.refs_28_) | copy-start | bytes 589828
  68.8 1.4 %collective-permute-start.27 = (bf16[384,256]{1,0:T(8,128)(2,1)S(1)}, bf16[384,256]{1,0:T(8,128)(2,1)S(1)}, u32[]{:S(2)}, u32[]{:S(2)}) collective-permute-start(bf16[384,256]{1,0:T(8,128)(2,1)S(1)} %collective-permute-done.26.refs_28_), channel_id=1, source_target_pairs={{0,1},{1,0},{2,3},{3,2},{4,5},{5,4},{6,7},{7,6},{8,9},{9,8},{10,11... | collective-permute-start | bytes 589832 | tf_op jit(solution)/shard_map/ppermute | solution.py:276
  68.9 1.5 %copy-start.26 = (bf16[384,256]{1,0:T(8,128)(2,1)}, bf16[384,256]{1,0:T(8,128)(2,1)S(1)}, u32[]{:S(2)}) copy-start(bf16[384,256]{1,0:T(8,128)(2,1)S(1)} %collective-permute-done.28.refs_30_) | copy-start | bytes 589828
  68.9 2.2 %collective-permute-start.29 = (bf16[384,256]{1,0:T(8,128)(2,1)S(1)}, bf16[384,256]{1,0:T(8,128)(2,1)}, u32[]{:S(2)}, u32[]{:S(2)}) collective-permute-start(bf16[384,256]{1,0:T(8,128)(2,1)S(1)} %collective-permute-done.28.refs_30_), channel_id=1, source_target_pairs={{0,1},{1,0},{2,3},{3,2},{4,5},{5,4},{6,7},{7,6},{8,9},{9,8},{10,11... | collective-permute-start | bytes 589832 | tf_op jit(solution)/shard_map/ppermute | solution.py:276
  99.1 25.0 %all-to-all-start.1 = ((f32[16,8,384]{2,1,0:T(8,128)}), f32[16,8,384]{2,1,0:T(8,128)S(1)}, u32[]{:S(2)}, u32[]{:S(2)}) async-start(f32[16,8,384]{2,1,0:T(8,128)} %bitcast.10), calls=%async_computation.1 | async-start | bytes 393216 | tf_op jit(solution)/shard_map/all_to_all | solution.py:343
  106.4 5.6 %collective-permute-start.30 = (f32[96,128]{1,0:T(8,128)S(1)}, f32[96,128]{1,0:T(8,128)S(1)}, u32[]{:S(2)}, u32[]{:S(2)}) collective-permute-start(f32[96,128]{1,0:T(8,128)S(1)} %get-tuple-element.21), channel_id=1, source_target_pairs={{0,64},{64,128},{128,192},{192,0},{1,65},{65,129},{129,193},{193,1... | collective-permute-start | bytes 147464 | tf_op jit(solution)/shard_map/ppermute | solution.py:272
  107.8 5.6 %collective-permute-start.31 = (f32[96,128]{1,0:T(8,128)S(1)}, f32[96,128]{1,0:T(8,128)S(1)}, u32[]{:S(2)}, u32[]{:S(2)}) collective-permute-start(f32[96,128]{1,0:T(8,128)S(1)} %get-tuple-element.22), channel_id=1, source_target_pairs={{0,128},{64,192},{128,0},{192,64},{1,129},{65,193},{129,1},{193,65... | collective-permute-start | bytes 147464 | tf_op jit(solution)/shard_map/ppermute | solution.py:272
  110.5 4.1 %collective-permute-start.32 = (f32[96,128]{1,0:T(8,128)S(1)}, f32[96,128]{1,0:T(8,128)S(1)}, u32[]{:S(2)}, u32[]{:S(2)}) collective-permute-start(f32[96,128]{1,0:T(8,128)S(1)} %get-tuple-element.23), channel_id=1, source_target_pairs={{0,192},{64,0},{128,64},{192,128},{1,193},{65,1},{129,65},{193,129... | collective-permute-start | bytes 147464 | tf_op jit(solution)/shard_map/ppermute | solution.py:272
  116.0 4.3 %collective-permute-start.35 = (f32[96,128]{1,0:T(8,128)}, f32[96,128]{1,0:T(8,128)S(1)}, u32[]{:S(2)}, u32[]{:S(2)}) collective-permute-start(f32[96,128]{1,0:T(8,128)} %meet.1.refs_0_), channel_id=1, source_target_pairs={{0,48},{16,0},{32,16},{48,32},{1,49},{17,1},{33,17},{49,33},{2,50}... | collective-permute-start | bytes 147464 | tf_op jit(solution)/shard_map/ppermute | solution.py:272
  116.9 5.8 %collective-permute-start.34 = (f32[96,128]{1,0:T(8,128)}, f32[96,128]{1,0:T(8,128)S(1)}, u32[]{:S(2)}, u32[]{:S(2)}) collective-permute-start(f32[96,128]{1,0:T(8,128)} %meet.1.refs_0_), channel_id=1, source_target_pairs={{0,32},{16,48},{32,0},{48,16},{1,33},{17,49},{33,1},{49,17},{2,34}... | collective-permute-start | bytes 147464 | tf_op jit(solution)/shard_map/ppermute | solution.py:272
  118.6 5.5 %collective-permute-start.33 = (f32[96,128]{1,0:T(8,128)}, f32[96,128]{1,0:T(8,128)S(1)}, u32[]{:S(2)}, u32[]{:S(2)}) collective-permute-start(f32[96,128]{1,0:T(8,128)} %meet.1.refs_0_), channel_id=1, source_target_pairs={{0,16},{16,32},{32,48},{48,0},{1,17},{17,33},{33,49},{49,1},{2,18}... | collective-permute-start | bytes 147464 | tf_op jit(solution)/shard_map/ppermute | solution.py:272
  (6 other events, 4.7 us)
Sparse Core Ops, SparseCore 0:
  10.5 68.9 all-gather.2

commit v7 on v6

--- a/solution.py
+++ b/solution.py
@@ -22,7 +22,7 @@
 LEFTS = NX * PER
 BLOCK = 128
 GROUP = 4
-TILE = 256
+TILE = 512
 
 VMEM = pl.BlockSpec(memory_space=pltpu.VMEM)
 HBM = pl.BlockSpec(memory_space=pltpu.HBM)

time: 134 us -> 134 us (level)
  no operation moved by 1% of the time
where the time goes in v7:
time: 134 us; the launch traced here: 133 us
  starting transfers between devices  43.4 us (32%)
  waiting for transfers between devices  41 us (31%)
  Pallas kernels  29.1 us (22%)
  between operations  14.4 us (11%)
  local copies, waits for them, and re-layouts  3.65 us (3%)
  other arithmetic  1.87 us (1%)
    ppermute x20, starting transfers between devices, shift(): lax.ppermute(value, axis, [(i, (i + by) % size) for i in range(size)])  29.4 us
    ppermute x20, waiting for transfers between devices, shift(): lax.ppermute(value, axis, [(i, (i + by) % size) for i in range(size)])  24.6 us
    pallas_call x1, Pallas kernels, correlate(): pl.pallas_call(kernel, grid_spec=pltpu.PrefetchScalarGridSpec(num_scalar_...  19 us
    all_gather x1, waiting for transfers between devices, body(): gathered = in_hbm(lax.all_gather(acts, ('x', 'dp'), axis=0, tiled=False))  8.4 us
    all_to_all x1, starting transfers between devices, body(): lax.all_to_all(right.reshape(NZ * NC, RSTEP, QUARTER), ('z', 'core'), spl...  7.18 us
    all_to_all x1, waiting for transfers between devices, body(): lax.all_to_all(slices, 'dp', split_axis=0, concat_axis=0, tiled=True)  7.12 us
    all_to_all x1, starting transfers between devices, body(): lax.all_to_all(slices, 'dp', split_axis=0, concat_axis=0, tiled=True)  4.46 us
  transfers between devices with their start and end apart: 39, of which 18 were waited for; matrix products, arithmetic and copies ran while one was open for 3% of the time, Pallas kernels for 4%

profile of v7, /device:TPU:32, one launch (start us, length us, event | category | flops | bytes accessed | tf_op | source)
XLA Modules:
  0.0 133.5 jit_solution(1847236915192039729)
XLA Ops:
  7.2 0.0 all-gather.3.cloned.1.call-start
  7.2 2.2 %prepare.1.acts_ref = bf16[2,64,1536]{2,1,0:T(8,128)(2,1)} custom-call(bf16[2,64,1536]{2,1,0:T(8,128)(2,1)} %codes_ref.1, f32[12,2,64]{2,1,0:T(2,128)} %bitcast.74), custom_call_target="tpu_custom_call" | custom-call | tf_op jit(solution)/shard_map/prepare/pallas_call | solution.py:41
  9.4 0.0 all-gather.3.cloned.1.call-update
  9.4 1.9 %turn.1 = bf16[4,384,128]{2,1,0:T(8,128)(2,1)} custom-call(bf16[2,64,1536]{2,1,0:T(8,128)(2,1)} %prepare.1.acts_ref), custom_call_target="tpu_custom_call" | custom-call | tf_op jit(solution)/shard_map/turn/pallas_call | solution.py:60
  11.4 4.5 %all-to-all-start = ((bf16[4,384,128]{2,1,0:T(8,128)(2,1)}), bf16[4,384,128]{2,1,0:T(8,128)(2,1)S(1)}, u32[]{:S(2)}, u32[]{:S(2)}) async-start(bf16[4,384,128]{2,1,0:T(8,128)(2,1)} %turn.1), calls=%async_computation | async-start | bytes 786432 | tf_op jit(solution)/shard_map/all_to_all | solution.py:317
  15.8 0.8 reshape.106
  16.8 7.1 %all-to-all-done.in_ref = bf16[4,384,128]{2,1,0:T(8,128)(2,1)S(1)} async-done(((bf16[4,384,128]{2,1,0:T(8,128)(2,1)}), bf16[4,384,128]{2,1,0:T(8,128)(2,1)S(1)}, u32[]{:S(2)}, u32[]{:S(2)}) %all-to-all-start) | async-done | bytes 393248 | tf_op jit(solution)/shard_map/all_to_all | solution.py:317
  23.9 0.8 copy-done.1
  24.7 2.4 %normalise.1 = (bf16[384,256]{1,0:T(8,128)(2,1)}, bf16[384,256]{1,0:T(8,128)(2,1)}) custom-call(bf16[4,384,128]{2,1,0:T(8,128)(2,1)} %copy-done.1), custom_call_target="tpu_custom_call" | custom-call | tf_op jit(solution)/shard_map/normalise/pallas_call | solution.py:81
  27.0 0.1 collective-permute-start.4
  27.2 1.9 %collective-permute-start.2 = (bf16[384,256]{1,0:T(8,128)(2,1)}, bf16[384,256]{1,0:T(8,128)(2,1)S(1)}, u32[]{:S(2)}, u32[]{:S(2)}) collective-permute-start(bf16[384,256]{1,0:T(8,128)(2,1)} %get-tuple-element.16.refs_0_), channel_id=1, source_target_pairs={{0,2},{2,4},{4,6},{6,8},{8,10},{10,12},{12,14},{14,0},{1,3},{3,5},... | collective-permute-start | bytes 589832 | tf_op jit(solution)/shard_map/ppermute | solution.py:272
  29.1 3.9 %collective-permute-start.8 = (bf16[384,256]{1,0:T(8,128)(2,1)}, bf16[384,256]{1,0:T(8,128)(2,1)S(1)}, u32[]{:S(2)}, u32[]{:S(2)}) collective-permute-start(bf16[384,256]{1,0:T(8,128)(2,1)} %get-tuple-element.17.refs_2_), channel_id=1, source_target_pairs={{0,14},{2,0},{4,2},{6,4},{8,6},{10,8},{12,10},{14,12},{1,15},{3,1}... | collective-permute-start | bytes 589832 | tf_op jit(solution)/shard_map/ppermute | solution.py:272
  33.0 0.2 collective-permute-done.4.refs_6_
  33.2 0.1 collective-permute-start.1
  33.3 3.5 %collective-permute-done.2.refs_4_ = bf16[384,256]{1,0:T(8,128)(2,1)S(1)} collective-permute-done((bf16[384,256]{1,0:T(8,128)(2,1)}, bf16[384,256]{1,0:T(8,128)(2,1)S(1)}, u32[]{:S(2)}, u32[]{:S(2)}) %collective-permute-start.2) | collective-permute-done | bytes 196640 | tf_op jit(solution)/shard_map/ppermute | solution.py:272
  36.9 3.2 %collective-permute-start.12 = (bf16[384,256]{1,0:T(8,128)(2,1)S(1)}, bf16[384,256]{1,0:T(8,128)(2,1)S(1)}, u32[]{:S(2)}, u32[]{:S(2)}) collective-permute-start(bf16[384,256]{1,0:T(8,128)(2,1)S(1)} %collective-permute-done.4.refs_6_), channel_id=1, source_target_pairs={{0,14},{2,0},{4,2},{6,4},{8,6},{10,8},{12,10},{14,12},{1,15},{3,1}... | collective-permute-start | bytes 589832 | tf_op jit(solution)/shard_map/ppermute | solution.py:272
  40.1 0.1 collective-permute-start.10
  40.2 1.6 %collective-permute-done.6.refs_8_ = bf16[384,256]{1,0:T(8,128)(2,1)S(1)} collective-permute-done((bf16[384,256]{1,0:T(8,128)(2,1)}, bf16[384,256]{1,0:T(8,128)(2,1)S(1)}, u32[]{:S(2)}, u32[]{:S(2)}) %collective-permute-start.6) | collective-permute-done | bytes 196640 | tf_op jit(solution)/shard_map/ppermute | solution.py:272
  41.8 0.2 convert_reduce_fusion
  42.0 0.1 select_reduce_fusion.order_ref
  42.1 3.0 %collective-permute-start.16 = (bf16[384,256]{1,0:T(8,128)(2,1)S(1)}, bf16[384,256]{1,0:T(8,128)(2,1)S(1)}, u32[]{:S(2)}, u32[]{:S(2)}) collective-permute-start(bf16[384,256]{1,0:T(8,128)(2,1)S(1)} %collective-permute-done.8.refs_10_), channel_id=1, source_target_pairs={{0,14},{2,0},{4,2},{6,4},{8,6},{10,8},{12,10},{14,12},{1,15},{3,1}... | collective-permute-start | bytes 589832 | tf_op jit(solution)/shard_map/ppermute | solution.py:272
  45.1 0.2 collective-permute-start.9
  45.3 2.1 %collective-permute-done.10.refs_12_ = bf16[384,256]{1,0:T(8,128)(2,1)S(1)} collective-permute-done((bf16[384,256]{1,0:T(8,128)(2,1)S(1)}, bf16[384,256]{1,0:T(8,128)(2,1)S(1)}, u32[]{:S(2)}, u32[]{:S(2)}) %collective-permute-start.10) | collective-permute-done | bytes 196640 | tf_op jit(solution)/shard_map/ppermute | solution.py:272
  47.5 2.4 %collective-permute-start.20 = (bf16[384,256]{1,0:T(8,128)(2,1)S(1)}, bf16[384,256]{1,0:T(8,128)(2,1)S(1)}, u32[]{:S(2)}, u32[]{:S(2)}) collective-permute-start(bf16[384,256]{1,0:T(8,128)(2,1)S(1)} %collective-permute-done.12.refs_14_), channel_id=1, source_target_pairs={{0,14},{2,0},{4,2},{6,4},{8,6},{10,8},{12,10},{14,12},{1,15},{3,1}... | collective-permute-start | bytes 589832 | tf_op jit(solution)/shard_map/ppermute | solution.py:272
  49.9 0.1 collective-permute-done.16.refs_18_
  49.9 0.2 collective-permute-start.13
  50.1 1.1 collective-permute-start.18
  51.3 1.1 collective-permute-done.14.refs_16_
  52.4 2.4 %collective-permute-start.24 = (bf16[384,256]{1,0:T(8,128)(2,1)S(1)}, bf16[384,256]{1,0:T(8,128)(2,1)S(1)}, u32[]{:S(2)}, u32[]{:S(2)}) collective-permute-start(bf16[384,256]{1,0:T(8,128)(2,1)S(1)} %collective-permute-done.16.refs_18_), channel_id=1, source_target_pairs={{0,14},{2,0},{4,2},{6,4},{8,6},{10,8},{12,10},{14,12},{1,15},{3,1}... | collective-permute-start | bytes 589832 | tf_op jit(solution)/shard_map/ppermute | solution.py:272
  54.9 0.2 collective-permute-start.17
  55.0 1.3 and_select_fusion.7
  56.3 0.7 broadcast_in_dim.34.choice_ref
  57.0 0.2 collective-permute-start.22
  57.2 0.8 collective-permute-done.18.refs_20_
  58.0 0.5 collective-permute-start.21
  58.5 1.3 collective-permute-done.24.refs_26_
  59.8 1.4 %collective-permute-start.26 = (bf16[384,256]{1,0:T(8,128)(2,1)S(1)}, bf16[384,256]{1,0:T(8,128)(2,1)S(1)}, u32[]{:S(2)}, u32[]{:S(2)}) collective-permute-start(bf16[384,256]{1,0:T(8,128)(2,1)S(1)} %collective-permute-done.18.refs_20_), channel_id=1, source_target_pairs={{0,2},{2,4},{4,6},{6,8},{8,10},{10,12},{12,14},{14,0},{1,3},{3,5},... | collective-permute-start | bytes 589832 | tf_op jit(solution)/shard_map/ppermute | solution.py:272
  61.1 1.1 collective-permute-start.28
  62.2 0.1 convert_reduce_fusion.1.start_ref
  62.3 2.5 %collective-permute-done.22.refs_24_ = bf16[384,256]{1,0:T(8,128)(2,1)S(1)} collective-permute-done((bf16[384,256]{1,0:T(8,128)(2,1)S(1)}, bf16[384,256]{1,0:T(8,128)(2,1)S(1)}, u32[]{:S(2)}, u32[]{:S(2)}) %collective-permute-start.22) | collective-permute-done | bytes 196640 | tf_op jit(solution)/shard_map/ppermute | solution.py:272
  64.9 0.5 collective-permute-start.25
  65.4 0.1 collective-permute-start.23
  65.5 3.4 %collective-permute-done.26.refs_28_ = bf16[384,256]{1,0:T(8,128)(2,1)S(1)} collective-permute-done((bf16[384,256]{1,0:T(8,128)(2,1)S(1)}, bf16[384,256]{1,0:T(8,128)(2,1)S(1)}, u32[]{:S(2)}, u32[]{:S(2)}) %collective-permute-start.26) | collective-permute-done | bytes 196640 | tf_op jit(solution)/shard_map/ppermute | solution.py:272
  68.9 0.5 collective-permute-start.29
  69.4 0.1 iota_add_fusion.lpos_ref
  69.5 0.8 collective-permute-done.27.refs_29_
  70.4 0.7 copy-done.30
  71.0 8.4 %all-gather.3.cloned.1.call-done = bf16[32,64,1536]{2,1,0:T(8,128)(2,1)} async-done(((bf16[2,64,1536]{2,1,0:T(8,128)(2,1)}), bf16[32,64,1536]{2,1,0:T(8,128)(2,1)}) %all-gather.3.cloned.1.call-update) | async-done | bytes 6291472 | tf_op jit(solution)/shard_map/all_gather | solution.py:318
  79.6 19.0 %correlate.1 = (f32[96,128]{1,0:T(8,128)S(1)}, f32[96,128]{1,0:T(8,128)S(1)}, f32[96,128]{1,0:T(8,128)S(1)}, f32[96,128]{1,0:T(8,128)S(1)}, f32[128,384]{1,0:T(8,128)}) custom-call(s32[9]{0:T(128)S(1)} %convert_reduce_fusion.1.start_ref, s32[32]{0:T(128)S(1)} %select_reduce_fusion.order_ref, s32[32]{0:T(128)S(1)} %get-tuple-element.30.jidx_ref, ...), custom_call_target="tpu_custom_call" | custom-call | tf_op jit(solution)/shard_map/correlate/pallas_call | solution.py:197
  98.6 0.6 copy-done
  99.2 7.2 %all-to-all-start.1 = ((f32[16,8,384]{2,1,0:T(8,128)}), f32[16,8,384]{2,1,0:T(8,128)S(1)}, u32[]{:S(2)}, u32[]{:S(2)}) async-start(f32[16,8,384]{2,1,0:T(8,128)} %bitcast.10), calls=%async_computation.1 | async-start | bytes 393216 | tf_op jit(solution)/shard_map/all_to_all | solution.py:343
  106.4 1.4 %collective-permute-start.30 = (f32[96,128]{1,0:T(8,128)S(1)}, f32[96,128]{1,0:T(8,128)S(1)}, u32[]{:S(2)}, u32[]{:S(2)}) collective-permute-start(f32[96,128]{1,0:T(8,128)S(1)} %get-tuple-element.21), channel_id=1, source_target_pairs={{0,64},{64,128},{128,192},{192,0},{1,65},{65,129},{129,193},{193,1... | collective-permute-start | bytes 147464 | tf_op jit(solution)/shard_map/ppermute | solution.py:272
  107.8 2.7 %collective-permute-start.31 = (f32[96,128]{1,0:T(8,128)S(1)}, f32[96,128]{1,0:T(8,128)S(1)}, u32[]{:S(2)}, u32[]{:S(2)}) collective-permute-start(f32[96,128]{1,0:T(8,128)S(1)} %get-tuple-element.22), channel_id=1, source_target_pairs={{0,128},{64,192},{128,0},{192,64},{1,129},{65,193},{129,1},{193,65... | collective-permute-start | bytes 147464 | tf_op jit(solution)/shard_map/ppermute | solution.py:272
  110.6 1.4 %collective-permute-start.32 = (f32[96,128]{1,0:T(8,128)S(1)}, f32[96,128]{1,0:T(8,128)S(1)}, u32[]{:S(2)}, u32[]{:S(2)}) collective-permute-start(f32[96,128]{1,0:T(8,128)S(1)} %get-tuple-element.23), channel_id=1, source_target_pairs={{0,192},{64,0},{128,64},{192,128},{1,193},{65,1},{129,65},{193,129... | collective-permute-start | bytes 147464 | tf_op jit(solution)/shard_map/ppermute | solution.py:272
  112.0 1.4 %collective-permute-done.31.refs_2_ = f32[96,128]{1,0:T(8,128)S(1)} collective-permute-done((f32[96,128]{1,0:T(8,128)S(1)}, f32[96,128]{1,0:T(8,128)S(1)}, u32[]{:S(2)}, u32[]{:S(2)}) %collective-permute-start.31) | collective-permute-done | bytes 49184 | tf_op jit(solution)/shard_map/ppermute | solution.py:272
  113.4 1.2 collective-permute-done.32.refs_3_
  114.7 1.4 %meet.1.refs_0_ = f32[96,128]{1,0:T(8,128)} custom-call(f32[96,128]{1,0:T(8,128)} %copy-done, f32[96,128]{1,0:T(8,128)S(1)} %collective-permute-done.30.refs_1_, f32[96,128]{1,0:T(8,128)S(1)} %collective-permute-done.31.refs_2_, f32[96,128]{1,0:T(8,128)S(1)} %collective-permute-done.32.refs_3_), custom_call_target="tpu_custom_call" | custom-call | tf_op jit(solution)/shard_map/meet/pallas_call | solution.py:254
  116.1 1.2 collective-permute-start.35
  117.3 1.6 %collective-permute-start.34 = (f32[96,128]{1,0:T(8,128)}, f32[96,128]{1,0:T(8,128)S(1)}, u32[]{:S(2)}, u32[]{:S(2)}) collective-permute-start(f32[96,128]{1,0:T(8,128)} %meet.1.refs_0_), channel_id=1, source_target_pairs={{0,32},{16,48},{32,0},{48,16},{1,33},{17,49},{33,1},{49,17},{2,34}... | collective-permute-start | bytes 147464 | tf_op jit(solution)/shard_map/ppermute | solution.py:272
  118.9 0.1 collective-permute-start.33
  119.1 1.3 collective-permute-done.35.refs_3_
  120.4 2.7 %collective-permute-done.34.refs_2_ = f32[96,128]{1,0:T(8,128)S(1)} collective-permute-done((f32[96,128]{1,0:T(8,128)}, f32[96,128]{1,0:T(8,128)S(1)}, u32[]{:S(2)}, u32[]{:S(2)}) %collective-permute-start.34) | collective-permute-done | bytes 49184 | tf_op jit(solution)/shard_map/ppermute | solution.py:272
  123.1 1.3 %collective-permute-done.33.refs_1_ = f32[96,128]{1,0:T(8,128)S(1)} collective-permute-done((f32[96,128]{1,0:T(8,128)}, f32[96,128]{1,0:T(8,128)S(1)}, u32[]{:S(2)}, u32[]{:S(2)}) %collective-permute-start.33) | collective-permute-done | bytes 49184 | tf_op jit(solution)/shard_map/ppermute | solution.py:272
  124.5 2.2 %finish.1 = (f32[32,384]{1,0:T(8,128)}, f32[32,384]{1,0:T(8,128)}) custom-call(s32[32]{0:T(128)} %get-tuple-element.14.rows_ref, f32[128,384]{1,0:T(8,128)S(1)} %bitcast.69, s32[32,128]{1,0:T(8,128)} %broadcast_in_dim.34.choice_ref, f32[96,128]{1,0:T(8,128)} %meet.1.refs_0_, f32[96,128]{1,0:T(8,128)S(1)} %collective-permute-done.33.refs_1_, ...), custom_call_target="tpu_custom_call" | custom-call | tf_op jit(solution)/shard_map/finish/pallas_call | solution.py:234
  (98 shorter events, 0.3 us)
Async XLA Ops:
  7.2 72.3 %all-gather.3.cloned.1.call-start = ((), (), s32[]{:S(2)}) async-start(), calls=%async_computation.2 | async-start | bytes 6684672 | tf_op jit(solution)/shard_map/all_gather | solution.py:318
  11.4 12.5 %all-to-all-start = ((bf16[4,384,128]{2,1,0:T(8,128)(2,1)}), bf16[4,384,128]{2,1,0:T(8,128)(2,1)S(1)}, u32[]{:S(2)}, u32[]{:S(2)}) async-start(bf16[4,384,128]{2,1,0:T(8,128)(2,1)} %turn.1), calls=%async_computation | async-start | bytes 786432 | tf_op jit(solution)/shard_map/all_to_all | solution.py:317
  27.0 6.2 %collective-permute-start.4 = (bf16[384,256]{1,0:T(8,128)(2,1)}, bf16[384,256]{1,0:T(8,128)(2,1)S(1)}, u32[]{:S(2)}, u32[]{:S(2)}) collective-permute-start(bf16[384,256]{1,0:T(8,128)(2,1)} %get-tuple-element.16.refs_0_), channel_id=1, source_target_pairs={{0,14},{2,0},{4,2},{6,4},{8,6},{10,8},{12,10},{14,12},{1,15},{3,1}... | collective-permute-start | bytes 589832 | tf_op jit(solution)/shard_map/ppermute | solution.py:272
  27.2 9.7 %collective-permute-start.2 = (bf16[384,256]{1,0:T(8,128)(2,1)}, bf16[384,256]{1,0:T(8,128)(2,1)S(1)}, u32[]{:S(2)}, u32[]{:S(2)}) collective-permute-start(bf16[384,256]{1,0:T(8,128)(2,1)} %get-tuple-element.16.refs_0_), channel_id=1, source_target_pairs={{0,2},{2,4},{4,6},{6,8},{8,10},{10,12},{12,14},{14,0},{1,3},{3,5},... | collective-permute-start | bytes 589832 | tf_op jit(solution)/shard_map/ppermute | solution.py:272
  29.1 11.0 %collective-permute-start = (bf16[384,256]{1,0:T(8,128)(2,1)}, bf16[384,256]{1,0:T(8,128)(2,1)S(1)}, u32[]{:S(2)}, u32[]{:S(2)}) collective-permute-start(bf16[384,256]{1,0:T(8,128)(2,1)} %get-tuple-element.16.refs_0_), channel_id=1, source_target_pairs={{0,1},{1,0},{2,3},{3,2},{4,5},{5,4},{6,7},{7,6},{8,9},{9,8},{10,11... | collective-permute-start | bytes 589832 | tf_op jit(solution)/shard_map/ppermute | solution.py:276
  29.1 11.0 %collective-permute-start.8 = (bf16[384,256]{1,0:T(8,128)(2,1)}, bf16[384,256]{1,0:T(8,128)(2,1)S(1)}, u32[]{:S(2)}, u32[]{:S(2)}) collective-permute-start(bf16[384,256]{1,0:T(8,128)(2,1)} %get-tuple-element.17.refs_2_), channel_id=1, source_target_pairs={{0,14},{2,0},{4,2},{6,4},{8,6},{10,8},{12,10},{14,12},{1,15},{3,1}... | collective-permute-start | bytes 589832 | tf_op jit(solution)/shard_map/ppermute | solution.py:272
  33.0 8.8 %collective-permute-start.6 = (bf16[384,256]{1,0:T(8,128)(2,1)}, bf16[384,256]{1,0:T(8,128)(2,1)S(1)}, u32[]{:S(2)}, u32[]{:S(2)}) collective-permute-start(bf16[384,256]{1,0:T(8,128)(2,1)} %get-tuple-element.17.refs_2_), channel_id=1, source_target_pairs={{0,2},{2,4},{4,6},{6,8},{8,10},{10,12},{12,14},{14,0},{1,3},{3,5},... | collective-permute-start | bytes 589832 | tf_op jit(solution)/shard_map/ppermute | solution.py:272
  33.2 46.2 %copy-start.2 = (bf16[384,256]{1,0:T(8,128)(2,1)}, bf16[384,256]{1,0:T(8,128)(2,1)S(1)}, u32[]{:S(2)}) copy-start(bf16[384,256]{1,0:T(8,128)(2,1)S(1)} %collective-permute-done.4.refs_6_) | copy-start | bytes 589828
  33.2 8.9 %collective-permute-start.1 = (bf16[384,256]{1,0:T(8,128)(2,1)}, bf16[384,256]{1,0:T(8,128)(2,1)S(1)}, u32[]{:S(2)}, u32[]{:S(2)}) collective-permute-start(bf16[384,256]{1,0:T(8,128)(2,1)} %get-tuple-element.17.refs_2_), channel_id=1, source_target_pairs={{0,1},{1,0},{2,3},{3,2},{4,5},{5,4},{6,7},{7,6},{8,9},{9,8},{10,11... | collective-permute-start | bytes 589832 | tf_op jit(solution)/shard_map/ppermute | solution.py:276
  36.9 42.6 %copy-start.3 = (bf16[384,256]{1,0:T(8,128)(2,1)}, bf16[384,256]{1,0:T(8,128)(2,1)S(1)}, u32[]{:S(2)}) copy-start(bf16[384,256]{1,0:T(8,128)(2,1)S(1)} %collective-permute-done.2.refs_4_) | copy-start | bytes 589828
  36.9 8.2 %collective-permute-start.12 = (bf16[384,256]{1,0:T(8,128)(2,1)S(1)}, bf16[384,256]{1,0:T(8,128)(2,1)S(1)}, u32[]{:S(2)}, u32[]{:S(2)}) collective-permute-start(bf16[384,256]{1,0:T(8,128)(2,1)S(1)} %collective-permute-done.4.refs_6_), channel_id=1, source_target_pairs={{0,14},{2,0},{4,2},{6,4},{8,6},{10,8},{12,10},{14,12},{1,15},{3,1}... | collective-permute-start | bytes 589832 | tf_op jit(solution)/shard_map/ppermute | solution.py:272
  40.1 39.4 %copy-start.4 = (bf16[384,256]{1,0:T(8,128)(2,1)}, bf16[384,256]{1,0:T(8,128)(2,1)S(1)}, u32[]{:S(2)}) copy-start(bf16[384,256]{1,0:T(8,128)(2,1)S(1)} %collective-permute-done.refs_1_) | copy-start | bytes 589828
  40.1 5.2 %collective-permute-start.5 = (bf16[384,256]{1,0:T(8,128)(2,1)S(1)}, bf16[384,256]{1,0:T(8,128)(2,1)S(1)}, u32[]{:S(2)}, u32[]{:S(2)}) collective-permute-start(bf16[384,256]{1,0:T(8,128)(2,1)S(1)} %collective-permute-done.4.refs_6_), channel_id=1, source_target_pairs={{0,1},{1,0},{2,3},{3,2},{4,5},{5,4},{6,7},{7,6},{8,9},{9,8},{10,11... | collective-permute-start | bytes 589832 | tf_op jit(solution)/shard_map/ppermute | solution.py:276
  40.1 39.4 %copy-start.5 = (bf16[384,256]{1,0:T(8,128)(2,1)}, bf16[384,256]{1,0:T(8,128)(2,1)S(1)}, u32[]{:S(2)}) copy-start(bf16[384,256]{1,0:T(8,128)(2,1)S(1)} %collective-permute-done.8.refs_10_) | copy-start | bytes 589828
  40.1 7.3 %collective-permute-start.10 = (bf16[384,256]{1,0:T(8,128)(2,1)S(1)}, bf16[384,256]{1,0:T(8,128)(2,1)S(1)}, u32[]{:S(2)}, u32[]{:S(2)}) collective-permute-start(bf16[384,256]{1,0:T(8,128)(2,1)S(1)} %collective-permute-done.2.refs_4_), channel_id=1, source_target_pairs={{0,2},{2,4},{4,6},{6,8},{8,10},{10,12},{12,14},{14,0},{1,3},{3,5},... | collective-permute-start | bytes 589832 | tf_op jit(solution)/shard_map/ppermute | solution.py:272
  41.8 37.7 %copy-start.6 = (bf16[384,256]{1,0:T(8,128)(2,1)}, bf16[384,256]{1,0:T(8,128)(2,1)S(1)}, u32[]{:S(2)}) copy-start(bf16[384,256]{1,0:T(8,128)(2,1)S(1)} %collective-permute-done.6.refs_8_) | copy-start | bytes 589828
  41.8 5.7 %collective-permute-start.3 = (bf16[384,256]{1,0:T(8,128)(2,1)S(1)}, bf16[384,256]{1,0:T(8,128)(2,1)S(1)}, u32[]{:S(2)}, u32[]{:S(2)}) collective-permute-start(bf16[384,256]{1,0:T(8,128)(2,1)S(1)} %collective-permute-done.2.refs_4_), channel_id=1, source_target_pairs={{0,1},{1,0},{2,3},{3,2},{4,5},{5,4},{6,7},{7,6},{8,9},{9,8},{10,11... | collective-permute-start | bytes 589832 | tf_op jit(solution)/shard_map/ppermute | solution.py:276
  42.1 37.4 %copy-start.7 = (bf16[384,256]{1,0:T(8,128)(2,1)}, bf16[384,256]{1,0:T(8,128)(2,1)S(1)}, u32[]{:S(2)}) copy-start(bf16[384,256]{1,0:T(8,128)(2,1)S(1)} %collective-permute-done.1.refs_3_) | copy-start | bytes 589828
  42.1 7.8 %collective-permute-start.16 = (bf16[384,256]{1,0:T(8,128)(2,1)S(1)}, bf16[384,256]{1,0:T(8,128)(2,1)S(1)}, u32[]{:S(2)}, u32[]{:S(2)}) collective-permute-start(bf16[384,256]{1,0:T(8,128)(2,1)S(1)} %collective-permute-done.8.refs_10_), channel_id=1, source_target_pairs={{0,14},{2,0},{4,2},{6,4},{8,6},{10,8},{12,10},{14,12},{1,15},{3,1}... | collective-permute-start | bytes 589832 | tf_op jit(solution)/shard_map/ppermute | solution.py:272
  45.1 34.4 %copy-start.8 = (bf16[384,256]{1,0:T(8,128)(2,1)}, bf16[384,256]{1,0:T(8,128)(2,1)S(1)}, u32[]{:S(2)}) copy-start(bf16[384,256]{1,0:T(8,128)(2,1)S(1)} %collective-permute-done.12.refs_14_) | copy-start | bytes 589828
  45.1 5.0 %collective-permute-start.9 = (bf16[384,256]{1,0:T(8,128)(2,1)S(1)}, bf16[384,256]{1,0:T(8,128)(2,1)S(1)}, u32[]{:S(2)}, u32[]{:S(2)}) collective-permute-start(bf16[384,256]{1,0:T(8,128)(2,1)S(1)} %collective-permute-done.8.refs_10_), channel_id=1, source_target_pairs={{0,1},{1,0},{2,3},{3,2},{4,5},{5,4},{6,7},{7,6},{8,9},{9,8},{10,11... | collective-permute-start | bytes 589832 | tf_op jit(solution)/shard_map/ppermute | solution.py:276
  45.3 34.2 %copy-start.9 = (bf16[384,256]{1,0:T(8,128)(2,1)}, bf16[384,256]{1,0:T(8,128)(2,1)S(1)}, u32[]{:S(2)}) copy-start(bf16[384,256]{1,0:T(8,128)(2,1)S(1)} %collective-permute-done.5.refs_7_) | copy-start | bytes 589828
  45.3 7.1 %collective-permute-start.14 = (bf16[384,256]{1,0:T(8,128)(2,1)S(1)}, bf16[384,256]{1,0:T(8,128)(2,1)S(1)}, u32[]{:S(2)}, u32[]{:S(2)}) collective-permute-start(bf16[384,256]{1,0:T(8,128)(2,1)S(1)} %collective-permute-done.6.refs_8_), channel_id=1, source_target_pairs={{0,2},{2,4},{4,6},{6,8},{8,10},{10,12},{12,14},{14,0},{1,3},{3,5},... | collective-permute-start | bytes 589832 | tf_op jit(solution)/shard_map/ppermute | solution.py:272
  47.4 32.1 %copy-start.10 = (bf16[384,256]{1,0:T(8,128)(2,1)}, bf16[384,256]{1,0:T(8,128)(2,1)S(1)}, u32[]{:S(2)}) copy-start(bf16[384,256]{1,0:T(8,128)(2,1)S(1)} %collective-permute-done.10.refs_12_) | copy-start | bytes 589828
  47.4 5.0 %collective-permute-start.7 = (bf16[384,256]{1,0:T(8,128)(2,1)S(1)}, bf16[384,256]{1,0:T(8,128)(2,1)S(1)}, u32[]{:S(2)}, u32[]{:S(2)}) collective-permute-start(bf16[384,256]{1,0:T(8,128)(2,1)S(1)} %collective-permute-done.6.refs_8_), channel_id=1, source_target_pairs={{0,1},{1,0},{2,3},{3,2},{4,5},{5,4},{6,7},{7,6},{8,9},{9,8},{10,11... | collective-permute-start | bytes 589832 | tf_op jit(solution)/shard_map/ppermute | solution.py:276
  47.4 32.1 %copy-start.11 = (bf16[384,256]{1,0:T(8,128)(2,1)}, bf16[384,256]{1,0:T(8,128)(2,1)S(1)}, u32[]{:S(2)}) copy-start(bf16[384,256]{1,0:T(8,128)(2,1)S(1)} %collective-permute-done.3.refs_5_) | copy-start | bytes 589828
  47.5 7.4 %collective-permute-start.20 = (bf16[384,256]{1,0:T(8,128)(2,1)S(1)}, bf16[384,256]{1,0:T(8,128)(2,1)S(1)}, u32[]{:S(2)}, u32[]{:S(2)}) collective-permute-start(bf16[384,256]{1,0:T(8,128)(2,1)S(1)} %collective-permute-done.12.refs_14_), channel_id=1, source_target_pairs={{0,14},{2,0},{4,2},{6,4},{8,6},{10,8},{12,10},{14,12},{1,15},{3,1}... | collective-permute-start | bytes 589832 | tf_op jit(solution)/shard_map/ppermute | solution.py:272
  49.9 29.6 %copy-start.12 = (bf16[384,256]{1,0:T(8,128)(2,1)}, bf16[384,256]{1,0:T(8,128)(2,1)S(1)}, u32[]{:S(2)}) copy-start(bf16[384,256]{1,0:T(8,128)(2,1)S(1)} %collective-permute-done.16.refs_18_) | copy-start | bytes 589828
  49.9 7.1 %collective-permute-start.13 = (bf16[384,256]{1,0:T(8,128)(2,1)S(1)}, bf16[384,256]{1,0:T(8,128)(2,1)S(1)}, u32[]{:S(2)}, u32[]{:S(2)}) collective-permute-start(bf16[384,256]{1,0:T(8,128)(2,1)S(1)} %collective-permute-done.12.refs_14_), channel_id=1, source_target_pairs={{0,1},{1,0},{2,3},{3,2},{4,5},{5,4},{6,7},{7,6},{8,9},{9,8},{10,11... | collective-permute-start | bytes 589832 | tf_op jit(solution)/shard_map/ppermute | solution.py:276
  50.1 29.4 %copy-start.13 = (bf16[384,256]{1,0:T(8,128)(2,1)}, bf16[384,256]{1,0:T(8,128)(2,1)S(1)}, u32[]{:S(2)}) copy-start(bf16[384,256]{1,0:T(8,128)(2,1)S(1)} %collective-permute-done.9.refs_11_) | copy-start | bytes 589828
  50.1 7.9 %collective-permute-start.18 = (bf16[384,256]{1,0:T(8,128)(2,1)S(1)}, bf16[384,256]{1,0:T(8,128)(2,1)S(1)}, u32[]{:S(2)}, u32[]{:S(2)}) collective-permute-start(bf16[384,256]{1,0:T(8,128)(2,1)S(1)} %collective-permute-done.10.refs_12_), channel_id=1, source_target_pairs={{0,2},{2,4},{4,6},{6,8},{8,10},{10,12},{12,14},{14,0},{1,3},{3,5},... | collective-permute-start | bytes 589832 | tf_op jit(solution)/shard_map/ppermute | solution.py:272
  52.4 27.1 %copy-start.14 = (bf16[384,256]{1,0:T(8,128)(2,1)}, bf16[384,256]{1,0:T(8,128)(2,1)S(1)}, u32[]{:S(2)}) copy-start(bf16[384,256]{1,0:T(8,128)(2,1)S(1)} %collective-permute-done.14.refs_16_) | copy-start | bytes 589828
  52.4 5.6 %collective-permute-start.11 = (bf16[384,256]{1,0:T(8,128)(2,1)S(1)}, bf16[384,256]{1,0:T(8,128)(2,1)S(1)}, u32[]{:S(2)}, u32[]{:S(2)}) collective-permute-start(bf16[384,256]{1,0:T(8,128)(2,1)S(1)} %collective-permute-done.10.refs_12_), channel_id=1, source_target_pairs={{0,1},{1,0},{2,3},{3,2},{4,5},{5,4},{6,7},{7,6},{8,9},{9,8},{10,11... | collective-permute-start | bytes 589832 | tf_op jit(solution)/shard_map/ppermute | solution.py:276
  52.4 27.1 %copy-start.15 = (bf16[384,256]{1,0:T(8,128)(2,1)}, bf16[384,256]{1,0:T(8,128)(2,1)S(1)}, u32[]{:S(2)}) copy-start(bf16[384,256]{1,0:T(8,128)(2,1)S(1)} %collective-permute-done.7.refs_9_) | copy-start | bytes 589828
  52.4 7.3 %collective-permute-start.24 = (bf16[384,256]{1,0:T(8,128)(2,1)S(1)}, bf16[384,256]{1,0:T(8,128)(2,1)S(1)}, u32[]{:S(2)}, u32[]{:S(2)}) collective-permute-start(bf16[384,256]{1,0:T(8,128)(2,1)S(1)} %collective-permute-done.16.refs_18_), channel_id=1, source_target_pairs={{0,14},{2,0},{4,2},{6,4},{8,6},{10,8},{12,10},{14,12},{1,15},{3,1}... | collective-permute-start | bytes 589832 | tf_op jit(solution)/shard_map/ppermute | solution.py:272
  54.9 24.7 %copy-start.16 = (bf16[384,256]{1,0:T(8,128)(2,1)}, bf16[384,256]{1,0:T(8,128)(2,1)S(1)}, u32[]{:S(2)}) copy-start(bf16[384,256]{1,0:T(8,128)(2,1)S(1)} %collective-permute-done.20.refs_22_) | copy-start | bytes 589828
  54.9 6.3 %collective-permute-start.17 = (bf16[384,256]{1,0:T(8,128)(2,1)S(1)}, bf16[384,256]{1,0:T(8,128)(2,1)S(1)}, u32[]{:S(2)}, u32[]{:S(2)}) collective-permute-start(bf16[384,256]{1,0:T(8,128)(2,1)S(1)} %collective-permute-done.16.refs_18_), channel_id=1, source_target_pairs={{0,1},{1,0},{2,3},{3,2},{4,5},{5,4},{6,7},{7,6},{8,9},{9,8},{10,11... | collective-permute-start | bytes 589832 | tf_op jit(solution)/shard_map/ppermute | solution.py:276
  57.0 22.6 %copy-start.17 = (bf16[384,256]{1,0:T(8,128)(2,1)}, bf16[384,256]{1,0:T(8,128)(2,1)S(1)}, u32[]{:S(2)}) copy-start(bf16[384,256]{1,0:T(8,128)(2,1)S(1)} %collective-permute-done.13.refs_15_) | copy-start | bytes 589828
  57.0 7.9 %collective-permute-start.22 = (bf16[384,256]{1,0:T(8,128)(2,1)S(1)}, bf16[384,256]{1,0:T(8,128)(2,1)S(1)}, u32[]{:S(2)}, u32[]{:S(2)}) collective-permute-start(bf16[384,256]{1,0:T(8,128)(2,1)S(1)} %collective-permute-done.14.refs_16_), channel_id=1, source_target_pairs={{0,2},{2,4},{4,6},{6,8},{8,10},{10,12},{12,14},{14,0},{1,3},{3,5},... | collective-permute-start | bytes 589832 | tf_op jit(solution)/shard_map/ppermute | solution.py:272
  58.0 21.5 %copy-start.18 = (bf16[384,256]{1,0:T(8,128)(2,1)}, bf16[384,256]{1,0:T(8,128)(2,1)S(1)}, u32[]{:S(2)}) copy-start(bf16[384,256]{1,0:T(8,128)(2,1)S(1)} %collective-permute-done.18.refs_20_) | copy-start | bytes 589828
  58.0 6.9 %collective-permute-start.15 = (bf16[384,256]{1,0:T(8,128)(2,1)S(1)}, bf16[384,256]{1,0:T(8,128)(2,1)S(1)}, u32[]{:S(2)}, u32[]{:S(2)}) collective-permute-start(bf16[384,256]{1,0:T(8,128)(2,1)S(1)} %collective-permute-done.14.refs_16_), channel_id=1, source_target_pairs={{0,1},{1,0},{2,3},{3,2},{4,5},{5,4},{6,7},{7,6},{8,9},{9,8},{10,11... | collective-permute-start | bytes 589832 | tf_op jit(solution)/shard_map/ppermute | solution.py:276
  58.0 11.4 %copy-start.19 = (bf16[384,256]{1,0:T(8,128)(2,1)}, bf16[384,256]{1,0:T(8,128)(2,1)S(1)}, u32[]{:S(2)}) copy-start(bf16[384,256]{1,0:T(8,128)(2,1)S(1)} %collective-permute-done.11.refs_13_) | copy-start | bytes 589828
  58.0 7.4 %collective-permute-start.21 = (bf16[384,256]{1,0:T(8,128)(2,1)S(1)}, bf16[384,256]{1,0:T(8,128)(2,1)S(1)}, u32[]{:S(2)}, u32[]{:S(2)}) collective-permute-start(bf16[384,256]{1,0:T(8,128)(2,1)S(1)} %collective-permute-done.20.refs_22_), channel_id=1, source_target_pairs={{0,1},{1,0},{2,3},{3,2},{4,5},{5,4},{6,7},{7,6},{8,9},{9,8},{10,11... | collective-permute-start | bytes 589832 | tf_op jit(solution)/shard_map/ppermute | solution.py:276
  59.8 9.7 %copy-start.20 = (bf16[384,256]{1,0:T(8,128)(2,1)}, bf16[384,256]{1,0:T(8,128)(2,1)S(1)}, u32[]{:S(2)}) copy-start(bf16[384,256]{1,0:T(8,128)(2,1)S(1)} %collective-permute-done.24.refs_26_) | copy-start | bytes 589828
  59.8 9.1 %collective-permute-start.26 = (bf16[384,256]{1,0:T(8,128)(2,1)S(1)}, bf16[384,256]{1,0:T(8,128)(2,1)S(1)}, u32[]{:S(2)}, u32[]{:S(2)}) collective-permute-start(bf16[384,256]{1,0:T(8,128)(2,1)S(1)} %collective-permute-done.18.refs_20_), channel_id=1, source_target_pairs={{0,2},{2,4},{4,6},{6,8},{8,10},{10,12},{12,14},{14,0},{1,3},{3,5},... | collective-permute-start | bytes 589832 | tf_op jit(solution)/shard_map/ppermute | solution.py:272
  61.1 8.4 %copy-start.21 = (bf16[384,256]{1,0:T(8,128)(2,1)}, bf16[384,256]{1,0:T(8,128)(2,1)S(1)}, u32[]{:S(2)}) copy-start(bf16[384,256]{1,0:T(8,128)(2,1)S(1)} %collective-permute-done.17.refs_19_) | copy-start | bytes 589828
  61.1 7.7 %collective-permute-start.28 = (bf16[384,256]{1,0:T(8,128)(2,1)S(1)}, bf16[384,256]{1,0:T(8,128)(2,1)S(1)}, u32[]{:S(2)}, u32[]{:S(2)}) collective-permute-start(bf16[384,256]{1,0:T(8,128)(2,1)S(1)} %collective-permute-done.24.refs_26_), channel_id=1, source_target_pairs={{0,14},{2,0},{4,2},{6,4},{8,6},{10,8},{12,10},{14,12},{1,15},{3,1}... | collective-permute-start | bytes 589832 | tf_op jit(solution)/shard_map/ppermute | solution.py:272
  64.8 5.5 %copy-start.22 = (bf16[384,256]{1,0:T(8,128)(2,1)}, bf16[384,256]{1,0:T(8,128)(2,1)S(1)}, u32[]{:S(2)}) copy-start(bf16[384,256]{1,0:T(8,128)(2,1)S(1)} %collective-permute-done.22.refs_24_) | copy-start | bytes 589828
  64.8 4.6 %collective-permute-start.19 = (bf16[384,256]{1,0:T(8,128)(2,1)S(1)}, bf16[384,256]{1,0:T(8,128)(2,1)S(1)}, u32[]{:S(2)}, u32[]{:S(2)}) collective-permute-start(bf16[384,256]{1,0:T(8,128)(2,1)S(1)} %collective-permute-done.18.refs_20_), channel_id=1, source_target_pairs={{0,1},{1,0},{2,3},{3,2},{4,5},{5,4},{6,7},{7,6},{8,9},{9,8},{10,11... | collective-permute-start | bytes 589832 | tf_op jit(solution)/shard_map/ppermute | solution.py:276
  64.9 5.4 %copy-start.23 = (bf16[384,256]{1,0:T(8,128)(2,1)}, bf16[384,256]{1,0:T(8,128)(2,1)S(1)}, u32[]{:S(2)}) copy-start(bf16[384,256]{1,0:T(8,128)(2,1)S(1)} %collective-permute-done.15.refs_17_) | copy-start | bytes 589828
  64.9 4.6 %collective-permute-start.25 = (bf16[384,256]{1,0:T(8,128)(2,1)S(1)}, bf16[384,256]{1,0:T(8,128)(2,1)S(1)}, u32[]{:S(2)}, u32[]{:S(2)}) collective-permute-start(bf16[384,256]{1,0:T(8,128)(2,1)S(1)} %collective-permute-done.24.refs_26_), channel_id=1, source_target_pairs={{0,1},{1,0},{2,3},{3,2},{4,5},{5,4},{6,7},{7,6},{8,9},{9,8},{10,11... | collective-permute-start | bytes 589832 | tf_op jit(solution)/shard_map/ppermute | solution.py:276
  65.4 4.9 %copy-start.24 = (bf16[384,256]{1,0:T(8,128)(2,1)}, bf16[384,256]{1,0:T(8,128)(2,1)S(1)}, u32[]{:S(2)}) copy-start(bf16[384,256]{1,0:T(8,128)(2,1)S(1)} %collective-permute-done.21.refs_23_) | copy-start | bytes 589828
  65.4 4.1 %collective-permute-start.23 = (bf16[384,256]{1,0:T(8,128)(2,1)S(1)}, bf16[384,256]{1,0:T(8,128)(2,1)S(1)}, u32[]{:S(2)}, u32[]{:S(2)}) collective-permute-start(bf16[384,256]{1,0:T(8,128)(2,1)S(1)} %collective-permute-done.22.refs_24_), channel_id=1, source_target_pairs={{0,1},{1,0},{2,3},{3,2},{4,5},{5,4},{6,7},{7,6},{8,9},{9,8},{10,11... | collective-permute-start | bytes 589832 | tf_op jit(solution)/shard_map/ppermute | solution.py:276
  68.8 1.5 %copy-start.25 = (bf16[384,256]{1,0:T(8,128)(2,1)}, bf16[384,256]{1,0:T(8,128)(2,1)S(1)}, u32[]{:S(2)}) copy-start(bf16[384,256]{1,0:T(8,128)(2,1)S(1)} %collective-permute-done.26.refs_28_) | copy-start | bytes 589828
  68.8 1.4 %collective-permute-start.27 = (bf16[384,256]{1,0:T(8,128)(2,1)S(1)}, bf16[384,256]{1,0:T(8,128)(2,1)S(1)}, u32[]{:S(2)}, u32[]{:S(2)}) collective-permute-start(bf16[384,256]{1,0:T(8,128)(2,1)S(1)} %collective-permute-done.26.refs_28_), channel_id=1, source_target_pairs={{0,1},{1,0},{2,3},{3,2},{4,5},{5,4},{6,7},{7,6},{8,9},{9,8},{10,11... | collective-permute-start | bytes 589832 | tf_op jit(solution)/shard_map/ppermute | solution.py:276
  68.9 1.5 %copy-start.26 = (bf16[384,256]{1,0:T(8,128)(2,1)}, bf16[384,256]{1,0:T(8,128)(2,1)S(1)}, u32[]{:S(2)}) copy-start(bf16[384,256]{1,0:T(8,128)(2,1)S(1)} %collective-permute-done.28.refs_30_) | copy-start | bytes 589828
  68.9 2.2 %collective-permute-start.29 = (bf16[384,256]{1,0:T(8,128)(2,1)S(1)}, bf16[384,256]{1,0:T(8,128)(2,1)}, u32[]{:S(2)}, u32[]{:S(2)}) collective-permute-start(bf16[384,256]{1,0:T(8,128)(2,1)S(1)} %collective-permute-done.28.refs_30_), channel_id=1, source_target_pairs={{0,1},{1,0},{2,3},{3,2},{4,5},{5,4},{6,7},{7,6},{8,9},{9,8},{10,11... | collective-permute-start | bytes 589832 | tf_op jit(solution)/shard_map/ppermute | solution.py:276
  99.2 25.2 %all-to-all-start.1 = ((f32[16,8,384]{2,1,0:T(8,128)}), f32[16,8,384]{2,1,0:T(8,128)S(1)}, u32[]{:S(2)}, u32[]{:S(2)}) async-start(f32[16,8,384]{2,1,0:T(8,128)} %bitcast.10), calls=%async_computation.1 | async-start | bytes 393216 | tf_op jit(solution)/shard_map/all_to_all | solution.py:343
  106.4 5.6 %collective-permute-start.30 = (f32[96,128]{1,0:T(8,128)S(1)}, f32[96,128]{1,0:T(8,128)S(1)}, u32[]{:S(2)}, u32[]{:S(2)}) collective-permute-start(f32[96,128]{1,0:T(8,128)S(1)} %get-tuple-element.21), channel_id=1, source_target_pairs={{0,64},{64,128},{128,192},{192,0},{1,65},{65,129},{129,193},{193,1... | collective-permute-start | bytes 147464 | tf_op jit(solution)/shard_map/ppermute | solution.py:272
  107.8 5.6 %collective-permute-start.31 = (f32[96,128]{1,0:T(8,128)S(1)}, f32[96,128]{1,0:T(8,128)S(1)}, u32[]{:S(2)}, u32[]{:S(2)}) collective-permute-start(f32[96,128]{1,0:T(8,128)S(1)} %get-tuple-element.22), channel_id=1, source_target_pairs={{0,128},{64,192},{128,0},{192,64},{1,129},{65,193},{129,1},{193,65... | collective-permute-start | bytes 147464 | tf_op jit(solution)/shard_map/ppermute | solution.py:272
  110.6 4.1 %collective-permute-start.32 = (f32[96,128]{1,0:T(8,128)S(1)}, f32[96,128]{1,0:T(8,128)S(1)}, u32[]{:S(2)}, u32[]{:S(2)}) collective-permute-start(f32[96,128]{1,0:T(8,128)S(1)} %get-tuple-element.23), channel_id=1, source_target_pairs={{0,192},{64,0},{128,64},{192,128},{1,193},{65,1},{129,65},{193,129... | collective-permute-start | bytes 147464 | tf_op jit(solution)/shard_map/ppermute | solution.py:272
  116.1 4.3 %collective-permute-start.35 = (f32[96,128]{1,0:T(8,128)}, f32[96,128]{1,0:T(8,128)S(1)}, u32[]{:S(2)}, u32[]{:S(2)}) collective-permute-start(f32[96,128]{1,0:T(8,128)} %meet.1.refs_0_), channel_id=1, source_target_pairs={{0,48},{16,0},{32,16},{48,32},{1,49},{17,1},{33,17},{49,33},{2,50}... | collective-permute-start | bytes 147464 | tf_op jit(solution)/shard_map/ppermute | solution.py:272
  117.3 5.8 %collective-permute-start.34 = (f32[96,128]{1,0:T(8,128)}, f32[96,128]{1,0:T(8,128)S(1)}, u32[]{:S(2)}, u32[]{:S(2)}) collective-permute-start(f32[96,128]{1,0:T(8,128)} %meet.1.refs_0_), channel_id=1, source_target_pairs={{0,32},{16,48},{32,0},{48,16},{1,33},{17,49},{33,1},{49,17},{2,34}... | collective-permute-start | bytes 147464 | tf_op jit(solution)/shard_map/ppermute | solution.py:272
  118.9 5.5 %collective-permute-start.33 = (f32[96,128]{1,0:T(8,128)}, f32[96,128]{1,0:T(8,128)S(1)}, u32[]{:S(2)}, u32[]{:S(2)}) collective-permute-start(f32[96,128]{1,0:T(8,128)} %meet.1.refs_0_), channel_id=1, source_target_pairs={{0,16},{16,32},{32,48},{48,0},{1,17},{17,33},{33,49},{49,1},{2,18}... | collective-permute-start | bytes 147464 | tf_op jit(solution)/shard_map/ppermute | solution.py:272
  (6 other events, 4.7 us)
Sparse Core Ops, SparseCore 0:
  10.5 68.9 all-gather.2
